TPU v7x, 256 devices: a whole 4x4x8 slice. The times are simulated.
256 devices in a mesh: grp: 16 (over y, z_lo, core), orb: 16 (over x, z_hi).
Axes of the slice: x: 4, y: 4, z: 8 (z_hi: 4, z_lo: 2; z = z_hi * 2 + z_lo), core: 2. Of those that a mesh axis runs over, the one named last changes fastest.
Arguments:
- slabs: float32 [256, 256, 1024], P(('grp', 'orb')), may hold values from -0.9 to 0.9
- eps_occ: float32 [256], P(('grp', 'orb')), may hold values from -1.5 to -0.5
- eps_vir: float32 [256], replicated, may hold values from 0.2 to 3
Outputs:
- gradient: float32 [256, 256, 1024], P(('grp', 'orb'))
- density: float32 [256, 256], P('orb')
All inputs are finite; a program needn't handle non-finite values.
Results may differ from a plain program's by a relative error of at most 0.0003.
Values sent between devices are 32-bit elements; how exact they have to be, the bound alone decides.
No kernel may reach another device: no remote copies, remote signals or barrier semaphores. Data moves between devices by JAX's collectives and lax.ppermute only.
A program may use at most 64 MiB of HBM per device.

v0:
```python
import jax
import jax.numpy as jnp
from jax import lax
from jax.experimental import pallas as pl
from jax.experimental.pallas import tpu as pltpu
from jax.sharding import PartitionSpec as P


RING = 4
CUTS = (0, 32, 128, 224, 256)
VMEM = pl.BlockSpec(memory_space=pltpu.VMEM)
SMEM = pl.BlockSpec(memory_space=pltpu.SMEM)
F32, BF16 = jnp.float32, jnp.bfloat16


def shift(value, step):
    size = lax.axis_size("orb")
    pairs = [
        (at, at // RING * RING + (at % RING + step) % RING) for at in range(size)
    ]
    return lax.ppermute(value, "orb", pairs)


def split(x):
    high = x.astype(BF16)
    return high, (x - high.astype(F32)).astype(BF16)


def mm(a, b, contract):
    dims = ((contract, ((), ())))
    dot = lambda p, q: lax.dot_general(p, q, dims, preferred_element_type=F32)
    return dot(a[0], b[0]) + (dot(a[0], b[1]) + dot(a[1], b[0]))


ROWS = ((1,), (1,))
PLAIN = ((1,), (0,))


def fill(chunks, high, low):
    for at, chunk in enumerate(chunks):
        h, l = split(chunk[...])
        high[CUTS[at] : CUTS[at + 1], :] = h
        low[CUTS[at] : CUTS[at + 1], :] = l


def density_kernel(core, own, *refs):
    lows, highs, (r_low, r_high, r_mid) = refs[:4], refs[4:8], refs[8:11]
    keep, send, s_low, s_high = refs[11:15]
    oh, ol, lh, ll, hh, hl, dens = refs[15:]
    fill((own.at[a:b] for a, b in zip(CUTS[:-1], CUTS[1:])), oh, ol)
    fill(lows, lh, ll)
    fill(highs, hh, hl)
    o, l, h = (oh[...], ol[...]), (lh[...], ll[...]), (hh[...], hl[...])

    def term(left, right, recip):
        t = mm(left, right, ROWS) * recip[...]
        s = 2.0 * t - t.T
        return mm(split(t), split(s), ROWS), s

    total, s_low[...] = term(o, l, r_low)
    part, s_high[...] = term(o, h, r_high)
    total = total + part
    part, _ = term(l, h, r_mid)
    dens[...] = total + part
    mine = core[0] * 8
    for at in range(16):
        keep[at] = dens[pl.ds(pl.multiple_of(at * 16 + mine, 8), 8), :]
        send[at] = dens[pl.ds(pl.multiple_of(at * 16 + 8 - mine, 8), 8), :]


def near_kernel(*refs):
    lows, highs, (s_low, s_high, grad, lh, ll, hh, hl) = refs[:4], refs[4:8], refs[8:]
    fill(lows, lh, ll)
    fill(highs, hh, hl)
    grad[...] = mm(split(s_low[...]), (lh[...], ll[...]), PLAIN) + mm(
        split(s_high[...]), (hh[...], hl[...]), PLAIN
    )


def far_kernel(own, *refs):
    fars, (recip, near, grad, oh, ol, fh, fl) = refs[:4], refs[4:]
    fill((own.at[a:b] for a, b in zip(CUTS[:-1], CUTS[1:])), oh, ol)
    fill(fars, fh, fl)
    f = (fh[...], fl[...])
    t = mm((oh[...], ol[...]), f, ROWS) * recip[...]
    s = 2.0 * t - t.T
    grad[...] = near[...] + mm(split(s), f, PLAIN)


def call(kernel, out, n_split, extra, flops, args, scalars=0):
    v, n = 256, 1024
    shapes = tuple(jax.ShapeDtypeStruct(s, F32) for s in out)
    return pl.pallas_call(
        kernel,
        out_shape=shapes,
        in_specs=[SMEM] * scalars + [VMEM] * (len(args) - scalars),
        out_specs=tuple(VMEM for _ in out),
        scratch_shapes=[pltpu.VMEM((v, n), BF16)] * (2 * n_split)
        + [pltpu.VMEM(s, F32) for s in extra],
        cost_estimate=pl.CostEstimate(
            flops=flops, bytes_accessed=1 << 20, transcendentals=0
        ),
        compiler_params=pltpu.CompilerParams(vmem_limit_bytes=24 << 20),
    )(*args)


def body(slabs, eps_occ, eps_vir):
    own = slabs[0]
    v = own.shape[0]
    n_orb, n_grp = lax.axis_size("orb"), lax.axis_size("grp")
    chunks = [own[a:b] for a, b in zip(CUTS[:-1], CUTS[1:])]
    lows = [shift(chunks[i], 1) for i in range(4)]
    highs = [shift(chunks[i], -1) for i in range(4)]
    e_low = shift(eps_occ, 1)
    e_high = shift(eps_occ, -1)
    e_far = shift(eps_occ, 2)
    fars = [shift(lows[0], 1), shift(lows[1], 1)]
    fars += [shift(highs[2], -1), shift(highs[3], -1)]

    def recip(energy):
        return 1.0 / (energy - eps_vir[:, None] - eps_vir[None, :])

    r_low = recip(eps_occ[0] + e_low[0])
    r_high = recip(eps_occ[0] + e_high[0])
    r_mid = recip(e_low[0] + e_high[0])
    r_far = recip(eps_occ[0] + e_far[0])

    core = lax.rem(lax.axis_index("grp"), 2).astype(jnp.int32)[None]
    half = v // n_orb // 2
    piece = (n_orb, half, v)
    keep, send, s_low, s_high = call(
        density_kernel,
        (piece, piece, (v, v), (v, v)),
        3,
        ((v, v),),
        1 << 32,
        (core, own, *lows, *highs, r_low, r_high, r_mid),
        scalars=1,
    )
    other = lax.ppermute(send, "grp", [(i, i ^ 1) for i in range(n_grp)])
    pieces = lax.all_to_all(
        keep + other, "orb", split_axis=0, concat_axis=0, tiled=True
    )
    share = jnp.sum(pieces, axis=0) * (1.0 / (n_orb * n_grp))
    copies = lax.all_to_all(
        jnp.broadcast_to(share[None], (n_grp,) + share.shape),
        "grp",
        split_axis=0,
        concat_axis=0,
        tiled=True,
    )
    density = jnp.sum(copies.reshape(n_grp // 2, 2 * half, v), axis=0)

    (near,) = call(
        near_kernel, (own.shape,), 2, (), 1 << 31, (*lows, *highs, s_low, s_high)
    )
    (grad,) = call(far_kernel, (own.shape,), 2, (), 1 << 31, (own, *fars, r_far, near))
    return grad[None], density


def solution(mesh):
    placed = (P(("grp", "orb"), None, None), P(("grp", "orb")), P())
    return jax.shard_map(
        body,
        mesh=mesh,
        in_specs=placed,
        out_specs=(P(("grp", "orb"), None, None), P("orb", None)),
        check_vma=False,
    )
```

profile of v0, /device:TPU:2, one launch (start us, length us, event | category | flops | bytes accessed | tf_op | source)
XLA Modules:
  0.0 116.5 jit_solution(1580513112423935765)
XLA Ops:
  0.6 3.3 %collective-permute-start.13 = (f32[1]{0:T(128)}, f32[1]{0:T(128)}, u32[]{:S(2)}, u32[]{:S(2)}) collective-permute-start(f32[1]{0:T(128)} %param.4), channel_id=1, source_target_pairs={{0,1},{1,2},{2,3},{3,0},{4,5},{5,6},{6,7},{7,4},{8,9},{9,10},{10,1... | collective-permute-start | bytes 20 | tf_op jit(solution)/shard_map/ppermute | solution.py:21
  4.0 3.1 %collective-permute-start.14 = (f32[1]{0:T(128)}, f32[1]{0:T(128)}, u32[]{:S(2)}, u32[]{:S(2)}) collective-permute-start(f32[1]{0:T(128)} %param.4), channel_id=1, source_target_pairs={{0,3},{1,0},{2,1},{3,2},{4,7},{5,4},{6,5},{7,6},{8,11},{9,8},{10,9... | collective-permute-start | bytes 20 | tf_op jit(solution)/shard_map/ppermute | solution.py:21
  7.1 4.9 %collective-permute-start.8 = (f32[1]{0:T(128)}, f32[1]{0:T(128)}, u32[]{:S(2)}, u32[]{:S(2)}) collective-permute-start(f32[1]{0:T(128)} %param.4), channel_id=1, source_target_pairs={{0,2},{1,3},{2,0},{3,1},{4,6},{5,7},{6,4},{7,5},{8,10},{9,11},{10,... | collective-permute-start | bytes 20 | tf_op jit(solution)/shard_map/ppermute | solution.py:21
  12.0 1.0 slice_bitcast_fusion.2
  13.4 3.9 %collective-permute-start.6 = (f32[32,1024]{1,0:T(8,128)S(1)}, f32[32,1024]{1,0:T(8,128)S(1)}, u32[]{:S(2)}, u32[]{:S(2)}) collective-permute-start(f32[32,1024]{1,0:T(8,128)S(1)} %get-tuple-element.10), channel_id=1, source_target_pairs={{0,3},{1,0},{2,1},{3,2},{4,7},{5,4},{6,5},{7,6},{8,11},{9,8},{10,9... | collective-permute-start | bytes 393224 | tf_op jit(solution)/shard_map/ppermute | solution.py:21
  17.9 1.3 %slice_bitcast_fusion = (f32[96,1024]{1,0:T(8,128)S(1)}, f32[96,1024]{1,0:T(8,128)S(1)}) fusion(f32[1,256,1024]{2,1,0:T(8,128)} %param.3), kind=kLoop, calls=%fused_computation | loop fusion | bytes 1572864 | tf_op jit(solution)/shard_map/slice | solution.py:111
  20.0 4.2 %collective-permute-start.12 = (f32[96,1024]{1,0:T(8,128)S(1)}, f32[96,1024]{1,0:T(8,128)S(1)}, u32[]{:S(2)}, u32[]{:S(2)}) collective-permute-start(f32[96,1024]{1,0:T(8,128)S(1)} %get-tuple-element.13), channel_id=1, source_target_pairs={{0,3},{1,0},{2,1},{3,2},{4,7},{5,4},{6,5},{7,6},{8,11},{9,8},{10,9... | collective-permute-start | bytes 1179656 | tf_op jit(solution)/shard_map/ppermute | solution.py:21
  26.9 2.8 %collective-permute-start.9 = (f32[96,1024]{1,0:T(8,128)S(1)}, f32[96,1024]{1,0:T(8,128)S(1)}, u32[]{:S(2)}, u32[]{:S(2)}) collective-permute-start(f32[96,1024]{1,0:T(8,128)S(1)} %get-tuple-element.12), channel_id=1, source_target_pairs={{0,1},{1,2},{2,3},{3,0},{4,5},{5,6},{6,7},{7,4},{8,9},{9,10},{10,1... | collective-permute-start | bytes 1179656 | tf_op jit(solution)/shard_map/ppermute | solution.py:21
  29.8 0.7 copy-done.9
  30.5 30.7 %collective-permute-done.10.refs_3_ = f32[32,1024]{1,0:T(8,128)S(1)} collective-permute-done((f32[32,1024]{1,0:T(8,128)S(1)}, f32[32,1024]{1,0:T(8,128)S(1)}, u32[]{:S(2)}, u32[]{:S(2)}) %collective-permute-start.10) | collective-permute-done | bytes 131104 | tf_op jit(solution)/shard_map/ppermute | solution.py:21
  61.2 1.0 collective-permute-start.11
  62.4 4.7 %collective-permute-done.11.refs_4_ = f32[32,1024]{1,0:T(8,128)S(1)} collective-permute-done((f32[32,1024]{1,0:T(8,128)S(1)}, f32[32,1024]{1,0:T(8,128)S(1)}, u32[]{:S(2)}, u32[]{:S(2)}) %collective-permute-start.11) | collective-permute-done | bytes 131104 | tf_op jit(solution)/shard_map/ppermute | solution.py:21
  67.1 2.8 %shard_map.50 = (f32[16,8,256]{2,1,0:T(8,128)S(1)}, f32[16,8,256]{2,1,0:T(8,128)S(1)}, f32[256,256]{1,0:T(8,128)S(1)}, f32[256,256]{1,0:T(8,128)S(1)}) custom-call(s32[1]{0:T(128)} %bitcast.6.core, f32[256,1024]{1,0:T(8,128)S(1)} %bitcast.18, f32[32,1024]{1,0:T(8,128)S(1)} %collective-permute-done.refs_0_, f32[96,1024]{1,0:T(8,128)S(1)} %collective-permute-done.2.refs_1_, ...), custom_call_target="tpu_custom_call" | custom-call | flops 4294967296 | bytes 1048576 | tf_op jit(solution)/shard_map/pallas_call | solution.py:93
  70.0 0.7 copy-done.5
  70.7 0.7 copy-done.7
  71.4 1.3 %collective-permute-done.15 = f32[16,8,256]{2,1,0:T(8,128)S(1)} collective-permute-done((f32[16,8,256]{2,1,0:T(8,128)S(1)}, f32[16,8,256]{2,1,0:T(8,128)S(1)}, u32[]{:S(2)}, u32[]{:S(2)}) %collective-permute-start.15) | collective-permute-done | bytes 131104 | tf_op jit(solution)/shard_map/ppermute | solution.py:140
  73.4 8.0 %all-to-all-start = ((f32[16,8,256]{2,1,0:T(8,128)}), f32[16,8,256]{2,1,0:T(8,128)}, u32[]{:S(2)}, u32[]{:S(2)}) async-start(f32[16,8,256]{2,1,0:T(8,128)} %add.35), calls=%async_computation | async-start | bytes 262144 | tf_op jit(solution)/shard_map/all_to_all | solution.py:141
  81.4 2.4 %collective-permute-start.1 = (f32[32,1024]{1,0:T(8,128)S(1)}, f32[32,1024]{1,0:T(8,128)}, u32[]{:S(2)}, u32[]{:S(2)}) collective-permute-start(f32[32,1024]{1,0:T(8,128)S(1)} %collective-permute-done.refs_0_), channel_id=1, source_target_pairs={{0,1},{1,2},{2,3},{3,0},{4,5},{5,6},{6,7},{7,4},{8,9},{9,10},{10,1... | collective-permute-start | bytes 393224 | tf_op jit(solution)/shard_map/ppermute | solution.py:21
  83.8 1.8 %collective-permute-start.7 = (f32[32,1024]{1,0:T(8,128)S(1)}, f32[32,1024]{1,0:T(8,128)}, u32[]{:S(2)}, u32[]{:S(2)}) collective-permute-start(f32[32,1024]{1,0:T(8,128)S(1)} %collective-permute-done.6.refs_7_), channel_id=1, source_target_pairs={{0,3},{1,0},{2,1},{3,2},{4,7},{5,4},{6,5},{7,6},{8,11},{9,8},{10,9... | collective-permute-start | bytes 393224 | tf_op jit(solution)/shard_map/ppermute | solution.py:21
  85.5 1.8 %collective-permute-start.3 = (f32[96,1024]{1,0:T(8,128)S(1)}, f32[96,1024]{1,0:T(8,128)S(1)}, u32[]{:S(2)}, u32[]{:S(2)}) collective-permute-start(f32[96,1024]{1,0:T(8,128)S(1)} %collective-permute-done.2.refs_1_), channel_id=1, source_target_pairs={{0,1},{1,2},{2,3},{3,0},{4,5},{5,6},{6,7},{7,4},{8,9},{9,10},{10,1... | collective-permute-start | bytes 1179656 | tf_op jit(solution)/shard_map/ppermute | solution.py:21
  87.3 2.3 %collective-permute-start.5 = (f32[96,1024]{1,0:T(8,128)S(1)}, f32[96,1024]{1,0:T(8,128)}, u32[]{:S(2)}, u32[]{:S(2)}) collective-permute-start(f32[96,1024]{1,0:T(8,128)S(1)} %collective-permute-done.4.refs_6_), channel_id=1, source_target_pairs={{0,3},{1,0},{2,1},{3,2},{4,7},{5,4},{6,5},{7,6},{8,11},{9,8},{10,9... | collective-permute-start | bytes 1179656 | tf_op jit(solution)/shard_map/ppermute | solution.py:21
  89.7 1.4 %all-to-all-done = f32[16,8,256]{2,1,0:T(8,128)} async-done(((f32[16,8,256]{2,1,0:T(8,128)}), f32[16,8,256]{2,1,0:T(8,128)}, u32[]{:S(2)}, u32[]{:S(2)}) %all-to-all-start) | async-done | bytes 131104 | tf_op jit(solution)/shard_map/all_to_all | solution.py:141
  91.1 0.9 reduce_sum.18
  92.7 5.6 %all-to-all-start.1 = ((f32[16,8,256]{2,1,0:T(8,128)}), f32[16,8,256]{2,1,0:T(8,128)}, u32[]{:S(2)}, u32[]{:S(2)}) async-start(f32[16,8,256]{2,1,0:T(8,128)} %broadcast_in_dim.8), calls=%async_computation.1 | async-start | bytes 262144 | tf_op jit(solution)/shard_map/all_to_all | solution.py:145
  98.3 0.9 copy-done.2
  99.2 0.9 copy-done.4
  100.1 0.9 copy-done.6
  101.1 0.9 copy-done.8
  102.0 1.0 shard_map.51.refs_5_
  103.1 7.9 %collective-permute-done.5.refs_2_ = f32[96,1024]{1,0:T(8,128)} collective-permute-done((f32[96,1024]{1,0:T(8,128)S(1)}, f32[96,1024]{1,0:T(8,128)}, u32[]{:S(2)}, u32[]{:S(2)}) %collective-permute-start.5) | collective-permute-done | bytes 393248 | tf_op jit(solution)/shard_map/ppermute | solution.py:21
  110.9 4.0 %shard_map.52 = f32[256,1024]{1,0:T(8,128)} custom-call(f32[256,1024]{1,0:T(8,128)S(1)} %bitcast.19, f32[32,1024]{1,0:T(8,128)} %collective-permute-done.1.refs_0_, f32[96,1024]{1,0:T(8,128)S(1)} %collective-permute-done.3.refs_1_, f32[96,1024]{1,0:T(8,128)} %collective-permute-done.5.refs_2_, f32[32,1024]{1,0:T(8,128)} %collective-permute-done.7.refs_3_, ...), custom_call_target="tpu_custom_call" | custom-call | flops 2147483648 | bytes 1048576 | tf_op jit(solution)/shard_map/pallas_call | solution.py:93
  114.9 1.5 %bitcast_reduce_fusion = f32[16,256]{1,0:T(8,128)} fusion(f32[8,16,256]{2,1,0:T(8,128)} %bitcast.17), kind=kLoop, calls=%fused_computation.6 | loop fusion | flops 28672 | bytes 147456 | tf_op jit(solution)/shard_map/reduce_sum | solution.py:152
  (36 shorter events, 2.4 us)
Async XLA Ops:
  0.6 18.5 %collective-permute-start.13 = (f32[1]{0:T(128)}, f32[1]{0:T(128)}, u32[]{:S(2)}, u32[]{:S(2)}) collective-permute-start(f32[1]{0:T(128)} %param.4), channel_id=1, source_target_pairs={{0,1},{1,2},{2,3},{3,0},{4,5},{5,6},{6,7},{7,4},{8,9},{9,10},{10,1... | collective-permute-start | bytes 20 | tf_op jit(solution)/shard_map/ppermute | solution.py:21
  4.0 16.0 %collective-permute-start.14 = (f32[1]{0:T(128)}, f32[1]{0:T(128)}, u32[]{:S(2)}, u32[]{:S(2)}) collective-permute-start(f32[1]{0:T(128)} %param.4), channel_id=1, source_target_pairs={{0,3},{1,0},{2,1},{3,2},{4,7},{5,4},{6,5},{7,6},{8,11},{9,8},{10,9... | collective-permute-start | bytes 20 | tf_op jit(solution)/shard_map/ppermute | solution.py:21
  7.1 18.9 %collective-permute-start.8 = (f32[1]{0:T(128)}, f32[1]{0:T(128)}, u32[]{:S(2)}, u32[]{:S(2)}) collective-permute-start(f32[1]{0:T(128)} %param.4), channel_id=1, source_target_pairs={{0,2},{1,3},{2,0},{3,1},{4,6},{5,7},{6,4},{7,5},{8,10},{9,11},{10,... | collective-permute-start | bytes 20 | tf_op jit(solution)/shard_map/ppermute | solution.py:21
  13.0 13.9 %collective-permute-start = (f32[32,1024]{1,0:T(8,128)S(1)}, f32[32,1024]{1,0:T(8,128)S(1)}, u32[]{:S(2)}, u32[]{:S(2)}) collective-permute-start(f32[32,1024]{1,0:T(8,128)S(1)} %get-tuple-element.11), channel_id=1, source_target_pairs={{0,1},{1,2},{2,3},{3,0},{4,5},{5,6},{6,7},{7,4},{8,9},{9,10},{10,1... | collective-permute-start | bytes 393224 | tf_op jit(solution)/shard_map/ppermute | solution.py:21
  13.4 16.4 %collective-permute-start.6 = (f32[32,1024]{1,0:T(8,128)S(1)}, f32[32,1024]{1,0:T(8,128)S(1)}, u32[]{:S(2)}, u32[]{:S(2)}) collective-permute-start(f32[32,1024]{1,0:T(8,128)S(1)} %get-tuple-element.10), channel_id=1, source_target_pairs={{0,3},{1,0},{2,1},{3,2},{4,7},{5,4},{6,5},{7,6},{8,11},{9,8},{10,9... | collective-permute-start | bytes 393224 | tf_op jit(solution)/shard_map/ppermute | solution.py:21
  17.9 49.2 %copy-start = (f32[1,256,1024]{2,1,0:T(8,128)S(1)}, f32[1,256,1024]{2,1,0:T(8,128)}, u32[]{:S(2)}) copy-start(f32[1,256,1024]{2,1,0:T(8,128)} %param.3) | copy-start | bytes 3145732
  19.2 47.9 %collective-permute-start.2 = (f32[96,1024]{1,0:T(8,128)S(1)}, f32[96,1024]{1,0:T(8,128)S(1)}, u32[]{:S(2)}, u32[]{:S(2)}) collective-permute-start(f32[96,1024]{1,0:T(8,128)S(1)} %get-tuple-element.13), channel_id=1, source_target_pairs={{0,1},{1,2},{2,3},{3,0},{4,5},{5,6},{6,7},{7,4},{8,9},{9,10},{10,1... | collective-permute-start | bytes 1179656 | tf_op jit(solution)/shard_map/ppermute | solution.py:21
  20.0 47.1 %collective-permute-start.12 = (f32[96,1024]{1,0:T(8,128)S(1)}, f32[96,1024]{1,0:T(8,128)S(1)}, u32[]{:S(2)}, u32[]{:S(2)}) collective-permute-start(f32[96,1024]{1,0:T(8,128)S(1)} %get-tuple-element.13), channel_id=1, source_target_pairs={{0,3},{1,0},{2,1},{3,2},{4,7},{5,4},{6,5},{7,6},{8,11},{9,8},{10,9... | collective-permute-start | bytes 1179656 | tf_op jit(solution)/shard_map/ppermute | solution.py:21
  26.0 41.1 %collective-permute-start.4 = (f32[96,1024]{1,0:T(8,128)S(1)}, f32[96,1024]{1,0:T(8,128)S(1)}, u32[]{:S(2)}, u32[]{:S(2)}) collective-permute-start(f32[96,1024]{1,0:T(8,128)S(1)} %get-tuple-element.12), channel_id=1, source_target_pairs={{0,3},{1,0},{2,1},{3,2},{4,7},{5,4},{6,5},{7,6},{8,11},{9,8},{10,9... | collective-permute-start | bytes 1179656 | tf_op jit(solution)/shard_map/ppermute | solution.py:21
  26.9 40.2 %collective-permute-start.9 = (f32[96,1024]{1,0:T(8,128)S(1)}, f32[96,1024]{1,0:T(8,128)S(1)}, u32[]{:S(2)}, u32[]{:S(2)}) collective-permute-start(f32[96,1024]{1,0:T(8,128)S(1)} %get-tuple-element.12), channel_id=1, source_target_pairs={{0,1},{1,2},{2,3},{3,0},{4,5},{5,6},{6,7},{7,4},{8,9},{9,10},{10,1... | collective-permute-start | bytes 1179656 | tf_op jit(solution)/shard_map/ppermute | solution.py:21
  29.7 31.5 %collective-permute-start.10 = (f32[32,1024]{1,0:T(8,128)S(1)}, f32[32,1024]{1,0:T(8,128)S(1)}, u32[]{:S(2)}, u32[]{:S(2)}) collective-permute-start(f32[32,1024]{1,0:T(8,128)S(1)} %get-tuple-element.10), channel_id=1, source_target_pairs={{0,1},{1,2},{2,3},{3,0},{4,5},{5,6},{6,7},{7,4},{8,9},{9,10},{10,1... | collective-permute-start | bytes 393224 | tf_op jit(solution)/shard_map/ppermute | solution.py:21
  29.8 0.7 copy-start.9
  61.2 5.9 %copy-start.1 = (f32[32,1024]{1,0:T(8,128)}, f32[32,1024]{1,0:T(8,128)S(1)}, u32[]{:S(2)}) copy-start(f32[32,1024]{1,0:T(8,128)S(1)} %collective-permute-done.10.refs_3_) | copy-start | bytes 393220
  61.2 5.9 %collective-permute-start.11 = (f32[32,1024]{1,0:T(8,128)S(1)}, f32[32,1024]{1,0:T(8,128)S(1)}, u32[]{:S(2)}, u32[]{:S(2)}) collective-permute-start(f32[32,1024]{1,0:T(8,128)S(1)} %get-tuple-element.11), channel_id=1, source_target_pairs={{0,3},{1,0},{2,1},{3,2},{4,7},{5,4},{6,5},{7,6},{8,11},{9,8},{10,9... | collective-permute-start | bytes 393224 | tf_op jit(solution)/shard_map/ppermute | solution.py:21
  67.1 2.9 %copy-start.3 = (f32[32,1024]{1,0:T(8,128)}, f32[32,1024]{1,0:T(8,128)S(1)}, u32[]{:S(2)}) copy-start(f32[32,1024]{1,0:T(8,128)S(1)} %collective-permute-done.11.refs_4_) | copy-start | bytes 393220
  70.0 0.7 copy-start.5
  70.7 0.7 copy-start.7
  71.4 1.3 %collective-permute-start.15 = (f32[16,8,256]{2,1,0:T(8,128)S(1)}, f32[16,8,256]{2,1,0:T(8,128)S(1)}, u32[]{:S(2)}, u32[]{:S(2)}) collective-permute-start(f32[16,8,256]{2,1,0:T(8,128)S(1)} %get-tuple-element.9), channel_id=1, source_target_pairs={{0,16},{16,0},{32,48},{48,32},{64,80},{80,64},{96,112},{112,96},{1... | collective-permute-start | bytes 393224 | tf_op jit(solution)/shard_map/ppermute | solution.py:140
  73.4 17.7 %all-to-all-start = ((f32[16,8,256]{2,1,0:T(8,128)}), f32[16,8,256]{2,1,0:T(8,128)}, u32[]{:S(2)}, u32[]{:S(2)}) async-start(f32[16,8,256]{2,1,0:T(8,128)} %add.35), calls=%async_computation | async-start | bytes 262144 | tf_op jit(solution)/shard_map/all_to_all | solution.py:141
  81.4 21.6 %collective-permute-start.1 = (f32[32,1024]{1,0:T(8,128)S(1)}, f32[32,1024]{1,0:T(8,128)}, u32[]{:S(2)}, u32[]{:S(2)}) collective-permute-start(f32[32,1024]{1,0:T(8,128)S(1)} %collective-permute-done.refs_0_), channel_id=1, source_target_pairs={{0,1},{1,2},{2,3},{3,0},{4,5},{5,6},{6,7},{7,4},{8,9},{9,10},{10,1... | collective-permute-start | bytes 393224 | tf_op jit(solution)/shard_map/ppermute | solution.py:21
  83.8 19.3 %collective-permute-start.7 = (f32[32,1024]{1,0:T(8,128)S(1)}, f32[32,1024]{1,0:T(8,128)}, u32[]{:S(2)}, u32[]{:S(2)}) collective-permute-start(f32[32,1024]{1,0:T(8,128)S(1)} %collective-permute-done.6.refs_7_), channel_id=1, source_target_pairs={{0,3},{1,0},{2,1},{3,2},{4,7},{5,4},{6,5},{7,6},{8,11},{9,8},{10,9... | collective-permute-start | bytes 393224 | tf_op jit(solution)/shard_map/ppermute | solution.py:21
  85.5 17.5 %collective-permute-start.3 = (f32[96,1024]{1,0:T(8,128)S(1)}, f32[96,1024]{1,0:T(8,128)S(1)}, u32[]{:S(2)}, u32[]{:S(2)}) collective-permute-start(f32[96,1024]{1,0:T(8,128)S(1)} %collective-permute-done.2.refs_1_), channel_id=1, source_target_pairs={{0,1},{1,2},{2,3},{3,0},{4,5},{5,6},{6,7},{7,4},{8,9},{9,10},{10,1... | collective-permute-start | bytes 1179656 | tf_op jit(solution)/shard_map/ppermute | solution.py:21
  87.3 23.6 %collective-permute-start.5 = (f32[96,1024]{1,0:T(8,128)S(1)}, f32[96,1024]{1,0:T(8,128)}, u32[]{:S(2)}, u32[]{:S(2)}) collective-permute-start(f32[96,1024]{1,0:T(8,128)S(1)} %collective-permute-done.4.refs_6_), channel_id=1, source_target_pairs={{0,3},{1,0},{2,1},{3,2},{4,7},{5,4},{6,5},{7,6},{8,11},{9,8},{10,9... | collective-permute-start | bytes 1179656 | tf_op jit(solution)/shard_map/ppermute | solution.py:21
  92.7 22.2 %all-to-all-start.1 = ((f32[16,8,256]{2,1,0:T(8,128)}), f32[16,8,256]{2,1,0:T(8,128)}, u32[]{:S(2)}, u32[]{:S(2)}) async-start(f32[16,8,256]{2,1,0:T(8,128)} %broadcast_in_dim.8), calls=%async_computation.1 | async-start | bytes 262144 | tf_op jit(solution)/shard_map/all_to_all | solution.py:145
  98.3 0.9 copy-start.2
  99.2 0.9 copy-start.4
  100.1 0.9 copy-start.6
  101.1 0.9 copy-start.8
where the time goes:
time: 117 us; the launch traced here: 116 us
  waiting for transfers between devices  46.3 us (40%)
  starting transfers between devices  45.8 us (39%)
  local copies, waits for them, and re-layouts  8.69 us (7%)
  Pallas kernels  7.84 us (7%)
  between operations  4.6 us (4%)
  other arithmetic  3.32 us (3%)
    ppermute x15, waiting for transfers between devices, shift(): return lax.ppermute(value, 'orb', pairs)  43.5 us
    ppermute x15, starting transfers between devices, shift(): return lax.ppermute(value, 'orb', pairs)  32.1 us
    all_to_all x1, starting transfers between devices, body(): lax.all_to_all(keep + other, 'orb', split_axis=0, concat_axis=0, tiled=True)  8.02 us
    pallas_call x3, Pallas kernels, call(): pl.pallas_call(kernel, out_shape=shapes, in_specs=[SMEM] * scalars + [VME...  7.84 us
    unnamed x20, local copies, waits for them, and re-layouts  5.79 us
    all_to_all x1, starting transfers between devices, body(): lax.all_to_all(jnp.broadcast_to(share[None], (n_grp,) + share.shape), 'gr...  5.62 us
  transfers between devices with their start and end apart: 18, of which 6 were waited for; matrix products, arithmetic and copies ran while one was open for 3% of the time, Pallas kernels for 4%

commit v1 on v0

--- a/solution.py
+++ b/solution.py
@@ -7,7 +7,8 @@
 
 
 RING = 4
-CUTS = (0, 32, 128, 224, 256)
+CUTS = (0, 128, 256)
+FAR = (0, 32, 128)
 VMEM = pl.BlockSpec(memory_space=pltpu.VMEM)
 SMEM = pl.BlockSpec(memory_space=pltpu.SMEM)
 F32, BF16 = jnp.float32, jnp.bfloat16
@@ -37,54 +38,55 @@
 
 
 def fill(chunks, high, low):
-    for at, chunk in enumerate(chunks):
-        h, l = split(chunk[...])
-        high[CUTS[at] : CUTS[at + 1], :] = h
-        low[CUTS[at] : CUTS[at + 1], :] = l
+    at = 0
+    for chunk in chunks:
+        end = at + chunk.shape[0]
+        high[at:end, :], low[at:end, :] = split(chunk[...])
+        at = end
 
 
 def density_kernel(core, own, *refs):
-    lows, highs, (r_low, r_high, r_mid) = refs[:4], refs[4:8], refs[8:11]
-    keep, send, s_low, s_high = refs[11:15]
-    oh, ol, lh, ll, hh, hl, dens = refs[15:]
-    fill((own.at[a:b] for a, b in zip(CUTS[:-1], CUTS[1:])), oh, ol)
+    lows, highs, (r_low, r_high, r_mid) = refs[:2], refs[2:4], refs[4:7]
+    keep, send, oh, ol, lh, ll, hh, hl, dens = refs[7:]
+    fill((own,), oh, ol)
     fill(lows, lh, ll)
     fill(highs, hh, hl)
     o, l, h = (oh[...], ol[...]), (lh[...], ll[...]), (hh[...], hl[...])
 
     def term(left, right, recip):
         t = mm(left, right, ROWS) * recip[...]
-        s = 2.0 * t - t.T
-        return mm(split(t), split(s), ROWS), s
+        return mm(split(t), split(2.0 * t - t.T), ROWS)
 
-    total, s_low[...] = term(o, l, r_low)
-    part, s_high[...] = term(o, h, r_high)
-    total = total + part
-    part, _ = term(l, h, r_mid)
-    dens[...] = total + part
+    dens[...] = term(o, l, r_low) + term(o, h, r_high) + term(l, h, r_mid)
     mine = core[0] * 8
     for at in range(16):
         keep[at] = dens[pl.ds(pl.multiple_of(at * 16 + mine, 8), 8), :]
         send[at] = dens[pl.ds(pl.multiple_of(at * 16 + 8 - mine, 8), 8), :]
 
 
-def near_kernel(*refs):
-    lows, highs, (s_low, s_high, grad, lh, ll, hh, hl) = refs[:4], refs[4:8], refs[8:]
+def gradient(own, other, recip):
+    t = mm(own, other, ROWS) * recip[...]
+    return mm(split(2.0 * t - t.T), other, PLAIN)
+
+
+def near_kernel(own, *refs):
+    lows, highs, (r_low, r_high, grad, oh, ol, lh, ll, hh, hl) = (
+        refs[:2],
+        refs[2:4],
+        refs[4:],
+    )
+    fill((own,), oh, ol)
     fill(lows, lh, ll)
     fill(highs, hh, hl)
-    grad[...] = mm(split(s_low[...]), (lh[...], ll[...]), PLAIN) + mm(
-        split(s_high[...]), (hh[...], hl[...]), PLAIN
-    )
+    o, l, h = (oh[...], ol[...]), (lh[...], ll[...]), (hh[...], hl[...])
+    grad[...] = gradient(o, l, r_low) + gradient(o, h, r_high)
 
 
 def far_kernel(own, *refs):
     fars, (recip, near, grad, oh, ol, fh, fl) = refs[:4], refs[4:]
-    fill((own.at[a:b] for a, b in zip(CUTS[:-1], CUTS[1:])), oh, ol)
+    fill((own,), oh, ol)
     fill(fars, fh, fl)
-    f = (fh[...], fl[...])
-    t = mm((oh[...], ol[...]), f, ROWS) * recip[...]
-    s = 2.0 * t - t.T
-    grad[...] = near[...] + mm(split(s), f, PLAIN)
+    grad[...] = near[...] + gradient((oh[...], ol[...]), (fh[...], fl[...]), recip)
 
 
 def call(kernel, out, n_split, extra, flops, args, scalars=0):
@@ -100,7 +102,7 @@
         cost_estimate=pl.CostEstimate(
             flops=flops, bytes_accessed=1 << 20, transcendentals=0
         ),
-        compiler_params=pltpu.CompilerParams(vmem_limit_bytes=24 << 20),
+        compiler_params=pltpu.CompilerParams(vmem_limit_bytes=20 << 20),
     )(*args)
 
 
@@ -109,13 +111,14 @@
     v = own.shape[0]
     n_orb, n_grp = lax.axis_size("orb"), lax.axis_size("grp")
     chunks = [own[a:b] for a, b in zip(CUTS[:-1], CUTS[1:])]
-    lows = [shift(chunks[i], 1) for i in range(4)]
-    highs = [shift(chunks[i], -1) for i in range(4)]
+    lows = [shift(chunks[i], 1) for i in range(2)]
+    highs = [shift(chunks[i], -1) for i in range(2)]
     e_low = shift(eps_occ, 1)
     e_high = shift(eps_occ, -1)
     e_far = shift(eps_occ, 2)
-    fars = [shift(lows[0], 1), shift(lows[1], 1)]
-    fars += [shift(highs[2], -1), shift(highs[3], -1)]
+    cut = FAR[1]
+    fars = [shift(lows[0][:cut], 1), shift(lows[0][cut:], 1)]
+    fars += [shift(highs[1][:-cut], -1), shift(highs[1][-cut:], -1)]
 
     def recip(energy):
         return 1.0 / (energy - eps_vir[:, None] - eps_vir[None, :])
@@ -128,9 +131,9 @@
     core = lax.rem(lax.axis_index("grp"), 2).astype(jnp.int32)[None]
     half = v // n_orb // 2
     piece = (n_orb, half, v)
-    keep, send, s_low, s_high = call(
+    keep, send = call(
         density_kernel,
-        (piece, piece, (v, v), (v, v)),
+        (piece, piece),
         3,
         ((v, v),),
         1 << 32,
@@ -152,7 +155,7 @@
     density = jnp.sum(copies.reshape(n_grp // 2, 2 * half, v), axis=0)
 
     (near,) = call(
-        near_kernel, (own.shape,), 2, (), 1 << 31, (*lows, *highs, s_low, s_high)
+        near_kernel, (own.shape,), 3, (), 1 << 31, (own, *lows, *highs, r_low, r_high)
     )
     (grad,) = call(far_kernel, (own.shape,), 2, (), 1 << 31, (own, *fars, r_far, near))
     return grad[None], density

time: 117 us -> 120 us (1.026)
  starting transfers between devices: 45.8 us -> 55.5 us
  waiting for transfers between devices: 46.3 us -> 38.1 us
  Pallas kernels: 7.84 us -> 12 us
  local copies, waits for them, and re-layouts: 8.69 us -> 5.83 us
    ppermute x15 -> x11, starting transfers between devices: 32.1 us -> 41.4 us  [shift(): return lax.ppermute(value, 'orb', pairs)]
    ppermute x15 -> x11, waiting for transfers between devices: 43.5 us -> 36.7 us  [shift(): return lax.ppermute(value, 'orb', pairs)]
    unnamed x20 -> x4, local copies, waits for them, and re-layouts: 5.79 us -> 0.01 us
    pallas_call x3, Pallas kernels: 7.84 us -> 12 us  [call(): pl.pallas_call(kernel, out_shape=shapes, in_specs=[SMEM] * scalars + [VME...]
    slice x0 -> x4, local copies, waits for them, and re-layouts: none -> 2.87 us  [the longest x2 1.44 us: body(): fars += [shift(highs[1][:-cut], -1), shift(highs[1][-cut:], -1)]]
    all_to_all x1, waiting for transfers between devices: 1.44 us -> 0.01 us  [body(): lax.all_to_all(keep + other, 'orb', split_axis=0, concat_axis=0, tiled=True)]
    all_to_all x1, starting transfers between devices: 8.02 us -> 9.37 us  [body(): lax.all_to_all(keep + other, 'orb', split_axis=0, concat_axis=0, tiled=True)]
  transfers between devices with their start and end apart: 18 -> 14, of which waited for: 6 -> 6; matrix products, arithmetic and copies ran while one was open for 3% -> 4% of each run, Pallas kernels for 4% -> 7%
where the time goes in v1:
time: 120 us; the launch traced here: 119 us
  starting transfers between devices  55.5 us (46%)
  waiting for transfers between devices  38.1 us (32%)
  Pallas kernels  12 us (10%)
  local copies, waits for them, and re-layouts  5.83 us (5%)
  between operations  4.42 us (4%)
  other arithmetic  3.34 us (3%)
    ppermute x11, starting transfers between devices, shift(): return lax.ppermute(value, 'orb', pairs)  41.4 us
    ppermute x11, waiting for transfers between devices, shift(): return lax.ppermute(value, 'orb', pairs)  36.7 us
    pallas_call x3, Pallas kernels, call(): pl.pallas_call(kernel, out_shape=shapes, in_specs=[SMEM] * scalars + [VME...  12 us
    all_to_all x1, starting transfers between devices, body(): lax.all_to_all(keep + other, 'orb', split_axis=0, concat_axis=0, tiled=True)  9.37 us
    all_to_all x1, starting transfers between devices, body(): lax.all_to_all(jnp.broadcast_to(share[None], (n_grp,) + share.shape), 'gr...  4.64 us
  transfers between devices with their start and end apart: 14, of which 6 were waited for; matrix products, arithmetic and copies ran while one was open for 4% of the time, Pallas kernels for 7%

profile of v1, /device:TPU:2, one launch (start us, length us, event | category | flops | bytes accessed | tf_op | source)
XLA Modules:
  0.0 119.1 jit_solution(10010101829727674928)
XLA Ops:
  0.6 2.3 %slice_bitcast_fusion = (f32[128,1024]{1,0:T(8,128)}, f32[128,1024]{1,0:T(8,128)}) fusion(f32[1,256,1024]{2,1,0:T(8,128)} %param.3), kind=kLoop, calls=%fused_computation | loop fusion | bytes 2097152 | tf_op jit(solution)/shard_map/slice | solution.py:113
  2.9 3.3 %collective-permute-start = (f32[128,1024]{1,0:T(8,128)}, f32[128,1024]{1,0:T(8,128)S(1)}, u32[]{:S(2)}, u32[]{:S(2)}) collective-permute-start(f32[128,1024]{1,0:T(8,128)} %get-tuple-element.7), channel_id=1, source_target_pairs={{0,1},{1,2},{2,3},{3,0},{4,5},{5,6},{6,7},{7,4},{8,9},{9,10},{10,1... | collective-permute-start | bytes 1572872 | tf_op jit(solution)/shard_map/ppermute | solution.py:22
  6.2 3.0 %collective-permute-start.3 = (f32[128,1024]{1,0:T(8,128)}, f32[128,1024]{1,0:T(8,128)S(1)}, u32[]{:S(2)}, u32[]{:S(2)}) collective-permute-start(f32[128,1024]{1,0:T(8,128)} %get-tuple-element.6), channel_id=1, source_target_pairs={{0,3},{1,0},{2,1},{3,2},{4,7},{5,4},{6,5},{7,6},{8,11},{9,8},{10,9... | collective-permute-start | bytes 1572872 | tf_op jit(solution)/shard_map/ppermute | solution.py:22
  9.2 1.5 %collective-permute-start.7 = (f32[128,1024]{1,0:T(8,128)}, f32[128,1024]{1,0:T(8,128)S(1)}, u32[]{:S(2)}, u32[]{:S(2)}) collective-permute-start(f32[128,1024]{1,0:T(8,128)} %get-tuple-element.6), channel_id=1, source_target_pairs={{0,1},{1,2},{2,3},{3,0},{4,5},{5,6},{6,7},{7,4},{8,9},{9,10},{10,1... | collective-permute-start | bytes 1572872 | tf_op jit(solution)/shard_map/ppermute | solution.py:22
  10.7 2.7 %collective-permute-start.8 = (f32[128,1024]{1,0:T(8,128)}, f32[128,1024]{1,0:T(8,128)}, u32[]{:S(2)}, u32[]{:S(2)}) collective-permute-start(f32[128,1024]{1,0:T(8,128)} %get-tuple-element.7), channel_id=1, source_target_pairs={{0,3},{1,0},{2,1},{3,2},{4,7},{5,4},{6,5},{7,6},{8,11},{9,8},{10,9... | collective-permute-start | bytes 1572872 | tf_op jit(solution)/shard_map/ppermute | solution.py:22
  13.4 1.5 %collective-permute-start.9 = (f32[1]{0:T(128)}, f32[1]{0:T(128)}, u32[]{:S(2)}, u32[]{:S(2)}) collective-permute-start(f32[1]{0:T(128)} %param.4), channel_id=1, source_target_pairs={{0,1},{1,2},{2,3},{3,0},{4,5},{5,6},{6,7},{7,4},{8,9},{9,10},{10,1... | collective-permute-start | bytes 20 | tf_op jit(solution)/shard_map/ppermute | solution.py:22
  15.5 26.2 %collective-permute-done.9 = f32[1]{0:T(128)} collective-permute-done((f32[1]{0:T(128)}, f32[1]{0:T(128)}, u32[]{:S(2)}, u32[]{:S(2)}) %collective-permute-start.9) | collective-permute-done | bytes 36 | tf_op jit(solution)/shard_map/ppermute | solution.py:22
  41.7 16.2 %collective-permute-start.10 = (f32[1]{0:T(128)}, f32[1]{0:T(128)}, u32[]{:S(2)}, u32[]{:S(2)}) collective-permute-start(f32[1]{0:T(128)} %param.4), channel_id=1, source_target_pairs={{0,3},{1,0},{2,1},{3,2},{4,7},{5,4},{6,5},{7,6},{8,11},{9,8},{10,9... | collective-permute-start | bytes 20 | tf_op jit(solution)/shard_map/ppermute | solution.py:22
  58.5 0.8 collective-permute-done.10
  59.3 5.1 %collective-permute-start.6 = (f32[1]{0:T(128)}, f32[1]{0:T(128)}, u32[]{:S(2)}, u32[]{:S(2)}) collective-permute-start(f32[1]{0:T(128)} %param.4), channel_id=1, source_target_pairs={{0,2},{1,3},{2,0},{3,1},{4,6},{5,7},{6,4},{7,5},{8,10},{9,11},{10,... | collective-permute-start | bytes 20 | tf_op jit(solution)/shard_map/ppermute | solution.py:22
  66.2 0.8 collective-permute-done.6
  67.6 0.2 subtract_divide_fusion
  67.9 3.9 %shard_map.52 = (f32[16,8,256]{2,1,0:T(8,128)S(1)}, f32[16,8,256]{2,1,0:T(8,128)S(1)}) custom-call(s32[1]{0:T(128)} %bitcast.7.core, f32[256,1024]{1,0:T(8,128)S(1)} %bitcast.14, f32[128,1024]{1,0:T(8,128)S(1)} %collective-permute-done.refs_0_, f32[128,1024]{1,0:T(8,128)S(1)} %collective-permute-done.7.refs_1_, f32[128,1024]{1,0:T(8,128)} %collective-permute-done.8.refs_2_, ...), custom_call_target="tpu_custom_call" | custom-call | flops 4294967296 | bytes 1048576 | tf_op jit(solution)/shard_map/pallas_call | solution.py:95
  71.8 1.3 %collective-permute-done.11 = f32[16,8,256]{2,1,0:T(8,128)S(1)} collective-permute-done((f32[16,8,256]{2,1,0:T(8,128)S(1)}, f32[16,8,256]{2,1,0:T(8,128)S(1)}, u32[]{:S(2)}, u32[]{:S(2)}) %collective-permute-start.11) | collective-permute-done | bytes 131104 | tf_op jit(solution)/shard_map/ppermute | solution.py:143
  73.2 0.7 add.35
  73.8 9.4 %all-to-all-start = ((f32[16,8,256]{2,1,0:T(8,128)}), f32[16,8,256]{2,1,0:T(8,128)}, u32[]{:S(2)}, u32[]{:S(2)}) async-start(f32[16,8,256]{2,1,0:T(8,128)} %add.35), calls=%async_computation | async-start | bytes 262144 | tf_op jit(solution)/shard_map/all_to_all | solution.py:144
  83.2 0.8 slice.33
  84.0 2.4 %collective-permute-start.2 = (f32[96,1024]{1,0:T(8,128)}, f32[96,1024]{1,0:T(8,128)}, u32[]{:S(2)}, u32[]{:S(2)}) collective-permute-start(f32[96,1024]{1,0:T(8,128)} %slice.33), channel_id=1, source_target_pairs={{0,1},{1,2},{2,3},{3,0},{4,5},{5,6},{6,7},{7,4},{8,9},{9,10},{10,1... | collective-permute-start | bytes 1179656 | tf_op jit(solution)/shard_map/ppermute | solution.py:22
  86.3 0.8 slice.34
  87.1 1.8 %collective-permute-start.4 = (f32[96,1024]{1,0:T(8,128)}, f32[96,1024]{1,0:T(8,128)}, u32[]{:S(2)}, u32[]{:S(2)}) collective-permute-start(f32[96,1024]{1,0:T(8,128)} %slice.34), channel_id=1, source_target_pairs={{0,3},{1,0},{2,1},{3,2},{4,7},{5,4},{6,5},{7,6},{8,11},{9,8},{10,9... | collective-permute-start | bytes 1179656 | tf_op jit(solution)/shard_map/ppermute | solution.py:22
  88.9 0.7 slice.32
  89.5 1.8 %collective-permute-start.1 = (f32[32,1024]{1,0:T(8,128)}, f32[32,1024]{1,0:T(8,128)S(1)}, u32[]{:S(2)}, u32[]{:S(2)}) collective-permute-start(f32[32,1024]{1,0:T(8,128)} %slice.32), channel_id=1, source_target_pairs={{0,1},{1,2},{2,3},{3,0},{4,5},{5,6},{6,7},{7,4},{8,9},{9,10},{10,1... | collective-permute-start | bytes 393224 | tf_op jit(solution)/shard_map/ppermute | solution.py:22
  91.4 0.7 slice.35
  92.0 2.3 %collective-permute-start.5 = (f32[32,1024]{1,0:T(8,128)}, f32[32,1024]{1,0:T(8,128)}, u32[]{:S(2)}, u32[]{:S(2)}) collective-permute-start(f32[32,1024]{1,0:T(8,128)} %slice.35), channel_id=1, source_target_pairs={{0,3},{1,0},{2,1},{3,2},{4,7},{5,4},{6,5},{7,6},{8,11},{9,8},{10,9... | collective-permute-start | bytes 393224 | tf_op jit(solution)/shard_map/ppermute | solution.py:22
  94.4 0.9 reduce_sum.18
  95.3 0.7 broadcast_in_dim.8
  96.0 4.6 %all-to-all-start.1 = ((f32[16,8,256]{2,1,0:T(8,128)}), f32[16,8,256]{2,1,0:T(8,128)}, u32[]{:S(2)}, u32[]{:S(2)}) async-start(f32[16,8,256]{2,1,0:T(8,128)} %broadcast_in_dim.8), calls=%async_computation.1 | async-start | bytes 262144 | tf_op jit(solution)/shard_map/all_to_all | solution.py:148
  100.6 4.0 %shard_map.50.refs_5_ = f32[256,1024]{1,0:T(8,128)S(1)} custom-call(f32[256,1024]{1,0:T(8,128)S(1)} %bitcast.15, f32[128,1024]{1,0:T(8,128)S(1)} %collective-permute-done.refs_0_, f32[128,1024]{1,0:T(8,128)S(1)} %collective-permute-done.7.refs_1_, f32[128,1024]{1,0:T(8,128)} %collective-permute-done.8.refs_2_, ...), custom_call_target="tpu_custom_call" | custom-call | flops 2147483648 | bytes 1048576 | tf_op jit(solution)/shard_map/pallas_call | solution.py:95
  104.6 5.2 %collective-permute-done.1.refs_0_ = f32[32,1024]{1,0:T(8,128)S(1)} collective-permute-done((f32[32,1024]{1,0:T(8,128)}, f32[32,1024]{1,0:T(8,128)S(1)}, u32[]{:S(2)}, u32[]{:S(2)}) %collective-permute-start.1) | collective-permute-done | bytes 131104 | tf_op jit(solution)/shard_map/ppermute | solution.py:22
  109.9 3.6 %collective-permute-done.5.refs_3_ = f32[32,1024]{1,0:T(8,128)} collective-permute-done((f32[32,1024]{1,0:T(8,128)}, f32[32,1024]{1,0:T(8,128)}, u32[]{:S(2)}, u32[]{:S(2)}) %collective-permute-start.5) | collective-permute-done | bytes 131104 | tf_op jit(solution)/shard_map/ppermute | solution.py:22
  113.5 4.1 %shard_map.51 = f32[256,1024]{1,0:T(8,128)} custom-call(f32[256,1024]{1,0:T(8,128)S(1)} %bitcast.16, f32[32,1024]{1,0:T(8,128)S(1)} %collective-permute-done.1.refs_0_, f32[96,1024]{1,0:T(8,128)} %collective-permute-done.2.refs_1_, f32[96,1024]{1,0:T(8,128)} %collective-permute-done.4.refs_2_, f32[32,1024]{1,0:T(8,128)} %collective-permute-done.5.refs_3_, ...), custom_call_target="tpu_custom_call" | custom-call | flops 2147483648 | bytes 1048576 | tf_op jit(solution)/shard_map/pallas_call | solution.py:95
  117.6 1.5 %bitcast_reduce_fusion = f32[16,256]{1,0:T(8,128)} fusion(f32[8,16,256]{2,1,0:T(8,128)} %bitcast.13), kind=kLoop, calls=%fused_computation.6 | loop fusion | flops 28672 | bytes 147456 | tf_op jit(solution)/shard_map/reduce_sum | solution.py:155
  (15 shorter events, 0.1 us)
Async XLA Ops:
  0.6 67.0 %copy-start.1 = (f32[256]{0:T(256)S(1)}, f32[256]{0:T(256)}, u32[]{:S(2)}) copy-start(f32[256]{0:T(256)} %param.5) | copy-start | bytes 3076
  2.9 64.9 %copy-start = (f32[1,256,1024]{2,1,0:T(8,128)S(1)}, f32[1,256,1024]{2,1,0:T(8,128)}, u32[]{:S(2)}) copy-start(f32[1,256,1024]{2,1,0:T(8,128)} %param.3) | copy-start | bytes 3145732
  2.9 64.9 %collective-permute-start = (f32[128,1024]{1,0:T(8,128)}, f32[128,1024]{1,0:T(8,128)S(1)}, u32[]{:S(2)}, u32[]{:S(2)}) collective-permute-start(f32[128,1024]{1,0:T(8,128)} %get-tuple-element.7), channel_id=1, source_target_pairs={{0,1},{1,2},{2,3},{3,0},{4,5},{5,6},{6,7},{7,4},{8,9},{9,10},{10,1... | collective-permute-start | bytes 1572872 | tf_op jit(solution)/shard_map/ppermute | solution.py:22
  6.2 61.6 %collective-permute-start.3 = (f32[128,1024]{1,0:T(8,128)}, f32[128,1024]{1,0:T(8,128)S(1)}, u32[]{:S(2)}, u32[]{:S(2)}) collective-permute-start(f32[128,1024]{1,0:T(8,128)} %get-tuple-element.6), channel_id=1, source_target_pairs={{0,3},{1,0},{2,1},{3,2},{4,7},{5,4},{6,5},{7,6},{8,11},{9,8},{10,9... | collective-permute-start | bytes 1572872 | tf_op jit(solution)/shard_map/ppermute | solution.py:22
  9.2 58.6 %collective-permute-start.7 = (f32[128,1024]{1,0:T(8,128)}, f32[128,1024]{1,0:T(8,128)S(1)}, u32[]{:S(2)}, u32[]{:S(2)}) collective-permute-start(f32[128,1024]{1,0:T(8,128)} %get-tuple-element.6), channel_id=1, source_target_pairs={{0,1},{1,2},{2,3},{3,0},{4,5},{5,6},{6,7},{7,4},{8,9},{9,10},{10,1... | collective-permute-start | bytes 1572872 | tf_op jit(solution)/shard_map/ppermute | solution.py:22
  10.7 57.2 %collective-permute-start.8 = (f32[128,1024]{1,0:T(8,128)}, f32[128,1024]{1,0:T(8,128)}, u32[]{:S(2)}, u32[]{:S(2)}) collective-permute-start(f32[128,1024]{1,0:T(8,128)} %get-tuple-element.7), channel_id=1, source_target_pairs={{0,3},{1,0},{2,1},{3,2},{4,7},{5,4},{6,5},{7,6},{8,11},{9,8},{10,9... | collective-permute-start | bytes 1572872 | tf_op jit(solution)/shard_map/ppermute | solution.py:22
  13.4 28.4 %collective-permute-start.9 = (f32[1]{0:T(128)}, f32[1]{0:T(128)}, u32[]{:S(2)}, u32[]{:S(2)}) collective-permute-start(f32[1]{0:T(128)} %param.4), channel_id=1, source_target_pairs={{0,1},{1,2},{2,3},{3,0},{4,5},{5,6},{6,7},{7,4},{8,9},{9,10},{10,1... | collective-permute-start | bytes 20 | tf_op jit(solution)/shard_map/ppermute | solution.py:22
  41.7 17.6 %collective-permute-start.10 = (f32[1]{0:T(128)}, f32[1]{0:T(128)}, u32[]{:S(2)}, u32[]{:S(2)}) collective-permute-start(f32[1]{0:T(128)} %param.4), channel_id=1, source_target_pairs={{0,3},{1,0},{2,1},{3,2},{4,7},{5,4},{6,5},{7,6},{8,11},{9,8},{10,9... | collective-permute-start | bytes 20 | tf_op jit(solution)/shard_map/ppermute | solution.py:22
  59.3 7.7 %collective-permute-start.6 = (f32[1]{0:T(128)}, f32[1]{0:T(128)}, u32[]{:S(2)}, u32[]{:S(2)}) collective-permute-start(f32[1]{0:T(128)} %param.4), channel_id=1, source_target_pairs={{0,2},{1,3},{2,0},{3,1},{4,6},{5,7},{6,4},{7,5},{8,10},{9,11},{10,... | collective-permute-start | bytes 20 | tf_op jit(solution)/shard_map/ppermute | solution.py:22
  71.7 1.4 %collective-permute-start.11 = (f32[16,8,256]{2,1,0:T(8,128)S(1)}, f32[16,8,256]{2,1,0:T(8,128)S(1)}, u32[]{:S(2)}, u32[]{:S(2)}) collective-permute-start(f32[16,8,256]{2,1,0:T(8,128)S(1)} %get-tuple-element.5), channel_id=1, source_target_pairs={{0,16},{16,0},{32,48},{48,32},{64,80},{80,64},{96,112},{112,96},{1... | collective-permute-start | bytes 393224 | tf_op jit(solution)/shard_map/ppermute | solution.py:143
  73.8 20.5 %all-to-all-start = ((f32[16,8,256]{2,1,0:T(8,128)}), f32[16,8,256]{2,1,0:T(8,128)}, u32[]{:S(2)}, u32[]{:S(2)}) async-start(f32[16,8,256]{2,1,0:T(8,128)} %add.35), calls=%async_computation | async-start | bytes 262144 | tf_op jit(solution)/shard_map/all_to_all | solution.py:144
  84.0 29.5 %collective-permute-start.2 = (f32[96,1024]{1,0:T(8,128)}, f32[96,1024]{1,0:T(8,128)}, u32[]{:S(2)}, u32[]{:S(2)}) collective-permute-start(f32[96,1024]{1,0:T(8,128)} %slice.33), channel_id=1, source_target_pairs={{0,1},{1,2},{2,3},{3,0},{4,5},{5,6},{6,7},{7,4},{8,9},{9,10},{10,1... | collective-permute-start | bytes 1179656 | tf_op jit(solution)/shard_map/ppermute | solution.py:22
  87.1 26.4 %collective-permute-start.4 = (f32[96,1024]{1,0:T(8,128)}, f32[96,1024]{1,0:T(8,128)}, u32[]{:S(2)}, u32[]{:S(2)}) collective-permute-start(f32[96,1024]{1,0:T(8,128)} %slice.34), channel_id=1, source_target_pairs={{0,3},{1,0},{2,1},{3,2},{4,7},{5,4},{6,5},{7,6},{8,11},{9,8},{10,9... | collective-permute-start | bytes 1179656 | tf_op jit(solution)/shard_map/ppermute | solution.py:22
  89.5 20.3 %collective-permute-start.1 = (f32[32,1024]{1,0:T(8,128)}, f32[32,1024]{1,0:T(8,128)S(1)}, u32[]{:S(2)}, u32[]{:S(2)}) collective-permute-start(f32[32,1024]{1,0:T(8,128)} %slice.32), channel_id=1, source_target_pairs={{0,1},{1,2},{2,3},{3,0},{4,5},{5,6},{6,7},{7,4},{8,9},{9,10},{10,1... | collective-permute-start | bytes 393224 | tf_op jit(solution)/shard_map/ppermute | solution.py:22
  92.0 21.5 %collective-permute-start.5 = (f32[32,1024]{1,0:T(8,128)}, f32[32,1024]{1,0:T(8,128)}, u32[]{:S(2)}, u32[]{:S(2)}) collective-permute-start(f32[32,1024]{1,0:T(8,128)} %slice.35), channel_id=1, source_target_pairs={{0,3},{1,0},{2,1},{3,2},{4,7},{5,4},{6,5},{7,6},{8,11},{9,8},{10,9... | collective-permute-start | bytes 393224 | tf_op jit(solution)/shard_map/ppermute | solution.py:22
  96.0 21.6 %all-to-all-start.1 = ((f32[16,8,256]{2,1,0:T(8,128)}), f32[16,8,256]{2,1,0:T(8,128)}, u32[]{:S(2)}, u32[]{:S(2)}) async-start(f32[16,8,256]{2,1,0:T(8,128)} %broadcast_in_dim.8), calls=%async_computation.1 | async-start | bytes 262144 | tf_op jit(solution)/shard_map/all_to_all | solution.py:148

commit v2 on v1

v2 whole, which is shorter than its diff:
```python
import jax
import jax.numpy as jnp
from jax import lax
from jax.experimental import pallas as pl
from jax.experimental.pallas import tpu as pltpu
from jax.sharding import PartitionSpec as P


RING = 4
EARLY = 96
VMEM = pl.BlockSpec(memory_space=pltpu.VMEM)
SMEM = pl.BlockSpec(memory_space=pltpu.SMEM)
HBM = pl.BlockSpec(memory_space=pltpu.MemorySpace.HBM)
F32, BF16 = jnp.float32, jnp.bfloat16
ROWS = ((1,), (1,))
PLAIN = ((1,), (0,))
MIB = 1 << 20


def shift(value, step):
    size = lax.axis_size("orb")
    pairs = [
        (at, at // RING * RING + (at % RING + step) % RING) for at in range(size)
    ]
    return lax.ppermute(value, "orb", pairs)


def split(x):
    high = x.astype(BF16)
    return high, (x - high.astype(F32)).astype(BF16)


def mm(a, b, contract):
    def dot(p, q):
        return lax.dot_general(p, q, (contract, ((), ())), preferred_element_type=F32)

    return dot(a[0], b[0]) + (dot(a[0], b[1]) + dot(a[1], b[0]))


def fill(chunks, high, low):
    at = 0
    for chunk in chunks:
        end = at + chunk.shape[0]
        high[at:end, :], low[at:end, :] = split(chunk[...])
        at = end
    return high[...], low[...]


def pair_base(eps_vir):
    row = jnp.broadcast_to(eps_vir[...], (eps_vir.shape[1],) * 2)
    return row + row.T


def amplitudes(left, right, energy, base):
    t = mm(left, right, ROWS) / (energy - base)
    return split(t), split(2.0 * t - t.T)


def density_kernel(core, own, *refs):
    lows, highs, (energy, eps_vir, keep, send) = refs[:2], refs[2:4], refs[4:8]
    oh, ol, lh, ll, hh, hl, dens = refs[8:]
    base = pair_base(eps_vir)
    o, l, h = fill((own,), oh, ol), fill(lows, lh, ll), fill(highs, hh, hl)
    total = None
    for at, (left, right) in enumerate(((o, l), (o, h), (l, h))):
        t, s = amplitudes(left, right, energy[at : at + 1, 0:1], base)
        part = mm(t, s, ROWS)
        total = part if total is None else total + part
    dens[...] = total
    mine = core[0] * 8
    for at in range(16):
        keep[at] = dens[pl.ds(pl.multiple_of(at * 16 + mine, 8), 8), :]
        send[at] = dens[pl.ds(pl.multiple_of(at * 16 + 8 - mine, 8), 8), :]


def near_kernel(own, *refs):
    lows, highs, (energy, eps_vir, grad) = refs[:2], refs[2:4], refs[4:7]
    oh, ol, lh, ll, hh, hl, total, sem = refs[7:]
    base = pair_base(eps_vir)
    o, l, h = fill((own,), oh, ol), fill(lows, lh, ll), fill(highs, hh, hl)
    _, s_low = amplitudes(o, l, energy[0:1, 0:1], base)
    _, s_high = amplitudes(o, h, energy[1:2, 0:1], base)
    total[...] = mm(s_low, l, PLAIN) + mm(s_high, h, PLAIN)
    out = pltpu.make_async_copy(total, grad, sem)
    out.start()
    out.wait()


def far_kernel(own, *refs):
    fars, (energy, eps_vir, near, grad) = refs[:4], refs[4:8]
    oh, ol, fh, fl, before, total, sem_in, sem_out = refs[8:]
    fetch = pltpu.make_async_copy(near, before, sem_in)
    fetch.start()
    base = pair_base(eps_vir)
    f = fill(fars, fh, fl)
    _, s = amplitudes(fill((own,), oh, ol), f, energy[3:4, 0:1], base)
    fetch.wait()
    blocks, width = 4, total.shape[1] // 4
    outs = []
    for at in range(blocks):
        cols = slice(at * width, (at + 1) * width)
        total[:, cols] = before[:, cols] + mm(s, (f[0][:, cols], f[1][:, cols]), PLAIN)
        outs.append(
            pltpu.make_async_copy(
                total.at[:, cols], grad.at[:, cols], sem_out.at[at]
            )
        )
        outs[-1].start()
    for out in outs:
        out.wait()


def fold_kernel(pieces, copies):
    total = pieces[0]
    for at in range(1, pieces.shape[0]):
        total = total + pieces[at]
    total = total * (1.0 / 256.0)
    for at in range(copies.shape[0]):
        copies[at] = total


def call(kernel, out, scratch, limit, flops, args, in_specs, out_specs):
    return pl.pallas_call(
        kernel,
        out_shape=tuple(
            pltpu.HBM(s, F32) if spec is HBM else jax.ShapeDtypeStruct(s, F32)
            for s, spec in zip(out, out_specs)
        ),
        in_specs=in_specs,
        out_specs=out_specs,
        scratch_shapes=scratch,
        cost_estimate=pl.CostEstimate(
            flops=flops, bytes_accessed=MIB, transcendentals=0
        ),
        compiler_params=pltpu.CompilerParams(vmem_limit_bytes=limit * MIB),
    )(*args)


def body(slabs, eps_occ, eps_vir):
    own = slabs[0]
    v, n = own.shape
    n_orb, n_grp = lax.axis_size("orb"), lax.axis_size("grp")
    mid = v // 2
    own_a = own[:mid]
    own_b = lax.optimization_barrier(slabs)[0, mid:]
    low_a = shift(own_a, 1)
    high_b = shift(own_b, -1)
    e_low = shift(eps_occ, 1)
    e_high = shift(eps_occ, -1)
    e_far = shift(eps_occ, 2)
    lows = (low_a, shift(own_b, 1))
    highs = (shift(own_a, -1), high_b)
    pieces = [low_a[:EARLY], high_b[-EARLY:]]
    pieces += [low_a[EARLY:], high_b[:-EARLY]]
    fars = (
        shift(pieces[0], 1),
        shift(pieces[2], 1),
        shift(pieces[3], -1),
        shift(pieces[1], -1),
    )
    row = lax.broadcasted_iota(jnp.int32, (8, 128), 0)
    first = jnp.where(row == 2, e_low, eps_occ)
    second = jnp.where(row == 0, e_low, jnp.where(row == 3, e_far, e_high))
    energy = first + second
    eps_row = eps_vir[None]

    core = lax.rem(lax.axis_index("grp"), 2).astype(jnp.int32)[None]
    half = v // n_orb // 2
    piece = (n_orb, half, v)
    wide = [pltpu.VMEM((v, n), BF16)]
    keep, send = call(
        density_kernel,
        (piece, piece),
        wide * 6 + [pltpu.VMEM((v, v), F32)],
        16,
        1 << 32,
        (core, own, *lows, *highs, energy, eps_row),
        [SMEM] + [VMEM] * 7,
        (VMEM, VMEM),
    )
    other = lax.ppermute(send, "grp", [(i, i ^ 1) for i in range(n_grp)])
    parts = lax.all_to_all(keep + other, "orb", split_axis=0, concat_axis=0, tiled=True)
    (copies,) = call(fold_kernel, (piece,), [], 4, 1 << 20, (parts,), [VMEM], (VMEM,))
    copies = lax.all_to_all(
        copies, "grp", split_axis=0, concat_axis=0, tiled=True
    )
    density = jnp.sum(copies.reshape(n_grp // 2, 2 * half, v), axis=0)

    (near,) = call(
        near_kernel,
        (own.shape,),
        wide * 6 + [pltpu.VMEM((v, n), F32), pltpu.SemaphoreType.DMA],
        16,
        1 << 31,
        (own, *lows, *highs, energy, eps_row),
        [VMEM] * 7,
        (HBM,),
    )
    (grad,) = call(
        far_kernel,
        (own.shape,),
        wide * 4
        + [pltpu.VMEM((v, n), F32)] * 2
        + [pltpu.SemaphoreType.DMA, pltpu.SemaphoreType.DMA((4,))],
        16,
        1 << 31,
        (own, *fars, energy, eps_row, pltpu.with_memory_space_constraint(near, pltpu.HBM)),
        [VMEM] * 7 + [HBM],
        (HBM,),
    )
    return grad[None], density


def solution(mesh):
    placed = (P(("grp", "orb"), None, None), P(("grp", "orb")), P())
    return jax.shard_map(
        body,
        mesh=mesh,
        in_specs=placed,
        out_specs=(P(("grp", "orb"), None, None), P("orb", None)),
        check_vma=False,
    )
```

time: 120 us -> 121 us (level)
  between operations: 4.42 us -> 1.44 us
  waiting for transfers between devices: 38.1 us -> 40 us
    ppermute x11, waiting for transfers between devices: 36.7 us -> 38.6 us  [shift(): return lax.ppermute(value, 'orb', pairs)]
    select_n x0 -> x2, other arithmetic: none -> 1.89 us  [the longest x1 1.26 us: body(): second = jnp.where(row == 0, e_low, jnp.where(row == 3, e_far, e_high))]
    pallas_call x3 -> x4, Pallas kernels: 12 us -> 11.7 us  [call(): pl.pallas_call(kernel, out_shape=tuple((pltpu.HBM(s, F32) if spec is HBM...]
  transfers between devices with their start and end apart: 14 -> 14, of which waited for: 6 -> 6; matrix products, arithmetic and copies ran while one was open for 4% -> 5% of each run, Pallas kernels for 7% -> 7%
where the time goes in v2:
time: 121 us; the launch traced here: 120 us
  starting transfers between devices  56.3 us (47%)
  waiting for transfers between devices  40 us (33%)
  Pallas kernels  11.7 us (10%)
  local copies, waits for them, and re-layouts  6.35 us (5%)
  other arithmetic  3.89 us (3%)
  between operations  1.44 us (1%)
    ppermute x11, starting transfers between devices, shift(): return lax.ppermute(value, 'orb', pairs)  42.2 us
    ppermute x11, waiting for transfers between devices, shift(): return lax.ppermute(value, 'orb', pairs)  38.6 us
    pallas_call x4, Pallas kernels, call(): pl.pallas_call(kernel, out_shape=tuple((pltpu.HBM(s, F32) if spec is HBM...  11.7 us
    all_to_all x1, starting transfers between devices, body(): lax.all_to_all(keep + other, 'orb', split_axis=0, concat_axis=0, tiled=True)  9.37 us
    all_to_all x1, starting transfers between devices, body(): lax.all_to_all(copies, 'grp', split_axis=0, concat_axis=0, tiled=True)  4.58 us
  transfers between devices with their start and end apart: 14, of which 6 were waited for; matrix products, arithmetic and copies ran while one was open for 5% of the time, Pallas kernels for 7%

profile of v2, /device:TPU:2, one launch (start us, length us, event | category | flops | bytes accessed | tf_op | source)
XLA Modules:
  0.0 119.6 jit_solution(6123628492555246451)
XLA Ops:
  0.6 2.0 %slice_bitcast_fusion.1 = f32[128,1024]{1,0:T(8,128)} fusion(f32[1,256,1024]{2,1,0:T(8,128)} %param.3), kind=kLoop, calls=%fused_computation.1 | loop fusion | bytes 1048576 | tf_op jit(solution)/shard_map/slice | solution.py:144
  2.6 3.3 %collective-permute-start = (f32[128,1024]{1,0:T(8,128)}, f32[128,1024]{1,0:T(8,128)S(1)}, u32[]{:S(2)}, u32[]{:S(2)}) collective-permute-start(f32[128,1024]{1,0:T(8,128)} %slice_bitcast_fusion.1), channel_id=1, source_target_pairs={{0,1},{1,2},{2,3},{3,0},{4,5},{5,6},{6,7},{7,4},{8,9},{9,10},{10,1... | collective-permute-start | bytes 1572872 | tf_op jit(solution)/shard_map/ppermute | solution.py:25
  5.9 3.0 %collective-permute-start.10 = (f32[128,1024]{1,0:T(8,128)}, f32[128,1024]{1,0:T(8,128)S(1)}, u32[]{:S(2)}, u32[]{:S(2)}) collective-permute-start(f32[128,1024]{1,0:T(8,128)} %slice_bitcast_fusion.1), channel_id=1, source_target_pairs={{0,3},{1,0},{2,1},{3,2},{4,7},{5,4},{6,5},{7,6},{8,11},{9,8},{10,9... | collective-permute-start | bytes 1572872 | tf_op jit(solution)/shard_map/ppermute | solution.py:25
  8.9 0.8 slice_bitcast_fusion
  9.7 2.9 %collective-permute-start.3 = (f32[128,1024]{1,0:T(8,128)}, f32[128,1024]{1,0:T(8,128)S(1)}, u32[]{:S(2)}, u32[]{:S(2)}) collective-permute-start(f32[128,1024]{1,0:T(8,128)} %slice_bitcast_fusion), channel_id=1, source_target_pairs={{0,3},{1,0},{2,1},{3,2},{4,7},{5,4},{6,5},{7,6},{8,11},{9,8},{10,9... | collective-permute-start | bytes 1572872 | tf_op jit(solution)/shard_map/ppermute | solution.py:25
  12.7 2.7 %collective-permute-start.6 = (f32[1]{0:T(128)}, f32[1]{0:T(128)}, u32[]{:S(2)}, u32[]{:S(2)}) collective-permute-start(f32[1]{0:T(128)} %param.4), channel_id=1, source_target_pairs={{0,1},{1,2},{2,3},{3,0},{4,5},{5,6},{6,7},{7,4},{8,9},{9,10},{10,1... | collective-permute-start | bytes 20 | tf_op jit(solution)/shard_map/ppermute | solution.py:25
  16.0 25.4 %collective-permute-done.6 = f32[1]{0:T(128)} collective-permute-done((f32[1]{0:T(128)}, f32[1]{0:T(128)}, u32[]{:S(2)}, u32[]{:S(2)}) %collective-permute-start.6) | collective-permute-done | bytes 36 | tf_op jit(solution)/shard_map/ppermute | solution.py:25
  41.4 18.1 %collective-permute-start.7 = (f32[1]{0:T(128)}, f32[1]{0:T(128)}, u32[]{:S(2)}, u32[]{:S(2)}) collective-permute-start(f32[1]{0:T(128)} %param.4), channel_id=1, source_target_pairs={{0,2},{1,3},{2,0},{3,1},{4,6},{5,7},{6,4},{7,5},{8,10},{9,11},{10,... | collective-permute-start | bytes 20 | tf_op jit(solution)/shard_map/ppermute | solution.py:25
  60.2 1.1 collective-permute-done.7
  61.3 4.0 %collective-permute-start.8 = (f32[1]{0:T(128)}, f32[1]{0:T(128)}, u32[]{:S(2)}, u32[]{:S(2)}) collective-permute-start(f32[1]{0:T(128)} %param.4), channel_id=1, source_target_pairs={{0,3},{1,0},{2,1},{3,2},{4,7},{5,4},{6,5},{7,6},{8,11},{9,8},{10,9... | collective-permute-start | bytes 20 | tf_op jit(solution)/shard_map/ppermute | solution.py:25
  65.3 1.4 %collective-permute-done.8 = f32[1]{0:T(128)} collective-permute-done((f32[1]{0:T(128)}, f32[1]{0:T(128)}, u32[]{:S(2)}, u32[]{:S(2)}) %collective-permute-start.8) | collective-permute-done | bytes 36 | tf_op jit(solution)/shard_map/ppermute | solution.py:25
  66.7 1.3 %compare_select_fusion = f32[8]{0:T(128)S(1)} fusion(f32[]{:T(128)} %bitcast.6, f32[]{:T(128)} %bitcast.5), kind=kLoop, calls=%fused_computation.4 | loop fusion | flops 16 | bytes 40 | tf_op jit(solution)/shard_map/jit(_where)/select_n | solution.py:163
  68.0 0.7 select_add_fusion.refs_4_
  68.7 0.7 copy-done.1
  69.4 2.9 %shard_map.55 = (f32[16,8,256]{2,1,0:T(8,128)S(1)}, f32[16,8,256]{2,1,0:T(8,128)S(1)}) custom-call(s32[1]{0:T(128)} %bitcast.9.core, f32[256,1024]{1,0:T(8,128)S(1)} %bitcast.16, f32[128,1024]{1,0:T(8,128)S(1)} %collective-permute-done.refs_0_, f32[128,1024]{1,0:T(8,128)S(1)} %collective-permute-done.9.refs_1_, ...), custom_call_target="tpu_custom_call" | custom-call | flops 4294967296 | bytes 1048576 | tf_op jit(solution)/shard_map/pallas_call | solution.py:123
  72.4 1.3 %collective-permute-done.11 = f32[16,8,256]{2,1,0:T(8,128)S(1)} collective-permute-done((f32[16,8,256]{2,1,0:T(8,128)S(1)}, f32[16,8,256]{2,1,0:T(8,128)S(1)}, u32[]{:S(2)}, u32[]{:S(2)}) %collective-permute-start.11) | collective-permute-done | bytes 131104 | tf_op jit(solution)/shard_map/ppermute | solution.py:181
  73.7 0.7 add.7
  74.4 9.4 %all-to-all-start = ((f32[16,8,256]{2,1,0:T(8,128)}), f32[16,8,256]{2,1,0:T(8,128)S(1)}, u32[]{:S(2)}, u32[]{:S(2)}) async-start(f32[16,8,256]{2,1,0:T(8,128)} %add.7), calls=%async_computation | async-start | bytes 262144 | tf_op jit(solution)/shard_map/all_to_all | solution.py:182
  83.7 0.8 slice.28
  84.5 2.4 %collective-permute-start.1 = (f32[96,1024]{1,0:T(8,128)}, f32[96,1024]{1,0:T(8,128)}, u32[]{:S(2)}, u32[]{:S(2)}) collective-permute-start(f32[96,1024]{1,0:T(8,128)} %slice.28), channel_id=1, source_target_pairs={{0,1},{1,2},{2,3},{3,0},{4,5},{5,6},{6,7},{7,4},{8,9},{9,10},{10,1... | collective-permute-start | bytes 1179656 | tf_op jit(solution)/shard_map/ppermute | solution.py:25
  86.9 0.8 slice.32
  87.7 1.8 %collective-permute-start.5 = (f32[96,1024]{1,0:T(8,128)}, f32[96,1024]{1,0:T(8,128)}, u32[]{:S(2)}, u32[]{:S(2)}) collective-permute-start(f32[96,1024]{1,0:T(8,128)} %slice.32), channel_id=1, source_target_pairs={{0,3},{1,0},{2,1},{3,2},{4,7},{5,4},{6,5},{7,6},{8,11},{9,8},{10,9... | collective-permute-start | bytes 1179656 | tf_op jit(solution)/shard_map/ppermute | solution.py:25
  89.4 0.7 slice.29
  90.1 1.8 %collective-permute-start.2 = (f32[32,1024]{1,0:T(8,128)}, f32[32,1024]{1,0:T(8,128)S(1)}, u32[]{:S(2)}, u32[]{:S(2)}) collective-permute-start(f32[32,1024]{1,0:T(8,128)} %slice.29), channel_id=1, source_target_pairs={{0,1},{1,2},{2,3},{3,0},{4,5},{5,6},{6,7},{7,4},{8,9},{9,10},{10,1... | collective-permute-start | bytes 393224 | tf_op jit(solution)/shard_map/ppermute | solution.py:25
  91.9 0.7 slice.31
  92.5 2.3 %collective-permute-start.4 = (f32[32,1024]{1,0:T(8,128)}, f32[32,1024]{1,0:T(8,128)S(1)}, u32[]{:S(2)}, u32[]{:S(2)}) collective-permute-start(f32[32,1024]{1,0:T(8,128)} %slice.31), channel_id=1, source_target_pairs={{0,3},{1,0},{2,1},{3,2},{4,7},{5,4},{6,5},{7,6},{8,11},{9,8},{10,9... | collective-permute-start | bytes 393224 | tf_op jit(solution)/shard_map/ppermute | solution.py:25
  94.9 0.7 shard_map.56
  95.6 4.6 %all-to-all-start.1 = ((f32[16,8,256]{2,1,0:T(8,128)}), f32[16,8,256]{2,1,0:T(8,128)S(1)}, u32[]{:S(2)}, u32[]{:S(2)}) async-start(f32[16,8,256]{2,1,0:T(8,128)} %shard_map.56), calls=%async_computation.1 | async-start | bytes 262144 | tf_op jit(solution)/shard_map/all_to_all | solution.py:184
  100.2 3.1 %shard_map.53.refs_6_ = f32[256,1024]{1,0:T(8,128)} custom-call(f32[256,1024]{1,0:T(8,128)S(1)} %bitcast.17, f32[128,1024]{1,0:T(8,128)S(1)} %collective-permute-done.refs_0_, f32[128,1024]{1,0:T(8,128)S(1)} %collective-permute-done.9.refs_1_, f32[128,1024]{1,0:T(8,128)S(1)} %collective-permute-done.10.refs_2_, ...), custom_call_target="tpu_custom_call" | custom-call | flops 2147483648 | bytes 1048576 | tf_op jit(solution)/shard_map/pallas_call | solution.py:123
  103.3 7.1 %collective-permute-done.2.refs_1_ = f32[32,1024]{1,0:T(8,128)S(1)} collective-permute-done((f32[32,1024]{1,0:T(8,128)}, f32[32,1024]{1,0:T(8,128)S(1)}, u32[]{:S(2)}, u32[]{:S(2)}) %collective-permute-start.2) | collective-permute-done | bytes 131104 | tf_op jit(solution)/shard_map/ppermute | solution.py:25
  110.4 3.6 %collective-permute-done.4.refs_2_ = f32[32,1024]{1,0:T(8,128)S(1)} collective-permute-done((f32[32,1024]{1,0:T(8,128)}, f32[32,1024]{1,0:T(8,128)S(1)}, u32[]{:S(2)}, u32[]{:S(2)}) %collective-permute-start.4) | collective-permute-done | bytes 131104 | tf_op jit(solution)/shard_map/ppermute | solution.py:25
  113.9 5.0 %shard_map.54 = f32[256,1024]{1,0:T(8,128)} custom-call(f32[256,1024]{1,0:T(8,128)S(1)} %bitcast.18, f32[96,1024]{1,0:T(8,128)} %collective-permute-done.1.refs_0_, f32[32,1024]{1,0:T(8,128)S(1)} %collective-permute-done.2.refs_1_, f32[32,1024]{1,0:T(8,128)S(1)} %collective-permute-done.4.refs_2_, f32[96,1024]{1,0:T(8,128)} %collective-permute-done.5.refs_3_, ...), custom_call_target="tpu_custom_call" | custom-call | flops 2147483648 | bytes 1048576 | tf_op jit(solution)/shard_map/pallas_call | solution.py:123
  (16 shorter events, 1.4 us)
Async XLA Ops:
  0.6 8.3 %copy-start = (f32[1,256,1024]{2,1,0:T(8,128)S(1)}, f32[1,256,1024]{2,1,0:T(8,128)}, u32[]{:S(2)}) copy-start(f32[1,256,1024]{2,1,0:T(8,128)} %param.3) | copy-start | bytes 3145732
  2.6 66.1 %collective-permute-start = (f32[128,1024]{1,0:T(8,128)}, f32[128,1024]{1,0:T(8,128)S(1)}, u32[]{:S(2)}, u32[]{:S(2)}) collective-permute-start(f32[128,1024]{1,0:T(8,128)} %slice_bitcast_fusion.1), channel_id=1, source_target_pairs={{0,1},{1,2},{2,3},{3,0},{4,5},{5,6},{6,7},{7,4},{8,9},{9,10},{10,1... | collective-permute-start | bytes 1572872 | tf_op jit(solution)/shard_map/ppermute | solution.py:25
  5.9 62.8 %collective-permute-start.10 = (f32[128,1024]{1,0:T(8,128)}, f32[128,1024]{1,0:T(8,128)S(1)}, u32[]{:S(2)}, u32[]{:S(2)}) collective-permute-start(f32[128,1024]{1,0:T(8,128)} %slice_bitcast_fusion.1), channel_id=1, source_target_pairs={{0,3},{1,0},{2,1},{3,2},{4,7},{5,4},{6,5},{7,6},{8,11},{9,8},{10,9... | collective-permute-start | bytes 1572872 | tf_op jit(solution)/shard_map/ppermute | solution.py:25
  9.7 58.9 %collective-permute-start.3 = (f32[128,1024]{1,0:T(8,128)}, f32[128,1024]{1,0:T(8,128)S(1)}, u32[]{:S(2)}, u32[]{:S(2)}) collective-permute-start(f32[128,1024]{1,0:T(8,128)} %slice_bitcast_fusion), channel_id=1, source_target_pairs={{0,3},{1,0},{2,1},{3,2},{4,7},{5,4},{6,5},{7,6},{8,11},{9,8},{10,9... | collective-permute-start | bytes 1572872 | tf_op jit(solution)/shard_map/ppermute | solution.py:25
  12.7 56.0 %collective-permute-start.9 = (f32[128,1024]{1,0:T(8,128)}, f32[128,1024]{1,0:T(8,128)S(1)}, u32[]{:S(2)}, u32[]{:S(2)}) collective-permute-start(f32[128,1024]{1,0:T(8,128)} %slice_bitcast_fusion), channel_id=1, source_target_pairs={{0,1},{1,2},{2,3},{3,0},{4,5},{5,6},{6,7},{7,4},{8,9},{9,10},{10,1... | collective-permute-start | bytes 1572872 | tf_op jit(solution)/shard_map/ppermute | solution.py:25
  12.7 28.7 %collective-permute-start.6 = (f32[1]{0:T(128)}, f32[1]{0:T(128)}, u32[]{:S(2)}, u32[]{:S(2)}) collective-permute-start(f32[1]{0:T(128)} %param.4), channel_id=1, source_target_pairs={{0,1},{1,2},{2,3},{3,0},{4,5},{5,6},{6,7},{7,4},{8,9},{9,10},{10,1... | collective-permute-start | bytes 20 | tf_op jit(solution)/shard_map/ppermute | solution.py:25
  41.4 19.9 %collective-permute-start.7 = (f32[1]{0:T(128)}, f32[1]{0:T(128)}, u32[]{:S(2)}, u32[]{:S(2)}) collective-permute-start(f32[1]{0:T(128)} %param.4), channel_id=1, source_target_pairs={{0,2},{1,3},{2,0},{3,1},{4,6},{5,7},{6,4},{7,5},{8,10},{9,11},{10,... | collective-permute-start | bytes 20 | tf_op jit(solution)/shard_map/ppermute | solution.py:25
  61.3 5.4 %collective-permute-start.8 = (f32[1]{0:T(128)}, f32[1]{0:T(128)}, u32[]{:S(2)}, u32[]{:S(2)}) collective-permute-start(f32[1]{0:T(128)} %param.4), channel_id=1, source_target_pairs={{0,3},{1,0},{2,1},{3,2},{4,7},{5,4},{6,5},{7,6},{8,11},{9,8},{10,9... | collective-permute-start | bytes 20 | tf_op jit(solution)/shard_map/ppermute | solution.py:25
  68.7 0.7 copy-start.1
  72.3 1.4 %collective-permute-start.11 = (f32[16,8,256]{2,1,0:T(8,128)S(1)}, f32[16,8,256]{2,1,0:T(8,128)S(1)}, u32[]{:S(2)}, u32[]{:S(2)}) collective-permute-start(f32[16,8,256]{2,1,0:T(8,128)S(1)} %get-tuple-element.5), channel_id=1, source_target_pairs={{0,16},{16,0},{32,48},{48,32},{64,80},{80,64},{96,112},{112,96},{1... | collective-permute-start | bytes 393224 | tf_op jit(solution)/shard_map/ppermute | solution.py:181
  74.4 20.5 %all-to-all-start = ((f32[16,8,256]{2,1,0:T(8,128)}), f32[16,8,256]{2,1,0:T(8,128)S(1)}, u32[]{:S(2)}, u32[]{:S(2)}) async-start(f32[16,8,256]{2,1,0:T(8,128)} %add.7), calls=%async_computation | async-start | bytes 262144 | tf_op jit(solution)/shard_map/all_to_all | solution.py:182
  84.5 29.4 %collective-permute-start.1 = (f32[96,1024]{1,0:T(8,128)}, f32[96,1024]{1,0:T(8,128)}, u32[]{:S(2)}, u32[]{:S(2)}) collective-permute-start(f32[96,1024]{1,0:T(8,128)} %slice.28), channel_id=1, source_target_pairs={{0,1},{1,2},{2,3},{3,0},{4,5},{5,6},{6,7},{7,4},{8,9},{9,10},{10,1... | collective-permute-start | bytes 1179656 | tf_op jit(solution)/shard_map/ppermute | solution.py:25
  87.7 26.3 %collective-permute-start.5 = (f32[96,1024]{1,0:T(8,128)}, f32[96,1024]{1,0:T(8,128)}, u32[]{:S(2)}, u32[]{:S(2)}) collective-permute-start(f32[96,1024]{1,0:T(8,128)} %slice.32), channel_id=1, source_target_pairs={{0,3},{1,0},{2,1},{3,2},{4,7},{5,4},{6,5},{7,6},{8,11},{9,8},{10,9... | collective-permute-start | bytes 1179656 | tf_op jit(solution)/shard_map/ppermute | solution.py:25
  90.1 20.3 %collective-permute-start.2 = (f32[32,1024]{1,0:T(8,128)}, f32[32,1024]{1,0:T(8,128)S(1)}, u32[]{:S(2)}, u32[]{:S(2)}) collective-permute-start(f32[32,1024]{1,0:T(8,128)} %slice.29), channel_id=1, source_target_pairs={{0,1},{1,2},{2,3},{3,0},{4,5},{5,6},{6,7},{7,4},{8,9},{9,10},{10,1... | collective-permute-start | bytes 393224 | tf_op jit(solution)/shard_map/ppermute | solution.py:25
  92.5 21.4 %collective-permute-start.4 = (f32[32,1024]{1,0:T(8,128)}, f32[32,1024]{1,0:T(8,128)S(1)}, u32[]{:S(2)}, u32[]{:S(2)}) collective-permute-start(f32[32,1024]{1,0:T(8,128)} %slice.31), channel_id=1, source_target_pairs={{0,3},{1,0},{2,1},{3,2},{4,7},{5,4},{6,5},{7,6},{8,11},{9,8},{10,9... | collective-permute-start | bytes 393224 | tf_op jit(solution)/shard_map/ppermute | solution.py:25
  95.6 23.4 %all-to-all-start.1 = ((f32[16,8,256]{2,1,0:T(8,128)}), f32[16,8,256]{2,1,0:T(8,128)S(1)}, u32[]{:S(2)}, u32[]{:S(2)}) async-start(f32[16,8,256]{2,1,0:T(8,128)} %shard_map.56), calls=%async_computation.1 | async-start | bytes 262144 | tf_op jit(solution)/shard_map/all_to_all | solution.py:184

commit v3 on v2

--- a/solution.py
+++ b/solution.py
@@ -7,10 +7,9 @@
 
 
 RING = 4
-EARLY = 96
 VMEM = pl.BlockSpec(memory_space=pltpu.VMEM)
 SMEM = pl.BlockSpec(memory_space=pltpu.SMEM)
-HBM = pl.BlockSpec(memory_space=pltpu.MemorySpace.HBM)
+HBM = pl.BlockSpec(memory_space=pltpu.HBM)
 F32, BF16 = jnp.float32, jnp.bfloat16
 ROWS = ((1,), (1,))
 PLAIN = ((1,), (0,))
@@ -56,14 +55,17 @@
     return split(t), split(2.0 * t - t.T)
 
 
-def density_kernel(core, own, *refs):
-    lows, highs, (energy, eps_vir, keep, send) = refs[:2], refs[2:4], refs[4:8]
-    oh, ol, lh, ll, hh, hl, dens = refs[8:]
+def density_kernel(core, e_own, e_low, e_high, *refs):
+    own, low, high, eps_vir, keep, send, oh, ol, lh, ll, hh, hl, dens = refs
     base = pair_base(eps_vir)
-    o, l, h = fill((own,), oh, ol), fill(lows, lh, ll), fill(highs, hh, hl)
+    o, l, h = fill((own,), oh, ol), fill((low,), lh, ll), fill((high,), hh, hl)
     total = None
-    for at, (left, right) in enumerate(((o, l), (o, h), (l, h))):
-        t, s = amplitudes(left, right, energy[at : at + 1, 0:1], base)
+    for left, right, energy in (
+        (o, l, e_own[0] + e_low[0]),
+        (o, h, e_own[0] + e_high[0]),
+        (l, h, e_low[0] + e_high[0]),
+    ):
+        t, s = amplitudes(left, right, energy, base)
         part = mm(t, s, ROWS)
         total = part if total is None else total + part
     dens[...] = total
@@ -73,29 +75,39 @@
         send[at] = dens[pl.ds(pl.multiple_of(at * 16 + 8 - mine, 8), 8), :]
 
 
-def near_kernel(own, *refs):
-    lows, highs, (energy, eps_vir, grad) = refs[:2], refs[2:4], refs[4:7]
-    oh, ol, lh, ll, hh, hl, total, sem = refs[7:]
+def near_kernel(e_own, e_low, e_high, own, low, high, eps_vir, grad, *scratch):
+    oh, ol, lh, ll, hh, hl, total, sem = scratch
     base = pair_base(eps_vir)
-    o, l, h = fill((own,), oh, ol), fill(lows, lh, ll), fill(highs, hh, hl)
-    _, s_low = amplitudes(o, l, energy[0:1, 0:1], base)
-    _, s_high = amplitudes(o, h, energy[1:2, 0:1], base)
+    o, l, h = fill((own,), oh, ol), fill((low,), lh, ll), fill((high,), hh, hl)
+    _, s_low = amplitudes(o, l, e_own[0] + e_low[0], base)
+    _, s_high = amplitudes(o, h, e_own[0] + e_high[0], base)
     total[...] = mm(s_low, l, PLAIN) + mm(s_high, h, PLAIN)
     out = pltpu.make_async_copy(total, grad, sem)
     out.start()
     out.wait()
 
 
-def far_kernel(own, *refs):
-    fars, (energy, eps_vir, near, grad) = refs[:4], refs[4:8]
-    oh, ol, fh, fl, before, total, sem_in, sem_out = refs[8:]
-    fetch = pltpu.make_async_copy(near, before, sem_in)
-    fetch.start()
+def far_kernel(e_own, e_far, eps_vir, own, far_a, far_b, near, grad, *scratch):
+    mine, far, before, total, sem_in, sem_out = scratch
+    half = far_a.shape[0]
+    fetches = [
+        pltpu.make_async_copy(own, mine, sem_in.at[0]),
+        pltpu.make_async_copy(far_a, far.at[:half, :], sem_in.at[1]),
+        pltpu.make_async_copy(far_b, far.at[half:, :], sem_in.at[2]),
+        pltpu.make_async_copy(near, before, sem_in.at[3]),
+    ]
+    for fetch in fetches:
+        fetch.start()
     base = pair_base(eps_vir)
-    f = fill(fars, fh, fl)
-    _, s = amplitudes(fill((own,), oh, ol), f, energy[3:4, 0:1], base)
-    fetch.wait()
-    blocks, width = 4, total.shape[1] // 4
+    fetches[0].wait()
+    o = split(mine[...])
+    fetches[1].wait()
+    fetches[2].wait()
+    f = split(far[...])
+    _, s = amplitudes(o, f, e_own[0] + e_far[0], base)
+    fetches[3].wait()
+    blocks = 4
+    width = total.shape[1] // blocks
     outs = []
     for at in range(blocks):
         cols = slice(at * width, (at + 1) * width)
@@ -141,41 +153,29 @@
     v, n = own.shape
     n_orb, n_grp = lax.axis_size("orb"), lax.axis_size("grp")
     mid = v // 2
-    own_a = own[:mid]
-    own_b = lax.optimization_barrier(slabs)[0, mid:]
-    low_a = shift(own_a, 1)
-    high_b = shift(own_b, -1)
+    low = shift(own, 1)
+    high = shift(own, -1)
     e_low = shift(eps_occ, 1)
     e_high = shift(eps_occ, -1)
-    e_far = shift(eps_occ, 2)
-    lows = (low_a, shift(own_b, 1))
-    highs = (shift(own_a, -1), high_b)
-    pieces = [low_a[:EARLY], high_b[-EARLY:]]
-    pieces += [low_a[EARLY:], high_b[:-EARLY]]
-    fars = (
-        shift(pieces[0], 1),
-        shift(pieces[2], 1),
-        shift(pieces[3], -1),
-        shift(pieces[1], -1),
-    )
-    row = lax.broadcasted_iota(jnp.int32, (8, 128), 0)
-    first = jnp.where(row == 2, e_low, eps_occ)
-    second = jnp.where(row == 0, e_low, jnp.where(row == 3, e_far, e_high))
-    energy = first + second
+    e_far = shift(e_low, 1)
+    low_a, high_b = low[:mid], high[mid:]
+    far_a = shift(low_a, 1)
+    far_b = shift(high_b, -1)
     eps_row = eps_vir[None]
 
     core = lax.rem(lax.axis_index("grp"), 2).astype(jnp.int32)[None]
     half = v // n_orb // 2
     piece = (n_orb, half, v)
     wide = [pltpu.VMEM((v, n), BF16)]
+    full = [pltpu.VMEM((v, n), F32)]
     keep, send = call(
         density_kernel,
         (piece, piece),
         wide * 6 + [pltpu.VMEM((v, v), F32)],
         16,
         1 << 32,
-        (core, own, *lows, *highs, energy, eps_row),
-        [SMEM] + [VMEM] * 7,
+        (core, eps_occ, e_low, e_high, own, low, high, eps_row),
+        [SMEM] * 4 + [VMEM] * 4,
         (VMEM, VMEM),
     )
     other = lax.ppermute(send, "grp", [(i, i ^ 1) for i in range(n_grp)])
@@ -189,23 +189,22 @@
     (near,) = call(
         near_kernel,
         (own.shape,),
-        wide * 6 + [pltpu.VMEM((v, n), F32), pltpu.SemaphoreType.DMA],
+        wide * 6 + full + [pltpu.SemaphoreType.DMA],
         16,
         1 << 31,
-        (own, *lows, *highs, energy, eps_row),
-        [VMEM] * 7,
+        (eps_occ, e_low, e_high, own, low, high, eps_row),
+        [SMEM] * 3 + [VMEM] * 4,
         (HBM,),
     )
+    hold = [pltpu.with_memory_space_constraint(x, pltpu.HBM) for x in (near,)]
     (grad,) = call(
         far_kernel,
         (own.shape,),
-        wide * 4
-        + [pltpu.VMEM((v, n), F32)] * 2
-        + [pltpu.SemaphoreType.DMA, pltpu.SemaphoreType.DMA((4,))],
+        full * 4 + [pltpu.SemaphoreType.DMA((4,))] * 2,
         16,
         1 << 31,
-        (own, *fars, energy, eps_row, pltpu.with_memory_space_constraint(near, pltpu.HBM)),
-        [VMEM] * 7 + [HBM],
+        (eps_occ, e_far, eps_row, own, far_a, far_b, *hold),
+        [SMEM] * 2 + [VMEM] + [HBM] * 4,
         (HBM,),
     )
     return grad[None], density

time: 121 us -> 114 us (0.942)
  the two profiles are of different devices: /device:TPU:2 before, /device:TPU:1 now
where the time goes in v3:
time: 114 us
  waiting for transfers between devices  62.7 us (55%)
  starting transfers between devices  31.7 us (28%)
  Pallas kernels  13.5 us (12%)
  local copies, waits for them, and re-layouts  3.57 us (3%)
  between operations  1.4 us (1%)
  other arithmetic  1.28 us (1%)
    ppermute x7, waiting for transfers between devices, shift(): return lax.ppermute(value, 'orb', pairs)  42.7 us
    all_to_all x1, waiting for transfers between devices, body(): lax.all_to_all(keep + other, 'orb', split_axis=0, concat_axis=0, tiled=True)  19.9 us
    ppermute x7, starting transfers between devices, shift(): return lax.ppermute(value, 'orb', pairs)  16.4 us
    pallas_call x4, Pallas kernels, call(): pl.pallas_call(kernel, out_shape=tuple((pltpu.HBM(s, F32) if spec is HBM...  13.5 us
    all_to_all x1, starting transfers between devices, body(): lax.all_to_all(keep + other, 'orb', split_axis=0, concat_axis=0, tiled=True)  7.08 us
    all_to_all x1, starting transfers between devices, body(): lax.all_to_all(copies, 'grp', split_axis=0, concat_axis=0, tiled=True)  7.08 us
  transfers between devices with their start and end apart: 10, of which 3 were waited for; matrix products, arithmetic and copies ran while one was open for 2% of the time, Pallas kernels for 8%

profile of v3, /device:TPU:1, one launch (start us, length us, event | category | flops | bytes accessed | tf_op | source)
XLA Modules:
  0.0 114.1 jit_solution(6548732727485625566)
XLA Ops:
  0.6 3.9 %collective-permute-start.2 = (f32[256,1024]{1,0:T(8,128)}, f32[256,1024]{1,0:T(8,128)S(1)}, u32[]{:S(2)}, u32[]{:S(2)}) collective-permute-start(f32[256,1024]{1,0:T(8,128)} %bitcast.7), channel_id=1, source_target_pairs={{0,1},{1,2},{2,3},{3,0},{4,5},{5,6},{6,7},{7,4},{8,9},{9,10},{10,1... | collective-permute-start | bytes 3145736 | tf_op jit(solution)/shard_map/ppermute | solution.py:24
  4.5 3.1 %collective-permute-start.4 = (f32[256,1024]{1,0:T(8,128)}, f32[256,1024]{1,0:T(8,128)S(1)}, u32[]{:S(2)}, u32[]{:S(2)}) collective-permute-start(f32[256,1024]{1,0:T(8,128)} %bitcast.8), channel_id=1, source_target_pairs={{0,3},{1,0},{2,1},{3,2},{4,7},{5,4},{6,5},{7,6},{8,11},{9,8},{10,9... | collective-permute-start | bytes 3145736 | tf_op jit(solution)/shard_map/ppermute | solution.py:24
  7.6 1.1 collective-permute-start
  8.7 2.5 %collective-permute-start.6 = (f32[1]{0:T(128)}, f32[1]{0:T(128)}, u32[]{:S(2)}, u32[]{:S(2)}) collective-permute-start(f32[1]{0:T(128)} %param.4), channel_id=1, source_target_pairs={{0,3},{1,0},{2,1},{3,2},{4,7},{5,4},{6,5},{7,6},{8,11},{9,8},{10,9... | collective-permute-start | bytes 20 | tf_op jit(solution)/shard_map/ppermute | solution.py:24
  11.9 27.3 %collective-permute-done.e_low = f32[1]{0:T(128)} collective-permute-done((f32[1]{0:T(128)}, f32[1]{0:T(128)}, u32[]{:S(2)}, u32[]{:S(2)}) %collective-permute-start) | collective-permute-done | bytes 36 | tf_op jit(solution)/shard_map/ppermute | solution.py:24
  39.2 15.4 %collective-permute-done.6.e_high = f32[1]{0:T(128)} collective-permute-done((f32[1]{0:T(128)}, f32[1]{0:T(128)}, u32[]{:S(2)}, u32[]{:S(2)}) %collective-permute-start.6) | collective-permute-done | bytes 36 | tf_op jit(solution)/shard_map/ppermute | solution.py:24
  54.6 0.0 collective-permute-done.2.low.refs_1_
  54.6 0.0 collective-permute-done.4.high.refs_2_
  54.6 0.0 copy-start.2
  54.6 0.7 copy-done.2
  55.3 1.2 %copy-done = f32[1,256,1024]{2,1,0:T(8,128)S(1)} copy-done((f32[1,256,1024]{2,1,0:T(8,128)S(1)}, f32[1,256,1024]{2,1,0:T(8,128)}, u32[]{:S(2)}) %copy-start) | copy-done | bytes 1048600
  56.5 4.0 %shard_map.52 = (f32[16,8,256]{2,1,0:T(8,128)S(1)}, f32[16,8,256]{2,1,0:T(8,128)S(1)}) custom-call(s32[1]{0:T(128)} %bitcast.3.core, f32[1]{0:T(128)S(6)} %copy.5.e_own, f32[1]{0:T(128)} %collective-permute-done.e_low, f32[1]{0:T(128)} %collective-permute-done.6.e_high, f32[256,1024]{1,0:T(8,128)S(1)} %bitcast.9, ...), custom_call_target="tpu_custom_call" | custom-call | flops 4294967296 | bytes 1048576 | tf_op jit(solution)/shard_map/pallas_call | solution.py:135
  60.5 1.1 collective-permute-start.7
  61.6 0.8 slice.8
  62.4 3.4 %collective-permute-start.3 = (f32[128,1024]{1,0:T(8,128)}, f32[128,1024]{1,0:T(8,128)}, u32[]{:S(2)}, u32[]{:S(2)}) collective-permute-start(f32[128,1024]{1,0:T(8,128)} %slice.8), channel_id=1, source_target_pairs={{0,1},{1,2},{2,3},{3,0},{4,5},{5,6},{6,7},{7,4},{8,9},{9,10},{10,1... | collective-permute-start | bytes 1572872 | tf_op jit(solution)/shard_map/ppermute | solution.py:24
  65.8 0.8 slice.9
  66.6 0.2 collective-permute-start.5
  66.9 0.0 collective-permute-done.7
  66.9 0.7 add.3
  67.5 7.1 %all-to-all-start = ((f32[16,8,256]{2,1,0:T(8,128)}), f32[16,8,256]{2,1,0:T(8,128)S(1)}, u32[]{:S(2)}, u32[]{:S(2)}) async-start(f32[16,8,256]{2,1,0:T(8,128)} %add.3), calls=%async_computation | async-start | bytes 262144 | tf_op jit(solution)/shard_map/all_to_all | solution.py:182
  74.6 2.3 %collective-permute-start.1 = (f32[1]{0:T(128)}, f32[1]{0:T(128)}, u32[]{:S(2)}, u32[]{:S(2)}) collective-permute-start(f32[1]{0:T(128)} %collective-permute-done.e_low), channel_id=1, source_target_pairs={{0,1},{1,2},{2,3},{3,0},{4,5},{5,6},{6,7},{7,4},{8,9},{9,10},{10,1... | collective-permute-start | bytes 20 | tf_op jit(solution)/shard_map/ppermute | solution.py:24
  76.9 19.9 %all-to-all-done.pieces = f32[16,8,256]{2,1,0:T(8,128)S(1)} async-done(((f32[16,8,256]{2,1,0:T(8,128)}), f32[16,8,256]{2,1,0:T(8,128)S(1)}, u32[]{:S(2)}, u32[]{:S(2)}) %all-to-all-start) | async-done | bytes 131104 | tf_op jit(solution)/shard_map/all_to_all | solution.py:182
  96.8 0.7 shard_map.53
  97.5 7.1 %all-to-all-start.1 = ((f32[16,8,256]{2,1,0:T(8,128)}), f32[16,8,256]{2,1,0:T(8,128)S(1)}, u32[]{:S(2)}, u32[]{:S(2)}) async-start(f32[16,8,256]{2,1,0:T(8,128)} %shard_map.53), calls=%async_computation.1 | async-start | bytes 262144 | tf_op jit(solution)/shard_map/all_to_all | solution.py:184
  104.6 0.0 copy-done.1
  104.6 4.2 %shard_map.50.near = f32[256,1024]{1,0:T(8,128)} custom-call(f32[1]{0:T(128)S(6)} %copy.5.e_own, f32[1]{0:T(128)} %collective-permute-done.e_low, f32[1]{0:T(128)} %collective-permute-done.6.e_high, f32[256,1024]{1,0:T(8,128)S(1)} %bitcast.10, f32[256,1024]{1,0:T(8,128)S(1)} %collective-permute-done.2.low.refs_1_, ...), custom_call_target="tpu_custom_call" | custom-call | flops 2147483648 | bytes 1048576 | tf_op jit(solution)/shard_map/pallas_call | solution.py:135
  108.8 0.0 collective-permute-done.1.e_far
  108.8 0.0 collective-permute-done.3.far_a
  108.8 0.0 collective-permute-done.5.far_b
  108.8 4.7 %shard_map.51 = f32[256,1024]{1,0:T(8,128)} custom-call(f32[1]{0:T(128)S(6)} %copy.5.e_own, f32[1]{0:T(128)} %collective-permute-done.1.e_far, f32[1,256]{1,0:T(1,128)S(1)} %bitcast.14, f32[256,1024]{1,0:T(8,128)S(1)} %bitcast.11, f32[128,1024]{1,0:T(8,128)} %collective-permute-done.3.far_a, f32[128,1024]{1,0:T(8,128)} %collective-permute-done.5.far_b, ...), custom_call_target="tpu_custom_call" | custom-call | flops 2147483648 | bytes 1048576 | tf_op jit(solution)/shard_map/pallas_call | solution.py:135
  113.5 0.0 all-to-all-done.1
  113.5 0.6 bitcast_reduce_fusion
  (2 shorter events, 0.0 us)
Async XLA Ops:
  0.6 54.0 %collective-permute-start.2 = (f32[256,1024]{1,0:T(8,128)}, f32[256,1024]{1,0:T(8,128)S(1)}, u32[]{:S(2)}, u32[]{:S(2)}) collective-permute-start(f32[256,1024]{1,0:T(8,128)} %bitcast.7), channel_id=1, source_target_pairs={{0,1},{1,2},{2,3},{3,0},{4,5},{5,6},{6,7},{7,4},{8,9},{9,10},{10,1... | collective-permute-start | bytes 3145736 | tf_op jit(solution)/shard_map/ppermute | solution.py:24
  4.5 50.1 %collective-permute-start.4 = (f32[256,1024]{1,0:T(8,128)}, f32[256,1024]{1,0:T(8,128)S(1)}, u32[]{:S(2)}, u32[]{:S(2)}) collective-permute-start(f32[256,1024]{1,0:T(8,128)} %bitcast.8), channel_id=1, source_target_pairs={{0,3},{1,0},{2,1},{3,2},{4,7},{5,4},{6,5},{7,6},{8,11},{9,8},{10,9... | collective-permute-start | bytes 3145736 | tf_op jit(solution)/shard_map/ppermute | solution.py:24
  7.6 31.6 %collective-permute-start = (f32[1]{0:T(128)}, f32[1]{0:T(128)}, u32[]{:S(2)}, u32[]{:S(2)}) collective-permute-start(f32[1]{0:T(128)} %param.4), channel_id=1, source_target_pairs={{0,1},{1,2},{2,3},{3,0},{4,5},{5,6},{6,7},{7,4},{8,9},{9,10},{10,1... | collective-permute-start | bytes 20 | tf_op jit(solution)/shard_map/ppermute | solution.py:24
  8.7 45.9 %collective-permute-start.6 = (f32[1]{0:T(128)}, f32[1]{0:T(128)}, u32[]{:S(2)}, u32[]{:S(2)}) collective-permute-start(f32[1]{0:T(128)} %param.4), channel_id=1, source_target_pairs={{0,3},{1,0},{2,1},{3,2},{4,7},{5,4},{6,5},{7,6},{8,11},{9,8},{10,9... | collective-permute-start | bytes 20 | tf_op jit(solution)/shard_map/ppermute | solution.py:24
  54.6 0.7 copy-start.2
  55.3 1.2 %copy-start = (f32[1,256,1024]{2,1,0:T(8,128)S(1)}, f32[1,256,1024]{2,1,0:T(8,128)}, u32[]{:S(2)}) copy-start(f32[1,256,1024]{2,1,0:T(8,128)} %param.3) | copy-start | bytes 3145732
  60.5 6.3 %collective-permute-start.7 = (f32[16,8,256]{2,1,0:T(8,128)S(1)}, f32[16,8,256]{2,1,0:T(8,128)S(1)}, u32[]{:S(2)}, u32[]{:S(2)}) collective-permute-start(f32[16,8,256]{2,1,0:T(8,128)S(1)} %get-tuple-element.5), channel_id=1, source_target_pairs={{0,16},{16,0},{32,48},{48,32},{64,80},{80,64},{96,112},{112,96},{1... | collective-permute-start | bytes 393224 | tf_op jit(solution)/shard_map/ppermute | solution.py:181
  62.4 42.1 %copy-start.1 = (f32[1,256,1024]{2,1,0:T(8,128)S(1)}, f32[1,256,1024]{2,1,0:T(8,128)}, u32[]{:S(2)}) copy-start(f32[1,256,1024]{2,1,0:T(8,128)} %param.3) | copy-start | bytes 3145732
  62.4 46.3 %collective-permute-start.3 = (f32[128,1024]{1,0:T(8,128)}, f32[128,1024]{1,0:T(8,128)}, u32[]{:S(2)}, u32[]{:S(2)}) collective-permute-start(f32[128,1024]{1,0:T(8,128)} %slice.8), channel_id=1, source_target_pairs={{0,1},{1,2},{2,3},{3,0},{4,5},{5,6},{6,7},{7,4},{8,9},{9,10},{10,1... | collective-permute-start | bytes 1572872 | tf_op jit(solution)/shard_map/ppermute | solution.py:24
  66.6 42.1 %collective-permute-start.5 = (f32[128,1024]{1,0:T(8,128)}, f32[128,1024]{1,0:T(8,128)}, u32[]{:S(2)}, u32[]{:S(2)}) collective-permute-start(f32[128,1024]{1,0:T(8,128)} %slice.9), channel_id=1, source_target_pairs={{0,3},{1,0},{2,1},{3,2},{4,7},{5,4},{6,5},{7,6},{8,11},{9,8},{10,9... | collective-permute-start | bytes 1572872 | tf_op jit(solution)/shard_map/ppermute | solution.py:24
  67.5 29.3 %all-to-all-start = ((f32[16,8,256]{2,1,0:T(8,128)}), f32[16,8,256]{2,1,0:T(8,128)S(1)}, u32[]{:S(2)}, u32[]{:S(2)}) async-start(f32[16,8,256]{2,1,0:T(8,128)} %add.3), calls=%async_computation | async-start | bytes 262144 | tf_op jit(solution)/shard_map/all_to_all | solution.py:182
  74.6 34.1 %collective-permute-start.1 = (f32[1]{0:T(128)}, f32[1]{0:T(128)}, u32[]{:S(2)}, u32[]{:S(2)}) collective-permute-start(f32[1]{0:T(128)} %collective-permute-done.e_low), channel_id=1, source_target_pairs={{0,1},{1,2},{2,3},{3,0},{4,5},{5,6},{6,7},{7,4},{8,9},{9,10},{10,1... | collective-permute-start | bytes 20 | tf_op jit(solution)/shard_map/ppermute | solution.py:24
  97.5 16.0 %all-to-all-start.1 = ((f32[16,8,256]{2,1,0:T(8,128)}), f32[16,8,256]{2,1,0:T(8,128)S(1)}, u32[]{:S(2)}, u32[]{:S(2)}) async-start(f32[16,8,256]{2,1,0:T(8,128)} %shard_map.53), calls=%async_computation.1 | async-start | bytes 262144 | tf_op jit(solution)/shard_map/all_to_all | solution.py:184

commit v4 on v3

v4 whole, which is shorter than its diff:
```python
import jax
import jax.numpy as jnp
from jax import lax
from jax.experimental import pallas as pl
from jax.experimental.pallas import tpu as pltpu
from jax.sharding import Mesh, PartitionSpec as P


FINE = ("y", "near", "core", "x", "far")
FINE_SHAPE = (4, 2, 2, 4, 4)
VMEM = pl.BlockSpec(memory_space=pltpu.VMEM)
SMEM = pl.BlockSpec(memory_space=pltpu.SMEM)
HBM = pl.BlockSpec(memory_space=pltpu.HBM)
F32, BF16 = jnp.float32, jnp.bfloat16
ROWS = ((1,), (1,))
PLAIN = ((1,), (0,))
MIB = 1 << 20


def shift(value, step):
    size = lax.axis_size("far")
    return lax.ppermute(value, "far", [(i, (i + step) % size) for i in range(size)])


def split(x):
    high = x.astype(BF16)
    return high, (x - high.astype(F32)).astype(BF16)


def mm(a, b, contract):
    def dot(p, q):
        return lax.dot_general(p, q, (contract, ((), ())), preferred_element_type=F32)

    return dot(a[0], b[0]) + (dot(a[0], b[1]) + dot(a[1], b[0]))


def fill(chunks, high, low):
    at = 0
    for chunk in chunks:
        end = at + chunk.shape[0]
        high[at:end, :], low[at:end, :] = split(chunk[...])
        at = end
    return high[...], low[...]


def base_kernel(eps_vir, base):
    row = jnp.broadcast_to(eps_vir[...], base.shape)
    base[...] = row + row.T


def join_kernel(keep, other, copies):
    for at in range(copies.shape[1]):
        piece = keep[at] + other[at]
        for copy in range(copies.shape[0]):
            copies[copy, at] = piece


def amplitudes(left, right, energy, base):
    return mm(left, right, ROWS) / (energy - base)


def spin(t):
    return split(2.0 * t - t.T)


def density_kernel(
    core, e_own, e_low, e_high, pairs, own, low, high, keep, send, down, up, *scratch
):
    oh, ol, lh, ll, hh, hl, dens, buf_down, buf_up, mine, sems = scratch
    half = down.shape[0]
    fetch = pltpu.make_async_copy(own, mine, sems.at[2])
    fetch.start()
    base = pairs[...]
    l, h = fill((low,), lh, ll), fill((high,), hh, hl)
    t = amplitudes(l, h, e_low[...] + e_high[...], base)
    s, r = spin(t), split(2.0 * t.T - t)
    buf_down[...] = mm([x[:half] for x in s], h, PLAIN)
    to_down = pltpu.make_async_copy(buf_down, down, sems.at[0])
    to_down.start()
    buf_up[...] = mm([x[half:] for x in r], l, PLAIN)
    to_up = pltpu.make_async_copy(buf_up, up, sems.at[1])
    to_up.start()
    total = mm(split(t), s, ROWS)
    fetch.wait()
    o = fill((mine,), oh, ol)
    for other, energy in ((l, e_low), (h, e_high)):
        t = amplitudes(o, other, e_own[...] + energy[...], base)
        total = total + mm(split(t), spin(t), ROWS)
    dens[...] = total
    first = core[0] * 8
    for at in range(16):
        keep[at] = dens[pl.ds(pl.multiple_of(at * 16 + first, 8), 8), :]
        send[at] = dens[pl.ds(pl.multiple_of(at * 16 + 8 - first, 8), 8), :]
    to_down.wait()
    to_up.wait()


def near_kernel(e_own, e_low, e_high, pairs, own, low, high, grad, *scratch):
    oh, ol, lh, ll, hh, hl, total, sem = scratch
    base = pairs[...]
    fetch = pltpu.make_async_copy(own, total, sem)
    fetch.start()
    l, h = fill((low,), lh, ll), fill((high,), hh, hl)
    fetch.wait()
    o = fill((total,), oh, ol)
    s_low = spin(amplitudes(o, l, e_own[...] + e_low[...], base))
    s_high = spin(amplitudes(o, h, e_own[...] + e_high[...], base))
    total[...] = mm(s_low, l, PLAIN) + mm(s_high, h, PLAIN)
    out = pltpu.make_async_copy(total, grad, sem)
    out.start()
    out.wait()


def sum_kernel(near, first, second, grad, mine, other, sems):
    half = first.shape[0]
    parts, step = 4, half // 2
    copies = []
    for at in range(parts):
        rows = pl.ds(at * step, step)
        source = (first, second)[at // 2].at[pl.ds(at % 2 * step, step), :]
        copies.append(
            (
                pltpu.make_async_copy(near.at[rows, :], mine.at[rows, :], sems.at[0, at]),
                pltpu.make_async_copy(source, other.at[rows, :], sems.at[1, at]),
                pltpu.make_async_copy(mine.at[rows, :], grad.at[rows, :], sems.at[2, at]),
            )
        )
        copies[-1][0].start()
        copies[-1][1].start()
    for at in range(parts):
        rows = slice(at * step, (at + 1) * step)
        copies[at][0].wait()
        copies[at][1].wait()
        mine[rows, :] = mine[rows, :] + other[rows, :]
        copies[at][2].start()
    for at in range(parts):
        copies[at][2].wait()


def fold_kernel(pieces, copies):
    total = pieces[0]
    for at in range(1, pieces.shape[0]):
        total = total + pieces[at]
    total = total * (1.0 / 256.0)
    for at in range(copies.shape[0]):
        row = at // 2 % 4 * 8
        copies[at] = total[row : row + 8, :]


def call(kernel, out, scratch, limit, flops, args, in_specs, out_specs):
    return pl.pallas_call(
        kernel,
        out_shape=tuple(
            pltpu.HBM(s, F32) if spec is HBM else jax.ShapeDtypeStruct(s, F32)
            for s, spec in zip(out, out_specs)
        ),
        in_specs=in_specs,
        out_specs=out_specs,
        scratch_shapes=scratch,
        cost_estimate=pl.CostEstimate(
            flops=flops, bytes_accessed=MIB, transcendentals=0
        ),
        compiler_params=pltpu.CompilerParams(vmem_limit_bytes=limit * MIB),
    )(*args)


def body(slabs, eps_occ, eps_vir):
    own = slabs[0]
    v, n = own.shape
    low = shift(own, 1)
    high = shift(own, -1)
    e_own = eps_occ[None]
    e_low = shift(eps_occ, 1)[None]
    e_high = shift(eps_occ, -1)[None]
    (pairs,) = call(base_kernel, ((v, v),), [], 4, 1 << 20, (eps_vir[None],), [VMEM], (VMEM,))

    source = pltpu.with_memory_space_constraint(own, pltpu.HBM)
    core = lax.axis_index("core").astype(jnp.int32)[None]
    piece = (16, 8, v)
    wide = [pltpu.VMEM((v, n), BF16)]
    full = [pltpu.VMEM((v, n), F32)]
    part = [pltpu.VMEM((v // 2, n), F32)]
    keep, send, down, up = call(
        density_kernel,
        (piece, piece, (v // 2, n), (v // 2, n)),
        wide * 6 + [pltpu.VMEM((v, v), F32)] + part * 2 + full + [pltpu.SemaphoreType.DMA((3,))],
        16,
        1 << 32,
        (core, e_own, e_low, e_high, pairs, source, low, high),
        [SMEM] + [VMEM] * 4 + [HBM] + [VMEM] * 2,
        (VMEM, VMEM, HBM, HBM),
    )
    other = lax.ppermute(send, "core", [(0, 1), (1, 0)])
    second = shift(up, 1)
    first = shift(down, -1)
    (mine,) = call(join_kernel, ((4,) + piece,), [], 4, 1 << 20, (keep, other), [VMEM] * 2, (VMEM,))
    parts = lax.all_to_all(
        mine.reshape(16, 32, v),
        ("y", "x"),
        split_axis=0,
        concat_axis=0,
        tiled=True,
    )
    (copies,) = call(fold_kernel, (piece,), [], 4, 1 << 20, (parts,), [VMEM], (VMEM,))
    copies = lax.all_to_all(
        copies, ("near", "far", "core"), split_axis=0, concat_axis=0, tiled=True
    )
    density = jnp.sum(copies.reshape(8, 16, v), axis=0)

    (near,) = call(
        near_kernel,
        (own.shape,),
        wide * 6 + full + [pltpu.SemaphoreType.DMA],
        16,
        1 << 31,
        (e_own, e_low, e_high, pairs, source, low, high),
        [VMEM] * 4 + [HBM] + [VMEM] * 2,
        (HBM,),
    )
    near = pltpu.with_memory_space_constraint(near, pltpu.HBM)
    (grad,) = call(
        sum_kernel,
        (own.shape,),
        full * 2 + [pltpu.SemaphoreType.DMA((3, 4))],
        8,
        1 << 20,
        (near, first, second),
        [HBM] * 3,
        (HBM,),
    )
    return grad[None], density


def solution(mesh):
    fine = Mesh(mesh.devices.reshape(FINE_SHAPE), FINE)
    placed = (P(FINE, None, None), P(FINE), P())
    return jax.shard_map(
        body,
        mesh=fine,
        in_specs=placed,
        out_specs=(P(FINE, None, None), P(("x", "far"), None)),
        check_vma=False,
    )
```

time: 114 us -> 104 us (0.912)
  the two profiles are of different devices: /device:TPU:1 before, /device:TPU:2 now
where the time goes in v4:
time: 104 us
  waiting for transfers between devices  57.5 us (55%)
  starting transfers between devices  27.2 us (26%)
  Pallas kernels  15.1 us (15%)
  local copies, waits for them, and re-layouts  1.9 us (2%)
  between operations  1.41 us (1%)
    ppermute x6, waiting for transfers between devices, shift(): lax.ppermute(value, 'far', [(i, (i + step) % size) for i in range(size)])  49.4 us
    pallas_call x6, Pallas kernels, call(): pl.pallas_call(kernel, out_shape=tuple((pltpu.HBM(s, F32) if spec is HBM...  15.1 us
    ppermute x6, starting transfers between devices, shift(): lax.ppermute(value, 'far', [(i, (i + step) % size) for i in range(size)])  14.3 us
    all_to_all x1, starting transfers between devices, body(): lax.all_to_all(mine.reshape(16, 32, v), ('y', 'x'), split_axis=0, concat_...  7.61 us
    all_to_all x1, waiting for transfers between devices, body(): lax.all_to_all(mine.reshape(16, 32, v), ('y', 'x'), split_axis=0, concat_...  6.76 us
    all_to_all x1, starting transfers between devices, body(): lax.all_to_all(copies, ('near', 'far', 'core'), split_axis=0, concat_axis...  5.2 us
  transfers between devices with their start and end apart: 9, of which 6 were waited for; matrix products, arithmetic and copies ran while one was open for 0% of the time, Pallas kernels for 8%

profile of v4, /device:TPU:2, one launch (start us, length us, event | category | flops | bytes accessed | tf_op | source)
XLA Modules:
  0.0 103.7 jit_solution(1422126020430766889)
XLA Ops:
  0.6 3.3 %collective-permute-start.2 = (f32[256,1024]{1,0:T(8,128)}, f32[256,1024]{1,0:T(8,128)S(1)}, u32[]{:S(2)}, u32[]{:S(2)}) collective-permute-start(f32[256,1024]{1,0:T(8,128)} %bitcast.16), channel_id=1, source_target_pairs={{0,1},{1,2},{2,3},{3,0},{4,5},{5,6},{6,7},{7,4},{8,9},{9,10},{10,1... | collective-permute-start | bytes 3145736 | tf_op jit(solution)/shard_map/ppermute | solution.py:22
  4.0 3.1 %collective-permute-start.3 = (f32[256,1024]{1,0:T(8,128)}, f32[256,1024]{1,0:T(8,128)S(1)}, u32[]{:S(2)}, u32[]{:S(2)}) collective-permute-start(f32[256,1024]{1,0:T(8,128)} %bitcast.17), channel_id=1, source_target_pairs={{0,3},{1,0},{2,1},{3,2},{4,7},{5,4},{6,5},{7,6},{8,11},{9,8},{10,9... | collective-permute-start | bytes 3145736 | tf_op jit(solution)/shard_map/ppermute | solution.py:22
  7.1 1.4 %collective-permute-start = (f32[1]{0:T(128)}, f32[1]{0:T(128)}, u32[]{:S(2)}, u32[]{:S(2)}) collective-permute-start(f32[1]{0:T(128)} %param.4), channel_id=1, source_target_pairs={{0,1},{1,2},{2,3},{3,0},{4,5},{5,6},{6,7},{7,4},{8,9},{9,10},{10,1... | collective-permute-start | bytes 20 | tf_op jit(solution)/shard_map/ppermute | solution.py:22
  8.5 2.8 %collective-permute-start.1 = (f32[1]{0:T(128)}, f32[1]{0:T(128)}, u32[]{:S(2)}, u32[]{:S(2)}) collective-permute-start(f32[1]{0:T(128)} %param.4), channel_id=1, source_target_pairs={{0,3},{1,0},{2,1},{3,2},{4,7},{5,4},{6,5},{7,6},{8,11},{9,8},{10,9... | collective-permute-start | bytes 20 | tf_op jit(solution)/shard_map/ppermute | solution.py:22
  11.9 0.0 copy-start
  11.9 0.7 copy-done
  12.6 0.1 shard_map.50.pairs
  12.7 26.8 %collective-permute-done = f32[1]{0:T(128)} collective-permute-done((f32[1]{0:T(128)}, f32[1]{0:T(128)}, u32[]{:S(2)}, u32[]{:S(2)}) %collective-permute-start) | collective-permute-done | bytes 36 | tf_op jit(solution)/shard_map/ppermute | solution.py:22
  39.5 14.6 %collective-permute-done.1 = f32[1]{0:T(128)} collective-permute-done((f32[1]{0:T(128)}, f32[1]{0:T(128)}, u32[]{:S(2)}, u32[]{:S(2)}) %collective-permute-start.1) | collective-permute-done | bytes 36 | tf_op jit(solution)/shard_map/ppermute | solution.py:22
  54.1 0.0 collective-permute-done.2.low
  54.1 0.0 collective-permute-done.3.high
  54.1 0.0 copy-start.1
  54.1 5.9 %shard_map.52 = (f32[16,8,256]{2,1,0:T(8,128)S(1)}, f32[16,8,256]{2,1,0:T(8,128)S(1)}, f32[128,1024]{1,0:T(8,128)}, f32[128,1024]{1,0:T(8,128)}) custom-call(s32[1]{0:T(128)} %bitcast.5.core, f32[1,1]{1,0:T(1,128)} %bitcast.12.e_own, f32[1,1]{1,0:T(1,128)} %bitcast.1.e_low, f32[1,1]{1,0:T(1,128)} %bitcast.2.e_high, f32[256,256]{1,0:T(8,128)S(1)} %shard_map.50.pairs, ...), custom_call_target="tpu_custom_call" | custom-call | flops 4294967296 | bytes 1048576 | tf_op jit(solution)/shard_map/pallas_call | solution.py:151
  60.1 0.0 copy-done.1
  60.1 0.1 collective-permute-start.6
  60.2 1.3 %collective-permute-done.6.other = f32[16,8,256]{2,1,0:T(8,128)S(1)} collective-permute-done((f32[16,8,256]{2,1,0:T(8,128)S(1)}, f32[16,8,256]{2,1,0:T(8,128)S(1)}, u32[]{:S(2)}, u32[]{:S(2)}) %collective-permute-start.6) | collective-permute-done | bytes 131104 | tf_op jit(solution)/shard_map/ppermute | solution.py:193
  61.5 0.8 shard_map.54
  62.3 7.6 %all-to-all-start = ((f32[16,32,256]{2,1,0:T(8,128)}), f32[16,32,256]{2,1,0:T(8,128)S(1)}, u32[]{:S(2)}, u32[]{:S(2)}) async-start(f32[16,32,256]{2,1,0:T(8,128)} %bitcast.7), calls=%async_computation | async-start | bytes 1048576 | tf_op jit(solution)/shard_map/all_to_all | solution.py:197
  70.0 2.7 %collective-permute-start.4 = (f32[128,1024]{1,0:T(8,128)}, f32[128,1024]{1,0:T(8,128)S(1)}, u32[]{:S(2)}, u32[]{:S(2)}) collective-permute-start(f32[128,1024]{1,0:T(8,128)} %get-tuple-element.6), channel_id=1, source_target_pairs={{0,3},{1,0},{2,1},{3,2},{4,7},{5,4},{6,5},{7,6},{8,11},{9,8},{10,9... | collective-permute-start | bytes 1572872 | tf_op jit(solution)/shard_map/ppermute | solution.py:22
  72.7 0.0 copy-done.3
  72.7 1.0 collective-permute-start.5
  73.7 6.8 %all-to-all-done.pieces = f32[16,32,256]{2,1,0:T(8,128)S(1)} async-done(((f32[16,32,256]{2,1,0:T(8,128)}), f32[16,32,256]{2,1,0:T(8,128)S(1)}, u32[]{:S(2)}, u32[]{:S(2)}) %all-to-all-start) | async-done | bytes 524320 | tf_op jit(solution)/shard_map/all_to_all | solution.py:197
  80.4 0.7 shard_map.55
  81.1 5.2 %all-to-all-start.1 = ((f32[16,8,256]{2,1,0:T(8,128)}), f32[16,8,256]{2,1,0:T(8,128)S(1)}, u32[]{:S(2)}, u32[]{:S(2)}) async-start(f32[16,8,256]{2,1,0:T(8,128)} %shard_map.55), calls=%async_computation.1 | async-start | bytes 262144 | tf_op jit(solution)/shard_map/all_to_all | solution.py:205
  86.3 0.0 copy-start.2
  86.3 1.2 %copy-done.2 = f32[256,1024]{1,0:T(8,128)S(1)} copy-done((f32[256,1024]{1,0:T(8,128)S(1)}, f32[256,1024]{1,0:T(8,128)}, u32[]{:S(2)}) %copy-start.2) | copy-done | bytes 1048600
  87.6 5.5 %shard_map.51.near = f32[256,1024]{1,0:T(8,128)} custom-call(f32[1,1]{1,0:T(1,128)} %bitcast.11.e_own, f32[1,1]{1,0:T(1,128)} %bitcast.1.e_low, f32[1,1]{1,0:T(1,128)} %bitcast.2.e_high, f32[256,256]{1,0:T(8,128)S(1)} %shard_map.50.pairs, f32[256,1024]{1,0:T(8,128)} %bitcast.19, f32[256,1024]{1,0:T(8,128)S(1)} %collective-permute-done.2.low, ...), custom_call_target="tpu_custom_call" | custom-call | flops 2147483648 | bytes 1048576 | tf_op jit(solution)/shard_map/pallas_call | solution.py:151
  93.0 4.1 %collective-permute-done.4.first = f32[128,1024]{1,0:T(8,128)S(1)} collective-permute-done((f32[128,1024]{1,0:T(8,128)}, f32[128,1024]{1,0:T(8,128)S(1)}, u32[]{:S(2)}, u32[]{:S(2)}) %collective-permute-start.4) | collective-permute-done | bytes 524320 | tf_op jit(solution)/shard_map/ppermute | solution.py:22
  97.2 3.9 %collective-permute-done.5.second = f32[128,1024]{1,0:T(8,128)S(1)} collective-permute-done((f32[128,1024]{1,0:T(8,128)S(1)}, f32[128,1024]{1,0:T(8,128)S(1)}, u32[]{:S(2)}, u32[]{:S(2)}) %collective-permute-start.5) | collective-permute-done | bytes 524320 | tf_op jit(solution)/shard_map/ppermute | solution.py:22
  101.1 2.0 %shard_map.53 = f32[256,1024]{1,0:T(8,128)} custom-call(f32[256,1024]{1,0:T(8,128)} %shard_map.51.near, f32[128,1024]{1,0:T(8,128)S(1)} %collective-permute-done.4.first, f32[128,1024]{1,0:T(8,128)S(1)} %collective-permute-done.5.second), custom_call_target="tpu_custom_call" | custom-call | flops 1048576 | bytes 1048576 | tf_op jit(solution)/shard_map/pallas_call | solution.py:151
  103.1 0.0 all-to-all-done.1
  103.1 0.6 bitcast_reduce_fusion
  (1 shorter events, 0.0 us)
Async XLA Ops:
  0.6 53.5 %collective-permute-start.2 = (f32[256,1024]{1,0:T(8,128)}, f32[256,1024]{1,0:T(8,128)S(1)}, u32[]{:S(2)}, u32[]{:S(2)}) collective-permute-start(f32[256,1024]{1,0:T(8,128)} %bitcast.16), channel_id=1, source_target_pairs={{0,1},{1,2},{2,3},{3,0},{4,5},{5,6},{6,7},{7,4},{8,9},{9,10},{10,1... | collective-permute-start | bytes 3145736 | tf_op jit(solution)/shard_map/ppermute | solution.py:22
  4.0 50.1 %collective-permute-start.3 = (f32[256,1024]{1,0:T(8,128)}, f32[256,1024]{1,0:T(8,128)S(1)}, u32[]{:S(2)}, u32[]{:S(2)}) collective-permute-start(f32[256,1024]{1,0:T(8,128)} %bitcast.17), channel_id=1, source_target_pairs={{0,3},{1,0},{2,1},{3,2},{4,7},{5,4},{6,5},{7,6},{8,11},{9,8},{10,9... | collective-permute-start | bytes 3145736 | tf_op jit(solution)/shard_map/ppermute | solution.py:22
  7.1 32.4 %collective-permute-start = (f32[1]{0:T(128)}, f32[1]{0:T(128)}, u32[]{:S(2)}, u32[]{:S(2)}) collective-permute-start(f32[1]{0:T(128)} %param.4), channel_id=1, source_target_pairs={{0,1},{1,2},{2,3},{3,0},{4,5},{5,6},{6,7},{7,4},{8,9},{9,10},{10,1... | collective-permute-start | bytes 20 | tf_op jit(solution)/shard_map/ppermute | solution.py:22
  8.5 45.6 %collective-permute-start.1 = (f32[1]{0:T(128)}, f32[1]{0:T(128)}, u32[]{:S(2)}, u32[]{:S(2)}) collective-permute-start(f32[1]{0:T(128)} %param.4), channel_id=1, source_target_pairs={{0,3},{1,0},{2,1},{3,2},{4,7},{5,4},{6,5},{7,6},{8,11},{9,8},{10,9... | collective-permute-start | bytes 20 | tf_op jit(solution)/shard_map/ppermute | solution.py:22
  11.9 0.7 copy-start
  54.1 6.0 %copy-start.1 = (f32[256,1024]{1,0:T(8,128)}, f32[256,1024]{1,0:T(8,128)S(1)}, u32[]{:S(2)}) copy-start(f32[256,1024]{1,0:T(8,128)S(1)} %collective-permute-done.3.high) | copy-start | bytes 3145732
  60.1 1.4 %collective-permute-start.6 = (f32[16,8,256]{2,1,0:T(8,128)S(1)}, f32[16,8,256]{2,1,0:T(8,128)S(1)}, u32[]{:S(2)}, u32[]{:S(2)}) collective-permute-start(f32[16,8,256]{2,1,0:T(8,128)S(1)} %get-tuple-element.9), channel_id=1, source_target_pairs={{0,16},{16,0},{1,17},{17,1},{2,18},{18,2},{3,19},{19,3},{4,20},{20... | collective-permute-start | bytes 393224 | tf_op jit(solution)/shard_map/ppermute | solution.py:193
  62.3 10.4 %copy-start.3 = (f32[128,1024]{1,0:T(8,128)S(1)}, f32[128,1024]{1,0:T(8,128)}, u32[]{:S(2)}) copy-start(f32[128,1024]{1,0:T(8,128)} %get-tuple-element.7) | copy-start | bytes 1572868
  62.3 18.1 %all-to-all-start = ((f32[16,32,256]{2,1,0:T(8,128)}), f32[16,32,256]{2,1,0:T(8,128)S(1)}, u32[]{:S(2)}, u32[]{:S(2)}) async-start(f32[16,32,256]{2,1,0:T(8,128)} %bitcast.7), calls=%async_computation | async-start | bytes 1048576 | tf_op jit(solution)/shard_map/all_to_all | solution.py:197
  70.0 27.2 %collective-permute-start.4 = (f32[128,1024]{1,0:T(8,128)}, f32[128,1024]{1,0:T(8,128)S(1)}, u32[]{:S(2)}, u32[]{:S(2)}) collective-permute-start(f32[128,1024]{1,0:T(8,128)} %get-tuple-element.6), channel_id=1, source_target_pairs={{0,3},{1,0},{2,1},{3,2},{4,7},{5,4},{6,5},{7,6},{8,11},{9,8},{10,9... | collective-permute-start | bytes 1572872 | tf_op jit(solution)/shard_map/ppermute | solution.py:22
  72.7 28.4 %collective-permute-start.5 = (f32[128,1024]{1,0:T(8,128)S(1)}, f32[128,1024]{1,0:T(8,128)S(1)}, u32[]{:S(2)}, u32[]{:S(2)}) collective-permute-start(f32[128,1024]{1,0:T(8,128)S(1)} %copy-done.3), channel_id=1, source_target_pairs={{0,1},{1,2},{2,3},{3,0},{4,5},{5,6},{6,7},{7,4},{8,9},{9,10},{10,1... | collective-permute-start | bytes 1572872 | tf_op jit(solution)/shard_map/ppermute | solution.py:22
  81.1 22.0 %all-to-all-start.1 = ((f32[16,8,256]{2,1,0:T(8,128)}), f32[16,8,256]{2,1,0:T(8,128)S(1)}, u32[]{:S(2)}, u32[]{:S(2)}) async-start(f32[16,8,256]{2,1,0:T(8,128)} %shard_map.55), calls=%async_computation.1 | async-start | bytes 262144 | tf_op jit(solution)/shard_map/all_to_all | solution.py:205
  86.3 1.2 %copy-start.2 = (f32[256,1024]{1,0:T(8,128)S(1)}, f32[256,1024]{1,0:T(8,128)}, u32[]{:S(2)}) copy-start(f32[256,1024]{1,0:T(8,128)} %copy-done.1) | copy-start | bytes 3145732

commit v5 on v4

--- a/solution.py
+++ b/solution.py
@@ -55,57 +55,82 @@
             copies[copy, at] = piece
 
 
-def amplitudes(left, right, energy, base):
-    return mm(left, right, ROWS) / (energy - base)
-
-
 def spin(t):
     return split(2.0 * t - t.T)
 
 
-def density_kernel(
-    core, e_own, e_low, e_high, pairs, own, low, high, keep, send, down, up, *scratch
-):
-    oh, ol, lh, ll, hh, hl, dens, buf_down, buf_up, mine, sems = scratch
+def scalars(refs, values, sems):
+    copies = [
+        pltpu.make_async_copy(ref, value, sems.at[at])
+        for at, (ref, value) in enumerate(zip(refs, values))
+    ]
+    for copy in copies:
+        copy.start()
+    return copies
+
+
+def mid_kernel(e_low, e_high, pairs, low, high, down, up, *scratch):
+    lh, ll, hh, hl, buf_down, buf_up, s_low, s_high, small, sems = scratch
+    copies = scalars((e_low, e_high), (s_low, s_high), small)
     half = down.shape[0]
-    fetch = pltpu.make_async_copy(own, mine, sems.at[2])
-    fetch.start()
-    base = pairs[...]
     l, h = fill((low,), lh, ll), fill((high,), hh, hl)
-    t = amplitudes(l, h, e_low[...] + e_high[...], base)
-    s, r = spin(t), split(2.0 * t.T - t)
-    buf_down[...] = mm([x[:half] for x in s], h, PLAIN)
+    k = mm(l, h, ROWS)
+    for copy in copies:
+        copy.wait()
+    t = k / (s_low[0] + s_high[0] - pairs[...])
+    turned = t.T
+    s = split(2.0 * t[:half] - turned[:half])
+    buf_down[...] = mm(s, h, PLAIN)
     to_down = pltpu.make_async_copy(buf_down, down, sems.at[0])
     to_down.start()
-    buf_up[...] = mm([x[half:] for x in r], l, PLAIN)
+    s = split(2.0 * turned[half:] - t[half:])
+    buf_up[...] = mm(s, l, PLAIN)
     to_up = pltpu.make_async_copy(buf_up, up, sems.at[1])
     to_up.start()
-    total = mm(split(t), s, ROWS)
+    to_down.wait()
+    to_up.wait()
+
+
+def density_kernel(
+    e_own, core, e_low, e_high, pairs, own, low, high, keep, send, *scratch
+):
+    oh, ol, lh, ll, hh, hl, dens, mine, sem, c, s_low, s_high, small = scratch
+    copies = scalars((core, e_low, e_high), (c, s_low, s_high), small)
+    fetch = pltpu.make_async_copy(own, mine, sem)
+    fetch.start()
+    l, h = fill((low,), lh, ll), fill((high,), hh, hl)
+    k = mm(l, h, ROWS)
+    for copy in copies:
+        copy.wait()
+    t = k / (s_low[0] + s_high[0] - pairs[...])
+    total = mm(split(t), spin(t), ROWS)
     fetch.wait()
     o = fill((mine,), oh, ol)
-    for other, energy in ((l, e_low), (h, e_high)):
-        t = amplitudes(o, other, e_own[...] + energy[...], base)
+    for other, energy in ((l, s_low), (h, s_high)):
+        t = mm(o, other, ROWS) / (e_own[0] + energy[0] - pairs[...])
         total = total + mm(split(t), spin(t), ROWS)
     dens[...] = total
-    first = core[0] * 8
+    first = c[0] * 8
     for at in range(16):
         keep[at] = dens[pl.ds(pl.multiple_of(at * 16 + first, 8), 8), :]
         send[at] = dens[pl.ds(pl.multiple_of(at * 16 + 8 - first, 8), 8), :]
-    to_down.wait()
-    to_up.wait()
 
 
 def near_kernel(e_own, e_low, e_high, pairs, own, low, high, grad, *scratch):
-    oh, ol, lh, ll, hh, hl, total, sem = scratch
-    base = pairs[...]
+    oh, ol, lh, ll, hh, hl, total, sem, s_low, s_high, small = scratch
+    copies = scalars((e_low, e_high), (s_low, s_high), small)
     fetch = pltpu.make_async_copy(own, total, sem)
     fetch.start()
     l, h = fill((low,), lh, ll), fill((high,), hh, hl)
     fetch.wait()
     o = fill((total,), oh, ol)
-    s_low = spin(amplitudes(o, l, e_own[...] + e_low[...], base))
-    s_high = spin(amplitudes(o, h, e_own[...] + e_high[...], base))
-    total[...] = mm(s_low, l, PLAIN) + mm(s_high, h, PLAIN)
+    for copy in copies:
+        copy.wait()
+    parts = [
+        spin(mm(o, other, ROWS) / (e_own[0] + energy[0] - pairs[...]))
+        for other, energy in ((l, s_low), (h, s_high))
+    ]
+    total[...] = mm(parts[0], l, PLAIN) + mm(parts[1], h, PLAIN)
     out = pltpu.make_async_copy(total, grad, sem)
     out.start()
     out.wait()
@@ -164,36 +189,60 @@
     )(*args)
 
 
+def in_hbm(x):
+    return pltpu.with_memory_space_constraint(x, pltpu.HBM)
+
+
 def body(slabs, eps_occ, eps_vir):
     own = slabs[0]
     v, n = own.shape
     low = shift(own, 1)
     high = shift(own, -1)
-    e_own = eps_occ[None]
-    e_low = shift(eps_occ, 1)[None]
-    e_high = shift(eps_occ, -1)[None]
-    (pairs,) = call(base_kernel, ((v, v),), [], 4, 1 << 20, (eps_vir[None],), [VMEM], (VMEM,))
-
-    source = pltpu.with_memory_space_constraint(own, pltpu.HBM)
+    e_own = eps_occ
+    e_low = shift(eps_occ, 1)
+    e_high = shift(eps_occ, -1)
+    (pairs,) = call(
+        base_kernel, ((v, v),), [], 4, 1 << 20, (eps_vir[None],), [VMEM], (VMEM,)
+    )
+
+    source = in_hbm(own)
     core = lax.axis_index("core").astype(jnp.int32)[None]
     piece = (16, 8, v)
     wide = [pltpu.VMEM((v, n), BF16)]
     full = [pltpu.VMEM((v, n), F32)]
     part = [pltpu.VMEM((v // 2, n), F32)]
-    keep, send, down, up = call(
+    one = pltpu.SMEM((1,), F32)
+    down, up = call(
+        mid_kernel,
+        ((v // 2, n), (v // 2, n)),
+        wide * 4 + part * 2 + [one] * 2 + [pltpu.SemaphoreType.DMA((2,))] * 2,
+        12,
+        1 << 31,
+        (e_low, e_high, pairs, low, high),
+        [HBM] * 2 + [VMEM] * 3,
+        (HBM, HBM),
+    )
+    first = shift(down, -1)
+    second = in_hbm(shift(up, 1))
+    keep, send = call(
         density_kernel,
-        (piece, piece, (v // 2, n), (v // 2, n)),
-        wide * 6 + [pltpu.VMEM((v, v), F32)] + part * 2 + full + [pltpu.SemaphoreType.DMA((3,))],
+        (piece, piece),
+        wide * 6
+        + [pltpu.VMEM((v, v), F32)]
+        + full
+        + [pltpu.SemaphoreType.DMA, pltpu.SMEM((1,), jnp.int32)]
+        + [one] * 2
+        + [pltpu.SemaphoreType.DMA((3,))],
         16,
-        1 << 32,
-        (core, e_own, e_low, e_high, pairs, source, low, high),
-        [SMEM] + [VMEM] * 4 + [HBM] + [VMEM] * 2,
-        (VMEM, VMEM, HBM, HBM),
+        1 << 31,
+        (e_own, core, e_low, e_high, pairs, source, low, high),
+        [SMEM] + [HBM] * 3 + [VMEM] + [HBM] + [VMEM] * 2,
+        (VMEM, VMEM),
     )
     other = lax.ppermute(send, "core", [(0, 1), (1, 0)])
-    second = shift(up, 1)
-    first = shift(down, -1)
-    (mine,) = call(join_kernel, ((4,) + piece,), [], 4, 1 << 20, (keep, other), [VMEM] * 2, (VMEM,))
+    (mine,) = call(
+        join_kernel, ((4,) + piece,), [], 4, 1 << 20, (keep, other), [VMEM] * 2, (VMEM,)
+    )
     parts = lax.all_to_all(
         mine.reshape(16, 32, v),
         ("y", "x"),
@@ -210,14 +259,18 @@
     (near,) = call(
         near_kernel,
         (own.shape,),
-        wide * 6 + full + [pltpu.SemaphoreType.DMA],
+        wide * 6
+        + full
+        + [pltpu.SemaphoreType.DMA]
+        + [one] * 2
+        + [pltpu.SemaphoreType.DMA((2,))],
         16,
         1 << 31,
         (e_own, e_low, e_high, pairs, source, low, high),
-        [VMEM] * 4 + [HBM] + [VMEM] * 2,
+        [SMEM] + [HBM] * 2 + [VMEM] + [HBM] + [VMEM] * 2,
         (HBM,),
     )
-    near = pltpu.with_memory_space_constraint(near, pltpu.HBM)
+    near = in_hbm(near)
     (grad,) = call(
         sum_kernel,
         (own.shape,),

time: 104 us -> 108 us (1.038)
  waiting for transfers between devices: 57.5 us -> 61.6 us
  Pallas kernels: 15.1 us -> 18.9 us
  starting transfers between devices: 27.2 us -> 24.6 us
  local copies, waits for them, and re-layouts: 1.9 us -> 0.67 us
    ppermute x6, waiting for transfers between devices: 49.4 us -> 57.3 us  [shift(): lax.ppermute(value, 'far', [(i, (i + step) % size) for i in range(size)])]
    pallas_call x6 -> x7, Pallas kernels: 15.1 us -> 18.9 us  [call(): pl.pallas_call(kernel, out_shape=tuple((pltpu.HBM(s, F32) if spec is HBM...]
    all_to_all x1, waiting for transfers between devices: 6.76 us -> 2.96 us  [body(): lax.all_to_all(mine.reshape(16, 32, v), ('y', 'x'), split_axis=0, concat_...]
    all_to_all x1, starting transfers between devices: 5.2 us -> 3.51 us  [body(): lax.all_to_all(copies, ('near', 'far', 'core'), split_axis=0, concat_axis...]
    unnamed x8 -> x2, local copies, waits for them, and re-layouts: 1.9 us -> 0.67 us
  transfers between devices with their start and end apart: 9 -> 9, of which waited for: 6 -> 5; matrix products, arithmetic and copies ran while one was open for 0% -> 0% of each run, Pallas kernels for 8% -> 12%
where the time goes in v5:
time: 108 us
  waiting for transfers between devices  61.6 us (57%)
  starting transfers between devices  24.6 us (23%)
  Pallas kernels  18.9 us (17%)
  between operations  1.4 us (1%)
    ppermute x6, waiting for transfers between devices, shift(): lax.ppermute(value, 'far', [(i, (i + step) % size) for i in range(size)])  57.3 us
    pallas_call x7, Pallas kernels, call(): pl.pallas_call(kernel, out_shape=tuple((pltpu.HBM(s, F32) if spec is HBM...  18.9 us
    ppermute x6, starting transfers between devices, shift(): lax.ppermute(value, 'far', [(i, (i + step) % size) for i in range(size)])  13.5 us
    all_to_all x1, starting transfers between devices, body(): lax.all_to_all(mine.reshape(16, 32, v), ('y', 'x'), split_axis=0, concat_...  7.48 us
    all_to_all x1, starting transfers between devices, body(): lax.all_to_all(copies, ('near', 'far', 'core'), split_axis=0, concat_axis...  3.51 us
    all_to_all x1, waiting for transfers between devices, body(): lax.all_to_all(mine.reshape(16, 32, v), ('y', 'x'), split_axis=0, concat_...  2.96 us
  transfers between devices with their start and end apart: 9, of which 5 were waited for; matrix products, arithmetic and copies ran while one was open for 0% of the time, Pallas kernels for 12%

profile of v5, /device:TPU:2, one launch (start us, length us, event | category | flops | bytes accessed | tf_op | source)
XLA Modules:
  0.0 107.9 jit_solution(13952037079974184662)
XLA Ops:
  0.6 6.4 %collective-permute-start.3 = (f32[256,1024]{1,0:T(8,128)}, f32[256,1024]{1,0:T(8,128)S(1)}, u32[]{:S(2)}, u32[]{:S(2)}) collective-permute-start(f32[256,1024]{1,0:T(8,128)} %bitcast.11), channel_id=1, source_target_pairs={{0,3},{1,0},{2,1},{3,2},{4,7},{5,4},{6,5},{7,6},{8,11},{9,8},{10,9... | collective-permute-start | bytes 3145736 | tf_op jit(solution)/shard_map/ppermute | solution.py:22
  7.0 0.0 collective-permute-start.2
  7.0 1.5 %collective-permute-start = (f32[1]{0:T(128)}, f32[1]{0:T(128)}, u32[]{:S(2)}, u32[]{:S(2)}) collective-permute-start(f32[1]{0:T(128)} %param.4), channel_id=1, source_target_pairs={{0,1},{1,2},{2,3},{3,0},{4,5},{5,6},{6,7},{7,4},{8,9},{9,10},{10,1... | collective-permute-start | bytes 20 | tf_op jit(solution)/shard_map/ppermute | solution.py:22
  8.6 2.6 %collective-permute-start.1 = (f32[1]{0:T(128)}, f32[1]{0:T(128)}, u32[]{:S(2)}, u32[]{:S(2)}) collective-permute-start(f32[1]{0:T(128)} %param.4), channel_id=1, source_target_pairs={{0,3},{1,0},{2,1},{3,2},{4,7},{5,4},{6,5},{7,6},{8,11},{9,8},{10,9... | collective-permute-start | bytes 20 | tf_op jit(solution)/shard_map/ppermute | solution.py:22
  11.9 0.0 copy-start
  11.9 0.7 copy-done
  12.5 0.1 shard_map.50.pairs
  12.6 43.4 %collective-permute-done.e_low = f32[1]{0:T(128)} collective-permute-done((f32[1]{0:T(128)}, f32[1]{0:T(128)}, u32[]{:S(2)}, u32[]{:S(2)}) %collective-permute-start) | collective-permute-done | bytes 36 | tf_op jit(solution)/shard_map/ppermute | solution.py:22
  56.0 0.0 collective-permute-done.1.e_high
  56.0 0.0 collective-permute-done.3.high
  56.0 0.0 collective-permute-done.2.low
  56.0 5.0 %shard_map.54 = (f32[16,8,256]{2,1,0:T(8,128)S(1)}, f32[16,8,256]{2,1,0:T(8,128)S(1)}) custom-call(f32[1]{0:T(128)S(6)} %copy.5.e_own, s32[1]{0:T(128)} %bitcast.3.core, f32[1]{0:T(128)} %collective-permute-done.e_low, f32[1]{0:T(128)} %collective-permute-done.1.e_high, f32[256,256]{1,0:T(8,128)S(1)} %shard_map.50.pairs, f32[256,1024]{1,0:T(8,128)} %bitcast.13, ...), custom_call_target="tpu_custom_call" | custom-call | flops 2147483648 | bytes 1048576 | tf_op jit(solution)/shard_map/pallas_call | solution.py:176
  61.1 0.1 collective-permute-start.6
  61.2 1.3 %collective-permute-done.6.other = f32[16,8,256]{2,1,0:T(8,128)S(1)} collective-permute-done((f32[16,8,256]{2,1,0:T(8,128)S(1)}, f32[16,8,256]{2,1,0:T(8,128)S(1)}, u32[]{:S(2)}, u32[]{:S(2)}) %collective-permute-start.6) | collective-permute-done | bytes 131104 | tf_op jit(solution)/shard_map/ppermute | solution.py:242
  62.5 0.8 shard_map.55
  63.3 7.5 %all-to-all-start = ((f32[16,32,256]{2,1,0:T(8,128)}), f32[16,32,256]{2,1,0:T(8,128)S(1)}, u32[]{:S(2)}, u32[]{:S(2)}) async-start(f32[16,32,256]{2,1,0:T(8,128)} %bitcast.4), calls=%async_computation | async-start | bytes 1048576 | tf_op jit(solution)/shard_map/all_to_all | solution.py:246
  70.8 4.5 %shard_map.52 = (f32[128,1024]{1,0:T(8,128)}, f32[128,1024]{1,0:T(8,128)}) custom-call(f32[1]{0:T(128)} %collective-permute-done.e_low, f32[1]{0:T(128)} %collective-permute-done.1.e_high, f32[256,256]{1,0:T(8,128)S(1)} %shard_map.50.pairs, f32[256,1024]{1,0:T(8,128)S(1)} %collective-permute-done.2.low, f32[256,1024]{1,0:T(8,128)S(1)} %collective-permute-done.3.high), custom_call_target="tpu_custom_call" | custom-call | flops 2147483648 | bytes 1048576 | tf_op jit(solution)/shard_map/pallas_call | solution.py:176
  75.3 0.9 collective-permute-start.4
  76.2 2.1 %collective-permute-start.5 = (f32[128,1024]{1,0:T(8,128)}, f32[128,1024]{1,0:T(8,128)}, u32[]{:S(2)}, u32[]{:S(2)}) collective-permute-start(f32[128,1024]{1,0:T(8,128)} %get-tuple-element.7), channel_id=1, source_target_pairs={{0,1},{1,2},{2,3},{3,0},{4,5},{5,6},{6,7},{7,4},{8,9},{9,10},{10,1... | collective-permute-start | bytes 1572872 | tf_op jit(solution)/shard_map/ppermute | solution.py:22
  78.3 3.0 %all-to-all-done.pieces = f32[16,32,256]{2,1,0:T(8,128)S(1)} async-done(((f32[16,32,256]{2,1,0:T(8,128)}), f32[16,32,256]{2,1,0:T(8,128)S(1)}, u32[]{:S(2)}, u32[]{:S(2)}) %all-to-all-start) | async-done | bytes 524320 | tf_op jit(solution)/shard_map/all_to_all | solution.py:246
  81.3 0.7 shard_map.56
  82.0 3.5 %all-to-all-start.1 = ((f32[16,8,256]{2,1,0:T(8,128)}), f32[16,8,256]{2,1,0:T(8,128)S(1)}, u32[]{:S(2)}, u32[]{:S(2)}) async-start(f32[16,8,256]{2,1,0:T(8,128)} %shard_map.56), calls=%async_computation.1 | async-start | bytes 262144 | tf_op jit(solution)/shard_map/all_to_all | solution.py:254
  85.5 5.6 %shard_map.51.near = f32[256,1024]{1,0:T(8,128)} custom-call(f32[1]{0:T(128)S(6)} %copy.5.e_own, f32[1]{0:T(128)} %collective-permute-done.e_low, f32[1]{0:T(128)} %collective-permute-done.1.e_high, f32[256,256]{1,0:T(8,128)S(1)} %shard_map.50.pairs, f32[256,1024]{1,0:T(8,128)} %bitcast.14, f32[256,1024]{1,0:T(8,128)S(1)} %collective-permute-done.2.low, ...), custom_call_target="tpu_custom_call" | custom-call | flops 2147483648 | bytes 1048576 | tf_op jit(solution)/shard_map/pallas_call | solution.py:176
  91.1 12.3 %collective-permute-done.4.first = f32[128,1024]{1,0:T(8,128)S(1)} collective-permute-done((f32[128,1024]{1,0:T(8,128)}, f32[128,1024]{1,0:T(8,128)S(1)}, u32[]{:S(2)}, u32[]{:S(2)}) %collective-permute-start.4) | collective-permute-done | bytes 524320 | tf_op jit(solution)/shard_map/ppermute | solution.py:22
  103.5 1.6 %collective-permute-done.5.second = f32[128,1024]{1,0:T(8,128)} collective-permute-done((f32[128,1024]{1,0:T(8,128)}, f32[128,1024]{1,0:T(8,128)}, u32[]{:S(2)}, u32[]{:S(2)}) %collective-permute-start.5) | collective-permute-done | bytes 524320 | tf_op jit(solution)/shard_map/ppermute | solution.py:22
  105.1 2.2 %shard_map.53 = f32[256,1024]{1,0:T(8,128)} custom-call(f32[256,1024]{1,0:T(8,128)} %shard_map.51.near, f32[128,1024]{1,0:T(8,128)S(1)} %collective-permute-done.4.first, f32[128,1024]{1,0:T(8,128)} %collective-permute-done.5.second), custom_call_target="tpu_custom_call" | custom-call | flops 1048576 | bytes 1048576 | tf_op jit(solution)/shard_map/pallas_call | solution.py:176
  107.3 0.0 all-to-all-done.1
  107.3 0.6 bitcast_reduce_fusion
Async XLA Ops:
  0.6 55.4 %collective-permute-start.3 = (f32[256,1024]{1,0:T(8,128)}, f32[256,1024]{1,0:T(8,128)S(1)}, u32[]{:S(2)}, u32[]{:S(2)}) collective-permute-start(f32[256,1024]{1,0:T(8,128)} %bitcast.11), channel_id=1, source_target_pairs={{0,3},{1,0},{2,1},{3,2},{4,7},{5,4},{6,5},{7,6},{8,11},{9,8},{10,9... | collective-permute-start | bytes 3145736 | tf_op jit(solution)/shard_map/ppermute | solution.py:22
  7.0 49.0 %collective-permute-start.2 = (f32[256,1024]{1,0:T(8,128)}, f32[256,1024]{1,0:T(8,128)S(1)}, u32[]{:S(2)}, u32[]{:S(2)}) collective-permute-start(f32[256,1024]{1,0:T(8,128)} %bitcast.12), channel_id=1, source_target_pairs={{0,1},{1,2},{2,3},{3,0},{4,5},{5,6},{6,7},{7,4},{8,9},{9,10},{10,1... | collective-permute-start | bytes 3145736 | tf_op jit(solution)/shard_map/ppermute | solution.py:22
  7.0 49.0 %collective-permute-start = (f32[1]{0:T(128)}, f32[1]{0:T(128)}, u32[]{:S(2)}, u32[]{:S(2)}) collective-permute-start(f32[1]{0:T(128)} %param.4), channel_id=1, source_target_pairs={{0,1},{1,2},{2,3},{3,0},{4,5},{5,6},{6,7},{7,4},{8,9},{9,10},{10,1... | collective-permute-start | bytes 20 | tf_op jit(solution)/shard_map/ppermute | solution.py:22
  8.6 47.5 %collective-permute-start.1 = (f32[1]{0:T(128)}, f32[1]{0:T(128)}, u32[]{:S(2)}, u32[]{:S(2)}) collective-permute-start(f32[1]{0:T(128)} %param.4), channel_id=1, source_target_pairs={{0,3},{1,0},{2,1},{3,2},{4,7},{5,4},{6,5},{7,6},{8,11},{9,8},{10,9... | collective-permute-start | bytes 20 | tf_op jit(solution)/shard_map/ppermute | solution.py:22
  11.9 0.7 copy-start
  61.1 1.4 %collective-permute-start.6 = (f32[16,8,256]{2,1,0:T(8,128)S(1)}, f32[16,8,256]{2,1,0:T(8,128)S(1)}, u32[]{:S(2)}, u32[]{:S(2)}) collective-permute-start(f32[16,8,256]{2,1,0:T(8,128)S(1)} %get-tuple-element.9), channel_id=1, source_target_pairs={{0,16},{16,0},{1,17},{17,1},{2,18},{18,2},{3,19},{19,3},{4,20},{20... | collective-permute-start | bytes 393224 | tf_op jit(solution)/shard_map/ppermute | solution.py:242
  63.3 18.0 %all-to-all-start = ((f32[16,32,256]{2,1,0:T(8,128)}), f32[16,32,256]{2,1,0:T(8,128)S(1)}, u32[]{:S(2)}, u32[]{:S(2)}) async-start(f32[16,32,256]{2,1,0:T(8,128)} %bitcast.4), calls=%async_computation | async-start | bytes 1048576 | tf_op jit(solution)/shard_map/all_to_all | solution.py:246
  75.3 28.1 %collective-permute-start.4 = (f32[128,1024]{1,0:T(8,128)}, f32[128,1024]{1,0:T(8,128)S(1)}, u32[]{:S(2)}, u32[]{:S(2)}) collective-permute-start(f32[128,1024]{1,0:T(8,128)} %get-tuple-element.6), channel_id=1, source_target_pairs={{0,3},{1,0},{2,1},{3,2},{4,7},{5,4},{6,5},{7,6},{8,11},{9,8},{10,9... | collective-permute-start | bytes 1572872 | tf_op jit(solution)/shard_map/ppermute | solution.py:22
  76.2 28.9 %collective-permute-start.5 = (f32[128,1024]{1,0:T(8,128)}, f32[128,1024]{1,0:T(8,128)}, u32[]{:S(2)}, u32[]{:S(2)}) collective-permute-start(f32[128,1024]{1,0:T(8,128)} %get-tuple-element.7), channel_id=1, source_target_pairs={{0,1},{1,2},{2,3},{3,0},{4,5},{5,6},{6,7},{7,4},{8,9},{9,10},{10,1... | collective-permute-start | bytes 1572872 | tf_op jit(solution)/shard_map/ppermute | solution.py:22
  82.0 25.3 %all-to-all-start.1 = ((f32[16,8,256]{2,1,0:T(8,128)}), f32[16,8,256]{2,1,0:T(8,128)S(1)}, u32[]{:S(2)}, u32[]{:S(2)}) async-start(f32[16,8,256]{2,1,0:T(8,128)} %shard_map.56), calls=%async_computation.1 | async-start | bytes 262144 | tf_op jit(solution)/shard_map/all_to_all | solution.py:254

commit v6 on v5

v6 whole, which is shorter than its diff:
```python
import jax
import jax.numpy as jnp
from jax import lax
from jax.experimental import pallas as pl
from jax.experimental.pallas import tpu as pltpu
from jax.sharding import Mesh, PartitionSpec as P


FINE = ("y", "near", "core", "x", "far")
FINE_SHAPE = (4, 2, 2, 4, 4)
VMEM = pl.BlockSpec(memory_space=pltpu.VMEM)
SMEM = pl.BlockSpec(memory_space=pltpu.SMEM)
HBM = pl.BlockSpec(memory_space=pltpu.HBM)
F32, BF16 = jnp.float32, jnp.bfloat16
ROWS = ((1,), (1,))
PLAIN = ((1,), (0,))
MIB = 1 << 20


def shift(value, step):
    size = lax.axis_size("far")
    return lax.ppermute(value, "far", [(i, (i + step) % size) for i in range(size)])


def split(x):
    high = x.astype(BF16)
    return high, (x - high.astype(F32)).astype(BF16)


def mm(a, b, contract):
    def dot(p, q):
        return lax.dot_general(p, q, (contract, ((), ())), preferred_element_type=F32)

    return dot(a[0], b[0]) + (dot(a[0], b[1]) + dot(a[1], b[0]))


def prepare_kernel(eps_vir, own, pairs, high, low):
    row = jnp.broadcast_to(eps_vir[...], pairs.shape)
    pairs[...] = row + row.T
    high[...], low[...] = split(own[...])


def spin(t):
    return split(2.0 * t - t.T)


def mid_kernel(energy, pairs, low, high, down, up, t_mid, lh, ll, hh, hl, *scratch):
    buf_down, buf_up, sems = scratch
    half = down.shape[0]
    lh[...], ll[...] = l = split(low[...])
    hh[...], hl[...] = h = split(high[...])
    t = mm(l, h, ROWS) / (energy[0:1, 0:1] - pairs[...])
    turned = t.T
    s = split(2.0 * t[:half] - turned[:half])
    buf_down[...] = mm(s, h, PLAIN)
    to_down = pltpu.make_async_copy(buf_down, down, sems.at[0])
    to_down.start()
    s = split(2.0 * turned[half:] - t[half:])
    buf_up[...] = mm(s, l, PLAIN)
    to_up = pltpu.make_async_copy(buf_up, up, sems.at[1])
    to_up.start()
    t_mid[...] = t
    to_down.wait()
    to_up.wait()


def density_kernel(
    upper, e_low, e_high, pairs, t_mid, oh, ol, lh, ll, hh, hl, keep, send, dens
):
    o, l, h = (oh[...], ol[...]), (lh[...], ll[...]), (hh[...], hl[...])
    t = t_mid[...]
    total = mm(split(t), spin(t), ROWS)
    for other, energy in ((l, e_low), (h, e_high)):
        t = mm(o, other, ROWS) / (energy[0:1, 0:1] - pairs[...])
        total = total + mm(split(t), spin(t), ROWS)
    dens[...] = total
    mine = upper[...] > 0.5
    for at in range(16):
        first = dens[at * 16 : at * 16 + 8, :]
        second = dens[at * 16 + 8 : at * 16 + 16, :]
        keep[at] = jnp.where(mine, second, first)
        send[at] = jnp.where(mine, first, second)


def near_kernel(e_low, e_high, pairs, oh, ol, lh, ll, hh, hl, grad, total, sem):
    o, l, h = (oh[...], ol[...]), (lh[...], ll[...]), (hh[...], hl[...])
    parts = [
        spin(mm(o, other, ROWS) / (energy[0:1, 0:1] - pairs[...]))
        for other, energy in ((l, e_low), (h, e_high))
    ]
    total[...] = mm(parts[0], l, PLAIN) + mm(parts[1], h, PLAIN)
    out = pltpu.make_async_copy(total, grad, sem)
    out.start()
    out.wait()


def sum_kernel(near, first, second, grad, mine, other, sems):
    half = first.shape[0]
    parts, step = 4, half // 2
    copies = []
    for at in range(parts):
        rows = pl.ds(at * step, step)
        source = (first, second)[at // 2].at[pl.ds(at % 2 * step, step), :]
        copies.append(
            (
                pltpu.make_async_copy(near.at[rows, :], mine.at[rows, :], sems.at[0, at]),
                pltpu.make_async_copy(source, other.at[rows, :], sems.at[1, at]),
                pltpu.make_async_copy(mine.at[rows, :], grad.at[rows, :], sems.at[2, at]),
            )
        )
        copies[-1][0].start()
        copies[-1][1].start()
    for at in range(parts):
        rows = slice(at * step, (at + 1) * step)
        copies[at][0].wait()
        copies[at][1].wait()
        mine[rows, :] = mine[rows, :] + other[rows, :]
        copies[at][2].start()
    for at in range(parts):
        copies[at][2].wait()


def fold_kernel(pieces, copies):
    total = pieces[0]
    for at in range(1, pieces.shape[0]):
        total = total + pieces[at]
    total = total * (1.0 / 256.0)
    for at in range(copies.shape[0]):
        copies[at] = total


def call(kernel, out, scratch, limit, flops, args, in_specs, out_specs):
    return pl.pallas_call(
        kernel,
        out_shape=tuple(
            pltpu.HBM(s, F32)
            if spec is HBM
            else jax.ShapeDtypeStruct(s, BF16 if s == (256, 1024) else F32)
            for s, spec in zip(out, out_specs)
        ),
        in_specs=in_specs,
        out_specs=out_specs,
        scratch_shapes=scratch,
        cost_estimate=pl.CostEstimate(
            flops=flops, bytes_accessed=MIB, transcendentals=0
        ),
        compiler_params=pltpu.CompilerParams(vmem_limit_bytes=limit * MIB),
    )(*args)


def in_hbm(x):
    return pltpu.with_memory_space_constraint(x, pltpu.HBM)


def body(slabs, eps_occ, eps_vir):
    own = slabs[0]
    v, n = own.shape
    low = shift(own, 1)
    high = shift(own, -1)
    tile = (8, 128)
    e_low, e_high = shift(eps_occ, 1), shift(eps_occ, -1)
    s_low = jnp.broadcast_to(eps_occ + e_low, tile)
    s_high = jnp.broadcast_to(eps_occ + e_high, tile)
    s_mid = jnp.broadcast_to(e_low + e_high, tile)
    upper = jnp.broadcast_to(lax.axis_index("core").astype(F32), (8, v))
    pairs, oh, ol = call(
        prepare_kernel,
        ((v, v), (v, n), (v, n)),
        [],
        8,
        1 << 20,
        (eps_vir[None], own),
        [VMEM] * 2,
        (VMEM,) * 3,
    )
    piece = (16, 8, v)
    part = [pltpu.VMEM((v // 2, n), F32)]
    down, up, t_mid, *splits = call(
        mid_kernel,
        ((v // 2, n), (v // 2, n), (v, v)) + ((v, n),) * 4,
        part * 2 + [pltpu.SemaphoreType.DMA((2,))],
        12,
        1 << 31,
        (s_mid, pairs, low, high),
        [VMEM] * 4,
        (HBM, HBM) + (VMEM,) * 5,
    )
    first = shift(down, -1)
    second = in_hbm(shift(up, 1))
    keep, send = call(
        density_kernel,
        (piece, piece),
        [pltpu.VMEM((v, v), F32)],
        12,
        1 << 31,
        (upper, s_low, s_high, pairs, t_mid, oh, ol, *splits),
        [VMEM] * 11,
        (VMEM, VMEM),
    )
    other = lax.ppermute(send, "core", [(0, 1), (1, 0)])
    parts = lax.all_to_all(
        keep + other, ("x", "far"), split_axis=0, concat_axis=0, tiled=True
    )
    (copies,) = call(fold_kernel, (piece,), [], 4, 1 << 20, (parts,), [VMEM], (VMEM,))
    copies = lax.all_to_all(
        copies, ("y", "near", "core"), split_axis=0, concat_axis=0, tiled=True
    )
    density = jnp.sum(copies.reshape(8, 16, v), axis=0)

    (near,) = call(
        near_kernel,
        ((v, n),),
        [pltpu.VMEM((v, n), F32), pltpu.SemaphoreType.DMA],
        12,
        1 << 31,
        (s_low, s_high, pairs, oh, ol, *splits),
        [VMEM] * 9,
        (HBM,),
    )
    (grad,) = call(
        sum_kernel,
        ((v, n),),
        [pltpu.VMEM((v, n), F32)] * 2 + [pltpu.SemaphoreType.DMA((3, 4))],
        8,
        1 << 20,
        (in_hbm(near), first, second),
        [HBM] * 3,
        (HBM,),
    )
    return grad[None], density


def solution(mesh):
    fine = Mesh(mesh.devices.reshape(FINE_SHAPE), FINE)
    placed = (P(FINE, None, None), P(FINE), P())
    return jax.shard_map(
        body,
        mesh=fine,
        in_specs=placed,
        out_specs=(P(FINE, None, None), P(("x", "far"), None)),
        check_vma=False,
    )
```

time: 108 us -> 114 us (1.056)
  the two profiles are of different devices: /device:TPU:2 before, /device:TPU:1 now
where the time goes in v6:
time: 114 us; the launch traced here: 113 us
  waiting for transfers between devices  40.5 us (36%)
  blocking collectives  30.9 us (27%)
  starting transfers between devices  21.3 us (19%)
  Pallas kernels  11.9 us (10%)
  between operations  4.04 us (4%)
  local copies, waits for them, and re-layouts  4.01 us (4%)
    ppermute x6, waiting for transfers between devices, shift(): lax.ppermute(value, 'far', [(i, (i + step) % size) for i in range(size)])  40.5 us
    all_to_all x1, blocking collectives, body(): lax.all_to_all(keep + other, ('x', 'far'), split_axis=0, concat_axis=0, t...  30.9 us
    ppermute x6, starting transfers between devices, shift(): lax.ppermute(value, 'far', [(i, (i + step) % size) for i in range(size)])  13.9 us
    pallas_call x6, Pallas kernels, call(): pl.pallas_call(kernel, out_shape=tuple((pltpu.HBM(s, F32) if spec is HBM...  11.9 us
    all_to_all x1, starting transfers between devices, body(): lax.all_to_all(copies, ('y', 'near', 'core'), split_axis=0, concat_axis=0...  6.3 us
    unnamed x20, local copies, waits for them, and re-layouts  4 us
  transfers between devices with their start and end apart: 8, of which 2 were waited for; matrix products, arithmetic and copies ran while one was open for 0% of the time, Pallas kernels for 5%

profile of v6, /device:TPU:1, one launch (start us, length us, event | category | flops | bytes accessed | tf_op | source)
XLA Modules:
  0.0 113.3 jit_solution(16513927453320522680)
XLA Ops:
  0.6 3.9 %collective-permute-start.2 = (f32[256,1024]{1,0:T(8,128)}, f32[256,1024]{1,0:T(8,128)S(1)}, u32[]{:S(2)}, u32[]{:S(2)}) collective-permute-start(f32[256,1024]{1,0:T(8,128)} %bitcast.9), channel_id=1, source_target_pairs={{0,1},{1,2},{2,3},{3,0},{4,5},{5,6},{6,7},{7,4},{8,9},{9,10},{10,1... | collective-permute-start | bytes 3145736 | tf_op jit(solution)/shard_map/ppermute | solution.py:22
  4.5 3.1 %collective-permute-start.3 = (f32[256,1024]{1,0:T(8,128)}, f32[256,1024]{1,0:T(8,128)S(1)}, u32[]{:S(2)}, u32[]{:S(2)}) collective-permute-start(f32[256,1024]{1,0:T(8,128)} %bitcast.10), channel_id=1, source_target_pairs={{0,3},{1,0},{2,1},{3,2},{4,7},{5,4},{6,5},{7,6},{8,11},{9,8},{10,9... | collective-permute-start | bytes 3145736 | tf_op jit(solution)/shard_map/ppermute | solution.py:22
  7.6 1.1 collective-permute-start
  8.7 2.5 %collective-permute-start.1 = (f32[1]{0:T(128)}, f32[1]{0:T(128)}, u32[]{:S(2)}, u32[]{:S(2)}) collective-permute-start(f32[1]{0:T(128)} %param.4), channel_id=1, source_target_pairs={{0,3},{1,0},{2,1},{3,2},{4,7},{5,4},{6,5},{7,6},{8,11},{9,8},{10,9... | collective-permute-start | bytes 20 | tf_op jit(solution)/shard_map/ppermute | solution.py:22
  11.9 0.0 copy-start.1
  11.9 0.7 copy-done.1
  12.6 1.2 %copy-done = f32[1,256,1024]{2,1,0:T(8,128)S(1)} copy-done((f32[1,256,1024]{2,1,0:T(8,128)S(1)}, f32[1,256,1024]{2,1,0:T(8,128)}, u32[]{:S(2)}) %copy-start) | copy-done | bytes 1048600
  13.8 0.3 shard_map.50
  14.1 25.1 %collective-permute-done = f32[1]{0:T(128)} collective-permute-done((f32[1]{0:T(128)}, f32[1]{0:T(128)}, u32[]{:S(2)}, u32[]{:S(2)}) %collective-permute-start) | collective-permute-done | bytes 36 | tf_op jit(solution)/shard_map/ppermute | solution.py:22
  39.2 15.4 %collective-permute-done.1 = f32[1]{0:T(128)} collective-permute-done((f32[1]{0:T(128)}, f32[1]{0:T(128)}, u32[]{:S(2)}, u32[]{:S(2)}) %collective-permute-start.1) | collective-permute-done | bytes 36 | tf_op jit(solution)/shard_map/ppermute | solution.py:22
  57.1 0.0 collective-permute-done.2.low
  57.1 0.0 collective-permute-done.3.high
  57.2 2.8 %shard_map.51 = (f32[128,1024]{1,0:T(8,128)}, f32[128,1024]{1,0:T(8,128)}, f32[256,256]{1,0:T(8,128)S(1)}, bf16[256,1024]{1,0:T(8,128)(2,1)S(1)}, bf16[256,1024]...) custom-call(f32[8,128]{1,0:T(8,128)S(1)} %broadcast_in_dim.27.energy, ...), custom_call_target="tpu_custom_call" | custom-call | flops 2147483648 | bytes 1048576 | tf_op jit(solution)/shard_map/pallas_call | solution.py:133
  60.0 0.0 copy-start.2
  60.0 0.0 copy-start.4
  60.0 0.0 copy-start.6
  60.1 2.9 %shard_map.54 = (f32[16,8,256]{2,1,0:T(8,128)S(1)}, f32[16,8,256]{2,1,0:T(8,128)S(1)}) custom-call(f32[8,256]{1,0:T(8,128)S(1)} %broadcast_in_dim.29.upper, f32[8,128]{1,0:T(8,128)S(1)} %broadcast_in_dim.24.e_low, f32[8,128]{1,0:T(8,128)S(1)} %broadcast_in_dim.25.e_high, f32[256,256]{1,0:T(8,128)S(1)} %get-tuple-element.14.pairs, ...), custom_call_target="tpu_custom_call" | custom-call | flops 2147483648 | bytes 1048576 | tf_op jit(solution)/shard_map/pallas_call | solution.py:133
  63.0 1.1 collective-permute-start.6
  64.1 2.5 %collective-permute-start.4 = (f32[128,1024]{1,0:T(8,128)}, f32[128,1024]{1,0:T(8,128)S(1)}, u32[]{:S(2)}, u32[]{:S(2)}) collective-permute-start(f32[128,1024]{1,0:T(8,128)} %get-tuple-element.21), channel_id=1, source_target_pairs={{0,3},{1,0},{2,1},{3,2},{4,7},{5,4},{6,5},{7,6},{8,11},{9,8},{10,9... | collective-permute-start | bytes 1572872 | tf_op jit(solution)/shard_map/ppermute | solution.py:22
  66.5 0.9 collective-permute-start.5
  67.4 0.0 collective-permute-done.6
  67.4 30.9 %all_to_all.10.pieces = f32[16,8,256]{2,1,0:T(8,128)S(1)} all-to-all(f32[16,8,256]{2,1,0:T(8,128)S(1)} %add.24), channel_id=1, replica_groups=mesh['y'=4,'near'=2,'core'=2,'x'=4,'far'=4] {'x','far'}, dimensions={0} | all-to-all | bytes 262144 | tf_op jit(solution)/shard_map/all_to_all | solution.py:201
  98.3 0.7 shard_map.55
  99.0 6.3 %all-to-all-start.1 = ((f32[16,8,256]{2,1,0:T(8,128)}), f32[16,8,256]{2,1,0:T(8,128)S(1)}, u32[]{:S(2)}, u32[]{:S(2)}) async-start(f32[16,8,256]{2,1,0:T(8,128)} %shard_map.55), calls=%async_computation.1 | async-start | bytes 262144 | tf_op jit(solution)/shard_map/all_to_all | solution.py:205
  105.4 1.0 copy-done.7
  106.4 1.0 copy-done.9
  107.4 3.0 %shard_map.52.near = f32[256,1024]{1,0:T(8,128)} custom-call(f32[8,128]{1,0:T(8,128)S(1)} %broadcast_in_dim.24.e_low, f32[8,128]{1,0:T(8,128)S(1)} %broadcast_in_dim.25.e_high, f32[256,256]{1,0:T(8,128)S(1)} %get-tuple-element.14.pairs, bf16[256,1024]{1,0:T(8,128)(2,1)S(1)} %get-tuple-element.15.oh, bf16[256,1024]{1,0:T(8,128)(2,1)S(1)} %get-tuple-element.16.ol, ...), custom_call_target="tpu_custom_call" | custom-call | flops 2147483648 | bytes 1048576 | tf_op jit(solution)/shard_map/pallas_call | solution.py:133
  110.4 0.0 collective-permute-done.4.first
  110.4 0.0 collective-permute-done.5.second
  110.5 2.2 %shard_map.53 = f32[256,1024]{1,0:T(8,128)} custom-call(f32[256,1024]{1,0:T(8,128)} %shard_map.52.near, f32[128,1024]{1,0:T(8,128)S(1)} %collective-permute-done.4.first, f32[128,1024]{1,0:T(8,128)} %collective-permute-done.5.second), custom_call_target="tpu_custom_call" | custom-call | flops 1048576 | bytes 1048576 | tf_op jit(solution)/shard_map/pallas_call | solution.py:133
  112.7 0.0 all-to-all-done.1
  112.7 0.6 bitcast_reduce_fusion
  (17 shorter events, 0.1 us)
Async XLA Ops:
  0.6 56.5 %collective-permute-start.2 = (f32[256,1024]{1,0:T(8,128)}, f32[256,1024]{1,0:T(8,128)S(1)}, u32[]{:S(2)}, u32[]{:S(2)}) collective-permute-start(f32[256,1024]{1,0:T(8,128)} %bitcast.9), channel_id=1, source_target_pairs={{0,1},{1,2},{2,3},{3,0},{4,5},{5,6},{6,7},{7,4},{8,9},{9,10},{10,1... | collective-permute-start | bytes 3145736 | tf_op jit(solution)/shard_map/ppermute | solution.py:22
  4.5 52.6 %collective-permute-start.3 = (f32[256,1024]{1,0:T(8,128)}, f32[256,1024]{1,0:T(8,128)S(1)}, u32[]{:S(2)}, u32[]{:S(2)}) collective-permute-start(f32[256,1024]{1,0:T(8,128)} %bitcast.10), channel_id=1, source_target_pairs={{0,3},{1,0},{2,1},{3,2},{4,7},{5,4},{6,5},{7,6},{8,11},{9,8},{10,9... | collective-permute-start | bytes 3145736 | tf_op jit(solution)/shard_map/ppermute | solution.py:22
  7.6 31.6 %collective-permute-start = (f32[1]{0:T(128)}, f32[1]{0:T(128)}, u32[]{:S(2)}, u32[]{:S(2)}) collective-permute-start(f32[1]{0:T(128)} %param.4), channel_id=1, source_target_pairs={{0,1},{1,2},{2,3},{3,0},{4,5},{5,6},{6,7},{7,4},{8,9},{9,10},{10,1... | collective-permute-start | bytes 20 | tf_op jit(solution)/shard_map/ppermute | solution.py:22
  8.7 45.9 %collective-permute-start.1 = (f32[1]{0:T(128)}, f32[1]{0:T(128)}, u32[]{:S(2)}, u32[]{:S(2)}) collective-permute-start(f32[1]{0:T(128)} %param.4), channel_id=1, source_target_pairs={{0,3},{1,0},{2,1},{3,2},{4,7},{5,4},{6,5},{7,6},{8,11},{9,8},{10,9... | collective-permute-start | bytes 20 | tf_op jit(solution)/shard_map/ppermute | solution.py:22
  11.9 0.7 copy-start.1
  12.6 1.2 %copy-start = (f32[1,256,1024]{2,1,0:T(8,128)S(1)}, f32[1,256,1024]{2,1,0:T(8,128)}, u32[]{:S(2)}) copy-start(f32[1,256,1024]{2,1,0:T(8,128)} %param.3) | copy-start | bytes 3145732
  60.0 3.0 %copy-start.2 = (bf16[256,1024]{1,0:T(8,128)(2,1)}, bf16[256,1024]{1,0:T(8,128)(2,1)S(1)}, u32[]{:S(2)}) copy-start(bf16[256,1024]{1,0:T(8,128)(2,1)S(1)} %get-tuple-element.17.lh) | copy-start | bytes 1572868
  60.0 3.0 %copy-start.4 = (bf16[256,1024]{1,0:T(8,128)(2,1)}, bf16[256,1024]{1,0:T(8,128)(2,1)S(1)}, u32[]{:S(2)}) copy-start(bf16[256,1024]{1,0:T(8,128)(2,1)S(1)} %get-tuple-element.18.ll) | copy-start | bytes 1572868
  60.0 3.0 %copy-start.6 = (bf16[256,1024]{1,0:T(8,128)(2,1)}, bf16[256,1024]{1,0:T(8,128)(2,1)S(1)}, u32[]{:S(2)}) copy-start(bf16[256,1024]{1,0:T(8,128)(2,1)S(1)} %get-tuple-element.19.hh) | copy-start | bytes 1572868
  60.0 3.0 %copy-start.8 = (bf16[256,1024]{1,0:T(8,128)(2,1)}, bf16[256,1024]{1,0:T(8,128)(2,1)S(1)}, u32[]{:S(2)}) copy-start(bf16[256,1024]{1,0:T(8,128)(2,1)S(1)} %get-tuple-element.20.hl) | copy-start | bytes 1572868
  63.0 4.4 %collective-permute-start.6 = (f32[16,8,256]{2,1,0:T(8,128)S(1)}, f32[16,8,256]{2,1,0:T(8,128)S(1)}, u32[]{:S(2)}, u32[]{:S(2)}) collective-permute-start(f32[16,8,256]{2,1,0:T(8,128)S(1)} %get-tuple-element.25), channel_id=1, source_target_pairs={{0,16},{16,0},{1,17},{17,1},{2,18},{18,2},{3,19},{19,3},{4,20},{20... | collective-permute-start | bytes 393224 | tf_op jit(solution)/shard_map/ppermute | solution.py:200
  64.1 46.4 %collective-permute-start.4 = (f32[128,1024]{1,0:T(8,128)}, f32[128,1024]{1,0:T(8,128)S(1)}, u32[]{:S(2)}, u32[]{:S(2)}) collective-permute-start(f32[128,1024]{1,0:T(8,128)} %get-tuple-element.21), channel_id=1, source_target_pairs={{0,3},{1,0},{2,1},{3,2},{4,7},{5,4},{6,5},{7,6},{8,11},{9,8},{10,9... | collective-permute-start | bytes 1572872 | tf_op jit(solution)/shard_map/ppermute | solution.py:22
  66.5 43.9 %collective-permute-start.5 = (f32[128,1024]{1,0:T(8,128)}, f32[128,1024]{1,0:T(8,128)}, u32[]{:S(2)}, u32[]{:S(2)}) collective-permute-start(f32[128,1024]{1,0:T(8,128)} %get-tuple-element.22), channel_id=1, source_target_pairs={{0,1},{1,2},{2,3},{3,0},{4,5},{5,6},{6,7},{7,4},{8,9},{9,10},{10,1... | collective-permute-start | bytes 1572872 | tf_op jit(solution)/shard_map/ppermute | solution.py:22
  67.4 37.9 %copy-start.3 = (bf16[256,1024]{1,0:T(8,128)(2,1)S(1)}, bf16[256,1024]{1,0:T(8,128)(2,1)}, u32[]{:S(2)}) copy-start(bf16[256,1024]{1,0:T(8,128)(2,1)} %copy-done.2) | copy-start | bytes 1572868
  67.4 37.9 %copy-start.5 = (bf16[256,1024]{1,0:T(8,128)(2,1)S(1)}, bf16[256,1024]{1,0:T(8,128)(2,1)}, u32[]{:S(2)}) copy-start(bf16[256,1024]{1,0:T(8,128)(2,1)} %copy-done.4) | copy-start | bytes 1572868
  99.0 13.6 %all-to-all-start.1 = ((f32[16,8,256]{2,1,0:T(8,128)}), f32[16,8,256]{2,1,0:T(8,128)S(1)}, u32[]{:S(2)}, u32[]{:S(2)}) async-start(f32[16,8,256]{2,1,0:T(8,128)} %shard_map.55), calls=%async_computation.1 | async-start | bytes 262144 | tf_op jit(solution)/shard_map/all_to_all | solution.py:205
  105.3 1.0 copy-start.7
  106.4 1.0 copy-start.9

commit v7 on v6

--- a/solution.py
+++ b/solution.py
@@ -22,6 +22,12 @@
     return lax.ppermute(value, "far", [(i, (i + step) % size) for i in range(size)])
 
 
+def give(value, step, core):
+    size = lax.axis_size("far")
+    pairs = [(core * size + i, core * size + (i + step) % size) for i in range(size)]
+    return lax.ppermute(value, ("core", "far"), pairs)
+
+
 def split(x):
     high = x.astype(BF16)
     return high, (x - high.astype(F32)).astype(BF16)
@@ -44,12 +50,13 @@
     return split(2.0 * t - t.T)
 
 
-def mid_kernel(energy, pairs, low, high, down, up, t_mid, lh, ll, hh, hl, *scratch):
-    buf_down, buf_up, sems = scratch
+def mid_kernel(e_low, e_high, pairs, low, high, *refs):
+    down, up, t_mid, lh, ll, hh, hl, buf_down, buf_up, sems = refs
     half = down.shape[0]
     lh[...], ll[...] = l = split(low[...])
     hh[...], hl[...] = h = split(high[...])
-    t = mm(l, h, ROWS) / (energy[0:1, 0:1] - pairs[...])
+    energy = e_low[0:1, 0:1] + e_high[0:1, 0:1]
+    t = mm(l, h, ROWS) / (energy - pairs[...])
     turned = t.T
     s = split(2.0 * t[:half] - turned[:half])
     buf_down[...] = mm(s, h, PLAIN)
@@ -65,27 +72,32 @@
 
 
 def density_kernel(
-    upper, e_low, e_high, pairs, t_mid, oh, ol, lh, ll, hh, hl, keep, send, dens
+    upper, e_own, e_low, e_high, pairs, t_mid, oh, ol, lh, ll, hh, hl, *refs
 ):
+    keep, send, dens = refs
     o, l, h = (oh[...], ol[...]), (lh[...], ll[...]), (hh[...], hl[...])
+    mine = e_own[0:1, 0:1]
     t = t_mid[...]
     total = mm(split(t), spin(t), ROWS)
     for other, energy in ((l, e_low), (h, e_high)):
-        t = mm(o, other, ROWS) / (energy[0:1, 0:1] - pairs[...])
+        t = mm(o, other, ROWS) / (mine + energy[0:1, 0:1] - pairs[...])
         total = total + mm(split(t), spin(t), ROWS)
     dens[...] = total
-    mine = upper[...] > 0.5
+    odd = upper[...] > 0.5
     for at in range(16):
         first = dens[at * 16 : at * 16 + 8, :]
         second = dens[at * 16 + 8 : at * 16 + 16, :]
-        keep[at] = jnp.where(mine, second, first)
-        send[at] = jnp.where(mine, first, second)
-
-
-def near_kernel(e_low, e_high, pairs, oh, ol, lh, ll, hh, hl, grad, total, sem):
+        keep[at] = jnp.where(odd, second, first)
+        send[at] = jnp.where(odd, first, second)
+
+
+def near_kernel(
+    e_own, e_low, e_high, pairs, oh, ol, lh, ll, hh, hl, grad, total, sem
+):
+    mine = e_own[0:1, 0:1]
     o, l, h = (oh[...], ol[...]), (lh[...], ll[...]), (hh[...], hl[...])
     parts = [
-        spin(mm(o, other, ROWS) / (energy[0:1, 0:1] - pairs[...]))
+        spin(mm(o, other, ROWS) / (mine + energy[0:1, 0:1] - pairs[...]))
         for other, energy in ((l, e_low), (h, e_high))
     ]
     total[...] = mm(parts[0], l, PLAIN) + mm(parts[1], h, PLAIN)
@@ -94,30 +106,32 @@
     out.wait()
 
 
-def sum_kernel(near, first, second, grad, mine, other, sems):
-    half = first.shape[0]
+def sum_kernel(near, down0, up0, down1, up1, grad, mine, one, two, sems):
+    half = down0.shape[0]
     parts, step = 4, half // 2
     copies = []
     for at in range(parts):
         rows = pl.ds(at * step, step)
-        source = (first, second)[at // 2].at[pl.ds(at % 2 * step, step), :]
+        inner = pl.ds(at % 2 * step, step)
+        first, second = ((down0, down1), (up0, up1))[at // 2]
         copies.append(
             (
                 pltpu.make_async_copy(near.at[rows, :], mine.at[rows, :], sems.at[0, at]),
-                pltpu.make_async_copy(source, other.at[rows, :], sems.at[1, at]),
-                pltpu.make_async_copy(mine.at[rows, :], grad.at[rows, :], sems.at[2, at]),
+                pltpu.make_async_copy(first.at[inner, :], one.at[rows, :], sems.at[1, at]),
+                pltpu.make_async_copy(second.at[inner, :], two.at[rows, :], sems.at[2, at]),
+                pltpu.make_async_copy(mine.at[rows, :], grad.at[rows, :], sems.at[3, at]),
             )
         )
-        copies[-1][0].start()
-        copies[-1][1].start()
+        for copy in copies[-1][:3]:
+            copy.start()
     for at in range(parts):
         rows = slice(at * step, (at + 1) * step)
-        copies[at][0].wait()
-        copies[at][1].wait()
-        mine[rows, :] = mine[rows, :] + other[rows, :]
-        copies[at][2].start()
+        for copy in copies[at][:3]:
+            copy.wait()
+        mine[rows, :] = mine[rows, :] + (one[rows, :] + two[rows, :])
+        copies[at][3].start()
     for at in range(parts):
-        copies[at][2].wait()
+        copies[at][3].wait()
 
 
 def fold_kernel(pieces, copies):
@@ -158,10 +172,9 @@
     low = shift(own, 1)
     high = shift(own, -1)
     tile = (8, 128)
-    e_low, e_high = shift(eps_occ, 1), shift(eps_occ, -1)
-    s_low = jnp.broadcast_to(eps_occ + e_low, tile)
-    s_high = jnp.broadcast_to(eps_occ + e_high, tile)
-    s_mid = jnp.broadcast_to(e_low + e_high, tile)
+    s_low = jnp.broadcast_to(shift(eps_occ, 1), tile)
+    s_high = jnp.broadcast_to(shift(eps_occ, -1), tile)
+    s_own = jnp.broadcast_to(eps_occ, tile)
     upper = jnp.broadcast_to(lax.axis_index("core").astype(F32), (8, v))
     pairs, oh, ol = call(
         prepare_kernel,
@@ -181,20 +194,19 @@
         part * 2 + [pltpu.SemaphoreType.DMA((2,))],
         12,
         1 << 31,
-        (s_mid, pairs, low, high),
-        [VMEM] * 4,
+        (s_low, s_high, pairs, low, high),
+        [VMEM] * 5,
         (HBM, HBM) + (VMEM,) * 5,
     )
-    first = shift(down, -1)
-    second = in_hbm(shift(up, 1))
+    given = [give(down, -1, 0), give(up, 1, 0), give(down, -1, 1), give(up, 1, 1)]
     keep, send = call(
         density_kernel,
         (piece, piece),
         [pltpu.VMEM((v, v), F32)],
         12,
         1 << 31,
-        (upper, s_low, s_high, pairs, t_mid, oh, ol, *splits),
-        [VMEM] * 11,
+        (upper, s_own, s_low, s_high, pairs, t_mid, oh, ol, *splits),
+        [VMEM] * 12,
         (VMEM, VMEM),
     )
     other = lax.ppermute(send, "core", [(0, 1), (1, 0)])
@@ -213,18 +225,18 @@
         [pltpu.VMEM((v, n), F32), pltpu.SemaphoreType.DMA],
         12,
         1 << 31,
-        (s_low, s_high, pairs, oh, ol, *splits),
-        [VMEM] * 9,
+        (s_own, s_low, s_high, pairs, oh, ol, *splits),
+        [VMEM] * 10,
         (HBM,),
     )
     (grad,) = call(
         sum_kernel,
         ((v, n),),
-        [pltpu.VMEM((v, n), F32)] * 2 + [pltpu.SemaphoreType.DMA((3, 4))],
+        [pltpu.VMEM((v, n), F32)] * 3 + [pltpu.SemaphoreType.DMA((4, 4))],
         8,
         1 << 20,
-        (in_hbm(near), first, second),
-        [HBM] * 3,
+        (in_hbm(near), *given),
+        [HBM] * 5,
         (HBM,),
     )
     return grad[None], density

time: 114 us -> 118 us (1.035)
  starting transfers between devices: 21.3 us -> 24.8 us
  local copies, waits for them, and re-layouts: 4.01 us -> 7.34 us
  between operations: 4.04 us -> 1.57 us
    ppermute x0 -> x4, starting transfers between devices: none -> 8.56 us  [give(): return lax.ppermute(value, ('core', 'far'), pairs)]
    ppermute x6 -> x4, starting transfers between devices: 13.9 us -> 10.6 us  [shift(): lax.ppermute(value, 'far', [(i, (i + step) % size) for i in range(size)])]
    unnamed x20, local copies, waits for them, and re-layouts: 4 us -> 6.07 us
    all_to_all x1, starting transfers between devices: 6.3 us -> 4.6 us  [body(): lax.all_to_all(copies, ('y', 'near', 'core'), split_axis=0, concat_axis=0...]
    broadcast_in_dim x3, local copies, waits for them, and re-layouts: 0.02 us -> 1.26 us  [the longest x1 0.63 us: body(): s_high = jnp.broadcast_to(shift(eps_occ, -1), tile)]
    ppermute x6 -> x4, waiting for transfers between devices: 40.5 us -> 40.5 us  [shift(): lax.ppermute(value, 'far', [(i, (i + step) % size) for i in range(size)])]
  transfers between devices with their start and end apart: 8 -> 10, of which waited for: 2 -> 2; matrix products, arithmetic and copies ran while one was open for 0% -> 0% of each run, Pallas kernels for 5% -> 5%
where the time goes in v7:
time: 118 us; the launch traced here: 117 us
  waiting for transfers between devices  40.5 us (34%)
  blocking collectives  30.3 us (26%)
  starting transfers between devices  24.8 us (21%)
  Pallas kernels  11.8 us (10%)
  local copies, waits for them, and re-layouts  7.34 us (6%)
  between operations  1.57 us (1%)
    ppermute x4, waiting for transfers between devices, shift(): lax.ppermute(value, 'far', [(i, (i + step) % size) for i in range(size)])  40.5 us
    all_to_all x1, blocking collectives, body(): lax.all_to_all(keep + other, ('x', 'far'), split_axis=0, concat_axis=0, t...  30.3 us
    pallas_call x6, Pallas kernels, call(): pl.pallas_call(kernel, out_shape=tuple((pltpu.HBM(s, F32) if spec is HBM...  11.8 us
    ppermute x4, starting transfers between devices, shift(): lax.ppermute(value, 'far', [(i, (i + step) % size) for i in range(size)])  10.6 us
    ppermute x4, starting transfers between devices, give(): return lax.ppermute(value, ('core', 'far'), pairs)  8.56 us
    unnamed x20, local copies, waits for them, and re-layouts  6.07 us
    all_to_all x1, starting transfers between devices, body(): lax.all_to_all(copies, ('y', 'near', 'core'), split_axis=0, concat_axis=0...  4.6 us
  transfers between devices with their start and end apart: 10, of which 2 were waited for; matrix products, arithmetic and copies ran while one was open for 0% of the time, Pallas kernels for 5%

profile of v7, /device:TPU:1, one launch (start us, length us, event | category | flops | bytes accessed | tf_op | source)
XLA Modules:
  0.0 116.9 jit_solution(1117718866364666273)
XLA Ops:
  0.6 3.9 %collective-permute-start.2 = (f32[256,1024]{1,0:T(8,128)}, f32[256,1024]{1,0:T(8,128)S(1)}, u32[]{:S(2)}, u32[]{:S(2)}) collective-permute-start(f32[256,1024]{1,0:T(8,128)} %bitcast.10), channel_id=1, source_target_pairs={{0,1},{1,2},{2,3},{3,0},{4,5},{5,6},{6,7},{7,4},{8,9},{9,10},{10,1... | collective-permute-start | bytes 3145736 | tf_op jit(solution)/shard_map/ppermute | solution.py:22
  4.5 3.1 %collective-permute-start.3 = (f32[256,1024]{1,0:T(8,128)}, f32[256,1024]{1,0:T(8,128)S(1)}, u32[]{:S(2)}, u32[]{:S(2)}) collective-permute-start(f32[256,1024]{1,0:T(8,128)} %bitcast.11), channel_id=1, source_target_pairs={{0,3},{1,0},{2,1},{3,2},{4,7},{5,4},{6,5},{7,6},{8,11},{9,8},{10,9... | collective-permute-start | bytes 3145736 | tf_op jit(solution)/shard_map/ppermute | solution.py:22
  7.6 1.1 collective-permute-start
  8.7 2.5 %collective-permute-start.1 = (f32[1]{0:T(128)}, f32[1]{0:T(128)}, u32[]{:S(2)}, u32[]{:S(2)}) collective-permute-start(f32[1]{0:T(128)} %param.4), channel_id=1, source_target_pairs={{0,3},{1,0},{2,1},{3,2},{4,7},{5,4},{6,5},{7,6},{8,11},{9,8},{10,9... | collective-permute-start | bytes 20 | tf_op jit(solution)/shard_map/ppermute | solution.py:22
  11.9 0.7 copy-done.1
  12.6 1.2 %copy-done = f32[1,256,1024]{2,1,0:T(8,128)S(1)} copy-done((f32[1,256,1024]{2,1,0:T(8,128)S(1)}, f32[1,256,1024]{2,1,0:T(8,128)}, u32[]{:S(2)}) %copy-start) | copy-done | bytes 1048600
  13.8 0.3 shard_map.53
  14.1 25.1 %collective-permute-done = f32[1]{0:T(128)} collective-permute-done((f32[1]{0:T(128)}, f32[1]{0:T(128)}, u32[]{:S(2)}, u32[]{:S(2)}) %collective-permute-start) | collective-permute-done | bytes 36 | tf_op jit(solution)/shard_map/ppermute | solution.py:22
  39.2 15.4 %collective-permute-done.1 = f32[1]{0:T(128)} collective-permute-done((f32[1]{0:T(128)}, f32[1]{0:T(128)}, u32[]{:S(2)}, u32[]{:S(2)}) %collective-permute-start.1) | collective-permute-done | bytes 36 | tf_op jit(solution)/shard_map/ppermute | solution.py:22
  54.6 0.0 collective-permute-done.2.low
  54.6 0.0 collective-permute-done.3.high
  54.6 0.6 broadcast_in_dim.25.e_low
  55.3 0.6 broadcast_in_dim.26.e_high
  55.9 2.8 %shard_map.54 = (f32[128,1024]{1,0:T(8,128)}, f32[128,1024]{1,0:T(8,128)}, f32[256,256]{1,0:T(8,128)S(1)}, bf16[256,1024]{1,0:T(8,128)(2,1)S(1)}, bf16[256,1024]...) custom-call(f32[8,128]{1,0:T(8,128)S(1)} %broadcast_in_dim.25.e_low, ...), custom_call_target="tpu_custom_call" | custom-call | flops 2147483648 | bytes 1048576 | tf_op jit(solution)/shard_map/pallas_call | solution.py:147
  58.8 2.9 %shard_map.57 = (f32[16,8,256]{2,1,0:T(8,128)S(1)}, f32[16,8,256]{2,1,0:T(8,128)S(1)}) custom-call(f32[8,256]{1,0:T(8,128)S(1)} %broadcast_in_dim.29.upper, f32[8,128]{1,0:T(8,128)S(1)} %broadcast_in_dim.24.e_own, f32[8,128]{1,0:T(8,128)S(1)} %broadcast_in_dim.25.e_low, f32[8,128]{1,0:T(8,128)S(1)} %broadcast_in_dim.26.e_high, ...), custom_call_target="tpu_custom_call" | custom-call | flops 2147483648 | bytes 1048576 | tf_op jit(solution)/shard_map/pallas_call | solution.py:147
  61.7 1.1 collective-permute-start.8
  62.8 0.7 collective-permute-start.4
  63.5 0.7 collective-permute-start.5
  64.2 4.4 %collective-permute-start.6 = (f32[128,1024]{1,0:T(8,128)}, f32[128,1024]{1,0:T(8,128)S(1)}, u32[]{:S(2)}, u32[]{:S(2)}) collective-permute-start(f32[128,1024]{1,0:T(8,128)} %get-tuple-element.21), channel_id=1, source_target_pairs={{16,19},{17,16},{18,17},{19,18},{20,23},{21,20},{22,21},{23,22},{2... | collective-permute-start | bytes 1572872 | tf_op jit(solution)/shard_map/ppermute | solution.py:28
  68.5 2.8 %collective-permute-start.7 = (f32[128,1024]{1,0:T(8,128)}, f32[128,1024]{1,0:T(8,128)S(1)}, u32[]{:S(2)}, u32[]{:S(2)}) collective-permute-start(f32[128,1024]{1,0:T(8,128)} %get-tuple-element.22), channel_id=1, source_target_pairs={{16,17},{17,18},{18,19},{19,16},{20,21},{21,22},{22,23},{23,20},{2... | collective-permute-start | bytes 1572872 | tf_op jit(solution)/shard_map/ppermute | solution.py:28
  71.4 30.3 %all_to_all.10.pieces = f32[16,8,256]{2,1,0:T(8,128)S(1)} all-to-all(f32[16,8,256]{2,1,0:T(8,128)S(1)} %add.3), channel_id=1, replica_groups=mesh['y'=4,'near'=2,'core'=2,'x'=4,'far'=4] {'x','far'}, dimensions={0} | all-to-all | bytes 262144 | tf_op jit(solution)/shard_map/all_to_all | solution.py:213
  101.7 0.7 shard_map.58
  102.4 4.6 %all-to-all-start.1 = ((f32[16,8,256]{2,1,0:T(8,128)}), f32[16,8,256]{2,1,0:T(8,128)S(1)}, u32[]{:S(2)}, u32[]{:S(2)}) async-start(f32[16,8,256]{2,1,0:T(8,128)} %shard_map.58), calls=%async_computation.1 | async-start | bytes 262144 | tf_op jit(solution)/shard_map/all_to_all | solution.py:217
  107.0 1.0 copy-done.3
  108.0 1.0 copy-done.5
  109.1 1.0 copy-done.7
  110.1 1.0 copy-done.9
  111.1 3.0 %shard_map.55.near = f32[256,1024]{1,0:T(8,128)} custom-call(f32[8,128]{1,0:T(8,128)S(1)} %broadcast_in_dim.24.e_own, f32[8,128]{1,0:T(8,128)S(1)} %broadcast_in_dim.25.e_low, f32[8,128]{1,0:T(8,128)S(1)} %broadcast_in_dim.26.e_high, f32[256,256]{1,0:T(8,128)S(1)} %get-tuple-element.14.pairs, bf16[256,1024]{1,0:T(8,128)(2,1)S(1)} %get-tuple-element.15.oh, ...), custom_call_target="tpu_custom_call" | custom-call | flops 2147483648 | bytes 1048576 | tf_op jit(solution)/shard_map/pallas_call | solution.py:147
  114.2 0.0 collective-permute-done.4.down0
  114.2 0.0 collective-permute-done.5.up0
  114.2 2.1 %shard_map.56 = f32[256,1024]{1,0:T(8,128)} custom-call(f32[256,1024]{1,0:T(8,128)} %shard_map.55.near, f32[128,1024]{1,0:T(8,128)S(1)} %collective-permute-done.4.down0, f32[128,1024]{1,0:T(8,128)S(1)} %collective-permute-done.5.up0, f32[128,1024]{1,0:T(8,128)S(1)} %collective-permute-done.6.down1, f32[128,1024]{1,0:T(8,128)S(1)} %collective-permute-done.7.up1), custom_call_target="tpu_custom_call" | custom-call | flops 1048576 | bytes 1048576 | tf_op jit(solution)/shard_map/pallas_call | solution.py:147
  116.3 0.6 bitcast_reduce_fusion
  (21 shorter events, 0.1 us)
Async XLA Ops:
  0.6 54.0 %collective-permute-start.2 = (f32[256,1024]{1,0:T(8,128)}, f32[256,1024]{1,0:T(8,128)S(1)}, u32[]{:S(2)}, u32[]{:S(2)}) collective-permute-start(f32[256,1024]{1,0:T(8,128)} %bitcast.10), channel_id=1, source_target_pairs={{0,1},{1,2},{2,3},{3,0},{4,5},{5,6},{6,7},{7,4},{8,9},{9,10},{10,1... | collective-permute-start | bytes 3145736 | tf_op jit(solution)/shard_map/ppermute | solution.py:22
  4.5 50.1 %collective-permute-start.3 = (f32[256,1024]{1,0:T(8,128)}, f32[256,1024]{1,0:T(8,128)S(1)}, u32[]{:S(2)}, u32[]{:S(2)}) collective-permute-start(f32[256,1024]{1,0:T(8,128)} %bitcast.11), channel_id=1, source_target_pairs={{0,3},{1,0},{2,1},{3,2},{4,7},{5,4},{6,5},{7,6},{8,11},{9,8},{10,9... | collective-permute-start | bytes 3145736 | tf_op jit(solution)/shard_map/ppermute | solution.py:22
  7.6 31.6 %collective-permute-start = (f32[1]{0:T(128)}, f32[1]{0:T(128)}, u32[]{:S(2)}, u32[]{:S(2)}) collective-permute-start(f32[1]{0:T(128)} %param.4), channel_id=1, source_target_pairs={{0,1},{1,2},{2,3},{3,0},{4,5},{5,6},{6,7},{7,4},{8,9},{9,10},{10,1... | collective-permute-start | bytes 20 | tf_op jit(solution)/shard_map/ppermute | solution.py:22
  8.7 45.9 %collective-permute-start.1 = (f32[1]{0:T(128)}, f32[1]{0:T(128)}, u32[]{:S(2)}, u32[]{:S(2)}) collective-permute-start(f32[1]{0:T(128)} %param.4), channel_id=1, source_target_pairs={{0,3},{1,0},{2,1},{3,2},{4,7},{5,4},{6,5},{7,6},{8,11},{9,8},{10,9... | collective-permute-start | bytes 20 | tf_op jit(solution)/shard_map/ppermute | solution.py:22
  11.9 0.7 copy-start.1
  12.6 1.2 %copy-start = (f32[1,256,1024]{2,1,0:T(8,128)S(1)}, f32[1,256,1024]{2,1,0:T(8,128)}, u32[]{:S(2)}) copy-start(f32[1,256,1024]{2,1,0:T(8,128)} %param.3) | copy-start | bytes 3145732
  58.7 2.9 %copy-start.2 = (bf16[256,1024]{1,0:T(8,128)(2,1)}, bf16[256,1024]{1,0:T(8,128)(2,1)S(1)}, u32[]{:S(2)}) copy-start(bf16[256,1024]{1,0:T(8,128)(2,1)S(1)} %get-tuple-element.17.lh) | copy-start | bytes 1572868
  58.7 2.9 %copy-start.4 = (bf16[256,1024]{1,0:T(8,128)(2,1)}, bf16[256,1024]{1,0:T(8,128)(2,1)S(1)}, u32[]{:S(2)}) copy-start(bf16[256,1024]{1,0:T(8,128)(2,1)S(1)} %get-tuple-element.18.ll) | copy-start | bytes 1572868
  58.7 2.9 %copy-start.6 = (bf16[256,1024]{1,0:T(8,128)(2,1)}, bf16[256,1024]{1,0:T(8,128)(2,1)S(1)}, u32[]{:S(2)}) copy-start(bf16[256,1024]{1,0:T(8,128)(2,1)S(1)} %get-tuple-element.19.hh) | copy-start | bytes 1572868
  58.7 2.9 %copy-start.8 = (bf16[256,1024]{1,0:T(8,128)(2,1)}, bf16[256,1024]{1,0:T(8,128)(2,1)S(1)}, u32[]{:S(2)}) copy-start(bf16[256,1024]{1,0:T(8,128)(2,1)S(1)} %get-tuple-element.20.hl) | copy-start | bytes 1572868
  61.7 9.7 %collective-permute-start.8 = (f32[16,8,256]{2,1,0:T(8,128)S(1)}, f32[16,8,256]{2,1,0:T(8,128)S(1)}, u32[]{:S(2)}, u32[]{:S(2)}) collective-permute-start(f32[16,8,256]{2,1,0:T(8,128)S(1)} %get-tuple-element.25), channel_id=1, source_target_pairs={{0,16},{16,0},{1,17},{17,1},{2,18},{18,2},{3,19},{19,3},{4,20},{20... | collective-permute-start | bytes 393224 | tf_op jit(solution)/shard_map/ppermute | solution.py:212
  62.8 51.4 %collective-permute-start.4 = (f32[128,1024]{1,0:T(8,128)}, f32[128,1024]{1,0:T(8,128)S(1)}, u32[]{:S(2)}, u32[]{:S(2)}) collective-permute-start(f32[128,1024]{1,0:T(8,128)} %get-tuple-element.21), channel_id=1, source_target_pairs={{0,3},{1,0},{2,1},{3,2},{4,7},{5,4},{6,5},{7,6},{8,11},{9,8},{10,9... | collective-permute-start | bytes 1572872 | tf_op jit(solution)/shard_map/ppermute | solution.py:28
  63.5 50.7 %collective-permute-start.5 = (f32[128,1024]{1,0:T(8,128)}, f32[128,1024]{1,0:T(8,128)S(1)}, u32[]{:S(2)}, u32[]{:S(2)}) collective-permute-start(f32[128,1024]{1,0:T(8,128)} %get-tuple-element.22), channel_id=1, source_target_pairs={{0,1},{1,2},{2,3},{3,0},{4,5},{5,6},{6,7},{7,4},{8,9},{9,10},{10,1... | collective-permute-start | bytes 1572872 | tf_op jit(solution)/shard_map/ppermute | solution.py:28
  64.2 50.0 %collective-permute-start.6 = (f32[128,1024]{1,0:T(8,128)}, f32[128,1024]{1,0:T(8,128)S(1)}, u32[]{:S(2)}, u32[]{:S(2)}) collective-permute-start(f32[128,1024]{1,0:T(8,128)} %get-tuple-element.21), channel_id=1, source_target_pairs={{16,19},{17,16},{18,17},{19,18},{20,23},{21,20},{22,21},{23,22},{2... | collective-permute-start | bytes 1572872 | tf_op jit(solution)/shard_map/ppermute | solution.py:28
  68.5 45.7 %collective-permute-start.7 = (f32[128,1024]{1,0:T(8,128)}, f32[128,1024]{1,0:T(8,128)S(1)}, u32[]{:S(2)}, u32[]{:S(2)}) collective-permute-start(f32[128,1024]{1,0:T(8,128)} %get-tuple-element.22), channel_id=1, source_target_pairs={{16,17},{17,18},{18,19},{19,16},{20,21},{21,22},{22,23},{23,20},{2... | collective-permute-start | bytes 1572872 | tf_op jit(solution)/shard_map/ppermute | solution.py:28
  102.4 13.9 %all-to-all-start.1 = ((f32[16,8,256]{2,1,0:T(8,128)}), f32[16,8,256]{2,1,0:T(8,128)S(1)}, u32[]{:S(2)}, u32[]{:S(2)}) async-start(f32[16,8,256]{2,1,0:T(8,128)} %shard_map.58), calls=%async_computation.1 | async-start | bytes 262144 | tf_op jit(solution)/shard_map/all_to_all | solution.py:217
  107.0 1.0 copy-start.3
  108.0 1.0 copy-start.5
  109.1 1.0 copy-start.7
  110.1 1.0 copy-start.9

commit v8 on v7

--- a/solution.py
+++ b/solution.py
@@ -74,35 +74,27 @@
 def density_kernel(
     upper, e_own, e_low, e_high, pairs, t_mid, oh, ol, lh, ll, hh, hl, *refs
 ):
-    keep, send, dens = refs
+    keep, send, near, dens, total, sem = refs
     o, l, h = (oh[...], ol[...]), (lh[...], ll[...]), (hh[...], hl[...])
     mine = e_own[0:1, 0:1]
+    t_low = mm(o, l, ROWS) / (mine + e_low[0:1, 0:1] - pairs[...])
+    t_high = mm(o, h, ROWS) / (mine + e_high[0:1, 0:1] - pairs[...])
+    s_low, s_high = spin(t_low), spin(t_high)
+    total[...] = mm(s_low, l, PLAIN) + mm(s_high, h, PLAIN)
+    out = pltpu.make_async_copy(total, near, sem)
+    out.start()
     t = t_mid[...]
-    total = mm(split(t), spin(t), ROWS)
-    for other, energy in ((l, e_low), (h, e_high)):
-        t = mm(o, other, ROWS) / (mine + energy[0:1, 0:1] - pairs[...])
-        total = total + mm(split(t), spin(t), ROWS)
-    dens[...] = total
+    dens[...] = (
+        mm(split(t), spin(t), ROWS)
+        + mm(split(t_low), s_low, ROWS)
+        + mm(split(t_high), s_high, ROWS)
+    )
     odd = upper[...] > 0.5
     for at in range(16):
         first = dens[at * 16 : at * 16 + 8, :]
         second = dens[at * 16 + 8 : at * 16 + 16, :]
         keep[at] = jnp.where(odd, second, first)
         send[at] = jnp.where(odd, first, second)
-
-
-def near_kernel(
-    e_own, e_low, e_high, pairs, oh, ol, lh, ll, hh, hl, grad, total, sem
-):
-    mine = e_own[0:1, 0:1]
-    o, l, h = (oh[...], ol[...]), (lh[...], ll[...]), (hh[...], hl[...])
-    parts = [
-        spin(mm(o, other, ROWS) / (mine + energy[0:1, 0:1] - pairs[...]))
-        for other, energy in ((l, e_low), (h, e_high))
-    ]
-    total[...] = mm(parts[0], l, PLAIN) + mm(parts[1], h, PLAIN)
-    out = pltpu.make_async_copy(total, grad, sem)
-    out.start()
     out.wait()
 
 
@@ -199,15 +191,19 @@
         (HBM, HBM) + (VMEM,) * 5,
     )
     given = [give(down, -1, 0), give(up, 1, 0), give(down, -1, 1), give(up, 1, 1)]
-    keep, send = call(
+    keep, send, near = call(
         density_kernel,
-        (piece, piece),
-        [pltpu.VMEM((v, v), F32)],
+        (piece, piece, (v, n)),
+        [
+            pltpu.VMEM((v, v), F32),
+            pltpu.VMEM((v, n), F32),
+            pltpu.SemaphoreType.DMA,
+        ],
         12,
         1 << 31,
         (upper, s_own, s_low, s_high, pairs, t_mid, oh, ol, *splits),
         [VMEM] * 12,
-        (VMEM, VMEM),
+        (VMEM, VMEM, HBM),
     )
     other = lax.ppermute(send, "core", [(0, 1), (1, 0)])
     parts = lax.all_to_all(
@@ -219,16 +215,6 @@
     )
     density = jnp.sum(copies.reshape(8, 16, v), axis=0)
 
-    (near,) = call(
-        near_kernel,
-        ((v, n),),
-        [pltpu.VMEM((v, n), F32), pltpu.SemaphoreType.DMA],
-        12,
-        1 << 31,
-        (s_own, s_low, s_high, pairs, oh, ol, *splits),
-        [VMEM] * 10,
-        (HBM,),
-    )
     (grad,) = call(
         sum_kernel,
         ((v, n),),

time: 118 us -> 114 us (0.966)
  the two profiles are of different devices: /device:TPU:1 before, /device:TPU:2 now
where the time goes in v8:
time: 114 us; the launch traced here: 112 us
  waiting for transfers between devices  44.6 us (39%)
  blocking collectives  28.7 us (25%)
  starting transfers between devices  24.4 us (21%)
  Pallas kernels  9.11 us (8%)
  local copies, waits for them, and re-layouts  3.17 us (3%)
  between operations  1.52 us (1%)
    ppermute x4, waiting for transfers between devices, shift(): lax.ppermute(value, 'far', [(i, (i + step) % size) for i in range(size)])  40 us
    all_to_all x1, blocking collectives, body(): lax.all_to_all(keep + other, ('x', 'far'), split_axis=0, concat_axis=0, t...  28.7 us
    ppermute x4, starting transfers between devices, shift(): lax.ppermute(value, 'far', [(i, (i + step) % size) for i in range(size)])  10.6 us
    pallas_call x5, Pallas kernels, call(): pl.pallas_call(kernel, out_shape=tuple((pltpu.HBM(s, F32) if spec is HBM...  9.11 us
    ppermute x4, starting transfers between devices, give(): return lax.ppermute(value, ('core', 'far'), pairs)  8.85 us
    all_to_all x1, starting transfers between devices, body(): lax.all_to_all(copies, ('y', 'near', 'core'), split_axis=0, concat_axis=0...  4.84 us
    all_to_all x1, waiting for transfers between devices, body(): lax.all_to_all(copies, ('y', 'near', 'core'), split_axis=0, concat_axis=0...  4.52 us
  transfers between devices with their start and end apart: 10, of which 3 were waited for; matrix products, arithmetic and copies ran while one was open for 0% of the time, Pallas kernels for 3%

profile of v8, /device:TPU:2, one launch (start us, length us, event | category | flops | bytes accessed | tf_op | source)
XLA Modules:
  0.0 112.1 jit_solution(323371661243172563)
XLA Ops:
  0.6 3.3 %collective-permute-start.2 = (f32[256,1024]{1,0:T(8,128)}, f32[256,1024]{1,0:T(8,128)S(1)}, u32[]{:S(2)}, u32[]{:S(2)}) collective-permute-start(f32[256,1024]{1,0:T(8,128)} %bitcast.10), channel_id=1, source_target_pairs={{0,1},{1,2},{2,3},{3,0},{4,5},{5,6},{6,7},{7,4},{8,9},{9,10},{10,1... | collective-permute-start | bytes 3145736 | tf_op jit(solution)/shard_map/ppermute | solution.py:22
  4.0 3.1 %collective-permute-start.3 = (f32[256,1024]{1,0:T(8,128)}, f32[256,1024]{1,0:T(8,128)S(1)}, u32[]{:S(2)}, u32[]{:S(2)}) collective-permute-start(f32[256,1024]{1,0:T(8,128)} %bitcast.11), channel_id=1, source_target_pairs={{0,3},{1,0},{2,1},{3,2},{4,7},{5,4},{6,5},{7,6},{8,11},{9,8},{10,9... | collective-permute-start | bytes 3145736 | tf_op jit(solution)/shard_map/ppermute | solution.py:22
  7.1 1.4 %collective-permute-start = (f32[1]{0:T(128)}, f32[1]{0:T(128)}, u32[]{:S(2)}, u32[]{:S(2)}) collective-permute-start(f32[1]{0:T(128)} %param.4), channel_id=1, source_target_pairs={{0,1},{1,2},{2,3},{3,0},{4,5},{5,6},{6,7},{7,4},{8,9},{9,10},{10,1... | collective-permute-start | bytes 20 | tf_op jit(solution)/shard_map/ppermute | solution.py:22
  8.5 2.8 %collective-permute-start.1 = (f32[1]{0:T(128)}, f32[1]{0:T(128)}, u32[]{:S(2)}, u32[]{:S(2)}) collective-permute-start(f32[1]{0:T(128)} %param.4), channel_id=1, source_target_pairs={{0,3},{1,0},{2,1},{3,2},{4,7},{5,4},{6,5},{7,6},{8,11},{9,8},{10,9... | collective-permute-start | bytes 20 | tf_op jit(solution)/shard_map/ppermute | solution.py:22
  11.9 0.7 copy-done.1
  12.6 1.2 %copy-done = f32[1,256,1024]{2,1,0:T(8,128)S(1)} copy-done((f32[1,256,1024]{2,1,0:T(8,128)S(1)}, f32[1,256,1024]{2,1,0:T(8,128)}, u32[]{:S(2)}) %copy-start) | copy-done | bytes 1048600
  13.8 0.3 shard_map.53
  14.2 25.3 %collective-permute-done = f32[1]{0:T(128)} collective-permute-done((f32[1]{0:T(128)}, f32[1]{0:T(128)}, u32[]{:S(2)}, u32[]{:S(2)}) %collective-permute-start) | collective-permute-done | bytes 36 | tf_op jit(solution)/shard_map/ppermute | solution.py:22
  39.5 14.7 %collective-permute-done.1 = f32[1]{0:T(128)} collective-permute-done((f32[1]{0:T(128)}, f32[1]{0:T(128)}, u32[]{:S(2)}, u32[]{:S(2)}) %collective-permute-start.1) | collective-permute-done | bytes 36 | tf_op jit(solution)/shard_map/ppermute | solution.py:22
  54.2 0.0 collective-permute-done.2.low
  54.2 0.0 collective-permute-done.3.high
  54.2 0.6 broadcast_in_dim.26.e_low
  54.8 0.6 broadcast_in_dim.27.e_high
  55.5 2.8 %shard_map.54 = (f32[128,1024]{1,0:T(8,128)}, f32[128,1024]{1,0:T(8,128)}, f32[256,256]{1,0:T(8,128)S(1)}, bf16[256,1024]{1,0:T(8,128)(2,1)S(1)}, bf16[256,1024]...) custom-call(f32[8,128]{1,0:T(8,128)S(1)} %broadcast_in_dim.26.e_low, ...), custom_call_target="tpu_custom_call" | custom-call | flops 2147483648 | bytes 1048576 | tf_op jit(solution)/shard_map/pallas_call | solution.py:139
  58.3 0.0 copy-start.3
  58.4 3.2 %shard_map.55 = (f32[16,8,256]{2,1,0:T(8,128)S(1)}, f32[16,8,256]{2,1,0:T(8,128)S(1)}, f32[256,1024]{1,0:T(8,128)}) custom-call(f32[8,256]{1,0:T(8,128)S(1)} %broadcast_in_dim.24.upper, f32[8,128]{1,0:T(8,128)S(1)} %broadcast_in_dim.25.e_own, f32[8,128]{1,0:T(8,128)S(1)} %broadcast_in_dim.26.e_low, f32[8,128]{1,0:T(8,128)S(1)} %broadcast_in_dim.27.e_high, ...), custom_call_target="tpu_custom_call" | custom-call | flops 2147483648 | bytes 1048576 | tf_op jit(solution)/shard_map/pallas_call | solution.py:139
  61.5 0.1 collective-permute-start.8
  61.6 4.6 %collective-permute-start.4 = (f32[128,1024]{1,0:T(8,128)S(1)}, f32[128,1024]{1,0:T(8,128)S(1)}, u32[]{:S(2)}, u32[]{:S(2)}) collective-permute-start(f32[128,1024]{1,0:T(8,128)S(1)} %copy-done.3), channel_id=1, source_target_pairs={{0,3},{1,0},{2,1},{3,2},{4,7},{5,4},{6,5},{7,6},{8,11},{9,8},{10,9... | collective-permute-start | bytes 1572872 | tf_op jit(solution)/shard_map/ppermute | solution.py:28
  66.3 2.8 %collective-permute-start.5 = (f32[128,1024]{1,0:T(8,128)S(1)}, f32[128,1024]{1,0:T(8,128)S(1)}, u32[]{:S(2)}, u32[]{:S(2)}) collective-permute-start(f32[128,1024]{1,0:T(8,128)S(1)} %copy-done.2), channel_id=1, source_target_pairs={{0,1},{1,2},{2,3},{3,0},{4,5},{5,6},{6,7},{7,4},{8,9},{9,10},{10,1... | collective-permute-start | bytes 1572872 | tf_op jit(solution)/shard_map/ppermute | solution.py:28
  69.1 0.7 collective-permute-start.6
  69.8 0.7 collective-permute-start.7
  70.5 0.0 collective-permute-done.8
  70.6 28.7 %all_to_all.10.pieces = f32[16,8,256]{2,1,0:T(8,128)S(1)} all-to-all(f32[16,8,256]{2,1,0:T(8,128)S(1)} %add.3), channel_id=1, replica_groups=mesh['y'=4,'near'=2,'core'=2,'x'=4,'far'=4] {'x','far'}, dimensions={0} | all-to-all | bytes 262144 | tf_op jit(solution)/shard_map/all_to_all | solution.py:209
  99.3 0.7 shard_map.57
  100.0 4.8 %all-to-all-start.1 = ((f32[16,8,256]{2,1,0:T(8,128)}), f32[16,8,256]{2,1,0:T(8,128)S(1)}, u32[]{:S(2)}, u32[]{:S(2)}) async-start(f32[16,8,256]{2,1,0:T(8,128)} %shard_map.57), calls=%async_computation.1 | async-start | bytes 262144 | tf_op jit(solution)/shard_map/all_to_all | solution.py:213
  104.8 0.0 collective-permute-done.4.down0
  104.8 0.0 collective-permute-done.5.up0
  104.8 0.0 collective-permute-done.6.down1
  104.9 0.0 collective-permute-done.7.up1
  104.9 2.1 %shard_map.56 = f32[256,1024]{1,0:T(8,128)} custom-call(f32[256,1024]{1,0:T(8,128)} %get-tuple-element.23.near, f32[128,1024]{1,0:T(8,128)S(1)} %collective-permute-done.4.down0, f32[128,1024]{1,0:T(8,128)S(1)} %collective-permute-done.5.up0, f32[128,1024]{1,0:T(8,128)S(1)} %collective-permute-done.6.down1, f32[128,1024]{1,0:T(8,128)S(1)} %collective-permute-done.7.up1), custom_call_target="tpu_custom_call" | custom-call | flops 1048576 | bytes 1048576 | tf_op jit(solution)/shard_map/pallas_call | solution.py:139
  107.0 4.5 %all-to-all-done.1 = f32[16,8,256]{2,1,0:T(8,128)S(1)} async-done(((f32[16,8,256]{2,1,0:T(8,128)}), f32[16,8,256]{2,1,0:T(8,128)S(1)}, u32[]{:S(2)}, u32[]{:S(2)}) %all-to-all-start.1) | async-done | bytes 131104 | tf_op jit(solution)/shard_map/all_to_all | solution.py:213
  111.5 0.6 bitcast_reduce_fusion
  (8 shorter events, 0.0 us)
Async XLA Ops:
  0.6 53.6 %collective-permute-start.2 = (f32[256,1024]{1,0:T(8,128)}, f32[256,1024]{1,0:T(8,128)S(1)}, u32[]{:S(2)}, u32[]{:S(2)}) collective-permute-start(f32[256,1024]{1,0:T(8,128)} %bitcast.10), channel_id=1, source_target_pairs={{0,1},{1,2},{2,3},{3,0},{4,5},{5,6},{6,7},{7,4},{8,9},{9,10},{10,1... | collective-permute-start | bytes 3145736 | tf_op jit(solution)/shard_map/ppermute | solution.py:22
  4.0 50.2 %collective-permute-start.3 = (f32[256,1024]{1,0:T(8,128)}, f32[256,1024]{1,0:T(8,128)S(1)}, u32[]{:S(2)}, u32[]{:S(2)}) collective-permute-start(f32[256,1024]{1,0:T(8,128)} %bitcast.11), channel_id=1, source_target_pairs={{0,3},{1,0},{2,1},{3,2},{4,7},{5,4},{6,5},{7,6},{8,11},{9,8},{10,9... | collective-permute-start | bytes 3145736 | tf_op jit(solution)/shard_map/ppermute | solution.py:22
  7.1 32.4 %collective-permute-start = (f32[1]{0:T(128)}, f32[1]{0:T(128)}, u32[]{:S(2)}, u32[]{:S(2)}) collective-permute-start(f32[1]{0:T(128)} %param.4), channel_id=1, source_target_pairs={{0,1},{1,2},{2,3},{3,0},{4,5},{5,6},{6,7},{7,4},{8,9},{9,10},{10,1... | collective-permute-start | bytes 20 | tf_op jit(solution)/shard_map/ppermute | solution.py:22
  8.5 45.7 %collective-permute-start.1 = (f32[1]{0:T(128)}, f32[1]{0:T(128)}, u32[]{:S(2)}, u32[]{:S(2)}) collective-permute-start(f32[1]{0:T(128)} %param.4), channel_id=1, source_target_pairs={{0,3},{1,0},{2,1},{3,2},{4,7},{5,4},{6,5},{7,6},{8,11},{9,8},{10,9... | collective-permute-start | bytes 20 | tf_op jit(solution)/shard_map/ppermute | solution.py:22
  11.9 0.7 copy-start.1
  12.6 1.2 %copy-start = (f32[1,256,1024]{2,1,0:T(8,128)S(1)}, f32[1,256,1024]{2,1,0:T(8,128)}, u32[]{:S(2)}) copy-start(f32[1,256,1024]{2,1,0:T(8,128)} %param.3) | copy-start | bytes 3145732
  58.3 3.3 %copy-start.3 = (f32[128,1024]{1,0:T(8,128)S(1)}, f32[128,1024]{1,0:T(8,128)}, u32[]{:S(2)}) copy-start(f32[128,1024]{1,0:T(8,128)} %get-tuple-element.24) | copy-start | bytes 1572868
  58.3 8.0 %copy-start.2 = (f32[128,1024]{1,0:T(8,128)S(1)}, f32[128,1024]{1,0:T(8,128)}, u32[]{:S(2)}) copy-start(f32[128,1024]{1,0:T(8,128)} %get-tuple-element.25) | copy-start | bytes 1572868
  61.5 9.0 %collective-permute-start.8 = (f32[16,8,256]{2,1,0:T(8,128)S(1)}, f32[16,8,256]{2,1,0:T(8,128)S(1)}, u32[]{:S(2)}, u32[]{:S(2)}) collective-permute-start(f32[16,8,256]{2,1,0:T(8,128)S(1)} %get-tuple-element.27), channel_id=1, source_target_pairs={{0,16},{16,0},{1,17},{17,1},{2,18},{18,2},{3,19},{19,3},{4,20},{20... | collective-permute-start | bytes 393224 | tf_op jit(solution)/shard_map/ppermute | solution.py:208
  61.6 43.2 %collective-permute-start.4 = (f32[128,1024]{1,0:T(8,128)S(1)}, f32[128,1024]{1,0:T(8,128)S(1)}, u32[]{:S(2)}, u32[]{:S(2)}) collective-permute-start(f32[128,1024]{1,0:T(8,128)S(1)} %copy-done.3), channel_id=1, source_target_pairs={{0,3},{1,0},{2,1},{3,2},{4,7},{5,4},{6,5},{7,6},{8,11},{9,8},{10,9... | collective-permute-start | bytes 1572872 | tf_op jit(solution)/shard_map/ppermute | solution.py:28
  66.3 38.5 %collective-permute-start.5 = (f32[128,1024]{1,0:T(8,128)S(1)}, f32[128,1024]{1,0:T(8,128)S(1)}, u32[]{:S(2)}, u32[]{:S(2)}) collective-permute-start(f32[128,1024]{1,0:T(8,128)S(1)} %copy-done.2), channel_id=1, source_target_pairs={{0,1},{1,2},{2,3},{3,0},{4,5},{5,6},{6,7},{7,4},{8,9},{9,10},{10,1... | collective-permute-start | bytes 1572872 | tf_op jit(solution)/shard_map/ppermute | solution.py:28
  69.1 35.7 %collective-permute-start.6 = (f32[128,1024]{1,0:T(8,128)S(1)}, f32[128,1024]{1,0:T(8,128)S(1)}, u32[]{:S(2)}, u32[]{:S(2)}) collective-permute-start(f32[128,1024]{1,0:T(8,128)S(1)} %copy-done.3), channel_id=1, source_target_pairs={{16,19},{17,16},{18,17},{19,18},{20,23},{21,20},{22,21},{23,22},{2... | collective-permute-start | bytes 1572872 | tf_op jit(solution)/shard_map/ppermute | solution.py:28
  69.8 35.0 %collective-permute-start.7 = (f32[128,1024]{1,0:T(8,128)S(1)}, f32[128,1024]{1,0:T(8,128)S(1)}, u32[]{:S(2)}, u32[]{:S(2)}) collective-permute-start(f32[128,1024]{1,0:T(8,128)S(1)} %copy-done.2), channel_id=1, source_target_pairs={{16,17},{17,18},{18,19},{19,16},{20,21},{21,22},{22,23},{23,20},{2... | collective-permute-start | bytes 1572872 | tf_op jit(solution)/shard_map/ppermute | solution.py:28
  100.0 11.5 %all-to-all-start.1 = ((f32[16,8,256]{2,1,0:T(8,128)}), f32[16,8,256]{2,1,0:T(8,128)S(1)}, u32[]{:S(2)}, u32[]{:S(2)}) async-start(f32[16,8,256]{2,1,0:T(8,128)} %shard_map.57), calls=%async_computation.1 | async-start | bytes 262144 | tf_op jit(solution)/shard_map/all_to_all | solution.py:213

commit v9 on v8

v9 whole, which is shorter than its diff:
```python
import jax
import jax.numpy as jnp
from jax import lax
from jax.experimental import pallas as pl
from jax.experimental.pallas import tpu as pltpu
from jax.sharding import Mesh, PartitionSpec as P


FINE = ("y", "near", "core", "x", "far")
FINE_SHAPE = (4, 2, 2, 4, 4)
VMEM = pl.BlockSpec(memory_space=pltpu.VMEM)
SMEM = pl.BlockSpec(memory_space=pltpu.SMEM)
HBM = pl.BlockSpec(memory_space=pltpu.HBM)
F32, BF16 = jnp.float32, jnp.bfloat16
ROWS = ((1,), (1,))
PLAIN = ((1,), (0,))
MIB = 1 << 20


def shift(value, step):
    size = lax.axis_size("far")
    return lax.ppermute(value, "far", [(i, (i + step) % size) for i in range(size)])


def split(x):
    high = x.astype(BF16)
    return high, (x - high.astype(F32)).astype(BF16)


def mm(a, b, contract):
    def dot(p, q):
        return lax.dot_general(p, q, (contract, ((), ())), preferred_element_type=F32)

    return dot(a[0], b[0]) + (dot(a[0], b[1]) + dot(a[1], b[0]))


def prepare_kernel(eps_vir, own, pairs, high, low):
    row = jnp.broadcast_to(eps_vir[...], pairs.shape)
    pairs[...] = row + row.T
    high[...], low[...] = split(own[...])


def spin(t):
    return split(2.0 * t - t.T)


def fill(first, second, high, low):
    half = first.shape[0]
    high[:half, :], low[:half, :] = split(first[...])
    high[half:, :], low[half:, :] = split(second[...])
    return high[...], low[...]


def density_kernel(upper, e_own, e_low, e_high, pairs, oh, ol, *refs):
    low_a, low_b, high_a, high_b, keep, send, near = refs[:7]
    lh, ll, hh, hl, dens, total, sem = refs[7:]
    o = (oh[...], ol[...])
    l, h = fill(low_a, low_b, lh, ll), fill(high_a, high_b, hh, hl)
    mine, below, above = e_own[0:1, 0:1], e_low[0:1, 0:1], e_high[0:1, 0:1]
    t_low = mm(o, l, ROWS) / (mine + below - pairs[...])
    t_high = mm(o, h, ROWS) / (mine + above - pairs[...])
    s_low, s_high = spin(t_low), spin(t_high)
    total[...] = mm(s_low, l, PLAIN) + mm(s_high, h, PLAIN)
    out = pltpu.make_async_copy(total, near, sem)
    out.start()
    t = mm(l, h, ROWS) / (below + above - pairs[...])
    dens[...] = (
        mm(split(t), spin(t), ROWS)
        + mm(split(t_low), s_low, ROWS)
        + mm(split(t_high), s_high, ROWS)
    )
    odd = upper[...] > 0.5
    for at in range(16):
        first = dens[at * 16 : at * 16 + 8, :]
        second = dens[at * 16 + 8 : at * 16 + 16, :]
        keep[at] = jnp.where(odd, second, first)
        send[at] = jnp.where(odd, first, second)
    out.wait()


def far_kernel(e_own, e_far, pairs, oh, ol, far_a, far_b, near, grad, *scratch):
    fh, fl, before, total, sem_in, sem_out = scratch
    fetch = pltpu.make_async_copy(near, before, sem_in)
    fetch.start()
    f = fill(far_a, far_b, fh, fl)
    energy = e_own[0:1, 0:1] + e_far[0:1, 0:1]
    s = spin(mm((oh[...], ol[...]), f, ROWS) / (energy - pairs[...]))
    fetch.wait()
    blocks = 4
    width = total.shape[1] // blocks
    outs = []
    for at in range(blocks):
        cols = slice(at * width, (at + 1) * width)
        total[:, cols] = before[:, cols] + mm(s, (f[0][:, cols], f[1][:, cols]), PLAIN)
        outs.append(
            pltpu.make_async_copy(
                total.at[:, cols], grad.at[:, cols], sem_out.at[at]
            )
        )
        outs[-1].start()
    for out in outs:
        out.wait()


def fold_kernel(pieces, copies):
    total = pieces[0]
    for at in range(1, pieces.shape[0]):
        total = total + pieces[at]
    total = total * (1.0 / 256.0)
    for at in range(copies.shape[0]):
        copies[at] = total


def call(kernel, out, scratch, limit, flops, args, in_specs, out_specs):
    return pl.pallas_call(
        kernel,
        out_shape=tuple(
            pltpu.HBM(s, F32)
            if spec is HBM
            else jax.ShapeDtypeStruct(s, BF16 if s == (256, 1024) else F32)
            for s, spec in zip(out, out_specs)
        ),
        in_specs=in_specs,
        out_specs=out_specs,
        scratch_shapes=scratch,
        cost_estimate=pl.CostEstimate(
            flops=flops, bytes_accessed=MIB, transcendentals=0
        ),
        compiler_params=pltpu.CompilerParams(vmem_limit_bytes=limit * MIB),
    )(*args)


def in_hbm(x):
    return pltpu.with_memory_space_constraint(x, pltpu.HBM)


def body(slabs, eps_occ, eps_vir):
    own = slabs[0]
    v, n = own.shape
    mid = v // 2
    own_a, own_b = own[:mid], own[mid:]
    low_a = shift(own_a, 1)
    high_b = shift(own_b, -1)
    tile = (8, 128)
    e_low = shift(eps_occ, 1)
    e_high = shift(eps_occ, -1)
    e_far = shift(eps_occ, 2)
    s_low, s_high, s_far, s_own = (
        jnp.broadcast_to(e, tile) for e in (e_low, e_high, e_far, eps_occ)
    )
    slabs = (low_a, shift(own_b, 1), shift(own_a, -1), high_b)
    far_a = shift(low_a, 1)
    far_b = shift(high_b, -1)
    upper = jnp.broadcast_to(lax.axis_index("core").astype(F32), (8, v))
    pairs, oh, ol = call(
        prepare_kernel,
        ((v, v), (v, n), (v, n)),
        [],
        8,
        1 << 20,
        (eps_vir[None], own),
        [VMEM] * 2,
        (VMEM,) * 3,
    )
    piece = (16, 8, v)
    wide, full = pltpu.VMEM((v, n), BF16), pltpu.VMEM((v, n), F32)
    keep, send, near = call(
        density_kernel,
        (piece, piece, (v, n)),
        [wide] * 4 + [pltpu.VMEM((v, v), F32), full, pltpu.SemaphoreType.DMA],
        14,
        1 << 31,
        (upper, s_own, s_low, s_high, pairs, oh, ol, *slabs),
        [VMEM] * 11,
        (VMEM, VMEM, HBM),
    )
    other = lax.ppermute(send, "core", [(0, 1), (1, 0)])
    parts = lax.all_to_all(
        keep + other, ("x", "far"), split_axis=0, concat_axis=0, tiled=True
    )
    (copies,) = call(fold_kernel, (piece,), [], 4, 1 << 20, (parts,), [VMEM], (VMEM,))
    copies = lax.all_to_all(
        copies, ("y", "near", "core"), split_axis=0, concat_axis=0, tiled=True
    )
    density = jnp.sum(copies.reshape(8, 16, v), axis=0)

    (grad,) = call(
        far_kernel,
        ((v, n),),
        [wide] * 2
        + [full] * 2
        + [pltpu.SemaphoreType.DMA, pltpu.SemaphoreType.DMA((4,))],
        12,
        1 << 31,
        (s_own, s_far, pairs, oh, ol, far_a, far_b, in_hbm(near)),
        [VMEM] * 7 + [HBM],
        (HBM,),
    )
    return grad[None], density


def solution(mesh):
    fine = Mesh(mesh.devices.reshape(FINE_SHAPE), FINE)
    placed = (P(FINE, None, None), P(FINE), P())
    return jax.shard_map(
        body,
        mesh=fine,
        in_specs=placed,
        out_specs=(P(FINE, None, None), P(("x", "far"), None)),
        check_vma=False,
    )
```

time: 114 us -> 111 us (0.974)
  the two profiles are of different devices: /device:TPU:2 before, /device:TPU:1 now
where the time goes in v9:
time: 111 us
  starting transfers between devices  43.8 us (39%)
  waiting for transfers between devices  30.3 us (27%)
  blocking collectives  19.1 us (17%)
  Pallas kernels  10.7 us (10%)
  local copies, waits for them, and re-layouts  4.86 us (4%)
  between operations  1.43 us (1%)
    ppermute x9, starting transfers between devices, shift(): lax.ppermute(value, 'far', [(i, (i + step) % size) for i in range(size)])  33.1 us
    ppermute x9, waiting for transfers between devices, shift(): lax.ppermute(value, 'far', [(i, (i + step) % size) for i in range(size)])  29.3 us
    all_to_all x1, blocking collectives, body(): lax.all_to_all(keep + other, ('x', 'far'), split_axis=0, concat_axis=0, t...  19.1 us
    pallas_call x4, Pallas kernels, call(): pl.pallas_call(kernel, out_shape=tuple((pltpu.HBM(s, F32) if spec is HBM...  10.7 us
    all_to_all x1, starting transfers between devices, body(): lax.all_to_all(copies, ('y', 'near', 'core'), split_axis=0, concat_axis=0...  7.43 us
    ppermute x1, starting transfers between devices, body(): other = lax.ppermute(send, 'core', [(0, 1), (1, 0)])  3.21 us
    slice x1, local copies, waits for them, and re-layouts, body(): own_a, own_b = (own[:mid], own[mid:])  2.36 us
  transfers between devices with their start and end apart: 11, of which 3 were waited for; matrix products, arithmetic and copies ran while one was open for 2% of the time, Pallas kernels for 10%

profile of v9, /device:TPU:1, one launch (start us, length us, event | category | flops | bytes accessed | tf_op | source)
XLA Modules:
  0.0 110.8 jit_solution(14238529987209673795)
XLA Ops:
  0.6 2.4 %slice_bitcast_fusion = (f32[128,1024]{1,0:T(8,128)}, f32[128,1024]{1,0:T(8,128)}) fusion(f32[1,256,1024]{2,1,0:T(8,128)} %param.3), kind=kLoop, calls=%fused_computation | loop fusion | bytes 2097152 | tf_op jit(solution)/shard_map/slice | solution.py:141
  3.0 3.8 %collective-permute-start.1 = (f32[128,1024]{1,0:T(8,128)}, f32[128,1024]{1,0:T(8,128)S(1)}, u32[]{:S(2)}, u32[]{:S(2)}) collective-permute-start(f32[128,1024]{1,0:T(8,128)} %get-tuple-element.15), channel_id=1, source_target_pairs={{0,1},{1,2},{2,3},{3,0},{4,5},{5,6},{6,7},{7,4},{8,9},{9,10},{10,1... | collective-permute-start | bytes 1572872 | tf_op jit(solution)/shard_map/ppermute | solution.py:22
  6.8 3.0 %collective-permute-start.3 = (f32[128,1024]{1,0:T(8,128)}, f32[128,1024]{1,0:T(8,128)S(1)}, u32[]{:S(2)}, u32[]{:S(2)}) collective-permute-start(f32[128,1024]{1,0:T(8,128)} %get-tuple-element.14), channel_id=1, source_target_pairs={{0,3},{1,0},{2,1},{3,2},{4,7},{5,4},{6,5},{7,6},{8,11},{9,8},{10,9... | collective-permute-start | bytes 1572872 | tf_op jit(solution)/shard_map/ppermute | solution.py:22
  9.8 1.2 %collective-permute-start.7 = (f32[128,1024]{1,0:T(8,128)}, f32[128,1024]{1,0:T(8,128)}, u32[]{:S(2)}, u32[]{:S(2)}) collective-permute-start(f32[128,1024]{1,0:T(8,128)} %get-tuple-element.14), channel_id=1, source_target_pairs={{0,1},{1,2},{2,3},{3,0},{4,5},{5,6},{6,7},{7,4},{8,9},{9,10},{10,1... | collective-permute-start | bytes 1572872 | tf_op jit(solution)/shard_map/ppermute | solution.py:22
  11.0 2.4 %collective-permute-start.8 = (f32[128,1024]{1,0:T(8,128)}, f32[128,1024]{1,0:T(8,128)}, u32[]{:S(2)}, u32[]{:S(2)}) collective-permute-start(f32[128,1024]{1,0:T(8,128)} %get-tuple-element.15), channel_id=1, source_target_pairs={{0,3},{1,0},{2,1},{3,2},{4,7},{5,4},{6,5},{7,6},{8,11},{9,8},{10,9... | collective-permute-start | bytes 1572872 | tf_op jit(solution)/shard_map/ppermute | solution.py:22
  13.4 1.2 %collective-permute-start.5 = (f32[1]{0:T(128)}, f32[1]{0:T(128)}, u32[]{:S(2)}, u32[]{:S(2)}) collective-permute-start(f32[1]{0:T(128)} %param.4), channel_id=1, source_target_pairs={{0,1},{1,2},{2,3},{3,0},{4,5},{5,6},{6,7},{7,4},{8,9},{9,10},{10,1... | collective-permute-start | bytes 20 | tf_op jit(solution)/shard_map/ppermute | solution.py:22
  15.3 0.0 copy-start.1
  15.3 0.7 copy-done.1
  16.0 0.3 shard_map.53
  16.3 25.3 %collective-permute-done.5 = f32[1]{0:T(128)} collective-permute-done((f32[1]{0:T(128)}, f32[1]{0:T(128)}, u32[]{:S(2)}, u32[]{:S(2)}) %collective-permute-start.5) | collective-permute-done | bytes 36 | tf_op jit(solution)/shard_map/ppermute | solution.py:22
  41.6 2.1 %collective-permute-start.6 = (f32[1]{0:T(128)}, f32[1]{0:T(128)}, u32[]{:S(2)}, u32[]{:S(2)}) collective-permute-start(f32[1]{0:T(128)} %param.4), channel_id=1, source_target_pairs={{0,3},{1,0},{2,1},{3,2},{4,7},{5,4},{6,5},{7,6},{8,11},{9,8},{10,9... | collective-permute-start | bytes 20 | tf_op jit(solution)/shard_map/ppermute | solution.py:22
  43.7 0.0 collective-permute-done.1.refs_0_
  43.7 12.5 %collective-permute-start.2 = (f32[128,1024]{1,0:T(8,128)S(1)}, f32[128,1024]{1,0:T(8,128)S(1)}, u32[]{:S(2)}, u32[]{:S(2)}) collective-permute-start(f32[128,1024]{1,0:T(8,128)S(1)} %collective-permute-done.1.refs_0_), channel_id=1, source_target_pairs={{0,1},{1,2},{2,3},{3,0},{4,5},{5,6},{6,7},{7,4},{8,9},{9,10},{10,1... | collective-permute-start | bytes 1572872 | tf_op jit(solution)/shard_map/ppermute | solution.py:22
  56.1 0.0 collective-permute-done.3.refs_3_
  56.1 4.4 %collective-permute-start.4 = (f32[128,1024]{1,0:T(8,128)S(1)}, f32[128,1024]{1,0:T(8,128)}, u32[]{:S(2)}, u32[]{:S(2)}) collective-permute-start(f32[128,1024]{1,0:T(8,128)S(1)} %collective-permute-done.3.refs_3_), channel_id=1, source_target_pairs={{0,3},{1,0},{2,1},{3,2},{4,7},{5,4},{6,5},{7,6},{8,11},{9,8},{10,9... | collective-permute-start | bytes 1572872 | tf_op jit(solution)/shard_map/ppermute | solution.py:22
  60.5 0.0 collective-permute-done.6
  60.6 0.0 collective-permute-done.7.refs_1_
  60.6 0.0 collective-permute-done.8.refs_2_
  60.6 0.5 broadcast_in_dim.33.e_low
  61.1 0.6 broadcast_in_dim.34.e_high
  61.8 4.8 %shard_map.54 = (f32[16,8,256]{2,1,0:T(8,128)S(1)}, f32[16,8,256]{2,1,0:T(8,128)S(1)}, f32[256,1024]{1,0:T(8,128)}) custom-call(f32[8,256]{1,0:T(8,128)S(1)} %broadcast_in_dim.32.upper, f32[8,128]{1,0:T(8,128)S(1)} %broadcast_in_dim.14.e_own, f32[8,128]{1,0:T(8,128)S(1)} %broadcast_in_dim.33.e_low, f32[8,128]{1,0:T(8,128)S(1)} %broadcast_in_dim.34.e_high, ...), custom_call_target="tpu_custom_call" | custom-call | flops 2147483648 | bytes 1048576 | tf_op jit(solution)/shard_map/pallas_call | solution.py:115
  66.6 3.2 %collective-permute-start.9 = (f32[16,8,256]{2,1,0:T(8,128)S(1)}, f32[16,8,256]{2,1,0:T(8,128)S(1)}, u32[]{:S(2)}, u32[]{:S(2)}) collective-permute-start(f32[16,8,256]{2,1,0:T(8,128)S(1)} %get-tuple-element.13), channel_id=1, source_target_pairs={{0,16},{16,0},{1,17},{17,1},{2,18},{18,2},{3,19},{19,3},{4,20},{20... | collective-permute-start | bytes 393224 | tf_op jit(solution)/shard_map/ppermute | solution.py:177
  69.8 1.0 collective-permute-done.9
  70.8 19.1 %all_to_all.10.pieces = f32[16,8,256]{2,1,0:T(8,128)S(1)} all-to-all(f32[16,8,256]{2,1,0:T(8,128)S(1)} %add.3), channel_id=1, replica_groups=mesh['y'=4,'near'=2,'core'=2,'x'=4,'far'=4] {'x','far'}, dimensions={0} | all-to-all | bytes 262144 | tf_op jit(solution)/shard_map/all_to_all | solution.py:178
  89.9 0.7 shard_map.56
  90.6 7.4 %all-to-all-start.1 = ((f32[16,8,256]{2,1,0:T(8,128)}), f32[16,8,256]{2,1,0:T(8,128)S(1)}, u32[]{:S(2)}, u32[]{:S(2)}) async-start(f32[16,8,256]{2,1,0:T(8,128)} %shard_map.56), calls=%async_computation.1 | async-start | bytes 262144 | tf_op jit(solution)/shard_map/all_to_all | solution.py:182
  98.0 2.6 %collective-permute-start = (f32[1]{0:T(128)}, f32[1]{0:T(128)}, u32[]{:S(2)}, u32[]{:S(2)}) collective-permute-start(f32[1]{0:T(128)} %param.4), channel_id=1, source_target_pairs={{0,2},{1,3},{2,0},{3,1},{4,6},{5,7},{6,4},{7,5},{8,10},{9,11},{10,... | collective-permute-start | bytes 20 | tf_op jit(solution)/shard_map/ppermute | solution.py:22
  100.6 3.9 %collective-permute-done = f32[1]{0:T(128)} collective-permute-done((f32[1]{0:T(128)}, f32[1]{0:T(128)}, u32[]{:S(2)}, u32[]{:S(2)}) %collective-permute-start) | collective-permute-done | bytes 36 | tf_op jit(solution)/shard_map/ppermute | solution.py:22
  104.6 0.6 broadcast_in_dim.30.e_far
  105.2 5.0 %shard_map.55 = f32[256,1024]{1,0:T(8,128)} custom-call(f32[8,128]{1,0:T(8,128)S(1)} %broadcast_in_dim.14.e_own, f32[8,128]{1,0:T(8,128)S(1)} %broadcast_in_dim.30.e_far, f32[256,256]{1,0:T(8,128)S(1)} %get-tuple-element.8.pairs, bf16[256,1024]{1,0:T(8,128)(2,1)S(1)} %get-tuple-element.9.oh, bf16[256,1024]{1,0:T(8,128)(2,1)S(1)} %get-tuple-element.10.ol, ...), custom_call_target="tpu_custom_call" | custom-call | flops 2147483648 | bytes 1048576 | tf_op jit(solution)/shard_map/pallas_call | solution.py:115
  110.2 0.0 all-to-all-done.1
  110.2 0.6 bitcast_reduce_fusion
  (7 shorter events, 0.0 us)
Async XLA Ops:
  0.6 14.7 %copy-start = (f32[1,256,1024]{2,1,0:T(8,128)S(1)}, f32[1,256,1024]{2,1,0:T(8,128)}, u32[]{:S(2)}) copy-start(f32[1,256,1024]{2,1,0:T(8,128)} %param.3) | copy-start | bytes 3145732
  3.0 40.7 %collective-permute-start.1 = (f32[128,1024]{1,0:T(8,128)}, f32[128,1024]{1,0:T(8,128)S(1)}, u32[]{:S(2)}, u32[]{:S(2)}) collective-permute-start(f32[128,1024]{1,0:T(8,128)} %get-tuple-element.15), channel_id=1, source_target_pairs={{0,1},{1,2},{2,3},{3,0},{4,5},{5,6},{6,7},{7,4},{8,9},{9,10},{10,1... | collective-permute-start | bytes 1572872 | tf_op jit(solution)/shard_map/ppermute | solution.py:22
  6.8 49.3 %collective-permute-start.3 = (f32[128,1024]{1,0:T(8,128)}, f32[128,1024]{1,0:T(8,128)S(1)}, u32[]{:S(2)}, u32[]{:S(2)}) collective-permute-start(f32[128,1024]{1,0:T(8,128)} %get-tuple-element.14), channel_id=1, source_target_pairs={{0,3},{1,0},{2,1},{3,2},{4,7},{5,4},{6,5},{7,6},{8,11},{9,8},{10,9... | collective-permute-start | bytes 1572872 | tf_op jit(solution)/shard_map/ppermute | solution.py:22
  9.8 50.7 %collective-permute-start.7 = (f32[128,1024]{1,0:T(8,128)}, f32[128,1024]{1,0:T(8,128)}, u32[]{:S(2)}, u32[]{:S(2)}) collective-permute-start(f32[128,1024]{1,0:T(8,128)} %get-tuple-element.14), channel_id=1, source_target_pairs={{0,1},{1,2},{2,3},{3,0},{4,5},{5,6},{6,7},{7,4},{8,9},{9,10},{10,1... | collective-permute-start | bytes 1572872 | tf_op jit(solution)/shard_map/ppermute | solution.py:22
  11.0 49.5 %collective-permute-start.8 = (f32[128,1024]{1,0:T(8,128)}, f32[128,1024]{1,0:T(8,128)}, u32[]{:S(2)}, u32[]{:S(2)}) collective-permute-start(f32[128,1024]{1,0:T(8,128)} %get-tuple-element.15), channel_id=1, source_target_pairs={{0,3},{1,0},{2,1},{3,2},{4,7},{5,4},{6,5},{7,6},{8,11},{9,8},{10,9... | collective-permute-start | bytes 1572872 | tf_op jit(solution)/shard_map/ppermute | solution.py:22
  13.4 28.2 %collective-permute-start.5 = (f32[1]{0:T(128)}, f32[1]{0:T(128)}, u32[]{:S(2)}, u32[]{:S(2)}) collective-permute-start(f32[1]{0:T(128)} %param.4), channel_id=1, source_target_pairs={{0,1},{1,2},{2,3},{3,0},{4,5},{5,6},{6,7},{7,4},{8,9},{9,10},{10,1... | collective-permute-start | bytes 20 | tf_op jit(solution)/shard_map/ppermute | solution.py:22
  15.3 0.7 copy-start.1
  41.6 18.9 %collective-permute-start.6 = (f32[1]{0:T(128)}, f32[1]{0:T(128)}, u32[]{:S(2)}, u32[]{:S(2)}) collective-permute-start(f32[1]{0:T(128)} %param.4), channel_id=1, source_target_pairs={{0,3},{1,0},{2,1},{3,2},{4,7},{5,4},{6,5},{7,6},{8,11},{9,8},{10,9... | collective-permute-start | bytes 20 | tf_op jit(solution)/shard_map/ppermute | solution.py:22
  43.7 60.9 %collective-permute-start.2 = (f32[128,1024]{1,0:T(8,128)S(1)}, f32[128,1024]{1,0:T(8,128)S(1)}, u32[]{:S(2)}, u32[]{:S(2)}) collective-permute-start(f32[128,1024]{1,0:T(8,128)S(1)} %collective-permute-done.1.refs_0_), channel_id=1, source_target_pairs={{0,1},{1,2},{2,3},{3,0},{4,5},{5,6},{6,7},{7,4},{8,9},{9,10},{10,1... | collective-permute-start | bytes 1572872 | tf_op jit(solution)/shard_map/ppermute | solution.py:22
  56.1 48.4 %collective-permute-start.4 = (f32[128,1024]{1,0:T(8,128)S(1)}, f32[128,1024]{1,0:T(8,128)}, u32[]{:S(2)}, u32[]{:S(2)}) collective-permute-start(f32[128,1024]{1,0:T(8,128)S(1)} %collective-permute-done.3.refs_3_), channel_id=1, source_target_pairs={{0,3},{1,0},{2,1},{3,2},{4,7},{5,4},{6,5},{7,6},{8,11},{9,8},{10,9... | collective-permute-start | bytes 1572872 | tf_op jit(solution)/shard_map/ppermute | solution.py:22
  66.6 4.2 %collective-permute-start.9 = (f32[16,8,256]{2,1,0:T(8,128)S(1)}, f32[16,8,256]{2,1,0:T(8,128)S(1)}, u32[]{:S(2)}, u32[]{:S(2)}) collective-permute-start(f32[16,8,256]{2,1,0:T(8,128)S(1)} %get-tuple-element.13), channel_id=1, source_target_pairs={{0,16},{16,0},{1,17},{17,1},{2,18},{18,2},{3,19},{19,3},{4,20},{20... | collective-permute-start | bytes 393224 | tf_op jit(solution)/shard_map/ppermute | solution.py:177
  90.6 19.6 %all-to-all-start.1 = ((f32[16,8,256]{2,1,0:T(8,128)}), f32[16,8,256]{2,1,0:T(8,128)S(1)}, u32[]{:S(2)}, u32[]{:S(2)}) async-start(f32[16,8,256]{2,1,0:T(8,128)} %shard_map.56), calls=%async_computation.1 | async-start | bytes 262144 | tf_op jit(solution)/shard_map/all_to_all | solution.py:182
  98.0 6.6 %collective-permute-start = (f32[1]{0:T(128)}, f32[1]{0:T(128)}, u32[]{:S(2)}, u32[]{:S(2)}) collective-permute-start(f32[1]{0:T(128)} %param.4), channel_id=1, source_target_pairs={{0,2},{1,3},{2,0},{3,1},{4,6},{5,7},{6,4},{7,5},{8,10},{9,11},{10,... | collective-permute-start | bytes 20 | tf_op jit(solution)/shard_map/ppermute | solution.py:22

commit v10 on v6

v10 whole, which is shorter than its diff:
```python
import jax
import jax.numpy as jnp
from jax import lax
from jax.experimental import pallas as pl
from jax.experimental.pallas import tpu as pltpu
from jax.sharding import Mesh, PartitionSpec as P


FINE = ("y", "near", "core", "x", "far")
FINE_SHAPE = (4, 2, 2, 4, 4)
VMEM = pl.BlockSpec(memory_space=pltpu.VMEM)
SMEM = pl.BlockSpec(memory_space=pltpu.SMEM)
HBM = pl.BlockSpec(memory_space=pltpu.HBM)
F32, BF16 = jnp.float32, jnp.bfloat16
ROWS = ((1,), (1,))
PLAIN = ((1,), (0,))
MIB = 1 << 20


def role_shift(value, step):
    size = lax.axis_size("far")
    pairs = []
    for core, way in ((0, step), (1, -step)):
        base = core * size
        pairs += [(base + i, base + (i + way) % size) for i in range(size)]
    return lax.ppermute(value, ("core", "far"), pairs)


def split(x):
    high = x.astype(BF16)
    return high, (x - high.astype(F32)).astype(BF16)


def mm(a, b, contract):
    def dot(p, q):
        return lax.dot_general(p, q, (contract, ((), ())), preferred_element_type=F32)

    return dot(a[0], b[0]) + (dot(a[0], b[1]) + dot(a[1], b[0]))


def prepare_kernel(eps_vir, own, pairs, high, low):
    row = jnp.broadcast_to(eps_vir[...], pairs.shape)
    pairs[...] = row + row.T
    high[...], low[...] = split(own[...])


def spin(t):
    return split(2.0 * t - t.T)


def pair_kernel(upper, e_own, e_one, e_two, pairs, oh, ol, one, two, *refs):
    keep, send, gift, near, buf, total, dens, sems = refs
    o, a, b = (oh[...], ol[...]), split(one[...]), split(two[...])
    mine, first, second = e_own[0:1, 0:1], e_one[0:1, 0:1], e_two[0:1, 0:1]
    t = mm(b, a, ROWS) / (first + second - pairs[...])
    s = spin(t)
    buf[...] = mm(s, a, PLAIN)
    out = [pltpu.make_async_copy(buf, gift, sems.at[0])]
    out[0].start()
    t_one = mm(o, a, ROWS) / (mine + first - pairs[...])
    t_two = mm(o, b, ROWS) / (mine + second - pairs[...])
    s_one, s_two = spin(t_one), spin(t_two)
    total[...] = mm(s_one, a, PLAIN) + mm(s_two, b, PLAIN)
    out.append(pltpu.make_async_copy(total, near, sems.at[1]))
    out[1].start()
    dens[...] = (
        mm(split(t), s, ROWS)
        + mm(split(t_one), s_one, ROWS)
        + mm(split(t_two), s_two, ROWS)
    )
    odd = upper[...] > 0.5
    for at in range(16):
        low = dens[at * 16 : at * 16 + 8, :]
        high = dens[at * 16 + 8 : at * 16 + 16, :]
        keep[at] = jnp.where(odd, high, low)
        send[at] = jnp.where(odd, low, high)
    for copy in out:
        copy.wait()


def join_kernel(keep, other, copies):
    for at in range(copies.shape[1]):
        piece = keep[at] + other[at]
        for copy in range(copies.shape[0]):
            copies[copy, at] = piece


def sum_kernel(near, gift, grad, mine, other, sems):
    parts = 4
    step = mine.shape[0] // parts
    copies = []
    for at in range(parts):
        rows = pl.ds(at * step, step)
        copies.append(
            (
                pltpu.make_async_copy(near.at[rows, :], mine.at[rows, :], sems.at[0, at]),
                pltpu.make_async_copy(gift.at[rows, :], other.at[rows, :], sems.at[1, at]),
                pltpu.make_async_copy(mine.at[rows, :], grad.at[rows, :], sems.at[2, at]),
            )
        )
        copies[-1][0].start()
        copies[-1][1].start()
    for at in range(parts):
        rows = slice(at * step, (at + 1) * step)
        copies[at][0].wait()
        copies[at][1].wait()
        mine[rows, :] = mine[rows, :] + other[rows, :]
        copies[at][2].start()
    for at in range(parts):
        copies[at][2].wait()


def fold_kernel(pieces, copies):
    total = pieces[0]
    for at in range(1, pieces.shape[0]):
        total = total + pieces[at]
    total = total * (1.0 / 256.0)
    for at in range(copies.shape[0]):
        row = at // 2 % 4 * 8
        copies[at] = total[row : row + 8, :]


def call(kernel, out, scratch, limit, flops, args, in_specs, out_specs):
    return pl.pallas_call(
        kernel,
        out_shape=tuple(
            pltpu.HBM(s, F32)
            if spec is HBM
            else jax.ShapeDtypeStruct(s, BF16 if s == (256, 1024) else F32)
            for s, spec in zip(out, out_specs)
        ),
        in_specs=in_specs,
        out_specs=out_specs,
        scratch_shapes=scratch,
        cost_estimate=pl.CostEstimate(
            flops=flops, bytes_accessed=MIB, transcendentals=0
        ),
        compiler_params=pltpu.CompilerParams(vmem_limit_bytes=limit * MIB),
    )(*args)


def in_hbm(x):
    return pltpu.with_memory_space_constraint(x, pltpu.HBM)


def body(slabs, eps_occ, eps_vir):
    own = slabs[0]
    v, n = own.shape
    one = role_shift(own, 1)
    two = role_shift(own, -1)
    e_one = role_shift(eps_occ, 1)
    e_two = role_shift(eps_occ, -1)
    tile = (8, 128)
    s_one, s_two, s_own = (jnp.broadcast_to(e, tile) for e in (e_one, e_two, eps_occ))
    upper = jnp.broadcast_to(lax.axis_index("core").astype(F32), (8, v))
    pairs, oh, ol = call(
        prepare_kernel,
        ((v, v), (v, n), (v, n)),
        [],
        8,
        1 << 20,
        (eps_vir[None], own),
        [VMEM] * 2,
        (VMEM,) * 3,
    )
    piece = (16, 8, v)
    full = pltpu.VMEM((v, n), F32)
    keep, send, gift, near = call(
        pair_kernel,
        (piece, piece, (v, n), (v, n)),
        [full] * 2 + [pltpu.VMEM((v, v), F32), pltpu.SemaphoreType.DMA((2,))],
        14,
        1 << 31,
        (upper, s_own, s_one, s_two, pairs, oh, ol, one, two),
        [VMEM] * 9,
        (VMEM, VMEM, HBM, HBM),
    )
    other = lax.ppermute(send, "core", [(0, 1), (1, 0)])
    gift = role_shift(gift, 1)
    (mine,) = call(
        join_kernel, ((4,) + piece,), [], 4, 1 << 20, (keep, other), [VMEM] * 2, (VMEM,)
    )
    parts = lax.all_to_all(
        mine.reshape(16, 32, v), ("y", "x"), split_axis=0, concat_axis=0, tiled=True
    )
    (copies,) = call(fold_kernel, (piece,), [], 4, 1 << 20, (parts,), [VMEM], (VMEM,))
    copies = lax.all_to_all(
        copies, ("near", "far", "core"), split_axis=0, concat_axis=0, tiled=True
    )
    density = jnp.sum(copies.reshape(8, 16, v), axis=0)
    (grad,) = call(
        sum_kernel,
        ((v, n),),
        [full] * 2 + [pltpu.SemaphoreType.DMA((3, 4))],
        8,
        1 << 20,
        (in_hbm(near), gift),
        [HBM] * 2,
        (HBM,),
    )
    return grad[None], density


def solution(mesh):
    fine = Mesh(mesh.devices.reshape(FINE_SHAPE), FINE)
    placed = (P(FINE, None, None), P(FINE), P())
    return jax.shard_map(
        body,
        mesh=fine,
        in_specs=placed,
        out_specs=(P(FINE, None, None), P(("x", "far"), None)),
        check_vma=False,
    )
```

time: 114 us -> 99.9 us (0.88)
  starting transfers between devices: 21.3 us -> 13.1 us
  Pallas kernels: 11.9 us -> 6.96 us
  blocking collectives: 30.9 us -> 34.1 us
  between operations: 4.04 us -> 1.38 us
    all_to_all x1 -> x0, starting transfers between devices: 6.3 us -> none  [body(): lax.all_to_all(copies, ('y', 'near', 'core'), split_axis=0, concat_axis=0...]
    pallas_call x6 -> x5, Pallas kernels: 11.9 us -> 6.96 us  [call(): pl.pallas_call(kernel, out_shape=tuple((pltpu.HBM(s, F32) if spec is HBM...]
    all_to_all x1 -> x2, blocking collectives: 30.9 us -> 34.1 us  [the longest x1 19 us: body(): lax.all_to_all(mine.reshape(16, 32, v), ('y', 'x'), split_axis=0, concat_...]
    unnamed x20 -> x4, local copies, waits for them, and re-layouts: 4 us -> 1.9 us
    ppermute x6 -> x5, waiting for transfers between devices: 40.5 us -> 39 us  [role_shift(): return lax.ppermute(value, ('core', 'far'), pairs)]
    ppermute x1, waiting for transfers between devices: 0.01 us -> 1.35 us  [body(): other = lax.ppermute(send, 'core', [(0, 1), (1, 0)])]
    broadcast_in_dim x3, local copies, waits for them, and re-layouts: 0.02 us -> 1.24 us  [body(): jnp.broadcast_to(e, tile)]
    ppermute x6 -> x5, starting transfers between devices: 13.9 us -> 13.1 us  [role_shift(): return lax.ppermute(value, ('core', 'far'), pairs)]
  transfers between devices with their start and end apart: 8 -> 6, of which waited for: 2 -> 3; matrix products, arithmetic and copies ran while one was open for 0% -> 1% of each run, Pallas kernels for 5% -> 0%
where the time goes in v10:
time: 99.9 us; the launch traced here: 99.6 us
  waiting for transfers between devices  40.3 us (40%)
  blocking collectives  34.1 us (34%)
  starting transfers between devices  13.1 us (13%)
  Pallas kernels  6.96 us (7%)
  local copies, waits for them, and re-layouts  3.15 us (3%)
  between operations  1.38 us (1%)
    ppermute x5, waiting for transfers between devices, role_shift(): return lax.ppermute(value, ('core', 'far'), pairs)  39 us
    all_to_all x1, blocking collectives, body(): lax.all_to_all(mine.reshape(16, 32, v), ('y', 'x'), split_axis=0, concat_...  19 us
    all_to_all x1, blocking collectives, body(): lax.all_to_all(copies, ('near', 'far', 'core'), split_axis=0, concat_axis...  15.1 us
    ppermute x5, starting transfers between devices, role_shift(): return lax.ppermute(value, ('core', 'far'), pairs)  13.1 us
    pallas_call x5, Pallas kernels, call(): pl.pallas_call(kernel, out_shape=tuple((pltpu.HBM(s, F32) if spec is HBM...  6.96 us
  transfers between devices with their start and end apart: 6, of which 3 were waited for; matrix products, arithmetic and copies ran while one was open for 1% of the time, Pallas kernels for 0%

profile of v10, /device:TPU:1, one launch (start us, length us, event | category | flops | bytes accessed | tf_op | source)
XLA Modules:
  0.0 99.6 jit_solution(4661168363095203882)
XLA Ops:
  0.6 3.9 %collective-permute-start.3 = (f32[256,1024]{1,0:T(8,128)}, f32[256,1024]{1,0:T(8,128)S(1)}, u32[]{:S(2)}, u32[]{:S(2)}) collective-permute-start(f32[256,1024]{1,0:T(8,128)} %bitcast.12), channel_id=1, source_target_pairs={{0,3},{1,0},{2,1},{3,2},{16,17},{17,18},{18,19},{19,16},{4,7},{5,4... | collective-permute-start | bytes 3145736 | tf_op jit(solution)/shard_map/ppermute | solution.py:26
  4.5 3.1 %collective-permute-start.2 = (f32[256,1024]{1,0:T(8,128)}, f32[256,1024]{1,0:T(8,128)S(1)}, u32[]{:S(2)}, u32[]{:S(2)}) collective-permute-start(f32[256,1024]{1,0:T(8,128)} %bitcast.13), channel_id=1, source_target_pairs={{0,1},{1,2},{2,3},{3,0},{16,19},{17,16},{18,17},{19,18},{4,5},{5,6... | collective-permute-start | bytes 3145736 | tf_op jit(solution)/shard_map/ppermute | solution.py:26
  7.6 1.1 %collective-permute-start.1 = (f32[1]{0:T(128)}, f32[1]{0:T(128)}, u32[]{:S(2)}, u32[]{:S(2)}) collective-permute-start(f32[1]{0:T(128)} %param.4), channel_id=1, source_target_pairs={{0,3},{1,0},{2,1},{3,2},{16,17},{17,18},{18,19},{19,16},{4,7},{5,4... | collective-permute-start | bytes 20 | tf_op jit(solution)/shard_map/ppermute | solution.py:26
  8.7 2.5 %collective-permute-start = (f32[1]{0:T(128)}, f32[1]{0:T(128)}, u32[]{:S(2)}, u32[]{:S(2)}) collective-permute-start(f32[1]{0:T(128)} %param.4), channel_id=1, source_target_pairs={{0,1},{1,2},{2,3},{3,0},{16,19},{17,16},{18,17},{19,18},{4,5},{5,6... | collective-permute-start | bytes 20 | tf_op jit(solution)/shard_map/ppermute | solution.py:26
  11.9 0.0 copy-start.1
  11.9 0.7 copy-done.1
  12.6 0.0 copy-start
  12.6 1.2 %copy-done = f32[1,256,1024]{2,1,0:T(8,128)S(1)} copy-done((f32[1,256,1024]{2,1,0:T(8,128)S(1)}, f32[1,256,1024]{2,1,0:T(8,128)}, u32[]{:S(2)}) %copy-start) | copy-done | bytes 1048600
  13.8 0.3 shard_map.53
  14.1 20.9 %collective-permute-done.1 = f32[1]{0:T(128)} collective-permute-done((f32[1]{0:T(128)}, f32[1]{0:T(128)}, u32[]{:S(2)}, u32[]{:S(2)}) %collective-permute-start.1) | collective-permute-done | bytes 36 | tf_op jit(solution)/shard_map/ppermute | solution.py:26
  35.0 18.1 %collective-permute-done = f32[1]{0:T(128)} collective-permute-done((f32[1]{0:T(128)}, f32[1]{0:T(128)}, u32[]{:S(2)}, u32[]{:S(2)}) %collective-permute-start) | collective-permute-done | bytes 36 | tf_op jit(solution)/shard_map/ppermute | solution.py:26
  53.1 0.0 collective-permute-done.3.two
  53.1 0.0 collective-permute-done.2.one
  53.2 0.7 broadcast_in_dim.27.e_two
  53.8 0.6 broadcast_in_dim.26.e_one
  54.4 4.5 %shard_map.54 = (f32[16,8,256]{2,1,0:T(8,128)S(1)}, f32[16,8,256]{2,1,0:T(8,128)S(1)}, f32[256,1024]{1,0:T(8,128)}, f32[256,1024]{1,0:T(8,128)}) custom-call(f32[8,256]{1,0:T(8,128)S(1)} %broadcast_in_dim.24.upper, f32[8,128]{1,0:T(8,128)S(1)} %broadcast_in_dim.25.e_own, f32[8,128]{1,0:T(8,128)S(1)} %broadcast_in_dim.26.e_one, ...), custom_call_target="tpu_custom_call" | custom-call | flops 2147483648 | bytes 1048576 | tf_op jit(solution)/shard_map/pallas_call | solution.py:124
  58.9 2.5 %collective-permute-start.4 = (f32[256,1024]{1,0:T(8,128)}, f32[256,1024]{1,0:T(8,128)S(1)}, u32[]{:S(2)}, u32[]{:S(2)}) collective-permute-start(f32[256,1024]{1,0:T(8,128)} %get-tuple-element.13), channel_id=1, source_target_pairs={{0,1},{1,2},{2,3},{3,0},{16,19},{17,16},{18,17},{19,18},{4,5},{5,6... | collective-permute-start | bytes 3145736 | tf_op jit(solution)/shard_map/ppermute | solution.py:26
  61.4 0.0 collective-permute-start.5
  61.4 1.3 %collective-permute-done.5.other = f32[16,8,256]{2,1,0:T(8,128)S(1)} collective-permute-done((f32[16,8,256]{2,1,0:T(8,128)S(1)}, f32[16,8,256]{2,1,0:T(8,128)S(1)}, u32[]{:S(2)}, u32[]{:S(2)}) %collective-permute-start.5) | collective-permute-done | bytes 131104 | tf_op jit(solution)/shard_map/ppermute | solution.py:178
  62.8 19.0 %all_to_all.10.pieces = f32[16,32,256]{2,1,0:T(8,128)S(1)} all-to-all(f32[16,32,256]{2,1,0:T(8,128)S(1)} %bitcast.11), channel_id=1, replica_groups=mesh['y'=4,'near'=2,'core'=2,'x'=4,'far'=4] {'y','x'}, dimensions={0} | all-to-all | bytes 1048576 | tf_op jit(solution)/shard_map/all_to_all | solution.py:183
  81.9 15.1 %all_to_all.11 = f32[16,8,256]{2,1,0:T(8,128)S(1)} all-to-all(f32[16,8,256]{2,1,0:T(8,128)S(1)} %shard_map.57), channel_id=1, replica_groups=mesh['y'=4,'near'=2,'core'=2,'x'=4,'far'=4] {'near','far','core'}, dimensions={0} | all-to-all | bytes 262144 | tf_op jit(solution)/shard_map/all_to_all | solution.py:187
  96.9 0.6 bitcast_reduce_fusion
  97.5 0.0 collective-permute-done.4.gift
  97.5 2.0 %shard_map.55 = f32[256,1024]{1,0:T(8,128)} custom-call(f32[256,1024]{1,0:T(8,128)} %get-tuple-element.12.near, f32[256,1024]{1,0:T(8,128)S(1)} %collective-permute-done.4.gift), custom_call_target="tpu_custom_call" | custom-call | flops 1048576 | bytes 1048576 | tf_op jit(solution)/shard_map/pallas_call | solution.py:124
  (4 shorter events, 0.1 us)
Async XLA Ops:
  0.6 52.5 %collective-permute-start.3 = (f32[256,1024]{1,0:T(8,128)}, f32[256,1024]{1,0:T(8,128)S(1)}, u32[]{:S(2)}, u32[]{:S(2)}) collective-permute-start(f32[256,1024]{1,0:T(8,128)} %bitcast.12), channel_id=1, source_target_pairs={{0,3},{1,0},{2,1},{3,2},{16,17},{17,18},{18,19},{19,16},{4,7},{5,4... | collective-permute-start | bytes 3145736 | tf_op jit(solution)/shard_map/ppermute | solution.py:26
  4.5 48.6 %collective-permute-start.2 = (f32[256,1024]{1,0:T(8,128)}, f32[256,1024]{1,0:T(8,128)S(1)}, u32[]{:S(2)}, u32[]{:S(2)}) collective-permute-start(f32[256,1024]{1,0:T(8,128)} %bitcast.13), channel_id=1, source_target_pairs={{0,1},{1,2},{2,3},{3,0},{16,19},{17,16},{18,17},{19,18},{4,5},{5,6... | collective-permute-start | bytes 3145736 | tf_op jit(solution)/shard_map/ppermute | solution.py:26
  7.6 27.4 %collective-permute-start.1 = (f32[1]{0:T(128)}, f32[1]{0:T(128)}, u32[]{:S(2)}, u32[]{:S(2)}) collective-permute-start(f32[1]{0:T(128)} %param.4), channel_id=1, source_target_pairs={{0,3},{1,0},{2,1},{3,2},{16,17},{17,18},{18,19},{19,16},{4,7},{5,4... | collective-permute-start | bytes 20 | tf_op jit(solution)/shard_map/ppermute | solution.py:26
  8.7 44.4 %collective-permute-start = (f32[1]{0:T(128)}, f32[1]{0:T(128)}, u32[]{:S(2)}, u32[]{:S(2)}) collective-permute-start(f32[1]{0:T(128)} %param.4), channel_id=1, source_target_pairs={{0,1},{1,2},{2,3},{3,0},{16,19},{17,16},{18,17},{19,18},{4,5},{5,6... | collective-permute-start | bytes 20 | tf_op jit(solution)/shard_map/ppermute | solution.py:26
  11.9 0.7 copy-start.1
  12.6 1.2 %copy-start = (f32[1,256,1024]{2,1,0:T(8,128)S(1)}, f32[1,256,1024]{2,1,0:T(8,128)}, u32[]{:S(2)}) copy-start(f32[1,256,1024]{2,1,0:T(8,128)} %param.3) | copy-start | bytes 3145732
  58.9 38.6 %collective-permute-start.4 = (f32[256,1024]{1,0:T(8,128)}, f32[256,1024]{1,0:T(8,128)S(1)}, u32[]{:S(2)}, u32[]{:S(2)}) collective-permute-start(f32[256,1024]{1,0:T(8,128)} %get-tuple-element.13), channel_id=1, source_target_pairs={{0,1},{1,2},{2,3},{3,0},{16,19},{17,16},{18,17},{19,18},{4,5},{5,6... | collective-permute-start | bytes 3145736 | tf_op jit(solution)/shard_map/ppermute | solution.py:26
  61.4 1.3 %collective-permute-start.5 = (f32[16,8,256]{2,1,0:T(8,128)S(1)}, f32[16,8,256]{2,1,0:T(8,128)S(1)}, u32[]{:S(2)}, u32[]{:S(2)}) collective-permute-start(f32[16,8,256]{2,1,0:T(8,128)S(1)} %get-tuple-element.15), channel_id=1, source_target_pairs={{0,16},{16,0},{1,17},{17,1},{2,18},{18,2},{3,19},{19,3},{4,20},{20... | collective-permute-start | bytes 393224 | tf_op jit(solution)/shard_map/ppermute | solution.py:178

commit v11 on v10

--- a/solution.py
+++ b/solution.py
@@ -48,23 +48,31 @@
     return split(2.0 * t - t.T)
 
 
-def pair_kernel(upper, e_own, e_one, e_two, pairs, oh, ol, one, two, *refs):
-    keep, send, gift, near, buf, total, dens, sems = refs
-    o, a, b = (oh[...], ol[...]), split(one[...]), split(two[...])
+def gift_kernel(e_one, e_two, pairs, one, two, *refs):
+    gift, t_mid, ah, al, bh, bl, buf, sem = refs
+    ah[...], al[...] = a = split(one[...])
+    bh[...], bl[...] = b = split(two[...])
+    t = mm(b, a, ROWS) / (e_one[0:1, 0:1] + e_two[0:1, 0:1] - pairs[...])
+    buf[...] = mm(spin(t), a, PLAIN)
+    out = pltpu.make_async_copy(buf, gift, sem)
+    out.start()
+    t_mid[...] = t
+    out.wait()
+
+
+def density_kernel(upper, e_own, e_one, e_two, pairs, oh, ol, t_mid, *refs):
+    ah, al, bh, bl, keep, send, near, total, dens, sem = refs
+    o, a, b = (oh[...], ol[...]), (ah[...], al[...]), (bh[...], bl[...])
     mine, first, second = e_own[0:1, 0:1], e_one[0:1, 0:1], e_two[0:1, 0:1]
-    t = mm(b, a, ROWS) / (first + second - pairs[...])
-    s = spin(t)
-    buf[...] = mm(s, a, PLAIN)
-    out = [pltpu.make_async_copy(buf, gift, sems.at[0])]
-    out[0].start()
     t_one = mm(o, a, ROWS) / (mine + first - pairs[...])
     t_two = mm(o, b, ROWS) / (mine + second - pairs[...])
     s_one, s_two = spin(t_one), spin(t_two)
     total[...] = mm(s_one, a, PLAIN) + mm(s_two, b, PLAIN)
-    out.append(pltpu.make_async_copy(total, near, sems.at[1]))
-    out[1].start()
+    out = pltpu.make_async_copy(total, near, sem)
+    out.start()
+    t = t_mid[...]
     dens[...] = (
-        mm(split(t), s, ROWS)
+        mm(split(t), spin(t), ROWS)
         + mm(split(t_one), s_one, ROWS)
         + mm(split(t_two), s_two, ROWS)
     )
@@ -74,8 +82,7 @@
         high = dens[at * 16 + 8 : at * 16 + 16, :]
         keep[at] = jnp.where(odd, high, low)
         send[at] = jnp.where(odd, low, high)
-    for copy in out:
-        copy.wait()
+    out.wait()
 
 
 def join_kernel(keep, other, copies):
@@ -165,18 +172,28 @@
     )
     piece = (16, 8, v)
     full = pltpu.VMEM((v, n), F32)
-    keep, send, gift, near = call(
-        pair_kernel,
-        (piece, piece, (v, n), (v, n)),
-        [full] * 2 + [pltpu.VMEM((v, v), F32), pltpu.SemaphoreType.DMA((2,))],
-        14,
+    gift, t_mid, *splits = call(
+        gift_kernel,
+        ((v, n), (v, v)) + ((v, n),) * 4,
+        [full, pltpu.SemaphoreType.DMA],
+        12,
         1 << 31,
-        (upper, s_own, s_one, s_two, pairs, oh, ol, one, two),
-        [VMEM] * 9,
-        (VMEM, VMEM, HBM, HBM),
+        (s_one, s_two, pairs, one, two),
+        [VMEM] * 5,
+        (HBM,) + (VMEM,) * 5,
+    )
+    gift = role_shift(gift, 1)
+    keep, send, near = call(
+        density_kernel,
+        (piece, piece, (v, n)),
+        [full, pltpu.VMEM((v, v), F32), pltpu.SemaphoreType.DMA],
+        12,
+        1 << 31,
+        (upper, s_own, s_one, s_two, pairs, oh, ol, t_mid, *splits),
+        [VMEM] * 12,
+        (VMEM, VMEM, HBM),
     )
     other = lax.ppermute(send, "core", [(0, 1), (1, 0)])
-    gift = role_shift(gift, 1)
     (mine,) = call(
         join_kernel, ((4,) + piece,), [], 4, 1 << 20, (keep, other), [VMEM] * 2, (VMEM,)
     )

time: 99.9 us -> 102 us (1.021)
  starting transfers between devices: 13.1 us -> 17.8 us
  waiting for transfers between devices: 40.3 us -> 37.6 us
  blocking collectives: 34.1 us -> 32 us
  Pallas kernels: 6.96 us -> 8.59 us
    ppermute x5, starting transfers between devices: 13.1 us -> 17.7 us  [role_shift(): return lax.ppermute(value, ('core', 'far'), pairs)]
    ppermute x5, waiting for transfers between devices: 39 us -> 36.3 us  [role_shift(): return lax.ppermute(value, ('core', 'far'), pairs)]
    pallas_call x5 -> x6, Pallas kernels: 6.96 us -> 8.59 us  [call(): pl.pallas_call(kernel, out_shape=tuple((pltpu.HBM(s, F32) if spec is HBM...]
    all_to_all x1, blocking collectives: 19 us -> 17.5 us  [body(): lax.all_to_all(mine.reshape(16, 32, v), ('y', 'x'), split_axis=0, concat_...]
  transfers between devices with their start and end apart: 6 -> 6, of which waited for: 3 -> 2; matrix products, arithmetic and copies ran while one was open for 1% -> 1% of each run, Pallas kernels for 0% -> 4%
where the time goes in v11:
time: 102 us; the launch traced here: 101 us
  waiting for transfers between devices  37.6 us (37%)
  blocking collectives  32 us (31%)
  starting transfers between devices  17.8 us (17%)
  Pallas kernels  8.59 us (8%)
  local copies, waits for them, and re-layouts  3.21 us (3%)
  between operations  1.42 us (1%)
    ppermute x5, waiting for transfers between devices, role_shift(): return lax.ppermute(value, ('core', 'far'), pairs)  36.3 us
    ppermute x5, starting transfers between devices, role_shift(): return lax.ppermute(value, ('core', 'far'), pairs)  17.7 us
    all_to_all x1, blocking collectives, body(): lax.all_to_all(mine.reshape(16, 32, v), ('y', 'x'), split_axis=0, concat_...  17.5 us
    all_to_all x1, blocking collectives, body(): lax.all_to_all(copies, ('near', 'far', 'core'), split_axis=0, concat_axis...  14.5 us
    pallas_call x6, Pallas kernels, call(): pl.pallas_call(kernel, out_shape=tuple((pltpu.HBM(s, F32) if spec is HBM...  8.59 us
  transfers between devices with their start and end apart: 6, of which 2 were waited for; matrix products, arithmetic and copies ran while one was open for 1% of the time, Pallas kernels for 4%

profile of v11, /device:TPU:1, one launch (start us, length us, event | category | flops | bytes accessed | tf_op | source)
XLA Modules:
  0.0 101.3 jit_solution(17896257840836998965)
XLA Ops:
  0.6 6.9 %collective-permute-start.2 = (f32[256,1024]{1,0:T(8,128)}, f32[256,1024]{1,0:T(8,128)S(1)}, u32[]{:S(2)}, u32[]{:S(2)}) collective-permute-start(f32[256,1024]{1,0:T(8,128)} %bitcast.12), channel_id=1, source_target_pairs={{0,1},{1,2},{2,3},{3,0},{16,19},{17,16},{18,17},{19,18},{4,5},{5,6... | collective-permute-start | bytes 3145736 | tf_op jit(solution)/shard_map/ppermute | solution.py:26
  7.5 0.0 collective-permute-start.3
  7.5 3.6 %collective-permute-start = (f32[1]{0:T(128)}, f32[1]{0:T(128)}, u32[]{:S(2)}, u32[]{:S(2)}) collective-permute-start(f32[1]{0:T(128)} %param.4), channel_id=1, source_target_pairs={{0,1},{1,2},{2,3},{3,0},{16,19},{17,16},{18,17},{19,18},{4,5},{5,6... | collective-permute-start | bytes 20 | tf_op jit(solution)/shard_map/ppermute | solution.py:26
  11.1 0.0 collective-permute-start.1
  11.8 0.0 copy-start.1
  11.9 0.7 copy-done.1
  12.5 0.0 copy-start
  12.5 1.2 %copy-done = f32[1,256,1024]{2,1,0:T(8,128)S(1)} copy-done((f32[1,256,1024]{2,1,0:T(8,128)S(1)}, f32[1,256,1024]{2,1,0:T(8,128)}, u32[]{:S(2)}) %copy-start) | copy-done | bytes 1048600
  13.7 0.3 shard_map.53
  14.1 36.3 %collective-permute-done = f32[1]{0:T(128)} collective-permute-done((f32[1]{0:T(128)}, f32[1]{0:T(128)}, u32[]{:S(2)}, u32[]{:S(2)}) %collective-permute-start) | collective-permute-done | bytes 36 | tf_op jit(solution)/shard_map/ppermute | solution.py:26
  50.3 0.0 collective-permute-done.1
  50.3 0.0 collective-permute-done.2.one
  50.3 0.0 collective-permute-done.3.two
  50.3 0.7 broadcast_in_dim.26.e_one
  51.0 0.6 broadcast_in_dim.27.e_two
  51.7 3.0 %shard_map.54 = (f32[256,1024]{1,0:T(8,128)}, f32[256,256]{1,0:T(8,128)S(1)}, bf16[256,1024]{1,0:T(8,128)(2,1)S(1)}, bf16[256,1024]{1,0:T(8,128)(2,1)S(1)}, bf16...) custom-call(f32[8,128]{1,0:T(8,128)S(1)} %broadcast_in_dim.26.e_one, f32[8,128]{1,0:T(8,128)S(1)} %broadcast_in_dim.27.e_two, ...), custom_call_target="tpu_custom_call" | custom-call | flops 2147483648 | bytes 1048576 | tf_op jit(solution)/shard_map/pallas_call | solution.py:131
  54.7 7.2 %collective-permute-start.4 = (f32[256,1024]{1,0:T(8,128)}, f32[256,1024]{1,0:T(8,128)S(1)}, u32[]{:S(2)}, u32[]{:S(2)}) collective-permute-start(f32[256,1024]{1,0:T(8,128)} %get-tuple-element.23), channel_id=1, source_target_pairs={{0,1},{1,2},{2,3},{3,0},{16,19},{17,16},{18,17},{19,18},{4,5},{5,6... | collective-permute-start | bytes 3145736 | tf_op jit(solution)/shard_map/ppermute | solution.py:26
  61.9 3.2 %shard_map.55 = (f32[16,8,256]{2,1,0:T(8,128)S(1)}, f32[16,8,256]{2,1,0:T(8,128)S(1)}, f32[256,1024]{1,0:T(8,128)}) custom-call(f32[8,256]{1,0:T(8,128)S(1)} %broadcast_in_dim.24.upper, f32[8,128]{1,0:T(8,128)S(1)} %broadcast_in_dim.25.e_own, f32[8,128]{1,0:T(8,128)S(1)} %broadcast_in_dim.26.e_one, f32[8,128]{1,0:T(8,128)S(1)} %broadcast_in_dim.27.e_two, ...), custom_call_target="tpu_custom_call" | custom-call | flops 2147483648 | bytes 1048576 | tf_op jit(solution)/shard_map/pallas_call | solution.py:131
  65.1 0.1 collective-permute-start.5
  65.2 1.3 %collective-permute-done.5.other = f32[16,8,256]{2,1,0:T(8,128)S(1)} collective-permute-done((f32[16,8,256]{2,1,0:T(8,128)S(1)}, f32[16,8,256]{2,1,0:T(8,128)S(1)}, u32[]{:S(2)}, u32[]{:S(2)}) %collective-permute-start.5) | collective-permute-done | bytes 131104 | tf_op jit(solution)/shard_map/ppermute | solution.py:196
  66.6 17.5 %all_to_all.10.pieces = f32[16,32,256]{2,1,0:T(8,128)S(1)} all-to-all(f32[16,32,256]{2,1,0:T(8,128)S(1)} %bitcast.11), channel_id=1, replica_groups=mesh['y'=4,'near'=2,'core'=2,'x'=4,'far'=4] {'y','x'}, dimensions={0} | all-to-all | bytes 1048576 | tf_op jit(solution)/shard_map/all_to_all | solution.py:200
  84.1 14.5 %all_to_all.11 = f32[16,8,256]{2,1,0:T(8,128)S(1)} all-to-all(f32[16,8,256]{2,1,0:T(8,128)S(1)} %shard_map.58), channel_id=1, replica_groups=mesh['y'=4,'near'=2,'core'=2,'x'=4,'far'=4] {'near','far','core'}, dimensions={0} | all-to-all | bytes 262144 | tf_op jit(solution)/shard_map/all_to_all | solution.py:204
  98.6 0.6 bitcast_reduce_fusion
  99.2 0.0 collective-permute-done.4.gift
  99.2 2.0 %shard_map.56 = f32[256,1024]{1,0:T(8,128)} custom-call(f32[256,1024]{1,0:T(8,128)} %get-tuple-element.22.near, f32[256,1024]{1,0:T(8,128)S(1)} %collective-permute-done.4.gift), custom_call_target="tpu_custom_call" | custom-call | flops 1048576 | bytes 1048576 | tf_op jit(solution)/shard_map/pallas_call | solution.py:131
  (4 shorter events, 0.1 us)
Async XLA Ops:
  0.6 49.7 %collective-permute-start.2 = (f32[256,1024]{1,0:T(8,128)}, f32[256,1024]{1,0:T(8,128)S(1)}, u32[]{:S(2)}, u32[]{:S(2)}) collective-permute-start(f32[256,1024]{1,0:T(8,128)} %bitcast.12), channel_id=1, source_target_pairs={{0,1},{1,2},{2,3},{3,0},{16,19},{17,16},{18,17},{19,18},{4,5},{5,6... | collective-permute-start | bytes 3145736 | tf_op jit(solution)/shard_map/ppermute | solution.py:26
  7.5 42.8 %collective-permute-start.3 = (f32[256,1024]{1,0:T(8,128)}, f32[256,1024]{1,0:T(8,128)S(1)}, u32[]{:S(2)}, u32[]{:S(2)}) collective-permute-start(f32[256,1024]{1,0:T(8,128)} %bitcast.13), channel_id=1, source_target_pairs={{0,3},{1,0},{2,1},{3,2},{16,17},{17,18},{18,19},{19,16},{4,7},{5,4... | collective-permute-start | bytes 3145736 | tf_op jit(solution)/shard_map/ppermute | solution.py:26
  7.5 42.8 %collective-permute-start = (f32[1]{0:T(128)}, f32[1]{0:T(128)}, u32[]{:S(2)}, u32[]{:S(2)}) collective-permute-start(f32[1]{0:T(128)} %param.4), channel_id=1, source_target_pairs={{0,1},{1,2},{2,3},{3,0},{16,19},{17,16},{18,17},{19,18},{4,5},{5,6... | collective-permute-start | bytes 20 | tf_op jit(solution)/shard_map/ppermute | solution.py:26
  11.1 39.2 %collective-permute-start.1 = (f32[1]{0:T(128)}, f32[1]{0:T(128)}, u32[]{:S(2)}, u32[]{:S(2)}) collective-permute-start(f32[1]{0:T(128)} %param.4), channel_id=1, source_target_pairs={{0,3},{1,0},{2,1},{3,2},{16,17},{17,18},{18,19},{19,16},{4,7},{5,4... | collective-permute-start | bytes 20 | tf_op jit(solution)/shard_map/ppermute | solution.py:26
  11.8 0.7 copy-start.1
  12.5 1.2 %copy-start = (f32[1,256,1024]{2,1,0:T(8,128)S(1)}, f32[1,256,1024]{2,1,0:T(8,128)}, u32[]{:S(2)}) copy-start(f32[1,256,1024]{2,1,0:T(8,128)} %param.3) | copy-start | bytes 3145732
  54.7 44.6 %collective-permute-start.4 = (f32[256,1024]{1,0:T(8,128)}, f32[256,1024]{1,0:T(8,128)S(1)}, u32[]{:S(2)}, u32[]{:S(2)}) collective-permute-start(f32[256,1024]{1,0:T(8,128)} %get-tuple-element.23), channel_id=1, source_target_pairs={{0,1},{1,2},{2,3},{3,0},{16,19},{17,16},{18,17},{19,18},{4,5},{5,6... | collective-permute-start | bytes 3145736 | tf_op jit(solution)/shard_map/ppermute | solution.py:26
  65.1 1.4 %collective-permute-start.5 = (f32[16,8,256]{2,1,0:T(8,128)S(1)}, f32[16,8,256]{2,1,0:T(8,128)S(1)}, u32[]{:S(2)}, u32[]{:S(2)}) collective-permute-start(f32[16,8,256]{2,1,0:T(8,128)S(1)} %get-tuple-element.25), channel_id=1, source_target_pairs={{0,16},{16,0},{1,17},{17,1},{2,18},{18,2},{3,19},{19,3},{4,20},{20... | collective-permute-start | bytes 393224 | tf_op jit(solution)/shard_map/ppermute | solution.py:196

commit v12 on v10

--- a/solution.py
+++ b/solution.py
@@ -15,15 +15,16 @@
 ROWS = ((1,), (1,))
 PLAIN = ((1,), (0,))
 MIB = 1 << 20
+EARLY = 128
 
 
 def role_shift(value, step):
     size = lax.axis_size("far")
     pairs = []
-    for core, way in ((0, step), (1, -step)):
-        base = core * size
+    for near, way in ((0, -step), (1, step)):
+        base = near * size
         pairs += [(base + i, base + (i + way) % size) for i in range(size)]
-    return lax.ppermute(value, ("core", "far"), pairs)
+    return lax.ppermute(value, ("near", "far"), pairs)
 
 
 def split(x):
@@ -49,20 +50,24 @@
 
 
 def pair_kernel(upper, e_own, e_one, e_two, pairs, oh, ol, one, two, *refs):
-    keep, send, gift, near, buf, total, dens, sems = refs
+    keep, send, gift, later, near, buf, total, dens, sems = refs
     o, a, b = (oh[...], ol[...]), split(one[...]), split(two[...])
     mine, first, second = e_own[0:1, 0:1], e_one[0:1, 0:1], e_two[0:1, 0:1]
     t = mm(b, a, ROWS) / (first + second - pairs[...])
     s = spin(t)
     buf[...] = mm(s, a, PLAIN)
-    out = [pltpu.make_async_copy(buf, gift, sems.at[0])]
-    out[0].start()
+    out = [
+        pltpu.make_async_copy(buf.at[:EARLY, :], gift, sems.at[0]),
+        pltpu.make_async_copy(buf.at[EARLY:, :], later, sems.at[2]),
+    ]
+    for copy in out:
+        copy.start()
     t_one = mm(o, a, ROWS) / (mine + first - pairs[...])
     t_two = mm(o, b, ROWS) / (mine + second - pairs[...])
     s_one, s_two = spin(t_one), spin(t_two)
     total[...] = mm(s_one, a, PLAIN) + mm(s_two, b, PLAIN)
     out.append(pltpu.make_async_copy(total, near, sems.at[1]))
-    out[1].start()
+    out[2].start()
     dens[...] = (
         mm(split(t), s, ROWS)
         + mm(split(t_one), s_one, ROWS)
@@ -78,36 +83,28 @@
         copy.wait()
 
 
-def join_kernel(keep, other, copies):
-    for at in range(copies.shape[1]):
-        piece = keep[at] + other[at]
-        for copy in range(copies.shape[0]):
-            copies[copy, at] = piece
-
-
-def sum_kernel(near, gift, grad, mine, other, sems):
-    parts = 4
-    step = mine.shape[0] // parts
+def sum_kernel(near, gift, later, grad, mine, other, sems):
+    cuts = ((0, EARLY), (EARLY, EARLY + 64), (EARLY + 64, mine.shape[0]))
     copies = []
-    for at in range(parts):
-        rows = pl.ds(at * step, step)
+    for at, (low, high) in enumerate(cuts):
+        rows = pl.ds(low, high - low)
+        source = gift if at == 0 else later.at[pl.ds(low - EARLY, high - low), :]
         copies.append(
             (
                 pltpu.make_async_copy(near.at[rows, :], mine.at[rows, :], sems.at[0, at]),
-                pltpu.make_async_copy(gift.at[rows, :], other.at[rows, :], sems.at[1, at]),
+                pltpu.make_async_copy(source, other.at[rows, :], sems.at[1, at]),
                 pltpu.make_async_copy(mine.at[rows, :], grad.at[rows, :], sems.at[2, at]),
             )
         )
         copies[-1][0].start()
         copies[-1][1].start()
-    for at in range(parts):
-        rows = slice(at * step, (at + 1) * step)
+    for at, (low, high) in enumerate(cuts):
         copies[at][0].wait()
         copies[at][1].wait()
-        mine[rows, :] = mine[rows, :] + other[rows, :]
+        mine[low:high, :] = mine[low:high, :] + other[low:high, :]
         copies[at][2].start()
-    for at in range(parts):
-        copies[at][2].wait()
+    for copy in copies:
+        copy[2].wait()
 
 
 def fold_kernel(pieces, copies):
@@ -116,8 +113,7 @@
         total = total + pieces[at]
     total = total * (1.0 / 256.0)
     for at in range(copies.shape[0]):
-        row = at // 2 % 4 * 8
-        copies[at] = total[row : row + 8, :]
+        copies[at] = total
 
 
 def call(kernel, out, scratch, limit, flops, args, in_specs, out_specs):
@@ -165,37 +161,35 @@
     )
     piece = (16, 8, v)
     full = pltpu.VMEM((v, n), F32)
-    keep, send, gift, near = call(
+    keep, send, gift, later, near = call(
         pair_kernel,
-        (piece, piece, (v, n), (v, n)),
-        [full] * 2 + [pltpu.VMEM((v, v), F32), pltpu.SemaphoreType.DMA((2,))],
+        (piece, piece, (EARLY, n), (v - EARLY, n), (v, n)),
+        [full] * 2 + [pltpu.VMEM((v, v), F32), pltpu.SemaphoreType.DMA((3,))],
         14,
         1 << 31,
         (upper, s_own, s_one, s_two, pairs, oh, ol, one, two),
         [VMEM] * 9,
-        (VMEM, VMEM, HBM, HBM),
+        (VMEM, VMEM, HBM, HBM, HBM),
     )
     other = lax.ppermute(send, "core", [(0, 1), (1, 0)])
     gift = role_shift(gift, 1)
-    (mine,) = call(
-        join_kernel, ((4,) + piece,), [], 4, 1 << 20, (keep, other), [VMEM] * 2, (VMEM,)
-    )
+    later = role_shift(later, 1)
     parts = lax.all_to_all(
-        mine.reshape(16, 32, v), ("y", "x"), split_axis=0, concat_axis=0, tiled=True
+        keep + other, ("x", "far"), split_axis=0, concat_axis=0, tiled=True
     )
     (copies,) = call(fold_kernel, (piece,), [], 4, 1 << 20, (parts,), [VMEM], (VMEM,))
     copies = lax.all_to_all(
-        copies, ("near", "far", "core"), split_axis=0, concat_axis=0, tiled=True
+        copies, ("y", "near", "core"), split_axis=0, concat_axis=0, tiled=True
     )
     density = jnp.sum(copies.reshape(8, 16, v), axis=0)
     (grad,) = call(
         sum_kernel,
         ((v, n),),
-        [full] * 2 + [pltpu.SemaphoreType.DMA((3, 4))],
+        [full] * 2 + [pltpu.SemaphoreType.DMA((3, 3))],
         8,
         1 << 20,
-        (in_hbm(near), gift),
-        [HBM] * 2,
+        (in_hbm(near), gift, later),
+        [HBM] * 3,
         (HBM,),
     )
     return grad[None], density

time: 99.9 us -> 108 us (1.081)
  starting transfers between devices: 13.1 us -> 23.1 us
  blocking collectives: 34.1 us -> 29.9 us
  waiting for transfers between devices: 40.3 us -> 42.1 us
    all_to_all x0 -> x1, starting transfers between devices: none -> 5.55 us  [body(): lax.all_to_all(copies, ('y', 'near', 'core'), split_axis=0, concat_axis=0...]
    all_to_all x2 -> x1, blocking collectives: 34.1 us -> 29.9 us  [body(): lax.all_to_all(keep + other, ('x', 'far'), split_axis=0, concat_axis=0, t...]
    all_to_all x0 -> x1, waiting for transfers between devices: none -> 3.95 us  [body(): lax.all_to_all(copies, ('y', 'near', 'core'), split_axis=0, concat_axis=0...]
    ppermute x5 -> x6, starting transfers between devices: 13.1 us -> 16.8 us  [role_shift(): return lax.ppermute(value, ('near', 'far'), pairs)]
    ppermute x1, waiting for transfers between devices: 1.35 us -> 0.01 us  [body(): other = lax.ppermute(send, 'core', [(0, 1), (1, 0)])]
    ppermute x5 -> x6, waiting for transfers between devices: 39 us -> 38.1 us  [role_shift(): return lax.ppermute(value, ('near', 'far'), pairs)]
    pallas_call x5 -> x4, Pallas kernels: 6.96 us -> 7.69 us  [call(): pl.pallas_call(kernel, out_shape=tuple((pltpu.HBM(s, F32) if spec is HBM...]
  transfers between devices with their start and end apart: 6 -> 8, of which waited for: 3 -> 3; matrix products, arithmetic and copies ran while one was open for 1% -> 0% of each run, Pallas kernels for 0% -> 3%
where the time goes in v12:
time: 108 us
  waiting for transfers between devices  42.1 us (39%)
  blocking collectives  29.9 us (28%)
  starting transfers between devices  23.1 us (21%)
  Pallas kernels  7.69 us (7%)
  local copies, waits for them, and re-layouts  3.16 us (3%)
  between operations  1.4 us (1%)
    ppermute x6, waiting for transfers between devices, role_shift(): return lax.ppermute(value, ('near', 'far'), pairs)  38.1 us
    all_to_all x1, blocking collectives, body(): lax.all_to_all(keep + other, ('x', 'far'), split_axis=0, concat_axis=0, t...  29.9 us
    ppermute x6, starting transfers between devices, role_shift(): return lax.ppermute(value, ('near', 'far'), pairs)  16.8 us
    pallas_call x4, Pallas kernels, call(): pl.pallas_call(kernel, out_shape=tuple((pltpu.HBM(s, F32) if spec is HBM...  7.69 us
    all_to_all x1, starting transfers between devices, body(): lax.all_to_all(copies, ('y', 'near', 'core'), split_axis=0, concat_axis=0...  5.55 us
    all_to_all x1, waiting for transfers between devices, body(): lax.all_to_all(copies, ('y', 'near', 'core'), split_axis=0, concat_axis=0...  3.95 us
  transfers between devices with their start and end apart: 8, of which 3 were waited for; matrix products, arithmetic and copies ran while one was open for 0% of the time, Pallas kernels for 3%

profile of v12, /device:TPU:1, one launch (start us, length us, event | category | flops | bytes accessed | tf_op | source)
XLA Modules:
  0.0 107.9 jit_solution(15899928540609688801)
XLA Ops:
  0.6 3.9 %collective-permute-start.3 = (f32[256,1024]{1,0:T(8,128)}, f32[256,1024]{1,0:T(8,128)S(1)}, u32[]{:S(2)}, u32[]{:S(2)}) collective-permute-start(f32[256,1024]{1,0:T(8,128)} %bitcast.10), channel_id=1, source_target_pairs={{0,1},{1,2},{2,3},{3,0},{32,35},{33,32},{34,33},{35,34},{4,5},{5,6... | collective-permute-start | bytes 3145736 | tf_op jit(solution)/shard_map/ppermute | solution.py:27
  4.5 3.1 %collective-permute-start.2 = (f32[256,1024]{1,0:T(8,128)}, f32[256,1024]{1,0:T(8,128)S(1)}, u32[]{:S(2)}, u32[]{:S(2)}) collective-permute-start(f32[256,1024]{1,0:T(8,128)} %bitcast.11), channel_id=1, source_target_pairs={{0,3},{1,0},{2,1},{3,2},{32,33},{33,34},{34,35},{35,32},{4,7},{5,4... | collective-permute-start | bytes 3145736 | tf_op jit(solution)/shard_map/ppermute | solution.py:27
  7.6 1.1 %collective-permute-start.1 = (f32[1]{0:T(128)}, f32[1]{0:T(128)}, u32[]{:S(2)}, u32[]{:S(2)}) collective-permute-start(f32[1]{0:T(128)} %param.4), channel_id=1, source_target_pairs={{0,1},{1,2},{2,3},{3,0},{32,35},{33,32},{34,33},{35,34},{4,5},{5,6... | collective-permute-start | bytes 20 | tf_op jit(solution)/shard_map/ppermute | solution.py:27
  8.7 2.5 %collective-permute-start = (f32[1]{0:T(128)}, f32[1]{0:T(128)}, u32[]{:S(2)}, u32[]{:S(2)}) collective-permute-start(f32[1]{0:T(128)} %param.4), channel_id=1, source_target_pairs={{0,3},{1,0},{2,1},{3,2},{32,33},{33,34},{34,35},{35,32},{4,7},{5,4... | collective-permute-start | bytes 20 | tf_op jit(solution)/shard_map/ppermute | solution.py:27
  11.9 0.0 copy-start.1
  11.9 0.7 copy-done.1
  12.6 0.0 copy-start
  12.6 1.2 %copy-done = f32[1,256,1024]{2,1,0:T(8,128)S(1)} copy-done((f32[1,256,1024]{2,1,0:T(8,128)S(1)}, f32[1,256,1024]{2,1,0:T(8,128)}, u32[]{:S(2)}) %copy-start) | copy-done | bytes 1048600
  13.8 0.3 shard_map.53
  14.1 17.3 %collective-permute-done.1 = f32[1]{0:T(128)} collective-permute-done((f32[1]{0:T(128)}, f32[1]{0:T(128)}, u32[]{:S(2)}, u32[]{:S(2)}) %collective-permute-start.1) | collective-permute-done | bytes 36 | tf_op jit(solution)/shard_map/ppermute | solution.py:27
  31.5 20.8 %collective-permute-done = f32[1]{0:T(128)} collective-permute-done((f32[1]{0:T(128)}, f32[1]{0:T(128)}, u32[]{:S(2)}, u32[]{:S(2)}) %collective-permute-start) | collective-permute-done | bytes 36 | tf_op jit(solution)/shard_map/ppermute | solution.py:27
  52.2 0.0 collective-permute-done.3.two
  52.2 0.0 collective-permute-done.2.one
  52.3 0.6 broadcast_in_dim.27.e_two
  52.9 0.6 broadcast_in_dim.26.e_one
  53.5 4.5 %shard_map.54 = (f32[16,8,256]{2,1,0:T(8,128)S(1)}, f32[16,8,256]{2,1,0:T(8,128)S(1)}, f32[128,1024]{1,0:T(8,128)}, f32[128,1024]{1,0:T(8,128)}, f32[256,1024]{1,0:T(8,128)}) custom-call(f32[8,256]{1,0:T(8,128)S(1)} %broadcast_in_dim.24.upper, f32[8,128]{1,0:T(8,128)S(1)} %broadcast_in_dim.25.e_own, f32[8,128]{1,0:T(8,128)S(1)} %broadcast_in_dim.26.e_one, ...), custom_call_target="tpu_custom_call" | custom-call | flops 2147483648 | bytes 1048576 | tf_op jit(solution)/shard_map/pallas_call | solution.py:120
  58.1 0.7 collective-permute-start.6
  58.8 3.9 %collective-permute-start.4 = (f32[128,1024]{1,0:T(8,128)}, f32[128,1024]{1,0:T(8,128)S(1)}, u32[]{:S(2)}, u32[]{:S(2)}) collective-permute-start(f32[128,1024]{1,0:T(8,128)} %get-tuple-element.14), channel_id=1, source_target_pairs={{0,3},{1,0},{2,1},{3,2},{32,33},{33,34},{34,35},{35,32},{4,7},{5,4... | collective-permute-start | bytes 1572872 | tf_op jit(solution)/shard_map/ppermute | solution.py:27
  62.7 2.4 %collective-permute-start.5 = (f32[128,1024]{1,0:T(8,128)}, f32[128,1024]{1,0:T(8,128)S(1)}, u32[]{:S(2)}, u32[]{:S(2)}) collective-permute-start(f32[128,1024]{1,0:T(8,128)} %get-tuple-element.15), channel_id=1, source_target_pairs={{0,3},{1,0},{2,1},{3,2},{32,33},{33,34},{34,35},{35,32},{4,7},{5,4... | collective-permute-start | bytes 1572872 | tf_op jit(solution)/shard_map/ppermute | solution.py:27
  65.1 0.0 collective-permute-done.6
  65.1 29.9 %all_to_all.10.pieces = f32[16,8,256]{2,1,0:T(8,128)S(1)} all-to-all(f32[16,8,256]{2,1,0:T(8,128)S(1)} %add.3), channel_id=1, replica_groups=mesh['y'=4,'near'=2,'core'=2,'x'=4,'far'=4] {'x','far'}, dimensions={0} | all-to-all | bytes 262144 | tf_op jit(solution)/shard_map/all_to_all | solution.py:177
  95.0 0.7 shard_map.56
  95.7 5.5 %all-to-all-start.1 = ((f32[16,8,256]{2,1,0:T(8,128)}), f32[16,8,256]{2,1,0:T(8,128)S(1)}, u32[]{:S(2)}, u32[]{:S(2)}) async-start(f32[16,8,256]{2,1,0:T(8,128)} %shard_map.56), calls=%async_computation.1 | async-start | bytes 262144 | tf_op jit(solution)/shard_map/all_to_all | solution.py:181
  101.2 0.0 collective-permute-done.4.gift
  101.2 0.0 collective-permute-done.5.later
  101.2 2.1 %shard_map.55 = f32[256,1024]{1,0:T(8,128)} custom-call(f32[256,1024]{1,0:T(8,128)} %get-tuple-element.13.near, f32[128,1024]{1,0:T(8,128)S(1)} %collective-permute-done.4.gift, f32[128,1024]{1,0:T(8,128)S(1)} %collective-permute-done.5.later), custom_call_target="tpu_custom_call" | custom-call | flops 1048576 | bytes 1048576 | tf_op jit(solution)/shard_map/pallas_call | solution.py:120
  103.4 4.0 %all-to-all-done.1 = f32[16,8,256]{2,1,0:T(8,128)S(1)} async-done(((f32[16,8,256]{2,1,0:T(8,128)}), f32[16,8,256]{2,1,0:T(8,128)S(1)}, u32[]{:S(2)}, u32[]{:S(2)}) %all-to-all-start.1) | async-done | bytes 131104 | tf_op jit(solution)/shard_map/all_to_all | solution.py:181
  107.3 0.6 bitcast_reduce_fusion
  (3 shorter events, 0.0 us)
Async XLA Ops:
  0.6 51.6 %collective-permute-start.3 = (f32[256,1024]{1,0:T(8,128)}, f32[256,1024]{1,0:T(8,128)S(1)}, u32[]{:S(2)}, u32[]{:S(2)}) collective-permute-start(f32[256,1024]{1,0:T(8,128)} %bitcast.10), channel_id=1, source_target_pairs={{0,1},{1,2},{2,3},{3,0},{32,35},{33,32},{34,33},{35,34},{4,5},{5,6... | collective-permute-start | bytes 3145736 | tf_op jit(solution)/shard_map/ppermute | solution.py:27
  4.5 47.7 %collective-permute-start.2 = (f32[256,1024]{1,0:T(8,128)}, f32[256,1024]{1,0:T(8,128)S(1)}, u32[]{:S(2)}, u32[]{:S(2)}) collective-permute-start(f32[256,1024]{1,0:T(8,128)} %bitcast.11), channel_id=1, source_target_pairs={{0,3},{1,0},{2,1},{3,2},{32,33},{33,34},{34,35},{35,32},{4,7},{5,4... | collective-permute-start | bytes 3145736 | tf_op jit(solution)/shard_map/ppermute | solution.py:27
  7.6 23.8 %collective-permute-start.1 = (f32[1]{0:T(128)}, f32[1]{0:T(128)}, u32[]{:S(2)}, u32[]{:S(2)}) collective-permute-start(f32[1]{0:T(128)} %param.4), channel_id=1, source_target_pairs={{0,1},{1,2},{2,3},{3,0},{32,35},{33,32},{34,33},{35,34},{4,5},{5,6... | collective-permute-start | bytes 20 | tf_op jit(solution)/shard_map/ppermute | solution.py:27
  8.7 43.5 %collective-permute-start = (f32[1]{0:T(128)}, f32[1]{0:T(128)}, u32[]{:S(2)}, u32[]{:S(2)}) collective-permute-start(f32[1]{0:T(128)} %param.4), channel_id=1, source_target_pairs={{0,3},{1,0},{2,1},{3,2},{32,33},{33,34},{34,35},{35,32},{4,7},{5,4... | collective-permute-start | bytes 20 | tf_op jit(solution)/shard_map/ppermute | solution.py:27
  11.9 0.7 copy-start.1
  12.6 1.2 %copy-start = (f32[1,256,1024]{2,1,0:T(8,128)S(1)}, f32[1,256,1024]{2,1,0:T(8,128)}, u32[]{:S(2)}) copy-start(f32[1,256,1024]{2,1,0:T(8,128)} %param.3) | copy-start | bytes 3145732
  58.1 7.0 %collective-permute-start.6 = (f32[16,8,256]{2,1,0:T(8,128)S(1)}, f32[16,8,256]{2,1,0:T(8,128)S(1)}, u32[]{:S(2)}, u32[]{:S(2)}) collective-permute-start(f32[16,8,256]{2,1,0:T(8,128)S(1)} %get-tuple-element.17), channel_id=1, source_target_pairs={{0,16},{16,0},{1,17},{17,1},{2,18},{18,2},{3,19},{19,3},{4,20},{20... | collective-permute-start | bytes 393224 | tf_op jit(solution)/shard_map/ppermute | solution.py:174
  58.8 42.4 %collective-permute-start.4 = (f32[128,1024]{1,0:T(8,128)}, f32[128,1024]{1,0:T(8,128)S(1)}, u32[]{:S(2)}, u32[]{:S(2)}) collective-permute-start(f32[128,1024]{1,0:T(8,128)} %get-tuple-element.14), channel_id=1, source_target_pairs={{0,3},{1,0},{2,1},{3,2},{32,33},{33,34},{34,35},{35,32},{4,7},{5,4... | collective-permute-start | bytes 1572872 | tf_op jit(solution)/shard_map/ppermute | solution.py:27
  62.7 38.5 %collective-permute-start.5 = (f32[128,1024]{1,0:T(8,128)}, f32[128,1024]{1,0:T(8,128)S(1)}, u32[]{:S(2)}, u32[]{:S(2)}) collective-permute-start(f32[128,1024]{1,0:T(8,128)} %get-tuple-element.15), channel_id=1, source_target_pairs={{0,3},{1,0},{2,1},{3,2},{32,33},{33,34},{34,35},{35,32},{4,7},{5,4... | collective-permute-start | bytes 1572872 | tf_op jit(solution)/shard_map/ppermute | solution.py:27
  95.7 11.7 %all-to-all-start.1 = ((f32[16,8,256]{2,1,0:T(8,128)}), f32[16,8,256]{2,1,0:T(8,128)S(1)}, u32[]{:S(2)}, u32[]{:S(2)}) async-start(f32[16,8,256]{2,1,0:T(8,128)} %shard_map.56), calls=%async_computation.1 | async-start | bytes 262144 | tf_op jit(solution)/shard_map/all_to_all | solution.py:181

commit v13 on v12

--- a/solution.py
+++ b/solution.py
@@ -21,10 +21,10 @@
 def role_shift(value, step):
     size = lax.axis_size("far")
     pairs = []
-    for near, way in ((0, -step), (1, step)):
-        base = near * size
+    for core, way in ((0, step), (1, -step)):
+        base = core * size
         pairs += [(base + i, base + (i + way) % size) for i in range(size)]
-    return lax.ppermute(value, ("near", "far"), pairs)
+    return lax.ppermute(value, ("core", "far"), pairs)
 
 
 def split(x):

time: 108 us -> 107 us (level)
  blocking collectives: 29.9 us -> 25.8 us
  starting transfers between devices: 23.1 us -> 24.8 us
    all_to_all x1, blocking collectives: 29.9 us -> 25.8 us  [body(): lax.all_to_all(keep + other, ('x', 'far'), split_axis=0, concat_axis=0, t...]
    all_to_all x1, starting transfers between devices: 5.55 us -> 8.14 us  [body(): lax.all_to_all(copies, ('y', 'near', 'core'), split_axis=0, concat_axis=0...]
where the time goes in v13:
time: 107 us; the launch traced here: 106 us
  waiting for transfers between devices  43 us (40%)
  blocking collectives  25.8 us (24%)
  starting transfers between devices  24.8 us (23%)
  Pallas kernels  7.69 us (7%)
  local copies, waits for them, and re-layouts  3.16 us (3%)
  between operations  1.4 us (1%)
    ppermute x6, waiting for transfers between devices, role_shift(): return lax.ppermute(value, ('core', 'far'), pairs)  39 us
    all_to_all x1, blocking collectives, body(): lax.all_to_all(keep + other, ('x', 'far'), split_axis=0, concat_axis=0, t...  25.8 us
    ppermute x6, starting transfers between devices, role_shift(): return lax.ppermute(value, ('core', 'far'), pairs)  16.1 us
    all_to_all x1, starting transfers between devices, body(): lax.all_to_all(copies, ('y', 'near', 'core'), split_axis=0, concat_axis=0...  8.14 us
    pallas_call x4, Pallas kernels, call(): pl.pallas_call(kernel, out_shape=tuple((pltpu.HBM(s, F32) if spec is HBM...  7.69 us
    all_to_all x1, waiting for transfers between devices, body(): lax.all_to_all(copies, ('y', 'near', 'core'), split_axis=0, concat_axis=0...  3.95 us
  transfers between devices with their start and end apart: 8, of which 3 were waited for; matrix products, arithmetic and copies ran while one was open for 0% of the time, Pallas kernels for 3%

profile of v13, /device:TPU:1, one launch (start us, length us, event | category | flops | bytes accessed | tf_op | source)
XLA Modules:
  0.0 106.4 jit_solution(12580300401009686020)
XLA Ops:
  0.6 3.9 %collective-permute-start.3 = (f32[256,1024]{1,0:T(8,128)}, f32[256,1024]{1,0:T(8,128)S(1)}, u32[]{:S(2)}, u32[]{:S(2)}) collective-permute-start(f32[256,1024]{1,0:T(8,128)} %bitcast.10), channel_id=1, source_target_pairs={{0,3},{1,0},{2,1},{3,2},{16,17},{17,18},{18,19},{19,16},{4,7},{5,4... | collective-permute-start | bytes 3145736 | tf_op jit(solution)/shard_map/ppermute | solution.py:27
  4.5 3.1 %collective-permute-start.2 = (f32[256,1024]{1,0:T(8,128)}, f32[256,1024]{1,0:T(8,128)S(1)}, u32[]{:S(2)}, u32[]{:S(2)}) collective-permute-start(f32[256,1024]{1,0:T(8,128)} %bitcast.11), channel_id=1, source_target_pairs={{0,1},{1,2},{2,3},{3,0},{16,19},{17,16},{18,17},{19,18},{4,5},{5,6... | collective-permute-start | bytes 3145736 | tf_op jit(solution)/shard_map/ppermute | solution.py:27
  7.6 1.1 %collective-permute-start.1 = (f32[1]{0:T(128)}, f32[1]{0:T(128)}, u32[]{:S(2)}, u32[]{:S(2)}) collective-permute-start(f32[1]{0:T(128)} %param.4), channel_id=1, source_target_pairs={{0,3},{1,0},{2,1},{3,2},{16,17},{17,18},{18,19},{19,16},{4,7},{5,4... | collective-permute-start | bytes 20 | tf_op jit(solution)/shard_map/ppermute | solution.py:27
  8.7 2.5 %collective-permute-start = (f32[1]{0:T(128)}, f32[1]{0:T(128)}, u32[]{:S(2)}, u32[]{:S(2)}) collective-permute-start(f32[1]{0:T(128)} %param.4), channel_id=1, source_target_pairs={{0,1},{1,2},{2,3},{3,0},{16,19},{17,16},{18,17},{19,18},{4,5},{5,6... | collective-permute-start | bytes 20 | tf_op jit(solution)/shard_map/ppermute | solution.py:27
  11.9 0.0 copy-start.1
  11.9 0.7 copy-done.1
  12.6 0.0 copy-start
  12.6 1.2 %copy-done = f32[1,256,1024]{2,1,0:T(8,128)S(1)} copy-done((f32[1,256,1024]{2,1,0:T(8,128)S(1)}, f32[1,256,1024]{2,1,0:T(8,128)}, u32[]{:S(2)}) %copy-start) | copy-done | bytes 1048600
  13.8 0.3 shard_map.53
  14.1 20.9 %collective-permute-done.1 = f32[1]{0:T(128)} collective-permute-done((f32[1]{0:T(128)}, f32[1]{0:T(128)}, u32[]{:S(2)}, u32[]{:S(2)}) %collective-permute-start.1) | collective-permute-done | bytes 36 | tf_op jit(solution)/shard_map/ppermute | solution.py:27
  35.0 18.1 %collective-permute-done = f32[1]{0:T(128)} collective-permute-done((f32[1]{0:T(128)}, f32[1]{0:T(128)}, u32[]{:S(2)}, u32[]{:S(2)}) %collective-permute-start) | collective-permute-done | bytes 36 | tf_op jit(solution)/shard_map/ppermute | solution.py:27
  53.1 0.0 collective-permute-done.3.two
  53.1 0.0 collective-permute-done.2.one
  53.2 0.6 broadcast_in_dim.27.e_two
  53.8 0.6 broadcast_in_dim.26.e_one
  54.4 4.5 %shard_map.54 = (f32[16,8,256]{2,1,0:T(8,128)S(1)}, f32[16,8,256]{2,1,0:T(8,128)S(1)}, f32[128,1024]{1,0:T(8,128)}, f32[128,1024]{1,0:T(8,128)}, f32[256,1024]{1,0:T(8,128)}) custom-call(f32[8,256]{1,0:T(8,128)S(1)} %broadcast_in_dim.24.upper, f32[8,128]{1,0:T(8,128)S(1)} %broadcast_in_dim.25.e_own, f32[8,128]{1,0:T(8,128)S(1)} %broadcast_in_dim.26.e_one, ...), custom_call_target="tpu_custom_call" | custom-call | flops 2147483648 | bytes 1048576 | tf_op jit(solution)/shard_map/pallas_call | solution.py:120
  59.0 0.5 collective-permute-start.6
  59.5 3.3 %collective-permute-start.4 = (f32[128,1024]{1,0:T(8,128)}, f32[128,1024]{1,0:T(8,128)S(1)}, u32[]{:S(2)}, u32[]{:S(2)}) collective-permute-start(f32[128,1024]{1,0:T(8,128)} %get-tuple-element.14), channel_id=1, source_target_pairs={{0,1},{1,2},{2,3},{3,0},{16,19},{17,16},{18,17},{19,18},{4,5},{5,6... | collective-permute-start | bytes 1572872 | tf_op jit(solution)/shard_map/ppermute | solution.py:27
  62.8 2.2 %collective-permute-start.5 = (f32[128,1024]{1,0:T(8,128)}, f32[128,1024]{1,0:T(8,128)S(1)}, u32[]{:S(2)}, u32[]{:S(2)}) collective-permute-start(f32[128,1024]{1,0:T(8,128)} %get-tuple-element.15), channel_id=1, source_target_pairs={{0,1},{1,2},{2,3},{3,0},{16,19},{17,16},{18,17},{19,18},{4,5},{5,6... | collective-permute-start | bytes 1572872 | tf_op jit(solution)/shard_map/ppermute | solution.py:27
  65.0 0.0 collective-permute-done.6
  65.1 25.8 %all_to_all.10.pieces = f32[16,8,256]{2,1,0:T(8,128)S(1)} all-to-all(f32[16,8,256]{2,1,0:T(8,128)S(1)} %add.3), channel_id=1, replica_groups=mesh['y'=4,'near'=2,'core'=2,'x'=4,'far'=4] {'x','far'}, dimensions={0} | all-to-all | bytes 262144 | tf_op jit(solution)/shard_map/all_to_all | solution.py:177
  90.9 0.7 shard_map.56
  91.6 8.1 %all-to-all-start.1 = ((f32[16,8,256]{2,1,0:T(8,128)}), f32[16,8,256]{2,1,0:T(8,128)S(1)}, u32[]{:S(2)}, u32[]{:S(2)}) async-start(f32[16,8,256]{2,1,0:T(8,128)} %shard_map.56), calls=%async_computation.1 | async-start | bytes 262144 | tf_op jit(solution)/shard_map/all_to_all | solution.py:181
  99.7 0.0 collective-permute-done.4.gift
  99.7 0.0 collective-permute-done.5.later
  99.7 2.1 %shard_map.55 = f32[256,1024]{1,0:T(8,128)} custom-call(f32[256,1024]{1,0:T(8,128)} %get-tuple-element.13.near, f32[128,1024]{1,0:T(8,128)S(1)} %collective-permute-done.4.gift, f32[128,1024]{1,0:T(8,128)S(1)} %collective-permute-done.5.later), custom_call_target="tpu_custom_call" | custom-call | flops 1048576 | bytes 1048576 | tf_op jit(solution)/shard_map/pallas_call | solution.py:120
  101.9 4.0 %all-to-all-done.1 = f32[16,8,256]{2,1,0:T(8,128)S(1)} async-done(((f32[16,8,256]{2,1,0:T(8,128)}), f32[16,8,256]{2,1,0:T(8,128)S(1)}, u32[]{:S(2)}, u32[]{:S(2)}) %all-to-all-start.1) | async-done | bytes 131104 | tf_op jit(solution)/shard_map/all_to_all | solution.py:181
  105.8 0.6 bitcast_reduce_fusion
  (3 shorter events, 0.0 us)
Async XLA Ops:
  0.6 52.5 %collective-permute-start.3 = (f32[256,1024]{1,0:T(8,128)}, f32[256,1024]{1,0:T(8,128)S(1)}, u32[]{:S(2)}, u32[]{:S(2)}) collective-permute-start(f32[256,1024]{1,0:T(8,128)} %bitcast.10), channel_id=1, source_target_pairs={{0,3},{1,0},{2,1},{3,2},{16,17},{17,18},{18,19},{19,16},{4,7},{5,4... | collective-permute-start | bytes 3145736 | tf_op jit(solution)/shard_map/ppermute | solution.py:27
  4.5 48.6 %collective-permute-start.2 = (f32[256,1024]{1,0:T(8,128)}, f32[256,1024]{1,0:T(8,128)S(1)}, u32[]{:S(2)}, u32[]{:S(2)}) collective-permute-start(f32[256,1024]{1,0:T(8,128)} %bitcast.11), channel_id=1, source_target_pairs={{0,1},{1,2},{2,3},{3,0},{16,19},{17,16},{18,17},{19,18},{4,5},{5,6... | collective-permute-start | bytes 3145736 | tf_op jit(solution)/shard_map/ppermute | solution.py:27
  7.6 27.4 %collective-permute-start.1 = (f32[1]{0:T(128)}, f32[1]{0:T(128)}, u32[]{:S(2)}, u32[]{:S(2)}) collective-permute-start(f32[1]{0:T(128)} %param.4), channel_id=1, source_target_pairs={{0,3},{1,0},{2,1},{3,2},{16,17},{17,18},{18,19},{19,16},{4,7},{5,4... | collective-permute-start | bytes 20 | tf_op jit(solution)/shard_map/ppermute | solution.py:27
  8.7 44.4 %collective-permute-start = (f32[1]{0:T(128)}, f32[1]{0:T(128)}, u32[]{:S(2)}, u32[]{:S(2)}) collective-permute-start(f32[1]{0:T(128)} %param.4), channel_id=1, source_target_pairs={{0,1},{1,2},{2,3},{3,0},{16,19},{17,16},{18,17},{19,18},{4,5},{5,6... | collective-permute-start | bytes 20 | tf_op jit(solution)/shard_map/ppermute | solution.py:27
  11.9 0.7 copy-start.1
  12.6 1.2 %copy-start = (f32[1,256,1024]{2,1,0:T(8,128)S(1)}, f32[1,256,1024]{2,1,0:T(8,128)}, u32[]{:S(2)}) copy-start(f32[1,256,1024]{2,1,0:T(8,128)} %param.3) | copy-start | bytes 3145732
  59.0 6.1 %collective-permute-start.6 = (f32[16,8,256]{2,1,0:T(8,128)S(1)}, f32[16,8,256]{2,1,0:T(8,128)S(1)}, u32[]{:S(2)}, u32[]{:S(2)}) collective-permute-start(f32[16,8,256]{2,1,0:T(8,128)S(1)} %get-tuple-element.17), channel_id=1, source_target_pairs={{0,16},{16,0},{1,17},{17,1},{2,18},{18,2},{3,19},{19,3},{4,20},{20... | collective-permute-start | bytes 393224 | tf_op jit(solution)/shard_map/ppermute | solution.py:174
  59.5 40.2 %collective-permute-start.4 = (f32[128,1024]{1,0:T(8,128)}, f32[128,1024]{1,0:T(8,128)S(1)}, u32[]{:S(2)}, u32[]{:S(2)}) collective-permute-start(f32[128,1024]{1,0:T(8,128)} %get-tuple-element.14), channel_id=1, source_target_pairs={{0,1},{1,2},{2,3},{3,0},{16,19},{17,16},{18,17},{19,18},{4,5},{5,6... | collective-permute-start | bytes 1572872 | tf_op jit(solution)/shard_map/ppermute | solution.py:27
  62.8 36.9 %collective-permute-start.5 = (f32[128,1024]{1,0:T(8,128)}, f32[128,1024]{1,0:T(8,128)S(1)}, u32[]{:S(2)}, u32[]{:S(2)}) collective-permute-start(f32[128,1024]{1,0:T(8,128)} %get-tuple-element.15), channel_id=1, source_target_pairs={{0,1},{1,2},{2,3},{3,0},{16,19},{17,16},{18,17},{19,18},{4,5},{5,6... | collective-permute-start | bytes 1572872 | tf_op jit(solution)/shard_map/ppermute | solution.py:27
  91.6 14.3 %all-to-all-start.1 = ((f32[16,8,256]{2,1,0:T(8,128)}), f32[16,8,256]{2,1,0:T(8,128)S(1)}, u32[]{:S(2)}, u32[]{:S(2)}) async-start(f32[16,8,256]{2,1,0:T(8,128)} %shard_map.56), calls=%async_computation.1 | async-start | bytes 262144 | tf_op jit(solution)/shard_map/all_to_all | solution.py:181

commit v14 on v11

--- a/solution.py
+++ b/solution.py
@@ -15,6 +15,7 @@
 ROWS = ((1,), (1,))
 PLAIN = ((1,), (0,))
 MIB = 1 << 20
+EARLY = 176
 
 
 def role_shift(value, step):
@@ -49,15 +50,20 @@
 
 
 def gift_kernel(e_one, e_two, pairs, one, two, *refs):
-    gift, t_mid, ah, al, bh, bl, buf, sem = refs
+    gift, later, t_mid, ah, al, bh, bl, buf, sems = refs
     ah[...], al[...] = a = split(one[...])
     bh[...], bl[...] = b = split(two[...])
     t = mm(b, a, ROWS) / (e_one[0:1, 0:1] + e_two[0:1, 0:1] - pairs[...])
     buf[...] = mm(spin(t), a, PLAIN)
-    out = pltpu.make_async_copy(buf, gift, sem)
-    out.start()
+    out = [
+        pltpu.make_async_copy(buf.at[:EARLY, :], gift, sems.at[0]),
+        pltpu.make_async_copy(buf.at[EARLY:, :], later, sems.at[1]),
+    ]
+    for copy in out:
+        copy.start()
     t_mid[...] = t
-    out.wait()
+    for copy in out:
+        copy.wait()
 
 
 def density_kernel(upper, e_own, e_one, e_two, pairs, oh, ol, t_mid, *refs):
@@ -86,35 +92,34 @@
 
 
 def join_kernel(keep, other, copies):
-    for at in range(copies.shape[1]):
+    for at in range(keep.shape[0]):
         piece = keep[at] + other[at]
-        for copy in range(copies.shape[0]):
-            copies[copy, at] = piece
-
-
-def sum_kernel(near, gift, grad, mine, other, sems):
-    parts = 4
-    step = mine.shape[0] // parts
+        copies[at // 4, 0, at % 4] = piece
+        copies[at // 4, 1, at % 4] = piece
+
+
+def sum_kernel(near, gift, later, grad, mine, other, sems):
+    cuts = ((0, EARLY), (EARLY, EARLY + 40), (EARLY + 40, mine.shape[0]))
     copies = []
-    for at in range(parts):
-        rows = pl.ds(at * step, step)
+    for at, (low, high) in enumerate(cuts):
+        rows = pl.ds(low, high - low)
+        source = gift if at == 0 else later.at[pl.ds(low - EARLY, high - low), :]
         copies.append(
             (
                 pltpu.make_async_copy(near.at[rows, :], mine.at[rows, :], sems.at[0, at]),
-                pltpu.make_async_copy(gift.at[rows, :], other.at[rows, :], sems.at[1, at]),
+                pltpu.make_async_copy(source, other.at[rows, :], sems.at[1, at]),
                 pltpu.make_async_copy(mine.at[rows, :], grad.at[rows, :], sems.at[2, at]),
             )
         )
         copies[-1][0].start()
         copies[-1][1].start()
-    for at in range(parts):
-        rows = slice(at * step, (at + 1) * step)
+    for at, (low, high) in enumerate(cuts):
         copies[at][0].wait()
         copies[at][1].wait()
-        mine[rows, :] = mine[rows, :] + other[rows, :]
+        mine[low:high, :] = mine[low:high, :] + other[low:high, :]
         copies[at][2].start()
-    for at in range(parts):
-        copies[at][2].wait()
+    for copy in copies:
+        copy[2].wait()
 
 
 def fold_kernel(pieces, copies):
@@ -123,8 +128,7 @@
         total = total + pieces[at]
     total = total * (1.0 / 256.0)
     for at in range(copies.shape[0]):
-        row = at // 2 % 4 * 8
-        copies[at] = total[row : row + 8, :]
+        copies[at] = total
 
 
 def call(kernel, out, scratch, limit, flops, args, in_specs, out_specs):
@@ -172,15 +176,15 @@
     )
     piece = (16, 8, v)
     full = pltpu.VMEM((v, n), F32)
-    gift, t_mid, *splits = call(
+    gift, later, t_mid, *splits = call(
         gift_kernel,
-        ((v, n), (v, v)) + ((v, n),) * 4,
-        [full, pltpu.SemaphoreType.DMA],
+        ((EARLY, n), (v - EARLY, n), (v, v)) + ((v, n),) * 4,
+        [full, pltpu.SemaphoreType.DMA((2,))],
         12,
         1 << 31,
         (s_one, s_two, pairs, one, two),
         [VMEM] * 5,
-        (HBM,) + (VMEM,) * 5,
+        (HBM, HBM) + (VMEM,) * 5,
     )
     gift = role_shift(gift, 1)
     keep, send, near = call(
@@ -194,25 +198,39 @@
         (VMEM, VMEM, HBM),
     )
     other = lax.ppermute(send, "core", [(0, 1), (1, 0)])
+    later = role_shift(later, 1)
     (mine,) = call(
-        join_kernel, ((4,) + piece,), [], 4, 1 << 20, (keep, other), [VMEM] * 2, (VMEM,)
+        join_kernel,
+        ((4, 2, 4, 8, v),),
+        [],
+        4,
+        1 << 20,
+        (keep, other),
+        [VMEM] * 2,
+        (VMEM,),
     )
     parts = lax.all_to_all(
-        mine.reshape(16, 32, v), ("y", "x"), split_axis=0, concat_axis=0, tiled=True
-    )
-    (copies,) = call(fold_kernel, (piece,), [], 4, 1 << 20, (parts,), [VMEM], (VMEM,))
+        mine.reshape(32, 8, v),
+        ("x", "near", "far"),
+        split_axis=0,
+        concat_axis=0,
+        tiled=True,
+    )
+    (copies,) = call(
+        fold_kernel, ((8, 8, v),), [], 4, 1 << 20, (parts,), [VMEM], (VMEM,)
+    )
     copies = lax.all_to_all(
-        copies, ("near", "far", "core"), split_axis=0, concat_axis=0, tiled=True
-    )
-    density = jnp.sum(copies.reshape(8, 16, v), axis=0)
+        copies, ("y", "core"), split_axis=0, concat_axis=0, tiled=True
+    )
+    density = jnp.sum(copies.reshape(4, 16, v), axis=0)
     (grad,) = call(
         sum_kernel,
         ((v, n),),
-        [full] * 2 + [pltpu.SemaphoreType.DMA((3, 4))],
+        [full] * 2 + [pltpu.SemaphoreType.DMA((3, 3))],
         8,
         1 << 20,
-        (in_hbm(near), gift),
-        [HBM] * 2,
+        (in_hbm(near), gift, later),
+        [HBM] * 3,
         (HBM,),
     )
     return grad[None], density

time: 102 us -> 107 us (1.049)
  blocking collectives: 32 us -> 11 us
  waiting for transfers between devices: 37.6 us -> 53.4 us
  starting transfers between devices: 17.8 us -> 27.9 us
    all_to_all x2 -> x1, blocking collectives: 32 us -> 11 us  [body(): lax.all_to_all(copies, ('y', 'core'), split_axis=0, concat_axis=0, tiled=...]
    all_to_all x0 -> x1, waiting for transfers between devices: none -> 17.1 us  [body(): lax.all_to_all(mine.reshape(32, 8, v), ('x', 'near', 'far'), split_axis=0...]
    all_to_all x0 -> x1, starting transfers between devices: none -> 6.23 us  [body(): lax.all_to_all(mine.reshape(32, 8, v), ('x', 'near', 'far'), split_axis=0...]
    ppermute x1, starting transfers between devices: 0.09 us -> 3.5 us  [body(): other = lax.ppermute(send, 'core', [(0, 1), (1, 0)])]
    ppermute x1, waiting for transfers between devices: 1.33 us -> 0.01 us  [body(): other = lax.ppermute(send, 'core', [(0, 1), (1, 0)])]
    ppermute x5 -> x6, starting transfers between devices: 17.7 us -> 18.1 us  [role_shift(): return lax.ppermute(value, ('core', 'far'), pairs)]
    ppermute x5 -> x6, waiting for transfers between devices: 36.3 us -> 36.3 us  [role_shift(): return lax.ppermute(value, ('core', 'far'), pairs)]
  transfers between devices with their start and end apart: 6 -> 8, of which waited for: 2 -> 2; matrix products, arithmetic and copies ran while one was open for 1% -> 1% of each run, Pallas kernels for 4% -> 1%
where the time goes in v14:
time: 107 us
  waiting for transfers between devices  53.4 us (50%)
  starting transfers between devices  27.9 us (26%)
  blocking collectives  11 us (10%)
  Pallas kernels  9.48 us (9%)
  local copies, waits for them, and re-layouts  3.11 us (3%)
  between operations  1.45 us (1%)
    ppermute x6, waiting for transfers between devices, role_shift(): return lax.ppermute(value, ('core', 'far'), pairs)  36.3 us
    ppermute x6, starting transfers between devices, role_shift(): return lax.ppermute(value, ('core', 'far'), pairs)  18.1 us
    all_to_all x1, waiting for transfers between devices, body(): lax.all_to_all(mine.reshape(32, 8, v), ('x', 'near', 'far'), split_axis=0...  17.1 us
    all_to_all x1, blocking collectives, body(): lax.all_to_all(copies, ('y', 'core'), split_axis=0, concat_axis=0, tiled=...  11 us
    pallas_call x6, Pallas kernels, call(): pl.pallas_call(kernel, out_shape=tuple((pltpu.HBM(s, F32) if spec is HBM...  9.48 us
    all_to_all x1, starting transfers between devices, body(): lax.all_to_all(mine.reshape(32, 8, v), ('x', 'near', 'far'), split_axis=0...  6.23 us
    ppermute x1, starting transfers between devices, body(): other = lax.ppermute(send, 'core', [(0, 1), (1, 0)])  3.5 us
  transfers between devices with their start and end apart: 8, of which 2 were waited for; matrix products, arithmetic and copies ran while one was open for 1% of the time, Pallas kernels for 1%

profile of v14, /device:TPU:1, one launch (start us, length us, event | category | flops | bytes accessed | tf_op | source)
XLA Modules:
  0.0 106.9 jit_solution(15735591230498762918)
XLA Ops:
  0.6 6.9 %collective-permute-start.2 = (f32[256,1024]{1,0:T(8,128)}, f32[256,1024]{1,0:T(8,128)S(1)}, u32[]{:S(2)}, u32[]{:S(2)}) collective-permute-start(f32[256,1024]{1,0:T(8,128)} %bitcast.11), channel_id=1, source_target_pairs={{0,1},{1,2},{2,3},{3,0},{16,19},{17,16},{18,17},{19,18},{4,5},{5,6... | collective-permute-start | bytes 3145736 | tf_op jit(solution)/shard_map/ppermute | solution.py:27
  7.5 0.0 collective-permute-start.3
  7.5 3.6 %collective-permute-start = (f32[1]{0:T(128)}, f32[1]{0:T(128)}, u32[]{:S(2)}, u32[]{:S(2)}) collective-permute-start(f32[1]{0:T(128)} %param.4), channel_id=1, source_target_pairs={{0,1},{1,2},{2,3},{3,0},{16,19},{17,16},{18,17},{19,18},{4,5},{5,6... | collective-permute-start | bytes 20 | tf_op jit(solution)/shard_map/ppermute | solution.py:27
  11.1 0.0 collective-permute-start.1
  11.8 0.0 copy-start.1
  11.9 0.7 copy-done.1
  12.5 0.0 copy-start
  12.5 1.2 %copy-done = f32[1,256,1024]{2,1,0:T(8,128)S(1)} copy-done((f32[1,256,1024]{2,1,0:T(8,128)S(1)}, f32[1,256,1024]{2,1,0:T(8,128)}, u32[]{:S(2)}) %copy-start) | copy-done | bytes 1048600
  13.7 0.3 shard_map.53
  14.1 36.3 %collective-permute-done = f32[1]{0:T(128)} collective-permute-done((f32[1]{0:T(128)}, f32[1]{0:T(128)}, u32[]{:S(2)}, u32[]{:S(2)}) %collective-permute-start) | collective-permute-done | bytes 36 | tf_op jit(solution)/shard_map/ppermute | solution.py:27
  50.3 0.0 collective-permute-done.1
  50.3 0.0 collective-permute-done.2.one
  50.3 0.0 collective-permute-done.3.two
  50.3 0.6 broadcast_in_dim.26.e_one
  50.9 0.6 broadcast_in_dim.27.e_two
  51.6 3.0 %shard_map.54 = (f32[176,1024]{1,0:T(8,128)}, f32[80,1024]{1,0:T(8,128)}, f32[256,256]{1,0:T(8,128)S(1)}, bf16[256,1024]{1,0:T(8,128)(2,1)S(1)}, bf16[256,1024]{...) custom-call(f32[8,128]{1,0:T(8,128)S(1)} %broadcast_in_dim.26.e_one, ...), custom_call_target="tpu_custom_call" | custom-call | flops 2147483648 | bytes 1048576 | tf_op jit(solution)/shard_map/pallas_call | solution.py:135
  54.6 0.0 copy-start.2
  54.6 3.2 %shard_map.55 = (f32[16,8,256]{2,1,0:T(8,128)S(1)}, f32[16,8,256]{2,1,0:T(8,128)S(1)}, f32[256,1024]{1,0:T(8,128)}) custom-call(f32[8,256]{1,0:T(8,128)S(1)} %broadcast_in_dim.24.upper, f32[8,128]{1,0:T(8,128)S(1)} %broadcast_in_dim.25.e_own, f32[8,128]{1,0:T(8,128)S(1)} %broadcast_in_dim.26.e_one, f32[8,128]{1,0:T(8,128)S(1)} %broadcast_in_dim.27.e_two, ...), custom_call_target="tpu_custom_call" | custom-call | flops 2147483648 | bytes 1048576 | tf_op jit(solution)/shard_map/pallas_call | solution.py:135
  57.8 3.5 %collective-permute-start.6 = (f32[16,8,256]{2,1,0:T(8,128)S(1)}, f32[16,8,256]{2,1,0:T(8,128)S(1)}, u32[]{:S(2)}, u32[]{:S(2)}) collective-permute-start(f32[16,8,256]{2,1,0:T(8,128)S(1)} %get-tuple-element.27), channel_id=1, source_target_pairs={{0,16},{16,0},{1,17},{17,1},{2,18},{18,2},{3,19},{19,3},{4,20},{20... | collective-permute-start | bytes 393224 | tf_op jit(solution)/shard_map/ppermute | solution.py:200
  61.3 0.0 copy-done.2
  61.3 4.2 %collective-permute-start.4 = (f32[176,1024]{1,0:T(8,128)S(1)}, f32[176,1024]{1,0:T(8,128)S(1)}, u32[]{:S(2)}, u32[]{:S(2)}) collective-permute-start(f32[176,1024]{1,0:T(8,128)S(1)} %copy-done.2), channel_id=1, source_target_pairs={{0,1},{1,2},{2,3},{3,0},{16,19},{17,16},{18,17},{19,18},{4,5},{5,6... | collective-permute-start | bytes 2162696 | tf_op jit(solution)/shard_map/ppermute | solution.py:27
  65.5 0.0 collective-permute-done.6.other
  65.5 0.7 shard_map.57
  66.2 6.2 %all-to-all-start = ((f32[32,8,256]{2,1,0:T(8,128)}), f32[32,8,256]{2,1,0:T(8,128)S(1)}, u32[]{:S(2)}, u32[]{:S(2)}) async-start(f32[32,8,256]{2,1,0:T(8,128)} %bitcast.6), calls=%async_computation | async-start | bytes 524288 | tf_op jit(solution)/shard_map/all_to_all | solution.py:212
  72.5 0.0 copy-done.3
  72.5 3.4 %collective-permute-start.5 = (f32[80,1024]{1,0:T(8,128)S(1)}, f32[80,1024]{1,0:T(8,128)S(1)}, u32[]{:S(2)}, u32[]{:S(2)}) collective-permute-start(f32[80,1024]{1,0:T(8,128)S(1)} %copy-done.3), channel_id=1, source_target_pairs={{0,1},{1,2},{2,3},{3,0},{16,19},{17,16},{18,17},{19,18},{4,5},{5,6... | collective-permute-start | bytes 983048 | tf_op jit(solution)/shard_map/ppermute | solution.py:27
  75.9 17.1 %all-to-all-done.pieces = f32[32,8,256]{2,1,0:T(8,128)S(1)} async-done(((f32[32,8,256]{2,1,0:T(8,128)}), f32[32,8,256]{2,1,0:T(8,128)S(1)}, u32[]{:S(2)}, u32[]{:S(2)}) %all-to-all-start) | async-done | bytes 262176 | tf_op jit(solution)/shard_map/all_to_all | solution.py:212
  93.0 11.0 %all_to_all.10 = f32[8,8,256]{2,1,0:T(8,128)S(1)} all-to-all(f32[8,8,256]{2,1,0:T(8,128)S(1)} %shard_map.58), channel_id=1, replica_groups=mesh['y'=4,'near'=2,'core'=2,'x'=4,'far'=4] {'y','core'}, dimensions={0} | all-to-all | bytes 131072 | tf_op jit(solution)/shard_map/all_to_all | solution.py:222
  104.1 0.6 bitcast_reduce_fusion
  104.7 0.0 collective-permute-done.5.later
  104.7 0.0 collective-permute-done.4.gift
  104.7 2.2 %shard_map.56 = f32[256,1024]{1,0:T(8,128)} custom-call(f32[256,1024]{1,0:T(8,128)} %get-tuple-element.23.near, f32[176,1024]{1,0:T(8,128)S(1)} %collective-permute-done.4.gift, f32[80,1024]{1,0:T(8,128)S(1)} %collective-permute-done.5.later), custom_call_target="tpu_custom_call" | custom-call | flops 1048576 | bytes 1048576 | tf_op jit(solution)/shard_map/pallas_call | solution.py:135
  (4 shorter events, 0.0 us)
Async XLA Ops:
  0.6 49.7 %collective-permute-start.2 = (f32[256,1024]{1,0:T(8,128)}, f32[256,1024]{1,0:T(8,128)S(1)}, u32[]{:S(2)}, u32[]{:S(2)}) collective-permute-start(f32[256,1024]{1,0:T(8,128)} %bitcast.11), channel_id=1, source_target_pairs={{0,1},{1,2},{2,3},{3,0},{16,19},{17,16},{18,17},{19,18},{4,5},{5,6... | collective-permute-start | bytes 3145736 | tf_op jit(solution)/shard_map/ppermute | solution.py:27
  7.5 42.8 %collective-permute-start.3 = (f32[256,1024]{1,0:T(8,128)}, f32[256,1024]{1,0:T(8,128)S(1)}, u32[]{:S(2)}, u32[]{:S(2)}) collective-permute-start(f32[256,1024]{1,0:T(8,128)} %bitcast.12), channel_id=1, source_target_pairs={{0,3},{1,0},{2,1},{3,2},{16,17},{17,18},{18,19},{19,16},{4,7},{5,4... | collective-permute-start | bytes 3145736 | tf_op jit(solution)/shard_map/ppermute | solution.py:27
  7.5 42.8 %collective-permute-start = (f32[1]{0:T(128)}, f32[1]{0:T(128)}, u32[]{:S(2)}, u32[]{:S(2)}) collective-permute-start(f32[1]{0:T(128)} %param.4), channel_id=1, source_target_pairs={{0,1},{1,2},{2,3},{3,0},{16,19},{17,16},{18,17},{19,18},{4,5},{5,6... | collective-permute-start | bytes 20 | tf_op jit(solution)/shard_map/ppermute | solution.py:27
  11.1 39.2 %collective-permute-start.1 = (f32[1]{0:T(128)}, f32[1]{0:T(128)}, u32[]{:S(2)}, u32[]{:S(2)}) collective-permute-start(f32[1]{0:T(128)} %param.4), channel_id=1, source_target_pairs={{0,3},{1,0},{2,1},{3,2},{16,17},{17,18},{18,19},{19,16},{4,7},{5,4... | collective-permute-start | bytes 20 | tf_op jit(solution)/shard_map/ppermute | solution.py:27
  11.8 0.7 copy-start.1
  12.5 1.2 %copy-start = (f32[1,256,1024]{2,1,0:T(8,128)S(1)}, f32[1,256,1024]{2,1,0:T(8,128)}, u32[]{:S(2)}) copy-start(f32[1,256,1024]{2,1,0:T(8,128)} %param.3) | copy-start | bytes 3145732
  54.6 6.7 %copy-start.2 = (f32[176,1024]{1,0:T(8,128)S(1)}, f32[176,1024]{1,0:T(8,128)}, u32[]{:S(2)}) copy-start(f32[176,1024]{1,0:T(8,128)} %get-tuple-element.24) | copy-start | bytes 2162692
  57.8 7.7 %collective-permute-start.6 = (f32[16,8,256]{2,1,0:T(8,128)S(1)}, f32[16,8,256]{2,1,0:T(8,128)S(1)}, u32[]{:S(2)}, u32[]{:S(2)}) collective-permute-start(f32[16,8,256]{2,1,0:T(8,128)S(1)} %get-tuple-element.27), channel_id=1, source_target_pairs={{0,16},{16,0},{1,17},{17,1},{2,18},{18,2},{3,19},{19,3},{4,20},{20... | collective-permute-start | bytes 393224 | tf_op jit(solution)/shard_map/ppermute | solution.py:200
  61.3 43.4 %collective-permute-start.4 = (f32[176,1024]{1,0:T(8,128)S(1)}, f32[176,1024]{1,0:T(8,128)S(1)}, u32[]{:S(2)}, u32[]{:S(2)}) collective-permute-start(f32[176,1024]{1,0:T(8,128)S(1)} %copy-done.2), channel_id=1, source_target_pairs={{0,1},{1,2},{2,3},{3,0},{16,19},{17,16},{18,17},{19,18},{4,5},{5,6... | collective-permute-start | bytes 2162696 | tf_op jit(solution)/shard_map/ppermute | solution.py:27
  66.2 6.2 %copy-start.3 = (f32[80,1024]{1,0:T(8,128)S(1)}, f32[80,1024]{1,0:T(8,128)}, u32[]{:S(2)}) copy-start(f32[80,1024]{1,0:T(8,128)} %get-tuple-element.25) | copy-start | bytes 983044
  66.2 26.8 %all-to-all-start = ((f32[32,8,256]{2,1,0:T(8,128)}), f32[32,8,256]{2,1,0:T(8,128)S(1)}, u32[]{:S(2)}, u32[]{:S(2)}) async-start(f32[32,8,256]{2,1,0:T(8,128)} %bitcast.6), calls=%async_computation | async-start | bytes 524288 | tf_op jit(solution)/shard_map/all_to_all | solution.py:212
  72.5 32.2 %collective-permute-start.5 = (f32[80,1024]{1,0:T(8,128)S(1)}, f32[80,1024]{1,0:T(8,128)S(1)}, u32[]{:S(2)}, u32[]{:S(2)}) collective-permute-start(f32[80,1024]{1,0:T(8,128)S(1)} %copy-done.3), channel_id=1, source_target_pairs={{0,1},{1,2},{2,3},{3,0},{16,19},{17,16},{18,17},{19,18},{4,5},{5,6... | collective-permute-start | bytes 983048 | tf_op jit(solution)/shard_map/ppermute | solution.py:27

commit v15 on v13

--- a/solution.py
+++ b/solution.py
@@ -15,7 +15,7 @@
 ROWS = ((1,), (1,))
 PLAIN = ((1,), (0,))
 MIB = 1 << 20
-EARLY = 128
+EARLY = 144
 
 
 def role_shift(value, step):
@@ -83,8 +83,15 @@
         copy.wait()
 
 
+def join_kernel(keep, other, copies):
+    for at in range(keep.shape[0]):
+        piece = keep[at] + other[at]
+        copies[at // 4, 0, at % 4] = piece
+        copies[at // 4, 1, at % 4] = piece
+
+
 def sum_kernel(near, gift, later, grad, mine, other, sems):
-    cuts = ((0, EARLY), (EARLY, EARLY + 64), (EARLY + 64, mine.shape[0]))
+    cuts = ((0, EARLY), (EARLY, EARLY + 56), (EARLY + 56, mine.shape[0]))
     copies = []
     for at, (low, high) in enumerate(cuts):
         rows = pl.ds(low, high - low)
@@ -174,14 +181,30 @@
     other = lax.ppermute(send, "core", [(0, 1), (1, 0)])
     gift = role_shift(gift, 1)
     later = role_shift(later, 1)
+    (mine,) = call(
+        join_kernel,
+        ((4, 2, 4, 8, v),),
+        [],
+        4,
+        1 << 20,
+        (keep, other),
+        [VMEM] * 2,
+        (VMEM,),
+    )
     parts = lax.all_to_all(
-        keep + other, ("x", "far"), split_axis=0, concat_axis=0, tiled=True
-    )
-    (copies,) = call(fold_kernel, (piece,), [], 4, 1 << 20, (parts,), [VMEM], (VMEM,))
+        mine.reshape(32, 8, v),
+        ("x", "near", "far"),
+        split_axis=0,
+        concat_axis=0,
+        tiled=True,
+    )
+    (copies,) = call(
+        fold_kernel, ((8, 8, v),), [], 4, 1 << 20, (parts,), [VMEM], (VMEM,)
+    )
     copies = lax.all_to_all(
-        copies, ("y", "near", "core"), split_axis=0, concat_axis=0, tiled=True
-    )
-    density = jnp.sum(copies.reshape(8, 16, v), axis=0)
+        copies, ("y", "core"), split_axis=0, concat_axis=0, tiled=True
+    )
+    density = jnp.sum(copies.reshape(4, 16, v), axis=0)
     (grad,) = call(
         sum_kernel,
         ((v, n),),

time: 107 us -> 102 us (0.953)
  blocking collectives: 25.8 us -> 0 us
  waiting for transfers between devices: 43 us -> 58.4 us
  starting transfers between devices: 24.8 us -> 30.1 us
    all_to_all x1 -> x0, blocking collectives: 25.8 us -> none  [body(): lax.all_to_all(keep + other, ('x', 'far'), split_axis=0, concat_axis=0, t...]
    all_to_all x1 -> x2, waiting for transfers between devices: 3.95 us -> 19.4 us  [the longest x1 16.7 us: body(): lax.all_to_all(mine.reshape(32, 8, v), ('x', 'near', 'far'), split_axis=0...]
    all_to_all x1 -> x2, starting transfers between devices: 8.14 us -> 12.3 us  [the longest x1 7.06 us: body(): lax.all_to_all(mine.reshape(32, 8, v), ('x', 'near', 'far'), split_axis=0...]
    ppermute x6, starting transfers between devices: 16.1 us -> 17.3 us  [role_shift(): return lax.ppermute(value, ('core', 'far'), pairs)]
    pallas_call x4 -> x5, Pallas kernels: 7.69 us -> 8.45 us  [call(): pl.pallas_call(kernel, out_shape=tuple((pltpu.HBM(s, F32) if spec is HBM...]
  transfers between devices with their start and end apart: 8 -> 9, of which waited for: 3 -> 4; matrix products, arithmetic and copies ran while one was open for 0% -> 0% of each run, Pallas kernels for 3% -> 4%
where the time goes in v15:
time: 102 us
  waiting for transfers between devices  58.4 us (57%)
  starting transfers between devices  30.1 us (30%)
  Pallas kernels  8.45 us (8%)
  local copies, waits for them, and re-layouts  3.1 us (3%)
  between operations  1.41 us (1%)
    ppermute x6, waiting for transfers between devices, role_shift(): return lax.ppermute(value, ('core', 'far'), pairs)  39 us
    ppermute x6, starting transfers between devices, role_shift(): return lax.ppermute(value, ('core', 'far'), pairs)  17.3 us
    all_to_all x1, waiting for transfers between devices, body(): lax.all_to_all(mine.reshape(32, 8, v), ('x', 'near', 'far'), split_axis=0...  16.7 us
    pallas_call x5, Pallas kernels, call(): pl.pallas_call(kernel, out_shape=tuple((pltpu.HBM(s, F32) if spec is HBM...  8.45 us
    all_to_all x1, starting transfers between devices, body(): lax.all_to_all(mine.reshape(32, 8, v), ('x', 'near', 'far'), split_axis=0...  7.06 us
    all_to_all x1, starting transfers between devices, body(): lax.all_to_all(copies, ('y', 'core'), split_axis=0, concat_axis=0, tiled=...  5.25 us
    all_to_all x1, waiting for transfers between devices, body(): lax.all_to_all(copies, ('y', 'core'), split_axis=0, concat_axis=0, tiled=...  2.62 us
  transfers between devices with their start and end apart: 9, of which 4 were waited for; matrix products, arithmetic and copies ran while one was open for 0% of the time, Pallas kernels for 4%

profile of v15, /device:TPU:1, one launch (start us, length us, event | category | flops | bytes accessed | tf_op | source)
XLA Modules:
  0.0 102.1 jit_solution(11399535795274337403)
XLA Ops:
  0.6 3.9 %collective-permute-start.3 = (f32[256,1024]{1,0:T(8,128)}, f32[256,1024]{1,0:T(8,128)S(1)}, u32[]{:S(2)}, u32[]{:S(2)}) collective-permute-start(f32[256,1024]{1,0:T(8,128)} %bitcast.11), channel_id=1, source_target_pairs={{0,3},{1,0},{2,1},{3,2},{16,17},{17,18},{18,19},{19,16},{4,7},{5,4... | collective-permute-start | bytes 3145736 | tf_op jit(solution)/shard_map/ppermute | solution.py:27
  4.5 3.1 %collective-permute-start.2 = (f32[256,1024]{1,0:T(8,128)}, f32[256,1024]{1,0:T(8,128)S(1)}, u32[]{:S(2)}, u32[]{:S(2)}) collective-permute-start(f32[256,1024]{1,0:T(8,128)} %bitcast.12), channel_id=1, source_target_pairs={{0,1},{1,2},{2,3},{3,0},{16,19},{17,16},{18,17},{19,18},{4,5},{5,6... | collective-permute-start | bytes 3145736 | tf_op jit(solution)/shard_map/ppermute | solution.py:27
  7.6 1.1 %collective-permute-start.1 = (f32[1]{0:T(128)}, f32[1]{0:T(128)}, u32[]{:S(2)}, u32[]{:S(2)}) collective-permute-start(f32[1]{0:T(128)} %param.4), channel_id=1, source_target_pairs={{0,3},{1,0},{2,1},{3,2},{16,17},{17,18},{18,19},{19,16},{4,7},{5,4... | collective-permute-start | bytes 20 | tf_op jit(solution)/shard_map/ppermute | solution.py:27
  8.7 2.5 %collective-permute-start = (f32[1]{0:T(128)}, f32[1]{0:T(128)}, u32[]{:S(2)}, u32[]{:S(2)}) collective-permute-start(f32[1]{0:T(128)} %param.4), channel_id=1, source_target_pairs={{0,1},{1,2},{2,3},{3,0},{16,19},{17,16},{18,17},{19,18},{4,5},{5,6... | collective-permute-start | bytes 20 | tf_op jit(solution)/shard_map/ppermute | solution.py:27
  11.9 0.0 copy-start.1
  11.9 0.7 copy-done.1
  12.6 0.0 copy-start
  12.6 1.2 %copy-done = f32[1,256,1024]{2,1,0:T(8,128)S(1)} copy-done((f32[1,256,1024]{2,1,0:T(8,128)S(1)}, f32[1,256,1024]{2,1,0:T(8,128)}, u32[]{:S(2)}) %copy-start) | copy-done | bytes 1048600
  13.8 0.3 shard_map.53
  14.1 20.9 %collective-permute-done.1 = f32[1]{0:T(128)} collective-permute-done((f32[1]{0:T(128)}, f32[1]{0:T(128)}, u32[]{:S(2)}, u32[]{:S(2)}) %collective-permute-start.1) | collective-permute-done | bytes 36 | tf_op jit(solution)/shard_map/ppermute | solution.py:27
  35.0 18.1 %collective-permute-done = f32[1]{0:T(128)} collective-permute-done((f32[1]{0:T(128)}, f32[1]{0:T(128)}, u32[]{:S(2)}, u32[]{:S(2)}) %collective-permute-start) | collective-permute-done | bytes 36 | tf_op jit(solution)/shard_map/ppermute | solution.py:27
  53.1 0.0 collective-permute-done.3.two
  53.1 0.0 collective-permute-done.2.one
  53.2 0.6 broadcast_in_dim.27.e_two
  53.8 0.6 broadcast_in_dim.26.e_one
  54.4 4.5 %shard_map.54 = (f32[16,8,256]{2,1,0:T(8,128)S(1)}, f32[16,8,256]{2,1,0:T(8,128)S(1)}, f32[144,1024]{1,0:T(8,128)}, f32[112,1024]{1,0:T(8,128)}, f32[256,1024]{1,0:T(8,128)}) custom-call(f32[8,256]{1,0:T(8,128)S(1)} %broadcast_in_dim.24.upper, f32[8,128]{1,0:T(8,128)S(1)} %broadcast_in_dim.25.e_own, f32[8,128]{1,0:T(8,128)S(1)} %broadcast_in_dim.26.e_one, ...), custom_call_target="tpu_custom_call" | custom-call | flops 2147483648 | bytes 1048576 | tf_op jit(solution)/shard_map/pallas_call | solution.py:127
  58.9 0.5 collective-permute-start.6
  59.4 3.3 %collective-permute-start.4 = (f32[144,1024]{1,0:T(8,128)}, f32[144,1024]{1,0:T(8,128)S(1)}, u32[]{:S(2)}, u32[]{:S(2)}) collective-permute-start(f32[144,1024]{1,0:T(8,128)} %get-tuple-element.14), channel_id=1, source_target_pairs={{0,1},{1,2},{2,3},{3,0},{16,19},{17,16},{18,17},{19,18},{4,5},{5,6... | collective-permute-start | bytes 1769480 | tf_op jit(solution)/shard_map/ppermute | solution.py:27
  62.7 0.0 collective-permute-done.6.other
  62.7 0.0 copy-start.2
  62.8 0.7 shard_map.56
  63.5 7.1 %all-to-all-start = ((f32[32,8,256]{2,1,0:T(8,128)}), f32[32,8,256]{2,1,0:T(8,128)S(1)}, u32[]{:S(2)}, u32[]{:S(2)}) async-start(f32[32,8,256]{2,1,0:T(8,128)} %bitcast.6), calls=%async_computation | async-start | bytes 524288 | tf_op jit(solution)/shard_map/all_to_all | solution.py:194
  70.5 0.0 copy-done.2
  70.5 3.4 %collective-permute-start.5 = (f32[112,1024]{1,0:T(8,128)S(1)}, f32[112,1024]{1,0:T(8,128)S(1)}, u32[]{:S(2)}, u32[]{:S(2)}) collective-permute-start(f32[112,1024]{1,0:T(8,128)S(1)} %copy-done.2), channel_id=1, source_target_pairs={{0,1},{1,2},{2,3},{3,0},{16,19},{17,16},{18,17},{19,18},{4,5},{5,6... | collective-permute-start | bytes 1376264 | tf_op jit(solution)/shard_map/ppermute | solution.py:27
  74.0 16.7 %all-to-all-done.pieces = f32[32,8,256]{2,1,0:T(8,128)S(1)} async-done(((f32[32,8,256]{2,1,0:T(8,128)}), f32[32,8,256]{2,1,0:T(8,128)S(1)}, u32[]{:S(2)}, u32[]{:S(2)}) %all-to-all-start) | async-done | bytes 262176 | tf_op jit(solution)/shard_map/all_to_all | solution.py:194
  90.7 0.7 shard_map.57
  91.4 5.3 %all-to-all-start.1 = ((f32[8,8,256]{2,1,0:T(8,128)}), f32[8,8,256]{2,1,0:T(8,128)S(1)}, u32[]{:S(2)}, u32[]{:S(2)}) async-start(f32[8,8,256]{2,1,0:T(8,128)} %shard_map.57), calls=%async_computation.1 | async-start | bytes 131072 | tf_op jit(solution)/shard_map/all_to_all | solution.py:204
  96.6 0.0 collective-permute-done.5.later
  96.6 0.0 collective-permute-done.4.gift
  96.6 2.2 %shard_map.55 = f32[256,1024]{1,0:T(8,128)} custom-call(f32[256,1024]{1,0:T(8,128)} %get-tuple-element.13.near, f32[144,1024]{1,0:T(8,128)S(1)} %collective-permute-done.4.gift, f32[112,1024]{1,0:T(8,128)S(1)} %collective-permute-done.5.later), custom_call_target="tpu_custom_call" | custom-call | flops 1048576 | bytes 1048576 | tf_op jit(solution)/shard_map/pallas_call | solution.py:127
  98.8 2.6 %all-to-all-done.1 = f32[8,8,256]{2,1,0:T(8,128)S(1)} async-done(((f32[8,8,256]{2,1,0:T(8,128)}), f32[8,8,256]{2,1,0:T(8,128)S(1)}, u32[]{:S(2)}, u32[]{:S(2)}) %all-to-all-start.1) | async-done | bytes 65568 | tf_op jit(solution)/shard_map/all_to_all | solution.py:204
  101.5 0.6 bitcast_reduce_fusion
  (2 shorter events, 0.0 us)
Async XLA Ops:
  0.6 52.5 %collective-permute-start.3 = (f32[256,1024]{1,0:T(8,128)}, f32[256,1024]{1,0:T(8,128)S(1)}, u32[]{:S(2)}, u32[]{:S(2)}) collective-permute-start(f32[256,1024]{1,0:T(8,128)} %bitcast.11), channel_id=1, source_target_pairs={{0,3},{1,0},{2,1},{3,2},{16,17},{17,18},{18,19},{19,16},{4,7},{5,4... | collective-permute-start | bytes 3145736 | tf_op jit(solution)/shard_map/ppermute | solution.py:27
  4.5 48.6 %collective-permute-start.2 = (f32[256,1024]{1,0:T(8,128)}, f32[256,1024]{1,0:T(8,128)S(1)}, u32[]{:S(2)}, u32[]{:S(2)}) collective-permute-start(f32[256,1024]{1,0:T(8,128)} %bitcast.12), channel_id=1, source_target_pairs={{0,1},{1,2},{2,3},{3,0},{16,19},{17,16},{18,17},{19,18},{4,5},{5,6... | collective-permute-start | bytes 3145736 | tf_op jit(solution)/shard_map/ppermute | solution.py:27
  7.6 27.4 %collective-permute-start.1 = (f32[1]{0:T(128)}, f32[1]{0:T(128)}, u32[]{:S(2)}, u32[]{:S(2)}) collective-permute-start(f32[1]{0:T(128)} %param.4), channel_id=1, source_target_pairs={{0,3},{1,0},{2,1},{3,2},{16,17},{17,18},{18,19},{19,16},{4,7},{5,4... | collective-permute-start | bytes 20 | tf_op jit(solution)/shard_map/ppermute | solution.py:27
  8.7 44.4 %collective-permute-start = (f32[1]{0:T(128)}, f32[1]{0:T(128)}, u32[]{:S(2)}, u32[]{:S(2)}) collective-permute-start(f32[1]{0:T(128)} %param.4), channel_id=1, source_target_pairs={{0,1},{1,2},{2,3},{3,0},{16,19},{17,16},{18,17},{19,18},{4,5},{5,6... | collective-permute-start | bytes 20 | tf_op jit(solution)/shard_map/ppermute | solution.py:27
  11.9 0.7 copy-start.1
  12.6 1.2 %copy-start = (f32[1,256,1024]{2,1,0:T(8,128)S(1)}, f32[1,256,1024]{2,1,0:T(8,128)}, u32[]{:S(2)}) copy-start(f32[1,256,1024]{2,1,0:T(8,128)} %param.3) | copy-start | bytes 3145732
  58.9 3.8 %collective-permute-start.6 = (f32[16,8,256]{2,1,0:T(8,128)S(1)}, f32[16,8,256]{2,1,0:T(8,128)S(1)}, u32[]{:S(2)}, u32[]{:S(2)}) collective-permute-start(f32[16,8,256]{2,1,0:T(8,128)S(1)} %get-tuple-element.17), channel_id=1, source_target_pairs={{0,16},{16,0},{1,17},{17,1},{2,18},{18,2},{3,19},{19,3},{4,20},{20... | collective-permute-start | bytes 393224 | tf_op jit(solution)/shard_map/ppermute | solution.py:181
  59.4 37.2 %collective-permute-start.4 = (f32[144,1024]{1,0:T(8,128)}, f32[144,1024]{1,0:T(8,128)S(1)}, u32[]{:S(2)}, u32[]{:S(2)}) collective-permute-start(f32[144,1024]{1,0:T(8,128)} %get-tuple-element.14), channel_id=1, source_target_pairs={{0,1},{1,2},{2,3},{3,0},{16,19},{17,16},{18,17},{19,18},{4,5},{5,6... | collective-permute-start | bytes 1769480 | tf_op jit(solution)/shard_map/ppermute | solution.py:27
  62.7 7.8 %copy-start.2 = (f32[112,1024]{1,0:T(8,128)S(1)}, f32[112,1024]{1,0:T(8,128)}, u32[]{:S(2)}) copy-start(f32[112,1024]{1,0:T(8,128)} %get-tuple-element.15) | copy-start | bytes 1376260
  63.5 27.2 %all-to-all-start = ((f32[32,8,256]{2,1,0:T(8,128)}), f32[32,8,256]{2,1,0:T(8,128)S(1)}, u32[]{:S(2)}, u32[]{:S(2)}) async-start(f32[32,8,256]{2,1,0:T(8,128)} %bitcast.6), calls=%async_computation | async-start | bytes 524288 | tf_op jit(solution)/shard_map/all_to_all | solution.py:194
  70.5 26.1 %collective-permute-start.5 = (f32[112,1024]{1,0:T(8,128)S(1)}, f32[112,1024]{1,0:T(8,128)S(1)}, u32[]{:S(2)}, u32[]{:S(2)}) collective-permute-start(f32[112,1024]{1,0:T(8,128)S(1)} %copy-done.2), channel_id=1, source_target_pairs={{0,1},{1,2},{2,3},{3,0},{16,19},{17,16},{18,17},{19,18},{4,5},{5,6... | collective-permute-start | bytes 1376264 | tf_op jit(solution)/shard_map/ppermute | solution.py:27
  91.4 10.1 %all-to-all-start.1 = ((f32[8,8,256]{2,1,0:T(8,128)}), f32[8,8,256]{2,1,0:T(8,128)S(1)}, u32[]{:S(2)}, u32[]{:S(2)}) async-start(f32[8,8,256]{2,1,0:T(8,128)} %shard_map.57), calls=%async_computation.1 | async-start | bytes 131072 | tf_op jit(solution)/shard_map/all_to_all | solution.py:204

commit v16 on v10

--- a/solution.py
+++ b/solution.py
@@ -49,20 +49,17 @@
 
 
 def pair_kernel(upper, e_own, e_one, e_two, pairs, oh, ol, one, two, *refs):
-    keep, send, gift, near, buf, total, dens, sems = refs
+    keep, send, gift, buf, dens, sem = refs
     o, a, b = (oh[...], ol[...]), split(one[...]), split(two[...])
     mine, first, second = e_own[0:1, 0:1], e_one[0:1, 0:1], e_two[0:1, 0:1]
     t = mm(b, a, ROWS) / (first + second - pairs[...])
     s = spin(t)
     buf[...] = mm(s, a, PLAIN)
-    out = [pltpu.make_async_copy(buf, gift, sems.at[0])]
-    out[0].start()
+    out = pltpu.make_async_copy(buf, gift, sem)
+    out.start()
     t_one = mm(o, a, ROWS) / (mine + first - pairs[...])
     t_two = mm(o, b, ROWS) / (mine + second - pairs[...])
     s_one, s_two = spin(t_one), spin(t_two)
-    total[...] = mm(s_one, a, PLAIN) + mm(s_two, b, PLAIN)
-    out.append(pltpu.make_async_copy(total, near, sems.at[1]))
-    out[1].start()
     dens[...] = (
         mm(split(t), s, ROWS)
         + mm(split(t_one), s_one, ROWS)
@@ -74,8 +71,18 @@
         high = dens[at * 16 + 8 : at * 16 + 16, :]
         keep[at] = jnp.where(odd, high, low)
         send[at] = jnp.where(odd, low, high)
-    for copy in out:
-        copy.wait()
+    out.wait()
+
+
+def near_kernel(e_own, e_one, e_two, pairs, oh, ol, one, two, near, total, sem):
+    o, a, b = (oh[...], ol[...]), split(one[...]), split(two[...])
+    mine, first, second = e_own[0:1, 0:1], e_one[0:1, 0:1], e_two[0:1, 0:1]
+    s_one = spin(mm(o, a, ROWS) / (mine + first - pairs[...]))
+    s_two = spin(mm(o, b, ROWS) / (mine + second - pairs[...]))
+    total[...] = mm(s_one, a, PLAIN) + mm(s_two, b, PLAIN)
+    out = pltpu.make_async_copy(total, near, sem)
+    out.start()
+    out.wait()
 
 
 def join_kernel(keep, other, copies):
@@ -165,15 +172,15 @@
     )
     piece = (16, 8, v)
     full = pltpu.VMEM((v, n), F32)
-    keep, send, gift, near = call(
+    keep, send, gift = call(
         pair_kernel,
-        (piece, piece, (v, n), (v, n)),
-        [full] * 2 + [pltpu.VMEM((v, v), F32), pltpu.SemaphoreType.DMA((2,))],
+        (piece, piece, (v, n)),
+        [full, pltpu.VMEM((v, v), F32), pltpu.SemaphoreType.DMA],
         14,
         1 << 31,
         (upper, s_own, s_one, s_two, pairs, oh, ol, one, two),
         [VMEM] * 9,
-        (VMEM, VMEM, HBM, HBM),
+        (VMEM, VMEM, HBM),
     )
     other = lax.ppermute(send, "core", [(0, 1), (1, 0)])
     gift = role_shift(gift, 1)
@@ -188,6 +195,16 @@
         copies, ("near", "far", "core"), split_axis=0, concat_axis=0, tiled=True
     )
     density = jnp.sum(copies.reshape(8, 16, v), axis=0)
+    (near,) = call(
+        near_kernel,
+        ((v, n),),
+        [full, pltpu.SemaphoreType.DMA],
+        14,
+        1 << 31,
+        (s_own, s_one, s_two, pairs, oh, ol, one, two),
+        [VMEM] * 8,
+        (HBM,),
+    )
     (grad,) = call(
         sum_kernel,
         ((v, n),),

time: 99.9 us -> 99.5 us (level)
  blocking collectives: 34.1 us -> 17.5 us
  starting transfers between devices: 13.1 us -> 23.4 us
  Pallas kernels: 6.96 us -> 9.35 us
  local copies, waits for them, and re-layouts: 3.15 us -> 5.25 us
  waiting for transfers between devices: 40.3 us -> 41.5 us
    all_to_all x1 -> x0, blocking collectives: 15.1 us -> none  [body(): lax.all_to_all(copies, ('near', 'far', 'core'), split_axis=0, concat_axis...]
    all_to_all x0 -> x1, starting transfers between devices: none -> 5.55 us  [body(): lax.all_to_all(copies, ('near', 'far', 'core'), split_axis=0, concat_axis...]
    ppermute x5, starting transfers between devices: 13.1 us -> 17.8 us  [role_shift(): return lax.ppermute(value, ('core', 'far'), pairs)]
    all_to_all x0 -> x1, waiting for transfers between devices: none -> 3.96 us  [body(): lax.all_to_all(copies, ('near', 'far', 'core'), split_axis=0, concat_axis...]
    ppermute x5, waiting for transfers between devices: 39 us -> 36.2 us  [role_shift(): return lax.ppermute(value, ('core', 'far'), pairs)]
    pallas_call x5 -> x6, Pallas kernels: 6.96 us -> 9.35 us  [call(): pl.pallas_call(kernel, out_shape=tuple((pltpu.HBM(s, F32) if spec is HBM...]
    unnamed x4 -> x12, local copies, waits for them, and re-layouts: 1.9 us -> 3.98 us
    all_to_all x1, blocking collectives: 19 us -> 17.5 us  [body(): lax.all_to_all(mine.reshape(16, 32, v), ('y', 'x'), split_axis=0, concat_...]
  transfers between devices with their start and end apart: 6 -> 7, of which waited for: 3 -> 3; matrix products, arithmetic and copies ran while one was open for 1% -> 1% of each run, Pallas kernels for 0% -> 4%
where the time goes in v16:
time: 99.5 us; the launch traced here: 99.1 us
  waiting for transfers between devices  41.5 us (42%)
  starting transfers between devices  23.4 us (24%)
  blocking collectives  17.5 us (18%)
  Pallas kernels  9.35 us (9%)
  local copies, waits for them, and re-layouts  5.25 us (5%)
  between operations  1.47 us (1%)
    ppermute x5, waiting for transfers between devices, role_shift(): return lax.ppermute(value, ('core', 'far'), pairs)  36.2 us
    ppermute x5, starting transfers between devices, role_shift(): return lax.ppermute(value, ('core', 'far'), pairs)  17.8 us
    all_to_all x1, blocking collectives, body(): lax.all_to_all(mine.reshape(16, 32, v), ('y', 'x'), split_axis=0, concat_...  17.5 us
    pallas_call x6, Pallas kernels, call(): pl.pallas_call(kernel, out_shape=tuple((pltpu.HBM(s, F32) if spec is HBM...  9.35 us
    all_to_all x1, starting transfers between devices, body(): lax.all_to_all(copies, ('near', 'far', 'core'), split_axis=0, concat_axis...  5.55 us
    unnamed x12, local copies, waits for them, and re-layouts  3.98 us
    all_to_all x1, waiting for transfers between devices, body(): lax.all_to_all(copies, ('near', 'far', 'core'), split_axis=0, concat_axis...  3.96 us
  transfers between devices with their start and end apart: 7, of which 3 were waited for; matrix products, arithmetic and copies ran while one was open for 1% of the time, Pallas kernels for 4%

profile of v16, /device:TPU:1, one launch (start us, length us, event | category | flops | bytes accessed | tf_op | source)
XLA Modules:
  0.0 99.1 jit_solution(11046691052991666860)
XLA Ops:
  0.6 6.9 %collective-permute-start.2 = (f32[256,1024]{1,0:T(8,128)}, f32[256,1024]{1,0:T(8,128)S(1)}, u32[]{:S(2)}, u32[]{:S(2)}) collective-permute-start(f32[256,1024]{1,0:T(8,128)} %bitcast.12), channel_id=1, source_target_pairs={{0,1},{1,2},{2,3},{3,0},{16,19},{17,16},{18,17},{19,18},{4,5},{5,6... | collective-permute-start | bytes 3145736 | tf_op jit(solution)/shard_map/ppermute | solution.py:26
  7.5 0.0 collective-permute-start.3
  7.5 3.6 %collective-permute-start = (f32[1]{0:T(128)}, f32[1]{0:T(128)}, u32[]{:S(2)}, u32[]{:S(2)}) collective-permute-start(f32[1]{0:T(128)} %param.4), channel_id=1, source_target_pairs={{0,1},{1,2},{2,3},{3,0},{16,19},{17,16},{18,17},{19,18},{4,5},{5,6... | collective-permute-start | bytes 20 | tf_op jit(solution)/shard_map/ppermute | solution.py:26
  11.1 0.0 collective-permute-start.1
  11.8 0.0 copy-start.1
  11.9 0.7 copy-done.1
  12.5 1.2 %copy-done = f32[1,256,1024]{2,1,0:T(8,128)S(1)} copy-done((f32[1,256,1024]{2,1,0:T(8,128)S(1)}, f32[1,256,1024]{2,1,0:T(8,128)}, u32[]{:S(2)}) %copy-start) | copy-done | bytes 1048600
  13.8 0.3 shard_map.53
  14.1 0.0 copy-start.2
  14.1 0.0 copy-start.4
  14.1 36.2 %collective-permute-done = f32[1]{0:T(128)} collective-permute-done((f32[1]{0:T(128)}, f32[1]{0:T(128)}, u32[]{:S(2)}, u32[]{:S(2)}) %collective-permute-start) | collective-permute-done | bytes 36 | tf_op jit(solution)/shard_map/ppermute | solution.py:26
  50.3 0.0 collective-permute-done.1
  50.3 0.0 collective-permute-done.2.one
  50.3 0.0 collective-permute-done.3.two
  50.3 0.6 broadcast_in_dim.25.e_one
  50.9 0.7 broadcast_in_dim.26.e_two
  51.6 3.2 %shard_map.55 = (f32[16,8,256]{2,1,0:T(8,128)S(1)}, f32[16,8,256]{2,1,0:T(8,128)S(1)}, f32[256,1024]{1,0:T(8,128)}) custom-call(f32[8,256]{1,0:T(8,128)S(1)} %broadcast_in_dim.28.upper, f32[8,128]{1,0:T(8,128)S(1)} %broadcast_in_dim.24.e_own, f32[8,128]{1,0:T(8,128)S(1)} %broadcast_in_dim.25.e_one, f32[8,128]{1,0:T(8,128)S(1)} %broadcast_in_dim.26.e_two, ...), custom_call_target="tpu_custom_call" | custom-call | flops 2147483648 | bytes 1048576 | tf_op jit(solution)/shard_map/pallas_call | solution.py:131
  54.8 0.0 copy-done.2
  54.9 0.0 copy-done.4
  54.9 7.3 %collective-permute-start.4 = (f32[256,1024]{1,0:T(8,128)}, f32[256,1024]{1,0:T(8,128)S(1)}, u32[]{:S(2)}, u32[]{:S(2)}) collective-permute-start(f32[256,1024]{1,0:T(8,128)} %get-tuple-element.11), channel_id=1, source_target_pairs={{0,1},{1,2},{2,3},{3,0},{16,19},{17,16},{18,17},{19,18},{4,5},{5,6... | collective-permute-start | bytes 3145736 | tf_op jit(solution)/shard_map/ppermute | solution.py:26
  62.2 0.0 collective-permute-start.5
  62.2 1.3 %collective-permute-done.5.other = f32[16,8,256]{2,1,0:T(8,128)S(1)} collective-permute-done((f32[16,8,256]{2,1,0:T(8,128)S(1)}, f32[16,8,256]{2,1,0:T(8,128)S(1)}, u32[]{:S(2)}, u32[]{:S(2)}) %collective-permute-start.5) | collective-permute-done | bytes 131104 | tf_op jit(solution)/shard_map/ppermute | solution.py:185
  63.6 17.5 %all_to_all.10.pieces = f32[16,32,256]{2,1,0:T(8,128)S(1)} all-to-all(f32[16,32,256]{2,1,0:T(8,128)S(1)} %bitcast.11), channel_id=1, replica_groups=mesh['y'=4,'near'=2,'core'=2,'x'=4,'far'=4] {'y','x'}, dimensions={0} | all-to-all | bytes 1048576 | tf_op jit(solution)/shard_map/all_to_all | solution.py:190
  81.0 0.7 shard_map.58
  81.7 5.5 %all-to-all-start.1 = ((f32[16,8,256]{2,1,0:T(8,128)}), f32[16,8,256]{2,1,0:T(8,128)S(1)}, u32[]{:S(2)}, u32[]{:S(2)}) async-start(f32[16,8,256]{2,1,0:T(8,128)} %shard_map.58), calls=%async_computation.1 | async-start | bytes 262144 | tf_op jit(solution)/shard_map/all_to_all | solution.py:194
  87.3 1.0 %copy-done.3 = bf16[256,1024]{1,0:T(8,128)(2,1)S(1)} copy-done((bf16[256,1024]{1,0:T(8,128)(2,1)S(1)}, bf16[256,1024]{1,0:T(8,128)(2,1)}, u32[]{:S(2)}) %copy-start.3) | copy-done | bytes 524312
  88.3 1.0 %copy-done.5 = bf16[256,1024]{1,0:T(8,128)(2,1)S(1)} copy-done((bf16[256,1024]{1,0:T(8,128)(2,1)S(1)}, bf16[256,1024]{1,0:T(8,128)(2,1)}, u32[]{:S(2)}) %copy-start.5) | copy-done | bytes 524312
  89.3 3.1 %shard_map.54.near = f32[256,1024]{1,0:T(8,128)} custom-call(f32[8,128]{1,0:T(8,128)S(1)} %broadcast_in_dim.24.e_own, f32[8,128]{1,0:T(8,128)S(1)} %broadcast_in_dim.25.e_one, f32[8,128]{1,0:T(8,128)S(1)} %broadcast_in_dim.26.e_two, f32[256,256]{1,0:T(8,128)S(1)} %get-tuple-element.8.pairs, bf16[256,1024]{1,0:T(8,128)(2,1)S(1)} %copy-done.3, ...), custom_call_target="tpu_custom_call" | custom-call | flops 2147483648 | bytes 1048576 | tf_op jit(solution)/shard_map/pallas_call | solution.py:131
  92.4 4.0 %all-to-all-done.1 = f32[16,8,256]{2,1,0:T(8,128)S(1)} async-done(((f32[16,8,256]{2,1,0:T(8,128)}), f32[16,8,256]{2,1,0:T(8,128)S(1)}, u32[]{:S(2)}, u32[]{:S(2)}) %all-to-all-start.1) | async-done | bytes 131104 | tf_op jit(solution)/shard_map/all_to_all | solution.py:194
  96.4 0.6 bitcast_reduce_fusion
  97.0 0.0 collective-permute-done.4.gift
  97.0 2.0 %shard_map.56 = f32[256,1024]{1,0:T(8,128)} custom-call(f32[256,1024]{1,0:T(8,128)} %shard_map.54.near, f32[256,1024]{1,0:T(8,128)S(1)} %collective-permute-done.4.gift), custom_call_target="tpu_custom_call" | custom-call | flops 1048576 | bytes 1048576 | tf_op jit(solution)/shard_map/pallas_call | solution.py:131
  (6 shorter events, 0.0 us)
Async XLA Ops:
  0.6 49.7 %collective-permute-start.2 = (f32[256,1024]{1,0:T(8,128)}, f32[256,1024]{1,0:T(8,128)S(1)}, u32[]{:S(2)}, u32[]{:S(2)}) collective-permute-start(f32[256,1024]{1,0:T(8,128)} %bitcast.12), channel_id=1, source_target_pairs={{0,1},{1,2},{2,3},{3,0},{16,19},{17,16},{18,17},{19,18},{4,5},{5,6... | collective-permute-start | bytes 3145736 | tf_op jit(solution)/shard_map/ppermute | solution.py:26
  7.5 42.8 %collective-permute-start.3 = (f32[256,1024]{1,0:T(8,128)}, f32[256,1024]{1,0:T(8,128)S(1)}, u32[]{:S(2)}, u32[]{:S(2)}) collective-permute-start(f32[256,1024]{1,0:T(8,128)} %bitcast.13), channel_id=1, source_target_pairs={{0,3},{1,0},{2,1},{3,2},{16,17},{17,18},{18,19},{19,16},{4,7},{5,4... | collective-permute-start | bytes 3145736 | tf_op jit(solution)/shard_map/ppermute | solution.py:26
  7.5 42.8 %collective-permute-start = (f32[1]{0:T(128)}, f32[1]{0:T(128)}, u32[]{:S(2)}, u32[]{:S(2)}) collective-permute-start(f32[1]{0:T(128)} %param.4), channel_id=1, source_target_pairs={{0,1},{1,2},{2,3},{3,0},{16,19},{17,16},{18,17},{19,18},{4,5},{5,6... | collective-permute-start | bytes 20 | tf_op jit(solution)/shard_map/ppermute | solution.py:26
  11.1 39.2 %collective-permute-start.1 = (f32[1]{0:T(128)}, f32[1]{0:T(128)}, u32[]{:S(2)}, u32[]{:S(2)}) collective-permute-start(f32[1]{0:T(128)} %param.4), channel_id=1, source_target_pairs={{0,3},{1,0},{2,1},{3,2},{16,17},{17,18},{18,19},{19,16},{4,7},{5,4... | collective-permute-start | bytes 20 | tf_op jit(solution)/shard_map/ppermute | solution.py:26
  11.8 0.7 copy-start.1
  12.5 1.2 %copy-start = (f32[1,256,1024]{2,1,0:T(8,128)S(1)}, f32[1,256,1024]{2,1,0:T(8,128)}, u32[]{:S(2)}) copy-start(f32[1,256,1024]{2,1,0:T(8,128)} %param.3) | copy-start | bytes 3145732
  14.1 40.8 %copy-start.2 = (bf16[256,1024]{1,0:T(8,128)(2,1)}, bf16[256,1024]{1,0:T(8,128)(2,1)S(1)}, u32[]{:S(2)}) copy-start(bf16[256,1024]{1,0:T(8,128)(2,1)S(1)} %get-tuple-element.9.oh) | copy-start | bytes 1572868
  14.1 40.8 %copy-start.4 = (bf16[256,1024]{1,0:T(8,128)(2,1)}, bf16[256,1024]{1,0:T(8,128)(2,1)S(1)}, u32[]{:S(2)}) copy-start(bf16[256,1024]{1,0:T(8,128)(2,1)S(1)} %get-tuple-element.10.ol) | copy-start | bytes 1572868
  54.9 42.1 %collective-permute-start.4 = (f32[256,1024]{1,0:T(8,128)}, f32[256,1024]{1,0:T(8,128)S(1)}, u32[]{:S(2)}, u32[]{:S(2)}) collective-permute-start(f32[256,1024]{1,0:T(8,128)} %get-tuple-element.11), channel_id=1, source_target_pairs={{0,1},{1,2},{2,3},{3,0},{16,19},{17,16},{18,17},{19,18},{4,5},{5,6... | collective-permute-start | bytes 3145736 | tf_op jit(solution)/shard_map/ppermute | solution.py:26
  62.2 1.3 %collective-permute-start.5 = (f32[16,8,256]{2,1,0:T(8,128)S(1)}, f32[16,8,256]{2,1,0:T(8,128)S(1)}, u32[]{:S(2)}, u32[]{:S(2)}) collective-permute-start(f32[16,8,256]{2,1,0:T(8,128)S(1)} %get-tuple-element.13), channel_id=1, source_target_pairs={{0,16},{16,0},{1,17},{17,1},{2,18},{18,2},{3,19},{19,3},{4,20},{20... | collective-permute-start | bytes 393224 | tf_op jit(solution)/shard_map/ppermute | solution.py:185
  81.7 14.7 %all-to-all-start.1 = ((f32[16,8,256]{2,1,0:T(8,128)}), f32[16,8,256]{2,1,0:T(8,128)S(1)}, u32[]{:S(2)}, u32[]{:S(2)}) async-start(f32[16,8,256]{2,1,0:T(8,128)} %shard_map.58), calls=%async_computation.1 | async-start | bytes 262144 | tf_op jit(solution)/shard_map/all_to_all | solution.py:194
  87.3 1.0 %copy-start.3 = (bf16[256,1024]{1,0:T(8,128)(2,1)S(1)}, bf16[256,1024]{1,0:T(8,128)(2,1)}, u32[]{:S(2)}) copy-start(bf16[256,1024]{1,0:T(8,128)(2,1)} %copy-done.2) | copy-start | bytes 1572868
  88.3 1.0 %copy-start.5 = (bf16[256,1024]{1,0:T(8,128)(2,1)S(1)}, bf16[256,1024]{1,0:T(8,128)(2,1)}, u32[]{:S(2)}) copy-start(bf16[256,1024]{1,0:T(8,128)(2,1)} %copy-done.4) | copy-start | bytes 1572868

commit v17 on v10

--- a/solution.py
+++ b/solution.py
@@ -38,7 +38,9 @@
     return dot(a[0], b[0]) + (dot(a[0], b[1]) + dot(a[1], b[0]))
 
 
-def prepare_kernel(eps_vir, own, pairs, high, low):
+def prepare_kernel(eps_vir, own, pairs, high, low, mask):
+    row = lax.broadcasted_iota(jnp.int32, mask.shape, 0)
+    mask[...] = jnp.where(row < 4, 1.0, 0.0)
     row = jnp.broadcast_to(eps_vir[...], pairs.shape)
     pairs[...] = row + row.T
     high[...], low[...] = split(own[...])
@@ -48,10 +50,10 @@
     return split(2.0 * t - t.T)
 
 
-def pair_kernel(upper, e_own, e_one, e_two, pairs, oh, ol, one, two, *refs):
+def pair_kernel(upper, e_own, both, pairs, oh, ol, one, two, *refs):
     keep, send, gift, near, buf, total, dens, sems = refs
     o, a, b = (oh[...], ol[...]), split(one[...]), split(two[...])
-    mine, first, second = e_own[0:1, 0:1], e_one[0:1, 0:1], e_two[0:1, 0:1]
+    mine, first, second = e_own[0:1, 0:1], both[0:1, 0:1], both[4:5, 0:1]
     t = mm(b, a, ROWS) / (first + second - pairs[...])
     s = spin(t)
     buf[...] = mm(s, a, PLAIN)
@@ -151,18 +153,19 @@
     e_one = role_shift(eps_occ, 1)
     e_two = role_shift(eps_occ, -1)
     tile = (8, 128)
-    s_one, s_two, s_own = (jnp.broadcast_to(e, tile) for e in (e_one, e_two, eps_occ))
+    s_own = jnp.broadcast_to(eps_occ, tile)
     upper = jnp.broadcast_to(lax.axis_index("core").astype(F32), (8, v))
-    pairs, oh, ol = call(
+    pairs, oh, ol, mask = call(
         prepare_kernel,
-        ((v, v), (v, n), (v, n)),
+        ((v, v), (v, n), (v, n), (8, 128)),
         [],
         8,
         1 << 20,
         (eps_vir[None], own),
         [VMEM] * 2,
-        (VMEM,) * 3,
-    )
+        (VMEM,) * 4,
+    )
+    both = e_one * mask + e_two * (1.0 - mask)
     piece = (16, 8, v)
     full = pltpu.VMEM((v, n), F32)
     keep, send, gift, near = call(
@@ -171,8 +174,8 @@
         [full] * 2 + [pltpu.VMEM((v, v), F32), pltpu.SemaphoreType.DMA((2,))],
         14,
         1 << 31,
-        (upper, s_own, s_one, s_two, pairs, oh, ol, one, two),
-        [VMEM] * 9,
+        (upper, s_own, both, pairs, oh, ol, one, two),
+        [VMEM] * 8,
         (VMEM, VMEM, HBM, HBM),
     )
     other = lax.ppermute(send, "core", [(0, 1), (1, 0)])

time: 99.9 us -> 99.9 us (level)
  local copies, waits for them, and re-layouts: 3.15 us -> 1.9 us
  other arithmetic: 0.62 us -> 1.86 us
    add x0 -> x1, other arithmetic: none -> 1.24 us  [body(): both = e_one * mask + e_two * (1.0 - mask)]
    broadcast_in_dim x3 -> x1, local copies, waits for them, and re-layouts: 1.24 us -> 0.01 us  [body(): s_own = jnp.broadcast_to(eps_occ, tile)]
  transfers between devices with their start and end apart: 6 -> 6, of which waited for: 3 -> 3; matrix products, arithmetic and copies ran while one was open for 1% -> 2% of each run, Pallas kernels for 0% -> 0%
where the time goes in v17:
time: 99.9 us; the launch traced here: 99.7 us
  waiting for transfers between devices  40.4 us (40%)
  blocking collectives  34.1 us (34%)
  starting transfers between devices  13 us (13%)
  Pallas kernels  6.97 us (7%)
  local copies, waits for them, and re-layouts  1.9 us (2%)
  other arithmetic  1.86 us (2%)
  between operations  1.39 us (1%)
    ppermute x5, waiting for transfers between devices, role_shift(): return lax.ppermute(value, ('core', 'far'), pairs)  39.1 us
    all_to_all x1, blocking collectives, body(): lax.all_to_all(mine.reshape(16, 32, v), ('y', 'x'), split_axis=0, concat_...  19 us
    all_to_all x1, blocking collectives, body(): lax.all_to_all(copies, ('near', 'far', 'core'), split_axis=0, concat_axis...  15.1 us
    ppermute x5, starting transfers between devices, role_shift(): return lax.ppermute(value, ('core', 'far'), pairs)  13 us
    pallas_call x5, Pallas kernels, call(): pl.pallas_call(kernel, out_shape=tuple((pltpu.HBM(s, F32) if spec is HBM...  6.97 us
  transfers between devices with their start and end apart: 6, of which 3 were waited for; matrix products, arithmetic and copies ran while one was open for 2% of the time, Pallas kernels for 0%

profile of v17, /device:TPU:1, one launch (start us, length us, event | category | flops | bytes accessed | tf_op | source)
XLA Modules:
  0.0 99.7 jit_solution(5914460980403009138)
XLA Ops:
  0.6 3.9 %collective-permute-start.3 = (f32[256,1024]{1,0:T(8,128)}, f32[256,1024]{1,0:T(8,128)S(1)}, u32[]{:S(2)}, u32[]{:S(2)}) collective-permute-start(f32[256,1024]{1,0:T(8,128)} %bitcast.12), channel_id=1, source_target_pairs={{0,3},{1,0},{2,1},{3,2},{16,17},{17,18},{18,19},{19,16},{4,7},{5,4... | collective-permute-start | bytes 3145736 | tf_op jit(solution)/shard_map/ppermute | solution.py:26
  4.5 3.1 %collective-permute-start.2 = (f32[256,1024]{1,0:T(8,128)}, f32[256,1024]{1,0:T(8,128)S(1)}, u32[]{:S(2)}, u32[]{:S(2)}) collective-permute-start(f32[256,1024]{1,0:T(8,128)} %bitcast.13), channel_id=1, source_target_pairs={{0,1},{1,2},{2,3},{3,0},{16,19},{17,16},{18,17},{19,18},{4,5},{5,6... | collective-permute-start | bytes 3145736 | tf_op jit(solution)/shard_map/ppermute | solution.py:26
  7.6 1.1 %collective-permute-start.1 = (f32[1]{0:T(128)}, f32[1]{0:T(128)}, u32[]{:S(2)}, u32[]{:S(2)}) collective-permute-start(f32[1]{0:T(128)} %param.4), channel_id=1, source_target_pairs={{0,3},{1,0},{2,1},{3,2},{16,17},{17,18},{18,19},{19,16},{4,7},{5,4... | collective-permute-start | bytes 20 | tf_op jit(solution)/shard_map/ppermute | solution.py:26
  8.7 2.5 %collective-permute-start = (f32[1]{0:T(128)}, f32[1]{0:T(128)}, u32[]{:S(2)}, u32[]{:S(2)}) collective-permute-start(f32[1]{0:T(128)} %param.4), channel_id=1, source_target_pairs={{0,1},{1,2},{2,3},{3,0},{16,19},{17,16},{18,17},{19,18},{4,5},{5,6... | collective-permute-start | bytes 20 | tf_op jit(solution)/shard_map/ppermute | solution.py:26
  11.9 0.0 copy-start.1
  11.9 0.7 copy-done.1
  12.6 0.0 copy-start
  12.6 1.2 %copy-done = f32[1,256,1024]{2,1,0:T(8,128)S(1)} copy-done((f32[1,256,1024]{2,1,0:T(8,128)S(1)}, f32[1,256,1024]{2,1,0:T(8,128)}, u32[]{:S(2)}) %copy-start) | copy-done | bytes 1048600
  13.8 0.3 shard_map.53
  14.1 20.9 %collective-permute-done.1 = f32[1]{0:T(128)} collective-permute-done((f32[1]{0:T(128)}, f32[1]{0:T(128)}, u32[]{:S(2)}, u32[]{:S(2)}) %collective-permute-start.1) | collective-permute-done | bytes 36 | tf_op jit(solution)/shard_map/ppermute | solution.py:26
  35.0 18.2 %collective-permute-done = f32[1]{0:T(128)} collective-permute-done((f32[1]{0:T(128)}, f32[1]{0:T(128)}, u32[]{:S(2)}, u32[]{:S(2)}) %collective-permute-start) | collective-permute-done | bytes 36 | tf_op jit(solution)/shard_map/ppermute | solution.py:26
  53.2 1.2 %multiply_add_fusion.both = f32[8,128]{1,0:T(8,128)S(1)} fusion(f32[8,128]{1,0:T(8,128)S(1)} %get-tuple-element.10, f32[]{:T(128)} %bitcast.4, f32[]{:T(128)} %bitcast.1), kind=kLoop, calls=%fused_computation.1 | loop fusion | flops 4096 | bytes 8200 | tf_op jit(solution)/shard_map/add | solution.py:168
  54.5 0.0 collective-permute-done.3.two
  54.5 0.0 collective-permute-done.2.one
  54.5 4.5 %shard_map.54 = (f32[16,8,256]{2,1,0:T(8,128)S(1)}, f32[16,8,256]{2,1,0:T(8,128)S(1)}, f32[256,1024]{1,0:T(8,128)}, f32[256,1024]{1,0:T(8,128)}) custom-call(f32[8,256]{1,0:T(8,128)S(1)} %broadcast_in_dim.16.upper, f32[8,128]{1,0:T(8,128)S(1)} %broadcast_in_dim.17.e_own, f32[8,128]{1,0:T(8,128)S(1)} %multiply_add_fusion.both, ...), custom_call_target="tpu_custom_call" | custom-call | flops 2147483648 | bytes 1048576 | tf_op jit(solution)/shard_map/pallas_call | solution.py:126
  59.1 2.4 %collective-permute-start.4 = (f32[256,1024]{1,0:T(8,128)}, f32[256,1024]{1,0:T(8,128)S(1)}, u32[]{:S(2)}, u32[]{:S(2)}) collective-permute-start(f32[256,1024]{1,0:T(8,128)} %get-tuple-element.15), channel_id=1, source_target_pairs={{0,1},{1,2},{2,3},{3,0},{16,19},{17,16},{18,17},{19,18},{4,5},{5,6... | collective-permute-start | bytes 3145736 | tf_op jit(solution)/shard_map/ppermute | solution.py:26
  61.4 0.0 collective-permute-start.5
  61.4 1.3 %collective-permute-done.5.other = f32[16,8,256]{2,1,0:T(8,128)S(1)} collective-permute-done((f32[16,8,256]{2,1,0:T(8,128)S(1)}, f32[16,8,256]{2,1,0:T(8,128)S(1)}, u32[]{:S(2)}, u32[]{:S(2)}) %collective-permute-start.5) | collective-permute-done | bytes 131104 | tf_op jit(solution)/shard_map/ppermute | solution.py:181
  62.8 19.0 %all_to_all.10.pieces = f32[16,32,256]{2,1,0:T(8,128)S(1)} all-to-all(f32[16,32,256]{2,1,0:T(8,128)S(1)} %bitcast.11), channel_id=1, replica_groups=mesh['y'=4,'near'=2,'core'=2,'x'=4,'far'=4] {'y','x'}, dimensions={0} | all-to-all | bytes 1048576 | tf_op jit(solution)/shard_map/all_to_all | solution.py:186
  81.9 15.1 %all_to_all.11 = f32[16,8,256]{2,1,0:T(8,128)S(1)} all-to-all(f32[16,8,256]{2,1,0:T(8,128)S(1)} %shard_map.57), channel_id=1, replica_groups=mesh['y'=4,'near'=2,'core'=2,'x'=4,'far'=4] {'near','far','core'}, dimensions={0} | all-to-all | bytes 262144 | tf_op jit(solution)/shard_map/all_to_all | solution.py:190
  97.0 0.6 bitcast_reduce_fusion
  97.6 0.0 collective-permute-done.4.gift
  97.6 2.0 %shard_map.55 = f32[256,1024]{1,0:T(8,128)} custom-call(f32[256,1024]{1,0:T(8,128)} %get-tuple-element.14.near, f32[256,1024]{1,0:T(8,128)S(1)} %collective-permute-done.4.gift), custom_call_target="tpu_custom_call" | custom-call | flops 1048576 | bytes 1048576 | tf_op jit(solution)/shard_map/pallas_call | solution.py:126
  (4 shorter events, 0.1 us)
Async XLA Ops:
  0.6 53.9 %collective-permute-start.3 = (f32[256,1024]{1,0:T(8,128)}, f32[256,1024]{1,0:T(8,128)S(1)}, u32[]{:S(2)}, u32[]{:S(2)}) collective-permute-start(f32[256,1024]{1,0:T(8,128)} %bitcast.12), channel_id=1, source_target_pairs={{0,3},{1,0},{2,1},{3,2},{16,17},{17,18},{18,19},{19,16},{4,7},{5,4... | collective-permute-start | bytes 3145736 | tf_op jit(solution)/shard_map/ppermute | solution.py:26
  4.5 50.0 %collective-permute-start.2 = (f32[256,1024]{1,0:T(8,128)}, f32[256,1024]{1,0:T(8,128)S(1)}, u32[]{:S(2)}, u32[]{:S(2)}) collective-permute-start(f32[256,1024]{1,0:T(8,128)} %bitcast.13), channel_id=1, source_target_pairs={{0,1},{1,2},{2,3},{3,0},{16,19},{17,16},{18,17},{19,18},{4,5},{5,6... | collective-permute-start | bytes 3145736 | tf_op jit(solution)/shard_map/ppermute | solution.py:26
  7.6 27.4 %collective-permute-start.1 = (f32[1]{0:T(128)}, f32[1]{0:T(128)}, u32[]{:S(2)}, u32[]{:S(2)}) collective-permute-start(f32[1]{0:T(128)} %param.4), channel_id=1, source_target_pairs={{0,3},{1,0},{2,1},{3,2},{16,17},{17,18},{18,19},{19,16},{4,7},{5,4... | collective-permute-start | bytes 20 | tf_op jit(solution)/shard_map/ppermute | solution.py:26
  8.7 44.5 %collective-permute-start = (f32[1]{0:T(128)}, f32[1]{0:T(128)}, u32[]{:S(2)}, u32[]{:S(2)}) collective-permute-start(f32[1]{0:T(128)} %param.4), channel_id=1, source_target_pairs={{0,1},{1,2},{2,3},{3,0},{16,19},{17,16},{18,17},{19,18},{4,5},{5,6... | collective-permute-start | bytes 20 | tf_op jit(solution)/shard_map/ppermute | solution.py:26
  11.9 0.7 copy-start.1
  12.6 1.2 %copy-start = (f32[1,256,1024]{2,1,0:T(8,128)S(1)}, f32[1,256,1024]{2,1,0:T(8,128)}, u32[]{:S(2)}) copy-start(f32[1,256,1024]{2,1,0:T(8,128)} %param.3) | copy-start | bytes 3145732
  59.1 38.6 %collective-permute-start.4 = (f32[256,1024]{1,0:T(8,128)}, f32[256,1024]{1,0:T(8,128)S(1)}, u32[]{:S(2)}, u32[]{:S(2)}) collective-permute-start(f32[256,1024]{1,0:T(8,128)} %get-tuple-element.15), channel_id=1, source_target_pairs={{0,1},{1,2},{2,3},{3,0},{16,19},{17,16},{18,17},{19,18},{4,5},{5,6... | collective-permute-start | bytes 3145736 | tf_op jit(solution)/shard_map/ppermute | solution.py:26
  61.4 1.3 %collective-permute-start.5 = (f32[16,8,256]{2,1,0:T(8,128)S(1)}, f32[16,8,256]{2,1,0:T(8,128)S(1)}, u32[]{:S(2)}, u32[]{:S(2)}) collective-permute-start(f32[16,8,256]{2,1,0:T(8,128)S(1)} %get-tuple-element.17), channel_id=1, source_target_pairs={{0,16},{16,0},{1,17},{17,1},{2,18},{18,2},{3,19},{19,3},{4,20},{20... | collective-permute-start | bytes 393224 | tf_op jit(solution)/shard_map/ppermute | solution.py:181

commit v18 on v15

--- a/solution.py
+++ b/solution.py
@@ -15,7 +15,7 @@
 ROWS = ((1,), (1,))
 PLAIN = ((1,), (0,))
 MIB = 1 << 20
-EARLY = 144
+EARLY = 112
 
 
 def role_shift(value, step):
@@ -50,7 +50,7 @@
 
 
 def pair_kernel(upper, e_own, e_one, e_two, pairs, oh, ol, one, two, *refs):
-    keep, send, gift, later, near, buf, total, dens, sems = refs
+    keep, send, gift, later, buf, dens, sems = refs
     o, a, b = (oh[...], ol[...]), split(one[...]), split(two[...])
     mine, first, second = e_own[0:1, 0:1], e_one[0:1, 0:1], e_two[0:1, 0:1]
     t = mm(b, a, ROWS) / (first + second - pairs[...])
@@ -58,16 +58,13 @@
     buf[...] = mm(s, a, PLAIN)
     out = [
         pltpu.make_async_copy(buf.at[:EARLY, :], gift, sems.at[0]),
-        pltpu.make_async_copy(buf.at[EARLY:, :], later, sems.at[2]),
+        pltpu.make_async_copy(buf.at[EARLY:, :], later, sems.at[1]),
     ]
     for copy in out:
         copy.start()
     t_one = mm(o, a, ROWS) / (mine + first - pairs[...])
     t_two = mm(o, b, ROWS) / (mine + second - pairs[...])
     s_one, s_two = spin(t_one), spin(t_two)
-    total[...] = mm(s_one, a, PLAIN) + mm(s_two, b, PLAIN)
-    out.append(pltpu.make_async_copy(total, near, sems.at[1]))
-    out[2].start()
     dens[...] = (
         mm(split(t), s, ROWS)
         + mm(split(t_one), s_one, ROWS)
@@ -83,6 +80,17 @@
         copy.wait()
 
 
+def near_kernel(e_own, e_one, e_two, pairs, oh, ol, one, two, near, total, sem):
+    o, a, b = (oh[...], ol[...]), split(one[...]), split(two[...])
+    mine, first, second = e_own[0:1, 0:1], e_one[0:1, 0:1], e_two[0:1, 0:1]
+    s_one = spin(mm(o, a, ROWS) / (mine + first - pairs[...]))
+    s_two = spin(mm(o, b, ROWS) / (mine + second - pairs[...]))
+    total[...] = mm(s_one, a, PLAIN) + mm(s_two, b, PLAIN)
+    out = pltpu.make_async_copy(total, near, sem)
+    out.start()
+    out.wait()
+
+
 def join_kernel(keep, other, copies):
     for at in range(keep.shape[0]):
         piece = keep[at] + other[at]
@@ -91,7 +99,7 @@
 
 
 def sum_kernel(near, gift, later, grad, mine, other, sems):
-    cuts = ((0, EARLY), (EARLY, EARLY + 56), (EARLY + 56, mine.shape[0]))
+    cuts = ((0, EARLY), (EARLY, EARLY + 72), (EARLY + 72, mine.shape[0]))
     copies = []
     for at, (low, high) in enumerate(cuts):
         rows = pl.ds(low, high - low)
@@ -168,15 +176,15 @@
     )
     piece = (16, 8, v)
     full = pltpu.VMEM((v, n), F32)
-    keep, send, gift, later, near = call(
+    keep, send, gift, later = call(
         pair_kernel,
-        (piece, piece, (EARLY, n), (v - EARLY, n), (v, n)),
-        [full] * 2 + [pltpu.VMEM((v, v), F32), pltpu.SemaphoreType.DMA((3,))],
+        (piece, piece, (EARLY, n), (v - EARLY, n)),
+        [full, pltpu.VMEM((v, v), F32), pltpu.SemaphoreType.DMA((2,))],
         14,
         1 << 31,
         (upper, s_own, s_one, s_two, pairs, oh, ol, one, two),
         [VMEM] * 9,
-        (VMEM, VMEM, HBM, HBM, HBM),
+        (VMEM, VMEM, HBM, HBM),
     )
     other = lax.ppermute(send, "core", [(0, 1), (1, 0)])
     gift = role_shift(gift, 1)
@@ -205,6 +213,16 @@
         copies, ("y", "core"), split_axis=0, concat_axis=0, tiled=True
     )
     density = jnp.sum(copies.reshape(4, 16, v), axis=0)
+    (near,) = call(
+        near_kernel,
+        ((v, n),),
+        [full, pltpu.SemaphoreType.DMA],
+        14,
+        1 << 31,
+        (s_own, s_one, s_two, pairs, oh, ol, one, two),
+        [VMEM] * 8,
+        (HBM,),
+    )
     (grad,) = call(
         sum_kernel,
         ((v, n),),

time: 102 us -> 104 us (1.020)
  waiting for transfers between devices: 58.4 us -> 48.2 us
  starting transfers between devices: 30.1 us -> 36.8 us
  local copies, waits for them, and re-layouts: 3.1 us -> 6.15 us
  Pallas kernels: 8.45 us -> 10.1 us
    all_to_all x1, waiting for transfers between devices: 16.7 us -> 3.89 us  [body(): lax.all_to_all(mine.reshape(32, 8, v), ('x', 'near', 'far'), split_axis=0...]
    ppermute x6, waiting for transfers between devices: 39 us -> 43.4 us  [role_shift(): return lax.ppermute(value, ('core', 'far'), pairs)]
    unnamed x6 -> x16, local copies, waits for them, and re-layouts: 1.9 us -> 4.94 us
    ppermute x1, starting transfers between devices: 0.54 us -> 3.5 us  [body(): other = lax.ppermute(send, 'core', [(0, 1), (1, 0)])]
    all_to_all x1, starting transfers between devices: 5.25 us -> 8.03 us  [body(): lax.all_to_all(copies, ('y', 'core'), split_axis=0, concat_axis=0, tiled=...]
    all_to_all x1, waiting for transfers between devices: 2.62 us -> 0.01 us  [body(): lax.all_to_all(copies, ('y', 'core'), split_axis=0, concat_axis=0, tiled=...]
    all_to_all x1, starting transfers between devices: 7.06 us -> 9.33 us  [body(): lax.all_to_all(mine.reshape(32, 8, v), ('x', 'near', 'far'), split_axis=0...]
    pallas_call x5 -> x6, Pallas kernels: 8.45 us -> 10.1 us  [call(): pl.pallas_call(kernel, out_shape=tuple((pltpu.HBM(s, F32) if spec is HBM...]
  transfers between devices with their start and end apart: 9 -> 9, of which waited for: 4 -> 4; matrix products, arithmetic and copies ran while one was open for 0% -> 0% of each run, Pallas kernels for 4% -> 6%
where the time goes in v18:
time: 104 us; the launch traced here: 103 us
  waiting for transfers between devices  48.2 us (46%)
  starting transfers between devices  36.8 us (35%)
  Pallas kernels  10.1 us (10%)
  local copies, waits for them, and re-layouts  6.15 us (6%)
  between operations  1.5 us (1%)
    ppermute x6, waiting for transfers between devices, role_shift(): return lax.ppermute(value, ('core', 'far'), pairs)  43.4 us
    ppermute x6, starting transfers between devices, role_shift(): return lax.ppermute(value, ('core', 'far'), pairs)  16 us
    pallas_call x6, Pallas kernels, call(): pl.pallas_call(kernel, out_shape=tuple((pltpu.HBM(s, F32) if spec is HBM...  10.1 us
    all_to_all x1, starting transfers between devices, body(): lax.all_to_all(mine.reshape(32, 8, v), ('x', 'near', 'far'), split_axis=0...  9.33 us
    all_to_all x1, starting transfers between devices, body(): lax.all_to_all(copies, ('y', 'core'), split_axis=0, concat_axis=0, tiled=...  8.03 us
    unnamed x16, local copies, waits for them, and re-layouts  4.94 us
    all_to_all x1, waiting for transfers between devices, body(): lax.all_to_all(mine.reshape(32, 8, v), ('x', 'near', 'far'), split_axis=0...  3.89 us
    ppermute x1, starting transfers between devices, body(): other = lax.ppermute(send, 'core', [(0, 1), (1, 0)])  3.5 us
  transfers between devices with their start and end apart: 9, of which 4 were waited for; matrix products, arithmetic and copies ran while one was open for 0% of the time, Pallas kernels for 6%

profile of v18, /device:TPU:1, one launch (start us, length us, event | category | flops | bytes accessed | tf_op | source)
XLA Modules:
  0.0 103.5 jit_solution(17044160523806931106)
XLA Ops:
  0.6 6.9 %collective-permute-start.2 = (f32[256,1024]{1,0:T(8,128)}, f32[256,1024]{1,0:T(8,128)S(1)}, u32[]{:S(2)}, u32[]{:S(2)}) collective-permute-start(f32[256,1024]{1,0:T(8,128)} %bitcast.11), channel_id=1, source_target_pairs={{0,1},{1,2},{2,3},{3,0},{16,19},{17,16},{18,17},{19,18},{4,5},{5,6... | collective-permute-start | bytes 3145736 | tf_op jit(solution)/shard_map/ppermute | solution.py:27
  7.5 0.0 collective-permute-start.3
  7.5 3.6 %collective-permute-start = (f32[1]{0:T(128)}, f32[1]{0:T(128)}, u32[]{:S(2)}, u32[]{:S(2)}) collective-permute-start(f32[1]{0:T(128)} %param.4), channel_id=1, source_target_pairs={{0,1},{1,2},{2,3},{3,0},{16,19},{17,16},{18,17},{19,18},{4,5},{5,6... | collective-permute-start | bytes 20 | tf_op jit(solution)/shard_map/ppermute | solution.py:27
  11.1 0.0 collective-permute-start.1
  11.9 0.7 copy-done.1
  12.5 1.2 %copy-done = f32[1,256,1024]{2,1,0:T(8,128)S(1)} copy-done((f32[1,256,1024]{2,1,0:T(8,128)S(1)}, f32[1,256,1024]{2,1,0:T(8,128)}, u32[]{:S(2)}) %copy-start) | copy-done | bytes 1048600
  13.8 0.3 shard_map.53
  14.1 36.2 %collective-permute-done = f32[1]{0:T(128)} collective-permute-done((f32[1]{0:T(128)}, f32[1]{0:T(128)}, u32[]{:S(2)}, u32[]{:S(2)}) %collective-permute-start) | collective-permute-done | bytes 36 | tf_op jit(solution)/shard_map/ppermute | solution.py:27
  50.3 0.0 collective-permute-done.1
  50.3 0.0 collective-permute-done.2.one
  50.3 0.0 collective-permute-done.3.two
  50.3 0.6 broadcast_in_dim.25.e_one
  50.9 0.6 broadcast_in_dim.26.e_two
  51.6 3.2 %shard_map.55 = (f32[16,8,256]{2,1,0:T(8,128)S(1)}, f32[16,8,256]{2,1,0:T(8,128)S(1)}, f32[112,1024]{1,0:T(8,128)}, f32[144,1024]{1,0:T(8,128)}) custom-call(f32[8,256]{1,0:T(8,128)S(1)} %broadcast_in_dim.28.upper, f32[8,128]{1,0:T(8,128)S(1)} %broadcast_in_dim.24.e_own, f32[8,128]{1,0:T(8,128)S(1)} %broadcast_in_dim.25.e_one, ...), custom_call_target="tpu_custom_call" | custom-call | flops 2147483648 | bytes 1048576 | tf_op jit(solution)/shard_map/pallas_call | solution.py:135
  54.8 3.5 %collective-permute-start.6 = (f32[16,8,256]{2,1,0:T(8,128)S(1)}, f32[16,8,256]{2,1,0:T(8,128)S(1)}, u32[]{:S(2)}, u32[]{:S(2)}) collective-permute-start(f32[16,8,256]{2,1,0:T(8,128)S(1)} %get-tuple-element.15), channel_id=1, source_target_pairs={{0,16},{16,0},{1,17},{17,1},{2,18},{18,2},{3,19},{19,3},{4,20},{20... | collective-permute-start | bytes 393224 | tf_op jit(solution)/shard_map/ppermute | solution.py:189
  58.3 1.0 collective-permute-done.6.other
  59.3 0.7 shard_map.57
  60.0 9.3 %all-to-all-start = ((f32[32,8,256]{2,1,0:T(8,128)}), f32[32,8,256]{2,1,0:T(8,128)S(1)}, u32[]{:S(2)}, u32[]{:S(2)}) async-start(f32[32,8,256]{2,1,0:T(8,128)} %bitcast.6), calls=%async_computation | async-start | bytes 524288 | tf_op jit(solution)/shard_map/all_to_all | solution.py:202
  69.4 3.4 %collective-permute-start.5 = (f32[144,1024]{1,0:T(8,128)}, f32[144,1024]{1,0:T(8,128)S(1)}, u32[]{:S(2)}, u32[]{:S(2)}) collective-permute-start(f32[144,1024]{1,0:T(8,128)} %get-tuple-element.13), channel_id=1, source_target_pairs={{0,1},{1,2},{2,3},{3,0},{16,19},{17,16},{18,17},{19,18},{4,5},{5,6... | collective-permute-start | bytes 1769480 | tf_op jit(solution)/shard_map/ppermute | solution.py:27
  72.8 2.1 %collective-permute-start.4 = (f32[112,1024]{1,0:T(8,128)}, f32[112,1024]{1,0:T(8,128)S(1)}, u32[]{:S(2)}, u32[]{:S(2)}) collective-permute-start(f32[112,1024]{1,0:T(8,128)} %get-tuple-element.12), channel_id=1, source_target_pairs={{0,1},{1,2},{2,3},{3,0},{16,19},{17,16},{18,17},{19,18},{4,5},{5,6... | collective-permute-start | bytes 1376264 | tf_op jit(solution)/shard_map/ppermute | solution.py:27
  74.9 3.9 %all-to-all-done.pieces = f32[32,8,256]{2,1,0:T(8,128)S(1)} async-done(((f32[32,8,256]{2,1,0:T(8,128)}), f32[32,8,256]{2,1,0:T(8,128)S(1)}, u32[]{:S(2)}, u32[]{:S(2)}) %all-to-all-start) | async-done | bytes 262176 | tf_op jit(solution)/shard_map/all_to_all | solution.py:202
  78.8 0.7 shard_map.58
  79.4 8.0 %all-to-all-start.1 = ((f32[8,8,256]{2,1,0:T(8,128)}), f32[8,8,256]{2,1,0:T(8,128)S(1)}, u32[]{:S(2)}, u32[]{:S(2)}) async-start(f32[8,8,256]{2,1,0:T(8,128)} %shard_map.58), calls=%async_computation.1 | async-start | bytes 131072 | tf_op jit(solution)/shard_map/all_to_all | solution.py:212
  87.5 1.0 %copy-done.3 = bf16[256,1024]{1,0:T(8,128)(2,1)S(1)} copy-done((bf16[256,1024]{1,0:T(8,128)(2,1)S(1)}, bf16[256,1024]{1,0:T(8,128)(2,1)}, u32[]{:S(2)}) %copy-start.3) | copy-done | bytes 524312
  88.5 1.0 %copy-done.5 = bf16[256,1024]{1,0:T(8,128)(2,1)S(1)} copy-done((bf16[256,1024]{1,0:T(8,128)(2,1)S(1)}, bf16[256,1024]{1,0:T(8,128)(2,1)}, u32[]{:S(2)}) %copy-start.5) | copy-done | bytes 524312
  89.6 0.9 copy-done.7
  90.5 3.0 %shard_map.54.near = f32[256,1024]{1,0:T(8,128)} custom-call(f32[8,128]{1,0:T(8,128)S(1)} %broadcast_in_dim.24.e_own, f32[8,128]{1,0:T(8,128)S(1)} %broadcast_in_dim.25.e_one, f32[8,128]{1,0:T(8,128)S(1)} %broadcast_in_dim.26.e_two, f32[256,256]{1,0:T(8,128)S(1)} %copy-done.7, bf16[256,1024]{1,0:T(8,128)(2,1)S(1)} %copy-done.3, ...), custom_call_target="tpu_custom_call" | custom-call | flops 2147483648 | bytes 1048576 | tf_op jit(solution)/shard_map/pallas_call | solution.py:135
  93.5 7.1 %collective-permute-done.4.gift = f32[112,1024]{1,0:T(8,128)S(1)} collective-permute-done((f32[112,1024]{1,0:T(8,128)}, f32[112,1024]{1,0:T(8,128)S(1)}, u32[]{:S(2)}, u32[]{:S(2)}) %collective-permute-start.4) | collective-permute-done | bytes 458784 | tf_op jit(solution)/shard_map/ppermute | solution.py:27
  100.7 0.0 collective-permute-done.5.later
  100.7 2.2 %shard_map.56 = f32[256,1024]{1,0:T(8,128)} custom-call(f32[256,1024]{1,0:T(8,128)} %shard_map.54.near, f32[112,1024]{1,0:T(8,128)S(1)} %collective-permute-done.4.gift, f32[144,1024]{1,0:T(8,128)S(1)} %collective-permute-done.5.later), custom_call_target="tpu_custom_call" | custom-call | flops 1048576 | bytes 1048576 | tf_op jit(solution)/shard_map/pallas_call | solution.py:135
  102.8 0.0 all-to-all-done.1
  102.9 0.6 bitcast_reduce_fusion
  (13 shorter events, 0.0 us)
Async XLA Ops:
  0.6 49.7 %collective-permute-start.2 = (f32[256,1024]{1,0:T(8,128)}, f32[256,1024]{1,0:T(8,128)S(1)}, u32[]{:S(2)}, u32[]{:S(2)}) collective-permute-start(f32[256,1024]{1,0:T(8,128)} %bitcast.11), channel_id=1, source_target_pairs={{0,1},{1,2},{2,3},{3,0},{16,19},{17,16},{18,17},{19,18},{4,5},{5,6... | collective-permute-start | bytes 3145736 | tf_op jit(solution)/shard_map/ppermute | solution.py:27
  7.5 42.8 %collective-permute-start.3 = (f32[256,1024]{1,0:T(8,128)}, f32[256,1024]{1,0:T(8,128)S(1)}, u32[]{:S(2)}, u32[]{:S(2)}) collective-permute-start(f32[256,1024]{1,0:T(8,128)} %bitcast.12), channel_id=1, source_target_pairs={{0,3},{1,0},{2,1},{3,2},{16,17},{17,18},{18,19},{19,16},{4,7},{5,4... | collective-permute-start | bytes 3145736 | tf_op jit(solution)/shard_map/ppermute | solution.py:27
  7.5 42.8 %collective-permute-start = (f32[1]{0:T(128)}, f32[1]{0:T(128)}, u32[]{:S(2)}, u32[]{:S(2)}) collective-permute-start(f32[1]{0:T(128)} %param.4), channel_id=1, source_target_pairs={{0,1},{1,2},{2,3},{3,0},{16,19},{17,16},{18,17},{19,18},{4,5},{5,6... | collective-permute-start | bytes 20 | tf_op jit(solution)/shard_map/ppermute | solution.py:27
  11.1 39.2 %collective-permute-start.1 = (f32[1]{0:T(128)}, f32[1]{0:T(128)}, u32[]{:S(2)}, u32[]{:S(2)}) collective-permute-start(f32[1]{0:T(128)} %param.4), channel_id=1, source_target_pairs={{0,3},{1,0},{2,1},{3,2},{16,17},{17,18},{18,19},{19,16},{4,7},{5,4... | collective-permute-start | bytes 20 | tf_op jit(solution)/shard_map/ppermute | solution.py:27
  11.8 0.7 copy-start.1
  12.5 1.2 %copy-start = (f32[1,256,1024]{2,1,0:T(8,128)S(1)}, f32[1,256,1024]{2,1,0:T(8,128)}, u32[]{:S(2)}) copy-start(f32[1,256,1024]{2,1,0:T(8,128)} %param.3) | copy-start | bytes 3145732
  14.1 40.7 %copy-start.2 = (bf16[256,1024]{1,0:T(8,128)(2,1)}, bf16[256,1024]{1,0:T(8,128)(2,1)S(1)}, u32[]{:S(2)}) copy-start(bf16[256,1024]{1,0:T(8,128)(2,1)S(1)} %get-tuple-element.10.oh) | copy-start | bytes 1572868
  14.1 40.7 %copy-start.4 = (bf16[256,1024]{1,0:T(8,128)(2,1)}, bf16[256,1024]{1,0:T(8,128)(2,1)S(1)}, u32[]{:S(2)}) copy-start(bf16[256,1024]{1,0:T(8,128)(2,1)S(1)} %get-tuple-element.11.ol) | copy-start | bytes 1572868
  14.1 40.7 %copy-start.6 = (f32[256,256]{1,0:T(8,128)}, f32[256,256]{1,0:T(8,128)S(1)}, u32[]{:S(2)}) copy-start(f32[256,256]{1,0:T(8,128)S(1)} %get-tuple-element.9.pairs) | copy-start | bytes 786436
  54.8 4.5 %collective-permute-start.6 = (f32[16,8,256]{2,1,0:T(8,128)S(1)}, f32[16,8,256]{2,1,0:T(8,128)S(1)}, u32[]{:S(2)}, u32[]{:S(2)}) collective-permute-start(f32[16,8,256]{2,1,0:T(8,128)S(1)} %get-tuple-element.15), channel_id=1, source_target_pairs={{0,16},{16,0},{1,17},{17,1},{2,18},{18,2},{3,19},{19,3},{4,20},{20... | collective-permute-start | bytes 393224 | tf_op jit(solution)/shard_map/ppermute | solution.py:189
  60.0 18.7 %all-to-all-start = ((f32[32,8,256]{2,1,0:T(8,128)}), f32[32,8,256]{2,1,0:T(8,128)S(1)}, u32[]{:S(2)}, u32[]{:S(2)}) async-start(f32[32,8,256]{2,1,0:T(8,128)} %bitcast.6), calls=%async_computation | async-start | bytes 524288 | tf_op jit(solution)/shard_map/all_to_all | solution.py:202
  69.4 31.3 %collective-permute-start.5 = (f32[144,1024]{1,0:T(8,128)}, f32[144,1024]{1,0:T(8,128)S(1)}, u32[]{:S(2)}, u32[]{:S(2)}) collective-permute-start(f32[144,1024]{1,0:T(8,128)} %get-tuple-element.13), channel_id=1, source_target_pairs={{0,1},{1,2},{2,3},{3,0},{16,19},{17,16},{18,17},{19,18},{4,5},{5,6... | collective-permute-start | bytes 1769480 | tf_op jit(solution)/shard_map/ppermute | solution.py:27
  72.8 27.8 %collective-permute-start.4 = (f32[112,1024]{1,0:T(8,128)}, f32[112,1024]{1,0:T(8,128)S(1)}, u32[]{:S(2)}, u32[]{:S(2)}) collective-permute-start(f32[112,1024]{1,0:T(8,128)} %get-tuple-element.12), channel_id=1, source_target_pairs={{0,1},{1,2},{2,3},{3,0},{16,19},{17,16},{18,17},{19,18},{4,5},{5,6... | collective-permute-start | bytes 1376264 | tf_op jit(solution)/shard_map/ppermute | solution.py:27
  79.4 23.4 %all-to-all-start.1 = ((f32[8,8,256]{2,1,0:T(8,128)}), f32[8,8,256]{2,1,0:T(8,128)S(1)}, u32[]{:S(2)}, u32[]{:S(2)}) async-start(f32[8,8,256]{2,1,0:T(8,128)} %shard_map.58), calls=%async_computation.1 | async-start | bytes 131072 | tf_op jit(solution)/shard_map/all_to_all | solution.py:212
  87.5 1.0 %copy-start.3 = (bf16[256,1024]{1,0:T(8,128)(2,1)S(1)}, bf16[256,1024]{1,0:T(8,128)(2,1)}, u32[]{:S(2)}) copy-start(bf16[256,1024]{1,0:T(8,128)(2,1)} %copy-done.2) | copy-start | bytes 1572868
  88.5 1.0 %copy-start.5 = (bf16[256,1024]{1,0:T(8,128)(2,1)S(1)}, bf16[256,1024]{1,0:T(8,128)(2,1)}, u32[]{:S(2)}) copy-start(bf16[256,1024]{1,0:T(8,128)(2,1)} %copy-done.4) | copy-start | bytes 1572868
  89.6 0.9 copy-start.7
